TPU v7x, 256 devices: a whole 4x4x8 slice. The times are simulated.
256 devices in a mesh: layer: 8 (over x, core), feat: 32 (over y, z).
Axes of the slice: x: 4, y: 4, z: 8, core: 2. Of those that a mesh axis runs over, the one named last changes fastest.
Arguments:
- gradient: bfloat16 [8, 2560, 2560], P('layer', 'feat'), may hold values from -3 to 3
- in_inverse: bfloat16 [8, 2560, 2560], P('layer', 'feat'), may hold values from -1 to 2.5, as said below
- in_coupling: bfloat16 [8, 2560, 2560], P('layer', 'feat'), may hold values from -0.125 to 0.125
- in_carry: bfloat16 [8, 2560, 2560], P('layer', 'feat'), may hold values from -0.125 to 0.125
- out_inverse: bfloat16 [8, 20, 128, 128], P('layer'), may hold values from -1 to 2.5, as said below
- out_coupling: bfloat16 [8, 20, 128, 128], P('layer'), may hold values from -0.5 to 0.5
Outputs:
- update: bfloat16 [8, 2560, 2560], P('layer', 'feat')
Inputs may be any that keep to these rules, and one draw needn't show every extreme that they name: `in_inverse`: symmetric in its last two dimensions. `out_inverse`: symmetric in its last two dimensions.
All inputs are finite; a program needn't handle non-finite values.
Results may differ from a plain program's by a relative error of at most 0.006.
Values may be sent and summed in bfloat16 or wider, within the bound.
No kernel may reach another device: no remote copies, remote signals or barrier semaphores. Data moves between devices by JAX's collectives and lax.ppermute only.
A program may use at most 64 MiB of HBM per device.

v0:
```python
import jax
import jax.numpy as jnp
from jax import lax
from jax.sharding import PartitionSpec as P


def from_behind(x, axis, by):
    size = lax.axis_size(axis)
    pairs = [(i, i + by) for i in range(size) if 0 <= i + by < size]
    return lax.ppermute(x, axis, pairs)


def block_apply(matrix, table, flipped):
    row_count = matrix.shape[0]
    blocks = table.shape[0]
    block_width = table.shape[1]
    grouped = matrix.reshape(row_count, blocks, block_width)
    pattern = "rnb,ncb->rnc" if flipped else "rnb,nbc->rnc"
    product = jnp.einsum(pattern, grouped, table, preferred_element_type=jnp.float32)
    return product.reshape(row_count, blocks * block_width)


def contract_rows(factor, piece):
    return jnp.dot(factor, piece, preferred_element_type=jnp.float32)


def local(gradient, in_inverse, in_coupling, in_carry, out_inverse, out_coupling):
    grad_rows = gradient[0]
    inverse_rows = in_inverse[0]
    coupling_rows = in_coupling[0]
    carry_rows = in_carry[0]
    out_inv = out_inverse[0]
    out_psi = out_coupling[0]
    psi_from_below = from_behind(out_psi, "layer", 1)
    from_above = from_behind(grad_rows, "layer", -1)
    near_rows = block_apply(from_above, out_psi, True).astype(jnp.bfloat16)
    coupled = contract_rows(coupling_rows, lax.all_gather(near_rows, "feat", axis=0, tiled=True))
    reduced = (grad_rows.astype(jnp.float32) - coupled).astype(jnp.bfloat16)
    piece = lax.all_gather(reduced, "feat", axis=0, tiled=True)
    whitened_acc = contract_rows(inverse_rows, piece)
    carried_acc = contract_rows(carry_rows, piece)
    whitened = whitened_acc.astype(jnp.bfloat16)
    carried = carried_acc.astype(jnp.bfloat16)
    local_term = block_apply(whitened, out_inv, False)
    middle = block_apply(carried, out_inv, False).astype(jnp.bfloat16)
    middle_from_below = from_behind(middle, "layer", 1)
    incoming = block_apply(middle_from_below, psi_from_below, False)
    return (local_term - incoming).astype(jnp.bfloat16)[None]


def solution(mesh):
    return jax.shard_map(
        local,
        mesh=mesh,
        in_specs=(
            P("layer", "feat", None),
            P("layer", "feat", None),
            P("layer", "feat", None),
            P("layer", "feat", None),
            P("layer", None, None, None),
            P("layer", None, None, None),
        ),
        out_specs=P("layer", "feat", None),
        check_vma=False,
    )
```

profile of v0, /device:TPU:2, one launch (start us, length us, event | category | flops | bytes accessed | tf_op | source)
XLA Modules:
  0.0 296.3 jit_solution(8207980276232798761)
XLA Ops:
  6.5 2.1 collective-permute-start
  8.6 5.8 %collective-permute-done = bf16[80,2560]{1,0:T(8,128)(2,1)S(1)} collective-permute-done((bf16[80,2560]{1,0:T(8,128)(2,1)}, bf16[80,2560]{1,0:T(8,128)(2,1)S(1)}, u32[]{:S(2)}, u32[]{:S(2)}) %collective-permute-start) | collective-permute-done | bytes 409632 | tf_op jit(solution)/shard_map/ppermute | solution.py:10
  14.4 1.7 fusion.6
  16.0 0.8 copy.41
  16.9 0.0 all-gather.3.cloned.1.call-update
  16.9 0.0 all-gather.5.cloned.1.call-start
  16.9 126.6 %all-gather.3.cloned.1.call-done = bf16[2560,2560]{1,0:T(8,128)(2,1)} async-done(((bf16[80,2560]{1,0:T(8,128)(2,1)}), bf16[2560,2560]{1,0:T(8,128)(2,1)}) %all-gather.3.cloned.1.call-update) | async-done | bytes 13107216 | tf_op jit(solution)/shard_map/all_gather | solution.py:37
  143.5 8.0 %fusion.1 = bf16[80,2560]{1,0:T(8,128)(2,1)} fusion(bf16[2560,2560]{1,0:T(8,128)(2,1)} %all-gather.3.cloned.1.call-done, bf16[1,80,2560]{2,1,0:T(8,128)(2,1)} %param.8, bf16[1,80,2560]{2,1,0:T(8,128)(2,1)} %param.6), kind=kOutput, calls=%fused_computation.2 | convolution fusion | flops 1049190400 | bytes 14336000 | tf_op jit(solution)/shard_map/dot_general | solution.py:24
  151.5 0.0 all-gather.5.cloned.1.call-update
  151.5 0.0 copy-done.4
  151.5 2.1 collective-permute-start.2
  153.6 117.4 %all-gather.5.cloned.1.call-done = bf16[2560,2560]{1,0:T(8,128)(2,1)} async-done(((bf16[80,2560]{1,0:T(8,128)(2,1)}), bf16[2560,2560]{1,0:T(8,128)(2,1)}) %all-gather.5.cloned.1.call-update) | async-done | bytes 13107216 | tf_op jit(solution)/shard_map/all_gather | solution.py:39
  271.0 7.3 %fusion.4 = bf16[10,20,8,128]{3,2,1,0:T(8,128)(2,1)S(1)} fusion(bf16[2560,2560]{1,0:T(8,128)(2,1)} %all-gather.5.cloned.1.call-done, bf16[1,80,2560]{2,1,0:T(8,128)(2,1)S(1)} %copy-done.2), kind=kOutput, calls=%fused_computation.10 | convolution fusion | flops 1048780800 | bytes 13926400 | tf_op jit(solution)/shard_map/dot_general | solution.py:24
  278.2 0.0 copy-done
  278.2 0.4 fusion.7
  278.6 0.1 copy.40
  278.7 1.9 collective-permute-start.1
  280.6 2.4 fusion.3
  283.0 0.4 fusion.9
  283.4 0.0 collective-permute-done.2
  283.4 4.6 %collective-permute-done.1 = bf16[80,2560]{1,0:T(8,128)(2,1)S(1)} collective-permute-done((bf16[80,2560]{1,0:T(8,128)(2,1)S(1)}, bf16[80,2560]{1,0:T(8,128)(2,1)S(1)}, u32[]{:S(2)}, u32[]{:S(2)}) %collective-permute-start.1) | collective-permute-done | bytes 409632 | tf_op jit(solution)/shard_map/ppermute | solution.py:10
  288.0 0.4 fusion.5
  288.3 0.1 copy.15
  288.5 1.0 convert_element_type.66
  (9 shorter events, 0.0 us)
Async XLA Ops:
  6.5 271.7 %copy-start = (bf16[1,20,128,128]{3,2,1,0:T(8,128)(2,1)S(1)}, bf16[1,20,128,128]{3,2,1,0:T(8,128)(2,1)}, u32[]{:S(2)}) copy-start(bf16[1,20,128,128]{3,2,1,0:T(8,128)(2,1)} %param.10) | copy-start | bytes 1966084
  6.5 145.0 %copy-start.4 = (bf16[1,20,128,128]{3,2,1,0:T(8,128)(2,1)S(1)}, bf16[1,20,128,128]{3,2,1,0:T(8,128)(2,1)}, u32[]{:S(2)}) copy-start(bf16[1,20,128,128]{3,2,1,0:T(8,128)(2,1)} %param.11) | copy-start | bytes 1966084
  6.5 264.4 %copy-start.2 = (bf16[1,80,2560]{2,1,0:T(8,128)(2,1)S(1)}, bf16[1,80,2560]{2,1,0:T(8,128)(2,1)}, u32[]{:S(2)}) copy-start(bf16[1,80,2560]{2,1,0:T(8,128)(2,1)} %param.9) | copy-start | bytes 1228804
  6.5 137.0 %all-gather.3.cloned.1.call-start = ((), (), s32[]{:S(2)}) async-start(), calls=%async_computation | async-start | bytes 13516800 | tf_op jit(solution)/shard_map/all_gather | solution.py:37
  6.5 7.8 %collective-permute-start = (bf16[80,2560]{1,0:T(8,128)(2,1)}, bf16[80,2560]{1,0:T(8,128)(2,1)S(1)}, u32[]{:S(2)}, u32[]{:S(2)}) collective-permute-start(bf16[80,2560]{1,0:T(8,128)(2,1)} %bitcast.72), channel_id=1, source_target_pairs={{32,0},{64,32},{96,64},{128,96},{160,128},{192,160},{224,192},{33,... | collective-permute-start | bytes 1228808 | tf_op jit(solution)/shard_map/ppermute | solution.py:10
  16.9 254.1 %all-gather.5.cloned.1.call-start = ((), (), s32[]{:S(2)}) async-start(), calls=%async_computation.1 | async-start | bytes 13516800 | tf_op jit(solution)/shard_map/all_gather | solution.py:39
  151.5 129.1 %copy-start.3 = (bf16[1,80,2560]{2,1,0:T(8,128)(2,1)S(1)}, bf16[1,80,2560]{2,1,0:T(8,128)(2,1)}, u32[]{:S(2)}) copy-start(bf16[1,80,2560]{2,1,0:T(8,128)(2,1)} %param.7) | copy-start | bytes 1228804
  151.5 131.9 %collective-permute-start.2 = (bf16[20,128,128]{2,1,0:T(8,128)(2,1)S(1)}, bf16[20,128,128]{2,1,0:T(8,128)(2,1)S(1)}, u32[]{:S(2)}, u32[]{:S(2)}) collective-permute-start(bf16[20,128,128]{2,1,0:T(8,128)(2,1)S(1)} %bitcast.70), channel_id=1, source_target_pairs={{0,32},{32,64},{64,96},{96,128},{128,160},{160,192},{192,224},{1,3... | collective-permute-start | bytes 1966088 | tf_op jit(solution)/shard_map/ppermute | solution.py:10
  271.0 9.7 %copy-start.1 = (bf16[2560,2560]{1,0:T(8,128)(2,1)S(1)}, bf16[2560,2560]{1,0:T(8,128)(2,1)}, u32[]{:S(2)}) copy-start(bf16[2560,2560]{1,0:T(8,128)(2,1)} %all-gather.5.cloned.1.call-done) | copy-start | bytes 39321604
  278.7 9.3 %collective-permute-start.1 = (bf16[80,2560]{1,0:T(8,128)(2,1)S(1)}, bf16[80,2560]{1,0:T(8,128)(2,1)S(1)}, u32[]{:S(2)}, u32[]{:S(2)}) collective-permute-start(bf16[80,2560]{1,0:T(8,128)(2,1)S(1)} %bitcast.71), channel_id=1, source_target_pairs={{0,32},{32,64},{64,96},{96,128},{128,160},{160,192},{192,224},{1,3... | collective-permute-start | bytes 1228808 | tf_op jit(solution)/shard_map/ppermute | solution.py:10
Sparse Core Ops, SparseCore 0:
  17.0 126.4 all-gather.2
  151.6 119.2 all-gather.4
where the time goes:
time: 297 us; the launch traced here: 296 us
  waiting for transfers between devices  254 us (86%)
  matrix products  20.4 us (7%)
  between operations  13.5 us (5%)
  starting transfers between devices  6.07 us (2%)
    all_gather x1, waiting for transfers between devices, local(): lax.all_gather(near_rows, 'feat', axis=0, tiled=True)  127 us
    all_gather x1, waiting for transfers between devices, local(): piece = lax.all_gather(reduced, 'feat', axis=0, tiled=True)  117 us
    dot_general x3, matrix products, contract_rows(): return jnp.dot(factor, piece, preferred_element_type=jnp.float32)  17.6 us
    ppermute x3, waiting for transfers between devices, from_behind(): return lax.ppermute(x, axis, pairs)  10.3 us
    ppermute x3, starting transfers between devices, from_behind(): return lax.ppermute(x, axis, pairs)  6.03 us
  transfers between devices with their start and end apart: 5, of which 4 were waited for; matrix products, arithmetic and copies ran while one was open for 4% of the time, Pallas kernels for 0%

commit v1 on v0

v1 whole, which is shorter than its diff:
```python
import jax
import jax.numpy as jnp
import numpy as np
from jax import lax
from jax.experimental import pallas as pl
from jax.experimental.pallas import tpu as pltpu
from jax.sharding import Mesh, PartitionSpec as P

BF = jnp.bfloat16
F32 = jnp.float32
BLK = 128
VMEM = pl.BlockSpec(memory_space=pltpu.VMEM)


def call(kernel, out, name, operands, scratch=(), mib=48, flops=0):
    moved = sum(x.size * x.dtype.itemsize for x in operands) + sum(x.size * x.dtype.itemsize for x in jax.tree.leaves(out))
    return pl.pallas_call(
        kernel,
        out_shape=out,
        in_specs=[VMEM] * len(operands),
        out_specs=jax.tree.map(lambda _: VMEM, out),
        scratch_shapes=list(scratch),
        compiler_params=pltpu.CompilerParams(vmem_limit_bytes=mib << 20),
        cost_estimate=pl.CostEstimate(flops=flops, bytes_accessed=moved, transcendentals=0),
        name=name,
    )(*operands)


def like(rows, cols, dtype):
    return jax.ShapeDtypeStruct((rows, cols), dtype)


def hop_z(x, by):
    size = lax.axis_size("z")
    return lax.ppermute(x, "z", [(i, (i + by) % size) for i in range(size)])


def hop_layer(x, by):
    size = lax.axis_size("layer")
    return lax.ppermute(x, "layer", [(i, i + by) for i in range(size) if 0 <= i + by < size])


def hop_y(x, layers, by):
    count, size = lax.axis_size("layer"), lax.axis_size("y")
    pairs = []
    for i in range(count):
        for j in range(size):
            if 0 <= i + layers < count:
                pairs.append((i * size + j, (i + layers) * size + (j + by) % size))
    return lax.ppermute(x, ("layer", "y"), pairs)


def after(x, *others):
    return lax.optimization_barrier((x, *others))[0]


def ring(tile):
    half = tile.shape[0] // 2
    up = down = tile
    pieces = [(tile, 0, 0)]
    for step in range(1, lax.axis_size("z") // 2):
        up, down = hop_z(up, 1), hop_z(down, -1)
        pieces += [(up, 0, -step), (down, 0, step)]
    far = lax.axis_size("z") // 2
    pieces += [(hop_z(up[:half], 1), 0, -far), (hop_z(down[half:], -1), half, far)]
    return pieces


def spread(refs, places, panel_ref, rows):
    y, z = lax.axis_index("y"), lax.axis_index("z")
    ys, zs = lax.axis_size("y"), lax.axis_size("z")
    for ref, (first, distance) in zip(refs, places, strict=True):
        source = lax.rem(z + (distance + zs), zs)
        for k in range(ref.shape[0] // rows):
            owner = lax.rem(y + (first // rows + k), ys)
            at = pl.multiple_of((owner * zs + source) * rows, 16)
            panel_ref[pl.ds(at, rows), :] = ref[pl.ds(k * rows, rows), :]


def near_tile(above, table):
    rows, width = above[0].shape
    blocks = width // BLK
    count = len(above)

    def kernel(*refs):
        table_ref, out_ref = refs[count:]
        y = lax.axis_index("y")
        for b in range(blocks):
            cols = pl.ds(b * BLK, BLK)
            block = table_ref[y * blocks + b]
            for k in range(count):
                near = lax.dot_general(refs[k][:, cols], block, (((1,), (1,)), ((), ())), preferred_element_type=F32)
                out_ref[pl.ds(k * rows, rows), cols] = near.astype(BF)

    return call(kernel, like(count * rows, width, BF), "near", [*above, table], flops=2 * count * rows * width * BLK)


def reduced_tile(pieces, factor, grads):
    rows, width = grads[0].shape
    tiles, places = [p[0] for p in pieces], [p[1:] for p in pieces]
    count, depth = len(tiles), factor.shape[1]

    def kernel(*refs):
        factor_ref, grad_refs = refs[count], refs[count + 1 : count + 1 + len(grads)]
        out_ref, panel_ref = refs[-2:]
        spread(refs[:count], places, panel_ref, rows)
        for at in range(0, width, 256):
            cols = pl.ds(at, min(256, width - at))
            coupled = jnp.dot(factor_ref[...], panel_ref[:, cols], preferred_element_type=F32)
            for k, grad_ref in enumerate(grad_refs):
                part = coupled[k * rows : (k + 1) * rows]
                out_ref[pl.ds(k * rows, rows), cols] = (grad_ref[:, cols].astype(F32) - part).astype(BF)

    return call(
        kernel,
        like(factor.shape[0], width, BF),
        "reduced",
        [*tiles, factor, *grads],
        [pltpu.VMEM((depth, width), BF)],
        flops=2 * factor.shape[0] * depth * width,
    )


def last_tiles(pieces, factors, table, shards):
    width = pieces[0][0].shape[1]
    tiles, places = [p[0] for p in pieces], [p[1:] for p in pieces]
    count, depth = len(tiles), factors.shape[1]
    rows = factors.shape[0] // (2 * shards)
    blocks = width // BLK

    def kernel(*refs):
        factors_ref, table_ref, local_ref, middle_ref, panel_ref = refs[count:]
        y = lax.axis_index("y")
        spread(refs[:count], places, panel_ref, rows)
        for at in range(0, width, 256):
            w = min(256, width - at)
            both = jnp.dot(factors_ref[...], panel_ref[:, pl.ds(at, w)], preferred_element_type=F32).astype(BF)
            for b in range(w // BLK):
                sub = pl.ds(at + b * BLK, BLK)
                block = table_ref[y * blocks + at // BLK + b]
                product = jnp.dot(both[:, b * BLK : (b + 1) * BLK], block, preferred_element_type=F32)
                for k in range(shards):
                    local_ref[pl.ds(k * rows, rows), sub] = product[2 * k * rows : (2 * k + 1) * rows]
                    middle_ref[pl.ds(k * rows, rows), sub] = product[(2 * k + 1) * rows : (2 * k + 2) * rows].astype(BF)

    return call(
        kernel,
        (like(shards * rows, width, F32), like(shards * rows, width, BF)),
        "last",
        [*tiles, factors, table],
        [pltpu.VMEM((depth, width), BF)],
        flops=2 * factors.shape[0] * depth * width,
    )


def update_tiles(local_term, middle, table, shards):
    rows, width = middle.shape[0] // shards, middle.shape[1]
    blocks = width // BLK

    def kernel(local_ref, middle_ref, table_ref, *out_refs):
        y = lax.axis_index("y")
        for b in range(blocks):
            cols = pl.ds(b * BLK, BLK)
            pushed = jnp.dot(middle_ref[:, cols], table_ref[y * blocks + b], preferred_element_type=F32)
            update = (local_ref[:, cols] - pushed).astype(BF)
            for k in range(shards):
                out_refs[k][:, cols] = update[k * rows : (k + 1) * rows]

    return call(
        kernel,
        tuple(like(rows, width, BF) for _ in range(shards)),
        "update",
        [local_term, middle, table],
        flops=2 * middle.size * BLK,
    )


def join_rows(pieces):
    rows, width = pieces[0].shape
    count = len(pieces)

    def kernel(*refs):
        y = lax.axis_index("y")
        for k in range(count):
            at = pl.multiple_of(lax.rem(y + (count - k), count) * width, BLK)
            refs[count][0, :, pl.ds(at, width)] = refs[k][...]

    return call(kernel, jax.ShapeDtypeStruct((1, rows, count * width), BF), "join", pieces)


def local(gradient, in_inverse, in_coupling, in_carry, out_inverse, out_coupling):
    shards = lax.axis_size("y")
    grad_rows = gradient[0]
    width = grad_rows.shape[1] // shards
    out_inv = out_inverse[0]
    out_psi = out_coupling[0]
    y = lax.axis_index("y")
    slices = [
        lax.dynamic_slice_in_dim(grad_rows, lax.rem(y + (shards - k), shards) * width, width, 1) for k in range(shards)
    ]
    above = [hop_y(slices[k], -1, -k) for k in range(shards)]
    near = near_tile(above, out_psi)
    near_ring = ring(near)
    first = near_ring[1][0], near_ring[2][0]
    second = near_ring[3][0], near_ring[4][0]
    grads = [slices[0]] + [hop_y(after(slices[k], near), 0, -k) for k in range(1, shards)]
    coupling = after(in_coupling[0], *first)
    factor = jnp.concatenate([coupling] + [hop_y(coupling, 0, -k) for k in range(1, shards)], 0)
    stacked = jnp.concatenate([in_inverse[0], in_carry[0]], 0)
    stacked = after(stacked, *second)
    factors = jnp.concatenate([stacked] + [hop_y(stacked, 0, -k) for k in range(1, shards)], 0)
    reduced = reduced_tile(near_ring, factor, grads)
    reduced_ring = ring(reduced)
    psi_below = hop_layer(after(out_psi, reduced), 1)
    local_term, middle = last_tiles(reduced_ring, factors, out_inv, shards)
    update = update_tiles(local_term, hop_layer(middle, 1), psi_below, shards)
    return join_rows([update[0]] + [hop_y(update[k], 0, k) for k in range(1, shards)])


def solution(mesh):
    layers = mesh.shape["layer"]
    fine = Mesh(np.asarray(mesh.devices).reshape(layers, 4, -1), ("layer", "y", "z"))
    rows = P("layer", ("y", "z"), None)
    table = P("layer", None, None, None)
    return jax.shard_map(
        local,
        mesh=fine,
        in_specs=(rows, rows, rows, rows, table, table),
        out_specs=rows,
        check_vma=False,
    )
```

time: 297 us -> 162 us (0.55)
  waiting for transfers between devices: 254 us -> 95.7 us
  starting transfers between devices: 6.07 us -> 50.8 us
  matrix products: 20.4 us -> 0 us
  between operations: 13.5 us -> 0.24 us
  Pallas kernels: 0 us -> 10.3 us
    all_gather x2 -> x0, waiting for transfers between devices: 244 us -> none  [the longest x1 127 us: local(): lax.all_gather(near_rows, 'feat', axis=0, tiled=True)]
    ppermute x3 -> x34, waiting for transfers between devices: 10.3 us -> 95.7 us  [the longest x16 48.2 us: hop_z(): return lax.ppermute(x, 'z', [(i, (i + by) % size) for i in range(size)])]
    ppermute x3 -> x34, starting transfers between devices: 6.03 us -> 50.8 us  [the longest x16 24.8 us: hop_z(): return lax.ppermute(x, 'z', [(i, (i + by) % size) for i in range(size)])]
    dot_general x7 -> x0, matrix products: 20.4 us -> none  [the longest x3 17.6 us: contract_rows(): return jnp.dot(factor, piece, preferred_element_type=jnp.float32)]
    pallas_call x0 -> x5, Pallas kernels: none -> 10.3 us  [call(): pl.pallas_call(kernel, out_shape=out, in_specs=[VMEM] * len(operands), ou...]
  transfers between devices with their start and end apart: 5 -> 34, of which waited for: 4 -> 21; matrix products, arithmetic and copies ran while one was open for 4% -> 1% of each run, Pallas kernels for 0% -> 4%
where the time goes in v1:
time: 162 us; the launch traced here: 161 us
  waiting for transfers between devices  95.7 us (59%)
  starting transfers between devices  50.8 us (31%)
  Pallas kernels  10.3 us (6%)
  local copies, waits for them, and re-layouts  2.33 us (1%)
  other arithmetic  1.94 us (1%)
    ppermute x16, waiting for transfers between devices, hop_z(): return lax.ppermute(x, 'z', [(i, (i + by) % size) for i in range(size)])  48.2 us
    ppermute x16, waiting for transfers between devices, hop_y(): return lax.ppermute(x, ('layer', 'y'), pairs)  40.1 us
    ppermute x16, starting transfers between devices, hop_z(): return lax.ppermute(x, 'z', [(i, (i + by) % size) for i in range(size)])  24.8 us
    ppermute x16, starting transfers between devices, hop_y(): return lax.ppermute(x, ('layer', 'y'), pairs)  22.2 us
    pallas_call x5, Pallas kernels, call(): pl.pallas_call(kernel, out_shape=out, in_specs=[VMEM] * len(operands), ou...  10.3 us
    ppermute x2, waiting for transfers between devices, hop_layer(): lax.ppermute(x, 'layer', [(i, i + by) for i in range(size) if 0 <= i + by...  7.33 us
    ppermute x2, starting transfers between devices, hop_layer(): lax.ppermute(x, 'layer', [(i, i + by) for i in range(size) if 0 <= i + by...  3.83 us
  transfers between devices with their start and end apart: 34, of which 21 were waited for; matrix products, arithmetic and copies ran while one was open for 1% of the time, Pallas kernels for 4%

profile of v1, /device:TPU:2, one launch (start us, length us, event | category | flops | bytes accessed | tf_op | source)
XLA Modules:
  0.0 161.2 jit_solution(18284998079423190106)
XLA Ops:
  3.1 5.0 %collective-permute-start.1 = (bf16[80,640]{1,0:T(8,128)(2,1)S(1)}, bf16[80,640]{1,0:T(8,128)(2,1)S(1)}, u32[]{:S(2)}, u32[]{:S(2)}) collective-permute-start(bf16[80,640]{1,0:T(8,128)(2,1)S(1)} %get-tuple-element.18), channel_id=1, source_target_pairs={{32,24},{40,0},{48,8},{56,16},{64,56},{72,32},{80,40},{88,48},{96,... | collective-permute-start | bytes 307208 | tf_op jit(solution)/shard_map/ppermute | solution.py:50
  12.1 3.4 %collective-permute-done.2.refs_2_ = bf16[80,640]{1,0:T(8,128)(2,1)S(1)} collective-permute-done((bf16[80,640]{1,0:T(8,128)(2,1)S(1)}, bf16[80,640]{1,0:T(8,128)(2,1)S(1)}, u32[]{:S(2)}, u32[]{:S(2)}) %collective-permute-start.2) | collective-permute-done | bytes 102432 | tf_op jit(solution)/shard_map/ppermute | solution.py:50
  21.4 4.0 %collective-permute-start.5 = (bf16[320,640]{1,0:T(8,128)(2,1)S(1)}, bf16[320,640]{1,0:T(8,128)(2,1)S(1)}, u32[]{:S(2)}, u32[]{:S(2)}) collective-permute-start(bf16[320,640]{1,0:T(8,128)(2,1)S(1)} %near.1.refs_0_), channel_id=1, source_target_pairs={{0,7},{1,0},{2,1},{3,2},{4,3},{5,4},{6,5},{7,6},{8,15},{9,8},{10,9... | collective-permute-start | bytes 1228808 | tf_op jit(solution)/shard_map/ppermute | solution.py:35
  25.5 10.0 %collective-permute-done.4.refs_1_ = bf16[320,640]{1,0:T(8,128)(2,1)S(1)} collective-permute-done((bf16[320,640]{1,0:T(8,128)(2,1)S(1)}, bf16[320,640]{1,0:T(8,128)(2,1)S(1)}, u32[]{:S(2)}, u32[]{:S(2)}) %collective-permute-start.4) | collective-permute-done | bytes 409632 | tf_op jit(solution)/shard_map/ppermute | solution.py:35
  35.4 3.5 %collective-permute-start.7 = (bf16[320,640]{1,0:T(8,128)(2,1)S(1)}, bf16[320,640]{1,0:T(8,128)(2,1)S(1)}, u32[]{:S(2)}, u32[]{:S(2)}) collective-permute-start(bf16[320,640]{1,0:T(8,128)(2,1)S(1)} %collective-permute-done.5.refs_2_), channel_id=1, source_target_pairs={{0,7},{1,0},{2,1},{3,2},{4,3},{5,4},{6,5},{7,6},{8,15},{9,8},{10,9... | collective-permute-start | bytes 1228808 | tf_op jit(solution)/shard_map/ppermute | solution.py:35
  38.9 9.2 %collective-permute-done.6.refs_3_ = bf16[320,640]{1,0:T(8,128)(2,1)S(1)} collective-permute-done((bf16[320,640]{1,0:T(8,128)(2,1)S(1)}, bf16[320,640]{1,0:T(8,128)(2,1)S(1)}, u32[]{:S(2)}, u32[]{:S(2)}) %collective-permute-start.6) | collective-permute-done | bytes 409632 | tf_op jit(solution)/shard_map/ppermute | solution.py:35
  48.1 3.5 %collective-permute-start.9 = (bf16[320,640]{1,0:T(8,128)(2,1)S(1)}, bf16[320,640]{1,0:T(8,128)(2,1)S(1)}, u32[]{:S(2)}, u32[]{:S(2)}) collective-permute-start(bf16[320,640]{1,0:T(8,128)(2,1)S(1)} %collective-permute-done.7.refs_4_), channel_id=1, source_target_pairs={{0,7},{1,0},{2,1},{3,2},{4,3},{5,4},{6,5},{7,6},{8,15},{9,8},{10,9... | collective-permute-start | bytes 1228808 | tf_op jit(solution)/shard_map/ppermute | solution.py:35
  53.7 6.3 %collective-permute-done.8.refs_5_ = bf16[320,640]{1,0:T(8,128)(2,1)S(1)} collective-permute-done((bf16[320,640]{1,0:T(8,128)(2,1)S(1)}, bf16[320,640]{1,0:T(8,128)(2,1)S(1)}, u32[]{:S(2)}, u32[]{:S(2)}) %collective-permute-start.8) | collective-permute-done | bytes 409632 | tf_op jit(solution)/shard_map/ppermute | solution.py:35
  62.0 2.3 %collective-permute-done.12 = bf16[80,2560]{1,0:T(8,128)(2,1)S(1)} collective-permute-done((bf16[80,2560]{1,0:T(8,128)(2,1)}, bf16[80,2560]{1,0:T(8,128)(2,1)S(1)}, u32[]{:S(2)}, u32[]{:S(2)}) %collective-permute-start.12) | collective-permute-done | bytes 409632 | tf_op jit(solution)/shard_map/ppermute | solution.py:50
  65.8 7.9 %collective-permute-done.14 = bf16[80,2560]{1,0:T(8,128)(2,1)S(1)} collective-permute-done((bf16[80,2560]{1,0:T(8,128)(2,1)}, bf16[80,2560]{1,0:T(8,128)(2,1)S(1)}, u32[]{:S(2)}, u32[]{:S(2)}) %collective-permute-start.14) | collective-permute-done | bytes 409632 | tf_op jit(solution)/shard_map/ppermute | solution.py:50
  76.9 3.7 %collective-permute-done.11.refs_8_ = bf16[160,640]{1,0:T(8,128)(2,1)S(1)} collective-permute-done((bf16[160,640]{1,0:T(8,128)(2,1)S(1)}, bf16[160,640]{1,0:T(8,128)(2,1)S(1)}, u32[]{:S(2)}, u32[]{:S(2)}) %collective-permute-start.11) | collective-permute-done | bytes 204832 | tf_op jit(solution)/shard_map/ppermute | solution.py:35
  82.4 3.2 %collective-permute-start.19 = (bf16[320,640]{1,0:T(8,128)(2,1)S(1)}, bf16[320,640]{1,0:T(8,128)(2,1)S(1)}, u32[]{:S(2)}, u32[]{:S(2)}) collective-permute-start(bf16[320,640]{1,0:T(8,128)(2,1)S(1)} %reduced.1.refs_0_), channel_id=1, source_target_pairs={{0,7},{1,0},{2,1},{3,2},{4,3},{5,4},{6,5},{7,6},{8,15},{9,8},{10,9... | collective-permute-start | bytes 1228808 | tf_op jit(solution)/shard_map/ppermute | solution.py:35
  85.6 8.4 %collective-permute-done.18.refs_1_ = bf16[320,640]{1,0:T(8,128)(2,1)S(1)} collective-permute-done((bf16[320,640]{1,0:T(8,128)(2,1)S(1)}, bf16[320,640]{1,0:T(8,128)(2,1)S(1)}, u32[]{:S(2)}, u32[]{:S(2)}) %collective-permute-start.18) | collective-permute-done | bytes 409632 | tf_op jit(solution)/shard_map/ppermute | solution.py:35
  94.1 3.3 %collective-permute-start.21 = (bf16[320,640]{1,0:T(8,128)(2,1)S(1)}, bf16[320,640]{1,0:T(8,128)(2,1)S(1)}, u32[]{:S(2)}, u32[]{:S(2)}) collective-permute-start(bf16[320,640]{1,0:T(8,128)(2,1)S(1)} %collective-permute-done.19.refs_2_), channel_id=1, source_target_pairs={{0,7},{1,0},{2,1},{3,2},{4,3},{5,4},{6,5},{7,6},{8,15},{9,8},{10,9... | collective-permute-start | bytes 1228808 | tf_op jit(solution)/shard_map/ppermute | solution.py:35
  97.4 2.4 %collective-permute-start.26 = (bf16[160,2560]{1,0:T(8,128)(2,1)S(1)}, bf16[160,2560]{1,0:T(8,128)(2,1)S(1)}, u32[]{:S(2)}, u32[]{:S(2)}) collective-permute-start(bf16[160,2560]{1,0:T(8,128)(2,1)S(1)} %pad_maximum_fusion.2), channel_id=1, source_target_pairs={{0,24},{8,0},{16,8},{24,16},{32,56},{40,32},{48,40},{56,48},{64,88... | collective-permute-start | bytes 2457608 | tf_op jit(solution)/shard_map/ppermute | solution.py:50
  100.7 4.0 %collective-permute-done.20.refs_3_ = bf16[320,640]{1,0:T(8,128)(2,1)S(1)} collective-permute-done((bf16[320,640]{1,0:T(8,128)(2,1)S(1)}, bf16[320,640]{1,0:T(8,128)(2,1)S(1)}, u32[]{:S(2)}, u32[]{:S(2)}) %collective-permute-start.20) | collective-permute-done | bytes 409632 | tf_op jit(solution)/shard_map/ppermute | solution.py:35
  104.8 3.2 %collective-permute-start.23 = (bf16[320,640]{1,0:T(8,128)(2,1)S(1)}, bf16[320,640]{1,0:T(8,128)(2,1)S(1)}, u32[]{:S(2)}, u32[]{:S(2)}) collective-permute-start(bf16[320,640]{1,0:T(8,128)(2,1)S(1)} %collective-permute-done.21.refs_4_), channel_id=1, source_target_pairs={{0,7},{1,0},{2,1},{3,2},{4,3},{5,4},{6,5},{7,6},{8,15},{9,8},{10,9... | collective-permute-start | bytes 1228808 | tf_op jit(solution)/shard_map/ppermute | solution.py:35
  108.0 6.6 %collective-permute-done.22.refs_5_ = bf16[320,640]{1,0:T(8,128)(2,1)S(1)} collective-permute-done((bf16[320,640]{1,0:T(8,128)(2,1)S(1)}, bf16[320,640]{1,0:T(8,128)(2,1)S(1)}, u32[]{:S(2)}, u32[]{:S(2)}) %collective-permute-start.22) | collective-permute-done | bytes 409632 | tf_op jit(solution)/shard_map/ppermute | solution.py:35
  120.2 2.4 %collective-permute-done.27 = bf16[160,2560]{1,0:T(8,128)(2,1)S(1)} collective-permute-done((bf16[160,2560]{1,0:T(8,128)(2,1)S(1)}, bf16[160,2560]{1,0:T(8,128)(2,1)S(1)}, u32[]{:S(2)}, u32[]{:S(2)}) %collective-permute-start.27) | collective-permute-done | bytes 819232 | tf_op jit(solution)/shard_map/ppermute | solution.py:50
  122.5 11.7 %collective-permute-done.28 = bf16[160,2560]{1,0:T(8,128)(2,1)S(1)} collective-permute-done((bf16[160,2560]{1,0:T(8,128)(2,1)S(1)}, bf16[160,2560]{1,0:T(8,128)(2,1)S(1)}, u32[]{:S(2)}, u32[]{:S(2)}) %collective-permute-start.28) | collective-permute-done | bytes 819232 | tf_op jit(solution)/shard_map/ppermute | solution.py:50
  136.0 6.9 %last.1 = (f32[320,640]{1,0:T(8,128)S(1)}, bf16[320,640]{1,0:T(8,128)(2,1)S(1)}) custom-call(bf16[320,640]{1,0:T(8,128)(2,1)S(1)} %reduced.1.refs_0_, bf16[320,640]{1,0:T(8,128)(2,1)S(1)} %collective-permute-done.18.refs_1_, bf16[320,640]{1,0:T(8,128)(2,1)S(1)} %collective-permute-done.19.refs_2_, bf16[320,640]{1,0:T(8,128)(2,1)S(1)} %collective-permute-done.20.refs_3_, ...), custom_call_target="tpu_custom_call" | custom-call | flops 2097152000 | bytes 8437760 | tf_op jit(solution)/shard_map/last/pallas_call | solution.py:17
  144.9 7.3 %collective-permute-done.29.middle_ref = bf16[320,640]{1,0:T(8,128)(2,1)S(1)} collective-permute-done((bf16[320,640]{1,0:T(8,128)(2,1)S(1)}, bf16[320,640]{1,0:T(8,128)(2,1)S(1)}, u32[]{:S(2)}, u32[]{:S(2)}) %collective-permute-start.29) | collective-permute-done | bytes 409632 | tf_op jit(solution)/shard_map/ppermute | solution.py:40
  152.6 2.6 %collective-permute-start.32 = (bf16[80,640]{1,0:T(8,128)(2,1)S(1)}, bf16[80,640]{1,0:T(8,128)(2,1)S(1)}, u32[]{:S(2)}, u32[]{:S(2)}) collective-permute-start(bf16[80,640]{1,0:T(8,128)(2,1)S(1)} %get-tuple-element.27), channel_id=1, source_target_pairs={{0,16},{8,24},{16,0},{24,8},{32,48},{40,56},{48,32},{56,40},{64,80... | collective-permute-start | bytes 307208 | tf_op jit(solution)/shard_map/ppermute | solution.py:50
  156.4 3.4 %collective-permute-done.31.refs_1_ = bf16[80,640]{1,0:T(8,128)(2,1)S(1)} collective-permute-done((bf16[80,640]{1,0:T(8,128)(2,1)S(1)}, bf16[80,640]{1,0:T(8,128)(2,1)S(1)}, u32[]{:S(2)}, u32[]{:S(2)}) %collective-permute-start.31) | collective-permute-done | bytes 102432 | tf_op jit(solution)/shard_map/ppermute | solution.py:50
  (69 shorter events, 36.7 us)
Async XLA Ops:
  1.1 11.0 %collective-permute-start = (bf16[80,640]{1,0:T(8,128)(2,1)S(1)}, bf16[80,640]{1,0:T(8,128)(2,1)S(1)}, u32[]{:S(2)}, u32[]{:S(2)}) collective-permute-start(bf16[80,640]{1,0:T(8,128)(2,1)S(1)} %get-tuple-element.31.refs_10_), channel_id=1, source_target_pairs={{32,0},{40,8},{48,16},{56,24},{64,32},{72,40},{80,48},{88,56},{96,... | collective-permute-start | bytes 307208 | tf_op jit(solution)/shard_map/ppermute | solution.py:50
  19.4 16.0 %collective-permute-start.4 = (bf16[320,640]{1,0:T(8,128)(2,1)S(1)}, bf16[320,640]{1,0:T(8,128)(2,1)S(1)}, u32[]{:S(2)}, u32[]{:S(2)}) collective-permute-start(bf16[320,640]{1,0:T(8,128)(2,1)S(1)} %near.1.refs_0_), channel_id=1, source_target_pairs={{0,1},{1,2},{2,3},{3,4},{4,5},{5,6},{6,7},{7,0},{8,9},{9,10},{10,1... | collective-permute-start | bytes 1228808 | tf_op jit(solution)/shard_map/ppermute | solution.py:35
  21.4 14.0 %collective-permute-start.5 = (bf16[320,640]{1,0:T(8,128)(2,1)S(1)}, bf16[320,640]{1,0:T(8,128)(2,1)S(1)}, u32[]{:S(2)}, u32[]{:S(2)}) collective-permute-start(bf16[320,640]{1,0:T(8,128)(2,1)S(1)} %near.1.refs_0_), channel_id=1, source_target_pairs={{0,7},{1,0},{2,1},{3,2},{4,3},{5,4},{6,5},{7,6},{8,15},{9,8},{10,9... | collective-permute-start | bytes 1228808 | tf_op jit(solution)/shard_map/ppermute | solution.py:35
  35.4 12.7 %collective-permute-start.6 = (bf16[320,640]{1,0:T(8,128)(2,1)S(1)}, bf16[320,640]{1,0:T(8,128)(2,1)S(1)}, u32[]{:S(2)}, u32[]{:S(2)}) collective-permute-start(bf16[320,640]{1,0:T(8,128)(2,1)S(1)} %collective-permute-done.4.refs_1_), channel_id=1, source_target_pairs={{0,1},{1,2},{2,3},{3,4},{4,5},{5,6},{6,7},{7,0},{8,9},{9,10},{10,1... | collective-permute-start | bytes 1228808 | tf_op jit(solution)/shard_map/ppermute | solution.py:35
  35.4 12.7 %collective-permute-start.7 = (bf16[320,640]{1,0:T(8,128)(2,1)S(1)}, bf16[320,640]{1,0:T(8,128)(2,1)S(1)}, u32[]{:S(2)}, u32[]{:S(2)}) collective-permute-start(bf16[320,640]{1,0:T(8,128)(2,1)S(1)} %collective-permute-done.5.refs_2_), channel_id=1, source_target_pairs={{0,7},{1,0},{2,1},{3,2},{4,3},{5,4},{6,5},{7,6},{8,15},{9,8},{10,9... | collective-permute-start | bytes 1228808 | tf_op jit(solution)/shard_map/ppermute | solution.py:35
  48.1 11.9 %collective-permute-start.8 = (bf16[320,640]{1,0:T(8,128)(2,1)S(1)}, bf16[320,640]{1,0:T(8,128)(2,1)S(1)}, u32[]{:S(2)}, u32[]{:S(2)}) collective-permute-start(bf16[320,640]{1,0:T(8,128)(2,1)S(1)} %collective-permute-done.6.refs_3_), channel_id=1, source_target_pairs={{0,1},{1,2},{2,3},{3,4},{4,5},{5,6},{6,7},{7,0},{8,9},{9,10},{10,1... | collective-permute-start | bytes 1228808 | tf_op jit(solution)/shard_map/ppermute | solution.py:35
  48.1 11.9 %collective-permute-start.9 = (bf16[320,640]{1,0:T(8,128)(2,1)S(1)}, bf16[320,640]{1,0:T(8,128)(2,1)S(1)}, u32[]{:S(2)}, u32[]{:S(2)}) collective-permute-start(bf16[320,640]{1,0:T(8,128)(2,1)S(1)} %collective-permute-done.7.refs_4_), channel_id=1, source_target_pairs={{0,7},{1,0},{2,1},{3,2},{4,3},{5,4},{6,5},{7,6},{8,15},{9,8},{10,9... | collective-permute-start | bytes 1228808 | tf_op jit(solution)/shard_map/ppermute | solution.py:35
  51.6 12.6 %collective-permute-start.12 = (bf16[80,2560]{1,0:T(8,128)(2,1)}, bf16[80,2560]{1,0:T(8,128)(2,1)S(1)}, u32[]{:S(2)}, u32[]{:S(2)}) collective-permute-start(bf16[80,2560]{1,0:T(8,128)(2,1)} %bitcast.16), channel_id=1, source_target_pairs={{0,24},{8,0},{16,8},{24,16},{32,56},{40,32},{48,40},{56,48},{64,88... | collective-permute-start | bytes 1228808 | tf_op jit(solution)/shard_map/ppermute | solution.py:50
  51.6 14.2 %collective-permute-start.13 = (bf16[80,2560]{1,0:T(8,128)(2,1)}, bf16[80,2560]{1,0:T(8,128)(2,1)S(1)}, u32[]{:S(2)}, u32[]{:S(2)}) collective-permute-start(bf16[80,2560]{1,0:T(8,128)(2,1)} %bitcast.17), channel_id=1, source_target_pairs={{0,16},{8,24},{16,0},{24,8},{32,48},{40,56},{48,32},{56,40},{64,80... | collective-permute-start | bytes 1228808 | tf_op jit(solution)/shard_map/ppermute | solution.py:50
  52.6 21.1 %collective-permute-start.14 = (bf16[80,2560]{1,0:T(8,128)(2,1)}, bf16[80,2560]{1,0:T(8,128)(2,1)S(1)}, u32[]{:S(2)}, u32[]{:S(2)}) collective-permute-start(bf16[80,2560]{1,0:T(8,128)(2,1)} %bitcast.18), channel_id=1, source_target_pairs={{0,8},{8,16},{16,24},{24,0},{32,40},{40,48},{48,56},{56,32},{64,72... | collective-permute-start | bytes 1228808 | tf_op jit(solution)/shard_map/ppermute | solution.py:50
  60.0 14.3 %collective-permute-start.15 = (bf16[80,640]{1,0:T(8,128)(2,1)S(1)}, bf16[80,640]{1,0:T(8,128)(2,1)S(1)}, u32[]{:S(2)}, u32[]{:S(2)}) collective-permute-start(bf16[80,640]{1,0:T(8,128)(2,1)S(1)} %get-tuple-element.18), channel_id=1, source_target_pairs={{0,24},{8,0},{16,8},{24,16},{32,56},{40,32},{48,40},{56,48},{64,88... | collective-permute-start | bytes 307208 | tf_op jit(solution)/shard_map/ppermute | solution.py:50
  60.0 15.9 %collective-permute-start.16 = (bf16[80,640]{1,0:T(8,128)(2,1)S(1)}, bf16[80,640]{1,0:T(8,128)(2,1)S(1)}, u32[]{:S(2)}, u32[]{:S(2)}) collective-permute-start(bf16[80,640]{1,0:T(8,128)(2,1)S(1)} %get-tuple-element.19), channel_id=1, source_target_pairs={{0,16},{8,24},{16,0},{24,8},{32,48},{40,56},{48,32},{56,40},{64,80... | collective-permute-start | bytes 307208 | tf_op jit(solution)/shard_map/ppermute | solution.py:50
  64.2 12.6 %collective-permute-start.17 = (bf16[80,640]{1,0:T(8,128)(2,1)S(1)}, bf16[80,640]{1,0:T(8,128)(2,1)S(1)}, u32[]{:S(2)}, u32[]{:S(2)}) collective-permute-start(bf16[80,640]{1,0:T(8,128)(2,1)S(1)} %get-tuple-element.20), channel_id=1, source_target_pairs={{0,8},{8,16},{16,24},{24,0},{32,40},{40,48},{48,56},{56,32},{64,72... | collective-permute-start | bytes 307208 | tf_op jit(solution)/shard_map/ppermute | solution.py:50
  65.8 11.1 %collective-permute-start.10 = (bf16[160,640]{1,0:T(8,128)(2,1)S(1)}, bf16[160,640]{1,0:T(8,128)(2,1)S(1)}, u32[]{:S(2)}, u32[]{:S(2)}) collective-permute-start(bf16[160,640]{1,0:T(8,128)(2,1)S(1)} %slice.16), channel_id=1, source_target_pairs={{0,1},{1,2},{2,3},{3,4},{4,5},{5,6},{6,7},{7,0},{8,9},{9,10},{10,1... | collective-permute-start | bytes 614408 | tf_op jit(solution)/shard_map/ppermute | solution.py:35
  82.3 11.7 %collective-permute-start.18 = (bf16[320,640]{1,0:T(8,128)(2,1)S(1)}, bf16[320,640]{1,0:T(8,128)(2,1)S(1)}, u32[]{:S(2)}, u32[]{:S(2)}) collective-permute-start(bf16[320,640]{1,0:T(8,128)(2,1)S(1)} %reduced.1.refs_0_), channel_id=1, source_target_pairs={{0,1},{1,2},{2,3},{3,4},{4,5},{5,6},{6,7},{7,0},{8,9},{9,10},{10,1... | collective-permute-start | bytes 1228808 | tf_op jit(solution)/shard_map/ppermute | solution.py:35
  82.4 11.7 %collective-permute-start.19 = (bf16[320,640]{1,0:T(8,128)(2,1)S(1)}, bf16[320,640]{1,0:T(8,128)(2,1)S(1)}, u32[]{:S(2)}, u32[]{:S(2)}) collective-permute-start(bf16[320,640]{1,0:T(8,128)(2,1)S(1)} %reduced.1.refs_0_), channel_id=1, source_target_pairs={{0,7},{1,0},{2,1},{3,2},{4,3},{5,4},{6,5},{7,6},{8,15},{9,8},{10,9... | collective-permute-start | bytes 1228808 | tf_op jit(solution)/shard_map/ppermute | solution.py:35
  94.0 10.7 %collective-permute-start.20 = (bf16[320,640]{1,0:T(8,128)(2,1)S(1)}, bf16[320,640]{1,0:T(8,128)(2,1)S(1)}, u32[]{:S(2)}, u32[]{:S(2)}) collective-permute-start(bf16[320,640]{1,0:T(8,128)(2,1)S(1)} %collective-permute-done.18.refs_1_), channel_id=1, source_target_pairs={{0,1},{1,2},{2,3},{3,4},{4,5},{5,6},{6,7},{7,0},{8,9},{9,10},{10,1... | collective-permute-start | bytes 1228808 | tf_op jit(solution)/shard_map/ppermute | solution.py:35
  97.4 21.2 %collective-permute-start.26 = (bf16[160,2560]{1,0:T(8,128)(2,1)S(1)}, bf16[160,2560]{1,0:T(8,128)(2,1)S(1)}, u32[]{:S(2)}, u32[]{:S(2)}) collective-permute-start(bf16[160,2560]{1,0:T(8,128)(2,1)S(1)} %pad_maximum_fusion.2), channel_id=1, source_target_pairs={{0,24},{8,0},{16,8},{24,16},{32,56},{40,32},{48,40},{56,48},{64,88... | collective-permute-start | bytes 2457608 | tf_op jit(solution)/shard_map/ppermute | solution.py:50
  99.9 22.7 %collective-permute-start.27 = (bf16[160,2560]{1,0:T(8,128)(2,1)S(1)}, bf16[160,2560]{1,0:T(8,128)(2,1)S(1)}, u32[]{:S(2)}, u32[]{:S(2)}) collective-permute-start(bf16[160,2560]{1,0:T(8,128)(2,1)S(1)} %pad_maximum_fusion.2), channel_id=1, source_target_pairs={{0,16},{8,24},{16,0},{24,8},{32,48},{40,56},{48,32},{56,40},{64,80... | collective-permute-start | bytes 2457608 | tf_op jit(solution)/shard_map/ppermute | solution.py:50
  99.9 34.3 %collective-permute-start.28 = (bf16[160,2560]{1,0:T(8,128)(2,1)S(1)}, bf16[160,2560]{1,0:T(8,128)(2,1)S(1)}, u32[]{:S(2)}, u32[]{:S(2)}) collective-permute-start(bf16[160,2560]{1,0:T(8,128)(2,1)S(1)} %pad_maximum_fusion.2), channel_id=1, source_target_pairs={{0,8},{8,16},{16,24},{24,0},{32,40},{40,48},{48,56},{56,32},{64,72... | collective-permute-start | bytes 2457608 | tf_op jit(solution)/shard_map/ppermute | solution.py:50
  104.8 11.7 %collective-permute-start.23 = (bf16[320,640]{1,0:T(8,128)(2,1)S(1)}, bf16[320,640]{1,0:T(8,128)(2,1)S(1)}, u32[]{:S(2)}, u32[]{:S(2)}) collective-permute-start(bf16[320,640]{1,0:T(8,128)(2,1)S(1)} %collective-permute-done.21.refs_4_), channel_id=1, source_target_pairs={{0,7},{1,0},{2,1},{3,2},{4,3},{5,4},{6,5},{7,6},{8,15},{9,8},{10,9... | collective-permute-start | bytes 1228808 | tf_op jit(solution)/shard_map/ppermute | solution.py:35
  114.5 30.3 %collective-permute-start.30 = (bf16[20,128,128]{2,1,0:T(8,128)(2,1)S(1)}, bf16[20,128,128]{2,1,0:T(8,128)(2,1)S(1)}, u32[]{:S(2)}, u32[]{:S(2)}) collective-permute-start(bf16[20,128,128]{2,1,0:T(8,128)(2,1)S(1)} %bitcast.14), channel_id=1, source_target_pairs={{0,32},{32,64},{64,96},{96,128},{128,160},{160,192},{192,224},{1,3... | collective-permute-start | bytes 1966088 | tf_op jit(solution)/shard_map/ppermute | solution.py:40
  116.5 19.5 %collective-permute-start.24 = (bf16[160,640]{1,0:T(8,128)(2,1)S(1)}, bf16[160,640]{1,0:T(8,128)(2,1)S(1)}, u32[]{:S(2)}, u32[]{:S(2)}) collective-permute-start(bf16[160,640]{1,0:T(8,128)(2,1)S(1)} %slice.18), channel_id=1, source_target_pairs={{0,1},{1,2},{2,3},{3,4},{4,5},{5,6},{6,7},{7,0},{8,9},{9,10},{10,1... | collective-permute-start | bytes 614408 | tf_op jit(solution)/shard_map/ppermute | solution.py:35
  118.6 17.4 %collective-permute-start.25 = (bf16[160,640]{1,0:T(8,128)(2,1)S(1)}, bf16[160,640]{1,0:T(8,128)(2,1)S(1)}, u32[]{:S(2)}, u32[]{:S(2)}) collective-permute-start(bf16[160,640]{1,0:T(8,128)(2,1)S(1)} %slice.19), channel_id=1, source_target_pairs={{0,7},{1,0},{2,1},{3,2},{4,3},{5,4},{6,5},{7,6},{8,15},{9,8},{10,9... | collective-permute-start | bytes 614408 | tf_op jit(solution)/shard_map/ppermute | solution.py:35
  (16 other events, 255.5 us)

commit v2 on v0

v2 whole, which is shorter than its diff:
```python
import jax
import jax.numpy as jnp
import numpy as np
from jax import lax
from jax.experimental import pallas as pl
from jax.experimental.pallas import tpu as pltpu
from jax.sharding import Mesh, PartitionSpec as P

BF = jnp.bfloat16
F32 = jnp.float32
HALF = jnp.float16
BLK = 128
CODE = 8
VMEM = pl.BlockSpec(memory_space=pltpu.VMEM)


def call(kernel, out, name, operands, scratch=(), mib=16, flops=0):
    moved = sum(x.size * x.dtype.itemsize for x in operands) + sum(x.size * x.dtype.itemsize for x in jax.tree.leaves(out))
    return pl.pallas_call(
        kernel,
        out_shape=out,
        in_specs=[VMEM] * len(operands),
        out_specs=jax.tree.map(lambda _: VMEM, out),
        scratch_shapes=list(scratch),
        compiler_params=pltpu.CompilerParams(vmem_limit_bytes=mib << 20),
        cost_estimate=pl.CostEstimate(flops=flops, bytes_accessed=moved, transcendentals=0),
        name=name,
    )(*operands)


def like(rows, cols, dtype):
    return jax.ShapeDtypeStruct((rows, cols), dtype)


def hop_layer(x, by):
    size = lax.axis_size("layer")
    return lax.ppermute(x, "layer", [(i, i + by) for i in range(size) if 0 <= i + by < size])


def chunks_of(width):
    return [(at, min(256, width - at)) for at in range(0, width, 256)]


def store_scaled(out_ref, values, at, shards, rows):
    width = values.shape[1]
    cols = pl.ds(at, width)
    line = lax.broadcasted_iota(jnp.int32, (CODE, width), 0)
    codes = jnp.full((CODE, width), 1.0, F32)
    for k in range(shards):
        part = values[k * rows : (k + 1) * rows]
        top = jnp.max(jnp.abs(part), axis=0, keepdims=True)
        scale = jnp.ones_like(top)
        code = jnp.full_like(top, 128.0)
        for bits in (64, 32, 16, 8):
            small = top < 2.0 ** (15 - bits)
            grow = jnp.where(small, 2.0**bits, 1.0)
            top = top * grow
            scale = scale * grow
            code = code * jnp.where(small, 2.0 ** (-(bits // 8)), 1.0)
        out_ref[pl.ds(k * rows, rows), cols] = (part * scale).astype(BF)
        codes = jnp.where(line == k, code, codes)
    out_ref[pl.ds(shards * rows, CODE), cols] = codes.astype(BF)


def load_scaled(in_ref, panel_ref, at, width, shards, rows):
    cols = pl.ds(at, width)
    count = in_ref.shape[0]
    for j in range(count):
        codes = in_ref[j, pl.ds(shards * rows, CODE), cols].astype(F32) * (1.0 / 128.0)
        codes = codes * codes
        codes = codes * codes
        codes = codes * codes
        for k in range(shards):
            part = in_ref[j, pl.ds(k * rows, rows), cols].astype(F32) * codes[k : k + 1]
            panel_ref[pl.ds((k * count + j) * rows, rows), cols] = part.astype(BF)


def near_tile(above, table, shards):
    tile, width = above.shape
    blocks = width // BLK

    def kernel(above_ref, table_ref, out_ref):
        y = lax.axis_index("y")
        for b in range(blocks):
            block = table_ref[y * blocks + b]
            near = lax.dot_general(
                above_ref[:, pl.ds(b * BLK, BLK)], block, (((1,), (1,)), ((), ())), preferred_element_type=F32
            )
            store_scaled(out_ref, near.astype(BF).astype(F32), b * BLK, shards, tile // shards)

    return call(kernel, like(tile + CODE, width, BF), "near", [above, table], flops=2 * tile * width * BLK)


def reduced_tile(panel, factor, grad, shards):
    tile, width = grad.shape
    depth = factor.shape[1]

    def kernel(panel_in, factor_ref, grad_ref, out_ref, panel_ref):
        for at, w in chunks_of(width):
            cols = pl.ds(at, w)
            load_scaled(panel_in, panel_ref, at, w, shards, tile // shards)
            coupled = jnp.dot(factor_ref[...], panel_ref[:, cols], preferred_element_type=F32)
            reduced = (grad_ref[:, cols].astype(F32) - coupled).astype(BF).astype(F32)
            store_scaled(out_ref, reduced, at, shards, tile // shards)

    return call(
        kernel,
        like(tile + CODE, width, BF),
        "reduced",
        [panel, factor, grad],
        [pltpu.VMEM((depth, width), BF)],
        flops=2 * tile * depth * width,
    )


def last_tiles(panel, factors, table, shards):
    tile, width = factors.shape[0] // 2, panel.shape[2]
    depth, rows, blocks = factors.shape[1], tile // shards, width // BLK

    def kernel(panel_in, factors_ref, table_ref, local_ref, middle_ref, panel_ref):
        y = lax.axis_index("y")
        for at, w in chunks_of(width):
            load_scaled(panel_in, panel_ref, at, w, shards, rows)
            both = jnp.dot(factors_ref[...], panel_ref[:, pl.ds(at, w)], preferred_element_type=F32).astype(BF)
            for b in range(w // BLK):
                sub = pl.ds(at + b * BLK, BLK)
                block = table_ref[y * blocks + at // BLK + b]
                product = jnp.dot(both[:, b * BLK : (b + 1) * BLK], block, preferred_element_type=F32)
                for k in range(shards):
                    local_ref[pl.ds(k * rows, rows), sub] = product[2 * k * rows : (2 * k + 1) * rows]
                    middle_ref[pl.ds(k * rows, rows), sub] = product[(2 * k + 1) * rows : (2 * k + 2) * rows].astype(BF)

    return call(
        kernel,
        (like(tile, width, F32), like(tile, width, BF)),
        "last",
        [panel, factors, table],
        [pltpu.VMEM((depth, width), BF)],
        flops=4 * tile * depth * width,
    )


def update_tile(local_term, middle, table):
    tile, width = middle.shape
    blocks = width // BLK

    def kernel(local_ref, middle_ref, table_ref, out_ref):
        y = lax.axis_index("y")
        for b in range(blocks):
            cols = pl.ds(b * BLK, BLK)
            pushed = jnp.dot(middle_ref[:, cols], table_ref[y * blocks + b], preferred_element_type=F32)
            out_ref[:, cols] = (local_ref[:, cols] - pushed).astype(BF)

    return call(kernel, like(tile, width, BF), "update", [local_term, middle, table], flops=2 * tile * width * BLK)


def split_columns(x, shards):
    _, rows, width = x.shape
    width //= shards

    def kernel(in_ref, out_ref):
        for k in range(shards):
            out_ref[pl.ds(k * rows, rows), :] = in_ref[0, :, pl.ds(k * width, width)]

    return call(kernel, like(shards * rows, width, x.dtype), "split", [x])


def join_columns(x, shards):
    rows, width = x.shape[0] // shards, x.shape[1]

    def kernel(in_ref, out_ref):
        for k in range(shards):
            out_ref[0, :, pl.ds(k * width, width)] = in_ref[pl.ds(k * rows, rows), :]

    return call(kernel, jax.ShapeDtypeStruct((1, rows, shards * width), x.dtype), "join", [x])


def gather_panel(tile):
    return lax.all_gather(tile.astype(HALF), "z", axis=0).astype(BF)


def local(gradient, in_inverse, in_coupling, in_carry, out_inverse, out_coupling):
    shards = lax.axis_size("y")
    out_psi = out_coupling[0]
    factor = lax.all_gather(in_coupling[0], "y", axis=0, tiled=True)
    stacked = jnp.concatenate([in_inverse[0], in_carry[0]], 0)
    grad = lax.all_to_all(split_columns(gradient, shards), "y", split_axis=0, concat_axis=0, tiled=True)
    stacked = lax.optimization_barrier((stacked, grad))[0]
    factors = lax.all_gather(stacked, "y", axis=0, tiled=True)
    psi_below = hop_layer(out_psi, 1)
    near = near_tile(hop_layer(grad, -1), out_psi, shards)
    reduced = reduced_tile(gather_panel(near), factor, grad, shards)
    local_term, middle = last_tiles(gather_panel(reduced), factors, out_inverse[0], shards)
    update = update_tile(local_term, hop_layer(middle, 1), psi_below)
    return join_columns(lax.all_to_all(update, "y", split_axis=0, concat_axis=0, tiled=True), shards)


def solution(mesh):
    layers = mesh.shape["layer"]
    fine = Mesh(np.asarray(mesh.devices).reshape(layers, 4, -1), ("layer", "y", "z"))
    rows = P("layer", ("y", "z"), None)
    table = P("layer", None, None, None)
    return jax.shard_map(
        local,
        mesh=fine,
        in_specs=(rows, rows, rows, rows, table, table),
        out_specs=rows,
        check_vma=False,
    )
```

time: 297 us -> 150 us (0.51)
  waiting for transfers between devices: 254 us -> 17 us
  blocking collectives: 0 us -> 87.2 us
  matrix products: 20.4 us -> 0 us
  Pallas kernels: 0 us -> 10.9 us
  starting transfers between devices: 6.07 us -> 11 us
  local copies, waits for them, and re-layouts: 2.04 us -> 6.44 us
  other arithmetic: 0 us -> 3.51 us
    all_gather x2, waiting for transfers between devices: 244 us -> 0.04 us  [the longest x1 0.02 us: local(): factor = lax.all_gather(in_coupling[0], 'y', axis=0, tiled=True)]
    all_gather x0 -> x2, blocking collectives: none -> 76.4 us  [gather_panel(): return lax.all_gather(tile.astype(HALF), 'z', axis=0).astype(BF)]
    dot_general x7 -> x0, matrix products: 20.4 us -> none  [the longest x3 17.6 us: contract_rows(): return jnp.dot(factor, piece, preferred_element_type=jnp.float32)]
    pallas_call x0 -> x6, Pallas kernels: none -> 10.9 us  [call(): pl.pallas_call(kernel, out_shape=out, in_specs=[VMEM] * len(operands), ou...]
    all_to_all x0 -> x1, blocking collectives: none -> 10.8 us  [local(): lax.all_to_all(update, 'y', split_axis=0, concat_axis=0, tiled=True)]
    unnamed x10 -> x12, local copies, waits for them, and re-layouts: 0.02 us -> 6.44 us
    all_to_all x0 -> x1, waiting for transfers between devices: none -> 6.15 us  [local(): lax.all_to_all(split_columns(gradient, shards), 'y', split_axis=0, concat...]
    all_to_all x0 -> x1, starting transfers between devices: none -> 4.46 us  [local(): lax.all_to_all(split_columns(gradient, shards), 'y', split_axis=0, concat...]
  transfers between devices with their start and end apart: 5 -> 6, of which waited for: 4 -> 3; matrix products, arithmetic and copies ran while one was open for 4% -> 2% of each run, Pallas kernels for 0% -> 6%
where the time goes in v2:
time: 150 us
  blocking collectives  87.2 us (58%)
  waiting for transfers between devices  17 us (11%)
  between operations  13.5 us (9%)
  starting transfers between devices  11 us (7%)
  Pallas kernels  10.9 us (7%)
  local copies, waits for them, and re-layouts  6.44 us (4%)
  other arithmetic  3.51 us (2%)
    all_gather x2, blocking collectives, gather_panel(): return lax.all_gather(tile.astype(HALF), 'z', axis=0).astype(BF)  76.4 us
    pallas_call x6, Pallas kernels, call(): pl.pallas_call(kernel, out_shape=out, in_specs=[VMEM] * len(operands), ou...  10.9 us
    all_to_all x1, blocking collectives, local(): lax.all_to_all(update, 'y', split_axis=0, concat_axis=0, tiled=True)  10.8 us
    ppermute x3, waiting for transfers between devices, hop_layer(): lax.ppermute(x, 'layer', [(i, i + by) for i in range(size) if 0 <= i + by...  10.1 us
    ppermute x3, starting transfers between devices, hop_layer(): lax.ppermute(x, 'layer', [(i, i + by) for i in range(size) if 0 <= i + by...  6.49 us
    unnamed x12, local copies, waits for them, and re-layouts  6.44 us
    all_to_all x1, waiting for transfers between devices, local(): lax.all_to_all(split_columns(gradient, shards), 'y', split_axis=0, concat...  6.15 us
    all_to_all x1, starting transfers between devices, local(): lax.all_to_all(split_columns(gradient, shards), 'y', split_axis=0, concat...  4.46 us
  transfers between devices with their start and end apart: 6, of which 3 were waited for; matrix products, arithmetic and copies ran while one was open for 2% of the time, Pallas kernels for 6%

profile of v2, /device:TPU:2, one launch (start us, length us, event | category | flops | bytes accessed | tf_op | source)
XLA Modules:
  0.0 149.6 jit_solution(10897099692396311856)
XLA Ops:
  6.5 0.7 all-gather.10.cloned.1.call-update
  7.3 1.0 copy-done.3
  8.3 0.8 split.1
  9.0 4.5 %all-to-all-start = ((bf16[4,80,640]{2,1,0:T(8,128)(2,1)}), bf16[4,80,640]{2,1,0:T(8,128)(2,1)S(1)}, u32[]{:S(2)}, u32[]{:S(2)}) async-start(bf16[4,80,640]{2,1,0:T(8,128)(2,1)} %bitcast), calls=%async_computation | async-start | bytes 819200 | tf_op jit(solution)/shard_map/all_to_all | solution.py:187
  13.5 2.1 %pad_maximum_fusion = bf16[160,2560]{1,0:T(8,128)(2,1)} fusion(bf16[80,2560]{1,0:T(8,128)(2,1)} %bitcast.19, bf16[80,2560]{1,0:T(8,128)(2,1)} %bitcast.20), kind=kLoop, calls=%fused_computation | loop fusion | flops 1638400 | bytes 1638400 | tf_op jit(solution)/shard_map/concatenate | solution.py:186
  15.6 6.1 %all-to-all-done = bf16[4,80,640]{2,1,0:T(8,128)(2,1)S(1)} async-done(((bf16[4,80,640]{2,1,0:T(8,128)(2,1)}), bf16[4,80,640]{2,1,0:T(8,128)(2,1)S(1)}, u32[]{:S(2)}, u32[]{:S(2)}) %all-to-all-start) | async-done | bytes 409632 | tf_op jit(solution)/shard_map/all_to_all | solution.py:187
  21.8 1.9 %collective-permute-start = (bf16[320,640]{1,0:T(8,128)(2,1)S(1)}, bf16[320,640]{1,0:T(8,128)(2,1)S(1)}, u32[]{:S(2)}, u32[]{:S(2)}) collective-permute-start(bf16[320,640]{1,0:T(8,128)(2,1)S(1)} %bitcast.16), channel_id=1, source_target_pairs={{32,0},{64,32},{96,64},{128,96},{160,128},{192,160},{224,192},{33,... | collective-permute-start | bytes 1228808 | tf_op jit(solution)/shard_map/ppermute | solution.py:37
  23.7 2.4 %collective-permute-start.2 = (bf16[20,128,128]{2,1,0:T(8,128)(2,1)}, bf16[20,128,128]{2,1,0:T(8,128)(2,1)}, u32[]{:S(2)}, u32[]{:S(2)}) collective-permute-start(bf16[20,128,128]{2,1,0:T(8,128)(2,1)} %bitcast.2.table_ref), channel_id=1, source_target_pairs={{0,32},{32,64},{64,96},{96,128},{128,160},{160,192},{192,224},{1,3... | collective-permute-start | bytes 1966088 | tf_op jit(solution)/shard_map/ppermute | solution.py:37
  26.1 3.0 %collective-permute-done.above_ref = bf16[320,640]{1,0:T(8,128)(2,1)S(1)} collective-permute-done((bf16[320,640]{1,0:T(8,128)(2,1)S(1)}, bf16[320,640]{1,0:T(8,128)(2,1)S(1)}, u32[]{:S(2)}, u32[]{:S(2)}) %collective-permute-start) | collective-permute-done | bytes 409632 | tf_op jit(solution)/shard_map/ppermute | solution.py:37
  29.2 1.5 near.1
  30.7 39.7 %all-gather.11 = f16[2624,640]{1,0:T(8,128)(2,1)S(1)} all-gather(f16[328,640]{1,0:T(8,128)(2,1)S(1)} %convert_element_type.12), channel_id=2, replica_groups=mesh['layer'=8,'y'=4,'z'=8] {'z'}, dimensions={0}, use_global_device_ids=true | all-gather | bytes 3778560 | tf_op jit(solution)/shard_map/all_gather | solution.py:179
  70.5 0.6 convert_element_type.16
  71.2 1.4 copy-done
  72.6 1.0 copy-done.2
  73.6 1.7 %reduced.1 = bf16[328,640]{1,0:T(8,128)(2,1)S(1)} custom-call(bf16[8,328,640]{2,1,0:T(8,128)(2,1)S(1)} %bitcast.11, bf16[320,2560]{1,0:T(8,128)(2,1)S(1)} %bitcast.13, bf16[320,640]{1,0:T(8,128)(2,1)S(1)} %bitcast.17), custom_call_target="tpu_custom_call" | custom-call | flops 1048576000 | bytes 5826560 | tf_op jit(solution)/shard_map/reduced/pallas_call | solution.py:19
  75.4 36.6 %all-gather.12 = f16[2624,640]{1,0:T(8,128)(2,1)S(1)} all-gather(f16[328,640]{1,0:T(8,128)(2,1)S(1)} %convert_element_type.14), channel_id=4, replica_groups=mesh['layer'=8,'y'=4,'z'=8] {'z'}, dimensions={0}, use_global_device_ids=true | all-gather | bytes 3778560 | tf_op jit(solution)/shard_map/all_gather | solution.py:179
  112.7 1.9 %copy-done.4 = bf16[640,2560]{1,0:T(8,128)(2,1)S(1)} copy-done((bf16[640,2560]{1,0:T(8,128)(2,1)S(1)}, bf16[640,2560]{1,0:T(8,128)(2,1)}, u32[]{:S(2)}) %copy-start.4) | copy-done | bytes 3276824
  114.6 1.1 copy-done.5
  115.7 4.8 %last.1 = (f32[320,640]{1,0:T(8,128)S(1)}, bf16[320,640]{1,0:T(8,128)(2,1)S(1)}) custom-call(bf16[8,328,640]{2,1,0:T(8,128)(2,1)S(1)} %bitcast.12, bf16[640,2560]{1,0:T(8,128)(2,1)S(1)} %copy-done.4, bf16[20,128,128]{2,1,0:T(8,128)(2,1)S(1)} %bitcast.18), custom_call_target="tpu_custom_call" | custom-call | flops 2097152000 | bytes 8519680 | tf_op jit(solution)/shard_map/last/pallas_call | solution.py:19
  120.5 2.2 %collective-permute-start.1 = (bf16[320,640]{1,0:T(8,128)(2,1)S(1)}, bf16[320,640]{1,0:T(8,128)(2,1)S(1)}, u32[]{:S(2)}, u32[]{:S(2)}) collective-permute-start(bf16[320,640]{1,0:T(8,128)(2,1)S(1)} %get-tuple-element.10), channel_id=1, source_target_pairs={{0,32},{32,64},{64,96},{96,128},{128,160},{160,192},{192,224},{1,3... | collective-permute-start | bytes 1228808 | tf_op jit(solution)/shard_map/ppermute | solution.py:37
  122.7 7.1 %collective-permute-done.1.middle_ref = bf16[320,640]{1,0:T(8,128)(2,1)S(1)} collective-permute-done((bf16[320,640]{1,0:T(8,128)(2,1)S(1)}, bf16[320,640]{1,0:T(8,128)(2,1)S(1)}, u32[]{:S(2)}, u32[]{:S(2)}) %collective-permute-start.1) | collective-permute-done | bytes 409632 | tf_op jit(solution)/shard_map/ppermute | solution.py:37
  129.8 1.3 update.1
  131.1 10.8 %all_to_all.22 = bf16[4,80,640]{2,1,0:T(8,128)(2,1)S(1)} all-to-all(bf16[4,80,640]{2,1,0:T(8,128)(2,1)S(1)} %bitcast.15), channel_id=1, replica_groups=mesh['layer'=8,'y'=4,'z'=8] {'y'}, dimensions={0} | all-to-all | bytes 819200 | tf_op jit(solution)/shard_map/all_to_all | solution.py:195
  142.0 0.8 join.1
  (16 shorter events, 0.9 us)
Async XLA Ops:
  6.5 64.6 %all-gather.10.cloned.1.call-start = ((), (), s32[]{:S(2)}) async-start(), calls=%async_computation.3 | async-start | bytes 2048000 | tf_op jit(solution)/shard_map/all_gather | solution.py:185
  7.3 1.0 copy-start.3
  9.0 12.7 %all-to-all-start = ((bf16[4,80,640]{2,1,0:T(8,128)(2,1)}), bf16[4,80,640]{2,1,0:T(8,128)(2,1)S(1)}, u32[]{:S(2)}, u32[]{:S(2)}) async-start(bf16[4,80,640]{2,1,0:T(8,128)(2,1)} %bitcast), calls=%async_computation | async-start | bytes 819200 | tf_op jit(solution)/shard_map/all_to_all | solution.py:187
  13.5 99.2 %all-gather.8.cloned.1.call-start = ((), (), s32[]{:S(2)}) async-start(), calls=%async_computation.2 | async-start | bytes 4096000 | tf_op jit(solution)/shard_map/all_gather | solution.py:189
  21.8 9.0 %copy-start.1 = (bf16[4,80,640]{2,1,0:T(8,128)(2,1)}, bf16[4,80,640]{2,1,0:T(8,128)(2,1)S(1)}, u32[]{:S(2)}) copy-start(bf16[4,80,640]{2,1,0:T(8,128)(2,1)S(1)} %all-to-all-done) | copy-start | bytes 1228804
  21.8 7.4 %collective-permute-start = (bf16[320,640]{1,0:T(8,128)(2,1)S(1)}, bf16[320,640]{1,0:T(8,128)(2,1)S(1)}, u32[]{:S(2)}, u32[]{:S(2)}) collective-permute-start(bf16[320,640]{1,0:T(8,128)(2,1)S(1)} %bitcast.16), channel_id=1, source_target_pairs={{32,0},{64,32},{96,64},{128,96},{160,128},{192,160},{224,192},{33,... | collective-permute-start | bytes 1228808 | tf_op jit(solution)/shard_map/ppermute | solution.py:37
  23.7 99.0 %collective-permute-start.2 = (bf16[20,128,128]{2,1,0:T(8,128)(2,1)}, bf16[20,128,128]{2,1,0:T(8,128)(2,1)}, u32[]{:S(2)}, u32[]{:S(2)}) collective-permute-start(bf16[20,128,128]{2,1,0:T(8,128)(2,1)} %bitcast.2.table_ref), channel_id=1, source_target_pairs={{0,32},{32,64},{64,96},{96,128},{128,160},{160,192},{192,224},{1,3... | collective-permute-start | bytes 1966088 | tf_op jit(solution)/shard_map/ppermute | solution.py:37
  71.1 1.4 copy-start
  72.6 1.0 copy-start.2
  112.7 1.9 %copy-start.4 = (bf16[640,2560]{1,0:T(8,128)(2,1)S(1)}, bf16[640,2560]{1,0:T(8,128)(2,1)}, u32[]{:S(2)}) copy-start(bf16[640,2560]{1,0:T(8,128)(2,1)} %all-gather.8.cloned.1.call-done.factors_ref) | copy-start | bytes 9830404
  114.6 1.1 copy-start.5
  120.5 9.3 %collective-permute-start.1 = (bf16[320,640]{1,0:T(8,128)(2,1)S(1)}, bf16[320,640]{1,0:T(8,128)(2,1)S(1)}, u32[]{:S(2)}, u32[]{:S(2)}) collective-permute-start(bf16[320,640]{1,0:T(8,128)(2,1)S(1)} %get-tuple-element.10), channel_id=1, source_target_pairs={{0,32},{32,64},{64,96},{96,128},{128,160},{160,192},{192,224},{1,3... | collective-permute-start | bytes 1228808 | tf_op jit(solution)/shard_map/ppermute | solution.py:37
Sparse Core Ops, SparseCore 0:
  9.2 32.5 all-gather.9
  43.6 43.1 all-gather.7

commit v3 on v2

--- a/solution.py
+++ b/solution.py
@@ -12,14 +12,15 @@
 BLK = 128
 CODE = 8
 VMEM = pl.BlockSpec(memory_space=pltpu.VMEM)
-
-
-def call(kernel, out, name, operands, scratch=(), mib=16, flops=0):
+HBM = pl.BlockSpec(memory_space=pltpu.HBM)
+
+
+def call(kernel, out, name, operands, scratch=(), mib=16, flops=0, far=()):
     moved = sum(x.size * x.dtype.itemsize for x in operands) + sum(x.size * x.dtype.itemsize for x in jax.tree.leaves(out))
     return pl.pallas_call(
         kernel,
         out_shape=out,
-        in_specs=[VMEM] * len(operands),
+        in_specs=[HBM if i in far else VMEM for i in range(len(operands))],
         out_specs=jax.tree.map(lambda _: VMEM, out),
         scratch_shapes=list(scratch),
         compiler_params=pltpu.CompilerParams(vmem_limit_bytes=mib << 20),
@@ -80,9 +81,8 @@
     blocks = width // BLK
 
     def kernel(above_ref, table_ref, out_ref):
-        y = lax.axis_index("y")
         for b in range(blocks):
-            block = table_ref[y * blocks + b]
+            block = table_ref[b]
             near = lax.dot_general(
                 above_ref[:, pl.ds(b * BLK, BLK)], block, (((1,), (1,)), ((), ())), preferred_element_type=F32
             )
@@ -93,38 +93,46 @@
 
 def reduced_tile(panel, factor, grad, shards):
     tile, width = grad.shape
-    depth = factor.shape[1]
-
-    def kernel(panel_in, factor_ref, grad_ref, out_ref, panel_ref):
+    depth, rows = factor[0].shape[1], tile // shards
+
+    def kernel(panel_in, grad_ref, *refs):
+        pieces, (out_ref, panel_ref, factor_ref) = refs[:shards], refs[shards:]
+        y = lax.axis_index("y")
+        for k in range(shards):
+            at = pl.multiple_of(lax.rem(y + (shards - k), shards) * rows, 16)
+            factor_ref[pl.ds(at, rows), :] = pieces[k][...]
         for at, w in chunks_of(width):
             cols = pl.ds(at, w)
-            load_scaled(panel_in, panel_ref, at, w, shards, tile // shards)
+            load_scaled(panel_in, panel_ref, at, w, shards, rows)
             coupled = jnp.dot(factor_ref[...], panel_ref[:, cols], preferred_element_type=F32)
             reduced = (grad_ref[:, cols].astype(F32) - coupled).astype(BF).astype(F32)
-            store_scaled(out_ref, reduced, at, shards, tile // shards)
+            store_scaled(out_ref, reduced, at, shards, rows)
 
     return call(
         kernel,
         like(tile + CODE, width, BF),
         "reduced",
-        [panel, factor, grad],
-        [pltpu.VMEM((depth, width), BF)],
+        [panel, grad, *factor],
+        [pltpu.VMEM((depth, width), BF), pltpu.VMEM((tile, depth), BF)],
         flops=2 * tile * depth * width,
     )
 
 
 def last_tiles(panel, factors, table, shards):
     tile, width = factors.shape[0] // 2, panel.shape[2]
-    depth, rows, blocks = factors.shape[1], tile // shards, width // BLK
-
-    def kernel(panel_in, factors_ref, table_ref, local_ref, middle_ref, panel_ref):
-        y = lax.axis_index("y")
+    depth, rows = factors.shape[1], tile // shards
+
+    def kernel(panel_in, factors_in, table_ref, local_ref, middle_ref, panel_ref, factors_ref, sem):
+        copy = pltpu.make_async_copy(factors_in, factors_ref, sem)
+        copy.start()
         for at, w in chunks_of(width):
             load_scaled(panel_in, panel_ref, at, w, shards, rows)
+            if at == 0:
+                copy.wait()
             both = jnp.dot(factors_ref[...], panel_ref[:, pl.ds(at, w)], preferred_element_type=F32).astype(BF)
             for b in range(w // BLK):
                 sub = pl.ds(at + b * BLK, BLK)
-                block = table_ref[y * blocks + at // BLK + b]
+                block = table_ref[at // BLK + b]
                 product = jnp.dot(both[:, b * BLK : (b + 1) * BLK], block, preferred_element_type=F32)
                 for k in range(shards):
                     local_ref[pl.ds(k * rows, rows), sub] = product[2 * k * rows : (2 * k + 1) * rows]
@@ -135,7 +143,8 @@
         (like(tile, width, F32), like(tile, width, BF)),
         "last",
         [panel, factors, table],
-        [pltpu.VMEM((depth, width), BF)],
+        [pltpu.VMEM((depth, width), BF), pltpu.VMEM(factors.shape, BF), pltpu.SemaphoreType.DMA],
+        far=(1,),
         flops=4 * tile * depth * width,
     )
 
@@ -145,24 +154,78 @@
     blocks = width // BLK
 
     def kernel(local_ref, middle_ref, table_ref, out_ref):
-        y = lax.axis_index("y")
         for b in range(blocks):
             cols = pl.ds(b * BLK, BLK)
-            pushed = jnp.dot(middle_ref[:, cols], table_ref[y * blocks + b], preferred_element_type=F32)
+            pushed = jnp.dot(middle_ref[:, cols], table_ref[b], preferred_element_type=F32)
             out_ref[:, cols] = (local_ref[:, cols] - pushed).astype(BF)
 
     return call(kernel, like(tile, width, BF), "update", [local_term, middle, table], flops=2 * tile * width * BLK)
 
 
-def split_columns(x, shards):
-    _, rows, width = x.shape
+def copies(kernel, out, name, operands, count):
+    def body(*refs):
+        sems = refs[-1]
+        started = []
+        for i, (source, target) in enumerate(kernel(*refs[:-1])):
+            copy = pltpu.make_async_copy(source, target, sems.at[i])
+            copy.start()
+            started.append(copy)
+        for copy in started:
+            copy.wait()
+
+    moved = 2 * sum(x.size * x.dtype.itemsize for x in jax.tree.leaves(out))
+    return pl.pallas_call(
+        body,
+        out_shape=out,
+        in_specs=[HBM] * len(operands),
+        out_specs=jax.tree.map(lambda _: VMEM, out),
+        scratch_shapes=[pltpu.SemaphoreType.DMA((count,))],
+        compiler_params=pltpu.CompilerParams(vmem_limit_bytes=16 << 20),
+        cost_estimate=pl.CostEstimate(flops=0, bytes_accessed=moved, transcendentals=0),
+        name=name,
+    )(*[pltpu.with_memory_space_constraint(x, pltpu.HBM) for x in operands])
+
+
+def prepare(gradient, out_inverse, out_coupling, shards):
+    _, rows, width = gradient.shape
     width //= shards
-
-    def kernel(in_ref, out_ref):
-        for k in range(shards):
-            out_ref[pl.ds(k * rows, rows), :] = in_ref[0, :, pl.ds(k * width, width)]
-
-    return call(kernel, like(shards * rows, width, x.dtype), "split", [x])
+    blocks = out_inverse.shape[1] // shards
+    table = jax.ShapeDtypeStruct((blocks, BLK, BLK), BF)
+
+    def kernel(grad_ref, inverse_ref, coupling_ref, split_ref, inv_ref, psi_ref):
+        mine = pl.ds(lax.axis_index("y") * blocks, blocks)
+        for k in range(shards):
+            yield grad_ref.at[0, :, pl.ds(k * width, width)], split_ref.at[pl.ds(k * rows, rows), :]
+        yield coupling_ref.at[0, mine], psi_ref
+        yield inverse_ref.at[0, mine], inv_ref
+
+    out = (like(shards * rows, width, BF), table, table)
+    return copies(kernel, out, "prepare", [gradient, out_inverse, out_coupling], shards + 2)
+
+
+def repeat_rows(parts, shards, name):
+    rows, width = parts[0].shape[1:]
+    count = len(parts)
+
+    def kernel(*refs):
+        for k in range(shards):
+            for i in range(count):
+                yield refs[i].at[0], refs[count].at[pl.ds((k * count + i) * rows, rows), :]
+
+    return copies(kernel, like(shards * count * rows, width, BF), name, parts, shards * count)
+
+
+def hop_y(x, by):
+    size = lax.axis_size("y")
+    return lax.ppermute(x, "y", [(i, (i + by) % size) for i in range(size)])
+
+
+def exchange(x):
+    return lax.all_to_all(x, "y", split_axis=0, concat_axis=0, tiled=True)
+
+
+def after(x, *others):
+    return lax.optimization_barrier((x, *others))[0]
 
 
 def join_columns(x, shards):
@@ -181,18 +244,18 @@
 
 def local(gradient, in_inverse, in_coupling, in_carry, out_inverse, out_coupling):
     shards = lax.axis_size("y")
-    out_psi = out_coupling[0]
-    factor = lax.all_gather(in_coupling[0], "y", axis=0, tiled=True)
-    stacked = jnp.concatenate([in_inverse[0], in_carry[0]], 0)
-    grad = lax.all_to_all(split_columns(gradient, shards), "y", split_axis=0, concat_axis=0, tiled=True)
-    stacked = lax.optimization_barrier((stacked, grad))[0]
-    factors = lax.all_gather(stacked, "y", axis=0, tiled=True)
-    psi_below = hop_layer(out_psi, 1)
-    near = near_tile(hop_layer(grad, -1), out_psi, shards)
+    split, inv, psi = prepare(gradient, out_inverse, out_coupling, shards)
+    psi_below = hop_layer(psi, 1)
+    grad = exchange(split)
+    above = hop_layer(grad, -1)
+    coupling = after(in_coupling, grad)[0]
+    factor = [coupling] + [hop_y(coupling, k) for k in range(1, shards)]
+    near = near_tile(above, psi, shards)
+    factors = exchange(after(repeat_rows([after(in_inverse, grad), in_carry], shards, "twice"), near))
     reduced = reduced_tile(gather_panel(near), factor, grad, shards)
-    local_term, middle = last_tiles(gather_panel(reduced), factors, out_inverse[0], shards)
+    local_term, middle = last_tiles(gather_panel(reduced), factors, inv, shards)
     update = update_tile(local_term, hop_layer(middle, 1), psi_below)
-    return join_columns(lax.all_to_all(update, "y", split_axis=0, concat_axis=0, tiled=True), shards)
+    return join_columns(exchange(update), shards)
 
 
 def solution(mesh):

time: 150 us -> 140 us (0.933)
  between operations: 13.5 us -> 0.17 us
  blocking collectives: 87.2 us -> 100 us
  waiting for transfers between devices: 17 us -> 5.58 us
  local copies, waits for them, and re-layouts: 6.44 us -> 1.25 us
  starting transfers between devices: 11 us -> 15.9 us
  Pallas kernels: 10.9 us -> 15.4 us
  other arithmetic: 3.51 us -> 1.42 us
    all_to_all x1 -> x2, blocking collectives: 10.8 us -> 24.4 us  [exchange(): return lax.all_to_all(x, 'y', split_axis=0, concat_axis=0, tiled=True)]
    all_to_all x1, waiting for transfers between devices: 6.15 us -> 0.01 us  [exchange(): return lax.all_to_all(x, 'y', split_axis=0, concat_axis=0, tiled=True)]
    unnamed x12 -> x6, local copies, waits for them, and re-layouts: 6.44 us -> 1.25 us
    ppermute x3, waiting for transfers between devices: 10.1 us -> 5.57 us  [hop_layer(): lax.ppermute(x, 'layer', [(i, i + by) for i in range(size) if 0 <= i + by...]
    pallas_call x6 -> x7, Pallas kernels: 10.9 us -> 15.4 us  [the longest x5 9.99 us: call(): pl.pallas_call(kernel, out_shape=out, in_specs=[HBM if i in far else VMEM...]
    ppermute x0 -> x3, starting transfers between devices: none -> 3.83 us  [hop_y(): return lax.ppermute(x, 'y', [(i, (i + by) % size) for i in range(size)])]
    concatenate x1 -> x0, other arithmetic: 2.1 us -> none  [local(): stacked = jnp.concatenate([in_inverse[0], in_carry[0]], 0)]
  transfers between devices with their start and end apart: 6 -> 7, of which waited for: 3 -> 1; matrix products, arithmetic and copies ran while one was open for 2% -> 1% of each run, Pallas kernels for 6% -> 5%
where the time goes in v3:
time: 140 us
  blocking collectives  100 us (71%)
  starting transfers between devices  15.9 us (11%)
  Pallas kernels  15.4 us (11%)
  waiting for transfers between devices  5.58 us (4%)
  other arithmetic  1.42 us (1%)
    all_gather x2, blocking collectives, gather_panel(): return lax.all_gather(tile.astype(HALF), 'z', axis=0).astype(BF)  76 us
    all_to_all x2, blocking collectives, exchange(): return lax.all_to_all(x, 'y', split_axis=0, concat_axis=0, tiled=True)  24.4 us
    pallas_call x5, Pallas kernels, call(): pl.pallas_call(kernel, out_shape=out, in_specs=[HBM if i in far else VMEM...  9.99 us
    ppermute x3, starting transfers between devices, hop_layer(): lax.ppermute(x, 'layer', [(i, i + by) for i in range(size) if 0 <= i + by...  7.36 us
    ppermute x3, waiting for transfers between devices, hop_layer(): lax.ppermute(x, 'layer', [(i, i + by) for i in range(size) if 0 <= i + by...  5.57 us
    pallas_call x2, Pallas kernels, copies(): pl.pallas_call(body, out_shape=out, in_specs=[HBM] * len(operands), out_s...  5.37 us
    all_to_all x1, starting transfers between devices, exchange(): return lax.all_to_all(x, 'y', split_axis=0, concat_axis=0, tiled=True)  4.71 us
    ppermute x3, starting transfers between devices, hop_y(): return lax.ppermute(x, 'y', [(i, (i + by) % size) for i in range(size)])  3.83 us
  transfers between devices with their start and end apart: 7, of which 1 were waited for; matrix products, arithmetic and copies ran while one was open for 1% of the time, Pallas kernels for 5%

profile of v3, /device:TPU:2, one launch (start us, length us, event | category | flops | bytes accessed | tf_op | source)
XLA Modules:
  0.0 140.0 jit_solution(16290689927816554904)
XLA Ops:
  0.0 1.3 prepare.1
  1.3 12.5 %all_to_all.33 = bf16[4,80,640]{2,1,0:T(8,128)(2,1)S(1)} all-to-all(bf16[4,80,640]{2,1,0:T(8,128)(2,1)S(1)} %bitcast.15), channel_id=1, replica_groups=mesh['layer'=8,'y'=4,'z'=8] {'y'}, dimensions={0} | all-to-all | bytes 819200 | tf_op jit(solution)/shard_map/all_to_all | solution.py:224
  13.8 1.9 %collective-permute-start = (bf16[320,640]{1,0:T(8,128)(2,1)S(1)}, bf16[320,640]{1,0:T(8,128)(2,1)S(1)}, u32[]{:S(2)}, u32[]{:S(2)}) collective-permute-start(bf16[320,640]{1,0:T(8,128)(2,1)S(1)} %bitcast.13), channel_id=1, source_target_pairs={{32,0},{64,32},{96,64},{128,96},{160,128},{192,160},{224,192},{33,... | collective-permute-start | bytes 1228808 | tf_op jit(solution)/shard_map/ppermute | solution.py:38
  15.7 0.6 collective-permute-start.1
  16.3 2.1 %collective-permute-start.2 = (bf16[80,2560]{1,0:T(8,128)(2,1)}, bf16[80,2560]{1,0:T(8,128)(2,1)S(1)}, u32[]{:S(2)}, u32[]{:S(2)}) collective-permute-start(bf16[80,2560]{1,0:T(8,128)(2,1)} %bitcast.17), channel_id=1, source_target_pairs={{0,16},{8,24},{16,0},{24,8},{1,17},{9,25},{17,1},{25,9},{2,18},{10... | collective-permute-start | bytes 1228808 | tf_op jit(solution)/shard_map/ppermute | solution.py:220
  18.4 1.1 collective-permute-start.3
  19.5 4.1 %twice.1 = bf16[640,2560]{1,0:T(8,128)(2,1)} custom-call(bf16[1,80,2560]{2,1,0:T(8,128)(2,1)} %refs_0_.2, bf16[1,80,2560]{2,1,0:T(8,128)(2,1)} %refs_1_.3), custom_call_target="tpu_custom_call" | custom-call | bytes 6553600 | tf_op jit(solution)/shard_map/twice/pallas_call | solution.py:177
  23.7 0.4 near.1
  24.2 4.7 %all-to-all-start.1 = ((bf16[4,160,2560]{2,1,0:T(8,128)(2,1)}), bf16[4,160,2560]{2,1,0:T(8,128)(2,1)}, u32[]{:S(2)}, u32[]{:S(2)}) async-start(bf16[4,160,2560]{2,1,0:T(8,128)(2,1)} %bitcast.5), calls=%async_computation.1 | async-start | bytes 6553600 | tf_op jit(solution)/shard_map/all_to_all | solution.py:224
  28.9 40.3 %all-gather.4 = f16[2624,640]{1,0:T(8,128)(2,1)S(1)} all-gather(f16[328,640]{1,0:T(8,128)(2,1)S(1)} %convert_element_type.12), channel_id=2, replica_groups=mesh['layer'=8,'y'=4,'z'=8] {'z'}, dimensions={0}, use_global_device_ids=true | all-gather | bytes 3778560 | tf_op jit(solution)/shard_map/all_gather | solution.py:242
  69.1 0.6 convert_element_type.16
  69.8 0.3 copy-done
  70.1 1.8 %reduced.1 = bf16[328,640]{1,0:T(8,128)(2,1)S(1)} custom-call(bf16[8,328,640]{2,1,0:T(8,128)(2,1)S(1)} %bitcast.9, bf16[320,640]{1,0:T(8,128)(2,1)S(1)} %bitcast.14, bf16[80,2560]{1,0:T(8,128)(2,1)S(1)} %bitcast.19, bf16[80,2560]{1,0:T(8,128)(2,1)S(1)} %collective-permute-done.1.refs_1_, bf16[80,2560]{1,0:T(8,128)(2,1)S(1)} %collective-permute-done.2.refs_2_, ...), custom_call_target="tpu_custom_call" | custom-call | flops 1048576000 | bytes 5826560 | tf_op jit(solution)/shard_map/reduced/pallas_call | solution.py:20
  72.0 0.1 convert_element_type.14
  72.0 35.7 %all-gather.5 = f16[2624,640]{1,0:T(8,128)(2,1)S(1)} all-gather(f16[328,640]{1,0:T(8,128)(2,1)S(1)} %convert_element_type.14), channel_id=3, replica_groups=mesh['layer'=8,'y'=4,'z'=8] {'z'}, dimensions={0}, use_global_device_ids=true | all-gather | bytes 3778560 | tf_op jit(solution)/shard_map/all_gather | solution.py:242
  107.7 0.6 convert_element_type.17
  108.4 0.9 copy-done.2
  109.3 6.8 %last.1 = (f32[320,640]{1,0:T(8,128)S(1)}, bf16[320,640]{1,0:T(8,128)(2,1)S(1)}) custom-call(bf16[8,328,640]{2,1,0:T(8,128)(2,1)S(1)} %bitcast.10, bf16[640,2560]{1,0:T(8,128)(2,1)} %bitcast.6.factors_in, bf16[5,128,128]{2,1,0:T(8,128)(2,1)S(1)} %copy-done.2), custom_call_target="tpu_custom_call" | custom-call | flops 2097152000 | bytes 8028160 | tf_op jit(solution)/shard_map/last/pallas_call | solution.py:20
  116.1 1.9 %collective-permute-start.4 = (bf16[320,640]{1,0:T(8,128)(2,1)S(1)}, bf16[320,640]{1,0:T(8,128)(2,1)S(1)}, u32[]{:S(2)}, u32[]{:S(2)}) collective-permute-start(bf16[320,640]{1,0:T(8,128)(2,1)S(1)} %get-tuple-element.20), channel_id=1, source_target_pairs={{0,32},{32,64},{64,96},{96,128},{128,160},{160,192},{192,224},{1,3... | collective-permute-start | bytes 1228808 | tf_op jit(solution)/shard_map/ppermute | solution.py:38
  118.0 3.5 %collective-permute-start.5 = (bf16[5,128,128]{2,1,0:T(8,128)(2,1)S(1)}, bf16[5,128,128]{2,1,0:T(8,128)(2,1)S(1)}, u32[]{:S(2)}, u32[]{:S(2)}) collective-permute-start(bf16[5,128,128]{2,1,0:T(8,128)(2,1)S(1)} %get-tuple-element.14.table_ref), channel_id=1, source_target_pairs={{0,32},{32,64},{64,96},{96,128},{128,160},{160,192},{192,224},{1,3... | collective-permute-start | bytes 491528 | tf_op jit(solution)/shard_map/ppermute | solution.py:38
  121.5 5.6 %collective-permute-done.5.table_ref = bf16[5,128,128]{2,1,0:T(8,128)(2,1)S(1)} collective-permute-done((bf16[5,128,128]{2,1,0:T(8,128)(2,1)S(1)}, bf16[5,128,128]{2,1,0:T(8,128)(2,1)S(1)}, u32[]{:S(2)}, u32[]{:S(2)}) %collective-permute-start.5) | collective-permute-done | bytes 163872 | tf_op jit(solution)/shard_map/ppermute | solution.py:38
  127.1 0.3 update.1
  127.4 11.9 %all_to_all.34 = bf16[4,80,640]{2,1,0:T(8,128)(2,1)S(1)} all-to-all(bf16[4,80,640]{2,1,0:T(8,128)(2,1)S(1)} %bitcast.11), channel_id=1, replica_groups=mesh['layer'=8,'y'=4,'z'=8] {'y'}, dimensions={0} | all-to-all | bytes 819200 | tf_op jit(solution)/shard_map/all_to_all | solution.py:224
  139.2 0.8 join.1
  (11 shorter events, 0.1 us)
Async XLA Ops:
  1.3 15.1 %copy-start.1 = (bf16[5,128,128]{2,1,0:T(8,128)(2,1)}, bf16[5,128,128]{2,1,0:T(8,128)(2,1)S(1)}, u32[]{:S(2)}) copy-start(bf16[5,128,128]{2,1,0:T(8,128)(2,1)S(1)} %get-tuple-element.18.table_ref) | copy-start | bytes 491524
  13.8 9.9 %collective-permute-start = (bf16[320,640]{1,0:T(8,128)(2,1)S(1)}, bf16[320,640]{1,0:T(8,128)(2,1)S(1)}, u32[]{:S(2)}, u32[]{:S(2)}) collective-permute-start(bf16[320,640]{1,0:T(8,128)(2,1)S(1)} %bitcast.13), channel_id=1, source_target_pairs={{32,0},{64,32},{96,64},{128,96},{160,128},{192,160},{224,192},{33,... | collective-permute-start | bytes 1228808 | tf_op jit(solution)/shard_map/ppermute | solution.py:38
  15.7 54.1 %collective-permute-start.1 = (bf16[80,2560]{1,0:T(8,128)(2,1)}, bf16[80,2560]{1,0:T(8,128)(2,1)S(1)}, u32[]{:S(2)}, u32[]{:S(2)}) collective-permute-start(bf16[80,2560]{1,0:T(8,128)(2,1)} %bitcast.16), channel_id=1, source_target_pairs={{0,8},{8,16},{16,24},{24,0},{1,9},{9,17},{17,25},{25,1},{2,10},{10... | collective-permute-start | bytes 1228808 | tf_op jit(solution)/shard_map/ppermute | solution.py:220
  16.3 53.4 %collective-permute-start.2 = (bf16[80,2560]{1,0:T(8,128)(2,1)}, bf16[80,2560]{1,0:T(8,128)(2,1)S(1)}, u32[]{:S(2)}, u32[]{:S(2)}) collective-permute-start(bf16[80,2560]{1,0:T(8,128)(2,1)} %bitcast.17), channel_id=1, source_target_pairs={{0,16},{8,24},{16,0},{24,8},{1,17},{9,25},{17,1},{25,9},{2,18},{10... | collective-permute-start | bytes 1228808 | tf_op jit(solution)/shard_map/ppermute | solution.py:220
  18.4 51.4 %collective-permute-start.3 = (bf16[80,2560]{1,0:T(8,128)(2,1)}, bf16[80,2560]{1,0:T(8,128)(2,1)S(1)}, u32[]{:S(2)}, u32[]{:S(2)}) collective-permute-start(bf16[80,2560]{1,0:T(8,128)(2,1)} %bitcast.18), channel_id=1, source_target_pairs={{0,24},{8,0},{16,8},{24,16},{1,25},{9,1},{17,9},{25,17},{2,26},{10... | collective-permute-start | bytes 1228808 | tf_op jit(solution)/shard_map/ppermute | solution.py:220
  24.2 84.2 %all-to-all-start.1 = ((bf16[4,160,2560]{2,1,0:T(8,128)(2,1)}), bf16[4,160,2560]{2,1,0:T(8,128)(2,1)}, u32[]{:S(2)}, u32[]{:S(2)}) async-start(bf16[4,160,2560]{2,1,0:T(8,128)(2,1)} %bitcast.5), calls=%async_computation.1 | async-start | bytes 6553600 | tf_op jit(solution)/shard_map/all_to_all | solution.py:224
  69.1 1.0 copy-start
  108.4 0.9 copy-start.2
  116.1 11.0 %collective-permute-start.4 = (bf16[320,640]{1,0:T(8,128)(2,1)S(1)}, bf16[320,640]{1,0:T(8,128)(2,1)S(1)}, u32[]{:S(2)}, u32[]{:S(2)}) collective-permute-start(bf16[320,640]{1,0:T(8,128)(2,1)S(1)} %get-tuple-element.20), channel_id=1, source_target_pairs={{0,32},{32,64},{64,96},{96,128},{128,160},{160,192},{192,224},{1,3... | collective-permute-start | bytes 1228808 | tf_op jit(solution)/shard_map/ppermute | solution.py:38
  118.0 9.1 %collective-permute-start.5 = (bf16[5,128,128]{2,1,0:T(8,128)(2,1)S(1)}, bf16[5,128,128]{2,1,0:T(8,128)(2,1)S(1)}, u32[]{:S(2)}, u32[]{:S(2)}) collective-permute-start(bf16[5,128,128]{2,1,0:T(8,128)(2,1)S(1)} %get-tuple-element.14.table_ref), channel_id=1, source_target_pairs={{0,32},{32,64},{64,96},{96,128},{128,160},{160,192},{192,224},{1,3... | collective-permute-start | bytes 491528 | tf_op jit(solution)/shard_map/ppermute | solution.py:38

commit v4 on v3

--- a/solution.py
+++ b/solution.py
@@ -97,10 +97,7 @@
 
     def kernel(panel_in, grad_ref, *refs):
         pieces, (out_ref, panel_ref, factor_ref) = refs[:shards], refs[shards:]
-        y = lax.axis_index("y")
-        for k in range(shards):
-            at = pl.multiple_of(lax.rem(y + (shards - k), shards) * rows, 16)
-            factor_ref[pl.ds(at, rows), :] = pieces[k][...]
+        gather_rows(pieces, factor_ref, rows)
         for at, w in chunks_of(width):
             cols = pl.ds(at, w)
             load_scaled(panel_in, panel_ref, at, w, shards, rows)
@@ -118,34 +115,60 @@
     )
 
 
-def last_tiles(panel, factors, table, shards):
-    tile, width = factors.shape[0] // 2, panel.shape[2]
-    depth, rows = factors.shape[1], tile // shards
-
-    def kernel(panel_in, factors_in, table_ref, local_ref, middle_ref, panel_ref, factors_ref, sem):
-        copy = pltpu.make_async_copy(factors_in, factors_ref, sem)
-        copy.start()
+def gather_rows(pieces, factor_ref, rows, first=0):
+    y, shards = lax.axis_index("y"), len(pieces)
+    for k in range(shards):
+        at = pl.multiple_of(lax.rem(y + (shards - k), shards) * rows, 16)
+        factor_ref[pl.ds(at, rows), :] = pieces[k][pl.ds(first, rows), :]
+
+
+def middle_tile(panel, factor, table, shards):
+    rows, depth = factor[0].shape[0] // 2, factor[0].shape[1]
+    tile, width = shards * rows, panel.shape[2]
+
+    def kernel(panel_in, table_ref, *refs):
+        pieces, (middle_ref, panel_ref, factor_ref) = refs[:shards], refs[shards:]
+        gather_rows(pieces, factor_ref, rows, rows)
         for at, w in chunks_of(width):
             load_scaled(panel_in, panel_ref, at, w, shards, rows)
-            if at == 0:
-                copy.wait()
-            both = jnp.dot(factors_ref[...], panel_ref[:, pl.ds(at, w)], preferred_element_type=F32).astype(BF)
+            carried = jnp.dot(factor_ref[...], panel_ref[:, pl.ds(at, w)], preferred_element_type=F32).astype(BF)
             for b in range(w // BLK):
-                sub = pl.ds(at + b * BLK, BLK)
-                block = table_ref[at // BLK + b]
-                product = jnp.dot(both[:, b * BLK : (b + 1) * BLK], block, preferred_element_type=F32)
-                for k in range(shards):
-                    local_ref[pl.ds(k * rows, rows), sub] = product[2 * k * rows : (2 * k + 1) * rows]
-                    middle_ref[pl.ds(k * rows, rows), sub] = product[(2 * k + 1) * rows : (2 * k + 2) * rows].astype(BF)
+                product = jnp.dot(
+                    carried[:, b * BLK : (b + 1) * BLK], table_ref[at // BLK + b], preferred_element_type=F32
+                )
+                middle_ref[:, pl.ds(at + b * BLK, BLK)] = product.astype(BF)
 
     return call(
         kernel,
-        (like(tile, width, F32), like(tile, width, BF)),
-        "last",
-        [panel, factors, table],
-        [pltpu.VMEM((depth, width), BF), pltpu.VMEM(factors.shape, BF), pltpu.SemaphoreType.DMA],
-        far=(1,),
-        flops=4 * tile * depth * width,
+        (like(tile, width, BF), like(depth, width, BF)),
+        "middle",
+        [panel, table, *factor],
+        [pltpu.VMEM((tile, depth), BF)],
+        flops=2 * tile * depth * width,
+    )
+
+
+def local_tile(panel, factor, table, shards):
+    rows, depth = factor[0].shape[0] // 2, factor[0].shape[1]
+    tile, width = shards * rows, panel.shape[1]
+
+    def kernel(panel_ref, table_ref, *refs):
+        pieces, (local_ref, factor_ref) = refs[:shards], refs[shards:]
+        gather_rows(pieces, factor_ref, rows)
+        for at, w in chunks_of(width):
+            whitened = jnp.dot(factor_ref[...], panel_ref[:, pl.ds(at, w)], preferred_element_type=F32).astype(BF)
+            for b in range(w // BLK):
+                local_ref[:, pl.ds(at + b * BLK, BLK)] = jnp.dot(
+                    whitened[:, b * BLK : (b + 1) * BLK], table_ref[at // BLK + b], preferred_element_type=F32
+                )
+
+    return call(
+        kernel,
+        like(tile, width, F32),
+        "local",
+        [panel, table, *factor],
+        [pltpu.VMEM((tile, depth), BF)],
+        flops=2 * tile * depth * width,
     )
 
 
@@ -203,16 +226,15 @@
     return copies(kernel, out, "prepare", [gradient, out_inverse, out_coupling], shards + 2)
 
 
-def repeat_rows(parts, shards, name):
+def stack(parts):
     rows, width = parts[0].shape[1:]
     count = len(parts)
 
     def kernel(*refs):
-        for k in range(shards):
-            for i in range(count):
-                yield refs[i].at[0], refs[count].at[pl.ds((k * count + i) * rows, rows), :]
-
-    return copies(kernel, like(shards * count * rows, width, BF), name, parts, shards * count)
+        for i in range(count):
+            yield refs[i].at[0], refs[count].at[pl.ds(i * rows, rows), :]
+
+    return copies(kernel, like(count * rows, width, BF), "stack", parts, count)
 
 
 def hop_y(x, by):
@@ -240,6 +262,10 @@
 
 def gather_panel(tile):
     return lax.all_gather(tile.astype(HALF), "z", axis=0).astype(BF)
+
+
+def from_peers(x, shards):
+    return [x] + [hop_y(x, k) for k in range(1, shards)]
 
 
 def local(gradient, in_inverse, in_coupling, in_carry, out_inverse, out_coupling):
@@ -248,12 +274,13 @@
     psi_below = hop_layer(psi, 1)
     grad = exchange(split)
     above = hop_layer(grad, -1)
-    coupling = after(in_coupling, grad)[0]
-    factor = [coupling] + [hop_y(coupling, k) for k in range(1, shards)]
-    near = near_tile(above, psi, shards)
-    factors = exchange(after(repeat_rows([after(in_inverse, grad), in_carry], shards, "twice"), near))
-    reduced = reduced_tile(gather_panel(near), factor, grad, shards)
-    local_term, middle = last_tiles(gather_panel(reduced), factors, inv, shards)
+    coupling = from_peers(after(in_coupling, grad)[0], shards)
+    both = stack([after(in_inverse, grad), in_carry])
+    near = near_tile(above, after(psi, psi_below), shards)
+    factors = from_peers(after(both, near), shards)
+    reduced = reduced_tile(gather_panel(near), coupling, grad, shards)
+    middle, panel = middle_tile(gather_panel(reduced), factors, inv, shards)
+    local_term = local_tile(panel, factors, inv, shards)
     update = update_tile(local_term, hop_layer(middle, 1), psi_below)
     return join_columns(exchange(update), shards)
 

time: 140 us -> 135 us (0.964)
  Pallas kernels: 15.4 us -> 11 us
  waiting for transfers between devices: 5.58 us -> 9 us
  blocking collectives: 100 us -> 97.9 us
    ppermute x3 -> x6, starting transfers between devices: 3.83 us -> 8.68 us  [hop_y(): return lax.ppermute(x, 'y', [(i, (i + by) % size) for i in range(size)])]
    all_to_all x1 -> x0, starting transfers between devices: 4.71 us -> none  [exchange(): return lax.all_to_all(x, 'y', split_axis=0, concat_axis=0, tiled=True)]
    ppermute x3, waiting for transfers between devices: 5.57 us -> 8.99 us  [hop_layer(): lax.ppermute(x, 'layer', [(i, i + by) for i in range(size) if 0 <= i + by...]
    pallas_call x2, Pallas kernels: 5.37 us -> 2.39 us  [copies(): pl.pallas_call(body, out_shape=out, in_specs=[HBM] * len(operands), out_s...]
    all_to_all x2, blocking collectives: 24.4 us -> 22.7 us  [exchange(): return lax.all_to_all(x, 'y', split_axis=0, concat_axis=0, tiled=True)]
    pallas_call x5 -> x6, Pallas kernels: 9.99 us -> 8.58 us  [call(): pl.pallas_call(kernel, out_shape=out, in_specs=[HBM if i in far else VMEM...]
  transfers between devices with their start and end apart: 7 -> 9, of which waited for: 1 -> 2; matrix products, arithmetic and copies ran while one was open for 1% -> 1% of each run, Pallas kernels for 5% -> 4%
where the time goes in v4:
time: 135 us; the launch traced here: 134 us
  blocking collectives  97.9 us (73%)
  starting transfers between devices  14.9 us (11%)
  Pallas kernels  11 us (8%)
  waiting for transfers between devices  9 us (7%)
  other arithmetic  1.42 us (1%)
    all_gather x2, blocking collectives, gather_panel(): return lax.all_gather(tile.astype(HALF), 'z', axis=0).astype(BF)  75.3 us
    all_to_all x2, blocking collectives, exchange(): return lax.all_to_all(x, 'y', split_axis=0, concat_axis=0, tiled=True)  22.7 us
    ppermute x3, waiting for transfers between devices, hop_layer(): lax.ppermute(x, 'layer', [(i, i + by) for i in range(size) if 0 <= i + by...  8.99 us
    ppermute x6, starting transfers between devices, hop_y(): return lax.ppermute(x, 'y', [(i, (i + by) % size) for i in range(size)])  8.68 us
    pallas_call x6, Pallas kernels, call(): pl.pallas_call(kernel, out_shape=out, in_specs=[HBM if i in far else VMEM...  8.58 us
    ppermute x3, starting transfers between devices, hop_layer(): lax.ppermute(x, 'layer', [(i, i + by) for i in range(size) if 0 <= i + by...  6.24 us
  transfers between devices with their start and end apart: 9, of which 2 were waited for; matrix products, arithmetic and copies ran while one was open for 1% of the time, Pallas kernels for 4%

profile of v4, /device:TPU:2, one launch (start us, length us, event | category | flops | bytes accessed | tf_op | source)
XLA Modules:
  0.0 134.4 jit_solution(6617872629707047158)
XLA Ops:
  0.0 1.3 prepare.1
  1.3 12.5 %all_to_all.22 = bf16[4,80,640]{2,1,0:T(8,128)(2,1)S(1)} all-to-all(bf16[4,80,640]{2,1,0:T(8,128)(2,1)S(1)} %bitcast.13), channel_id=1, replica_groups=mesh['layer'=8,'y'=4,'z'=8] {'y'}, dimensions={0} | all-to-all | bytes 819200 | tf_op jit(solution)/shard_map/all_to_all | solution.py:246
  13.8 1.9 %collective-permute-start = (bf16[320,640]{1,0:T(8,128)(2,1)S(1)}, bf16[320,640]{1,0:T(8,128)(2,1)S(1)}, u32[]{:S(2)}, u32[]{:S(2)}) collective-permute-start(bf16[320,640]{1,0:T(8,128)(2,1)S(1)} %bitcast.11), channel_id=1, source_target_pairs={{32,0},{64,32},{96,64},{128,96},{160,128},{192,160},{224,192},{33,... | collective-permute-start | bytes 1228808 | tf_op jit(solution)/shard_map/ppermute | solution.py:38
  15.7 2.4 %collective-permute-start.1 = (bf16[5,128,128]{2,1,0:T(8,128)(2,1)S(1)}, bf16[5,128,128]{2,1,0:T(8,128)(2,1)S(1)}, u32[]{:S(2)}, u32[]{:S(2)}) collective-permute-start(bf16[5,128,128]{2,1,0:T(8,128)(2,1)S(1)} %get-tuple-element.16.table_ref), channel_id=1, source_target_pairs={{0,32},{32,64},{64,96},{96,128},{128,160},{160,192},{192,224},{1,3... | collective-permute-start | bytes 491528 | tf_op jit(solution)/shard_map/ppermute | solution.py:38
  18.1 4.2 %collective-permute-done.1.table_ref = bf16[5,128,128]{2,1,0:T(8,128)(2,1)S(1)} collective-permute-done((bf16[5,128,128]{2,1,0:T(8,128)(2,1)S(1)}, bf16[5,128,128]{2,1,0:T(8,128)(2,1)S(1)}, u32[]{:S(2)}, u32[]{:S(2)}) %collective-permute-start.1) | collective-permute-done | bytes 163872 | tf_op jit(solution)/shard_map/ppermute | solution.py:38
  22.3 0.6 collective-permute-start.2
  22.9 2.1 %collective-permute-start.3 = (bf16[80,2560]{1,0:T(8,128)(2,1)}, bf16[80,2560]{1,0:T(8,128)(2,1)S(1)}, u32[]{:S(2)}, u32[]{:S(2)}) collective-permute-start(bf16[80,2560]{1,0:T(8,128)(2,1)} %bitcast.15), channel_id=1, source_target_pairs={{0,16},{8,24},{16,0},{24,8},{1,17},{9,25},{17,1},{25,9},{2,18},{10... | collective-permute-start | bytes 1228808 | tf_op jit(solution)/shard_map/ppermute | solution.py:242
  25.0 1.1 collective-permute-start.4
  26.1 1.1 stack.1.refs_0_
  27.2 0.4 near.1
  27.7 1.0 collective-permute-start.5
  28.7 1.6 %collective-permute-start.6 = (bf16[160,2560]{1,0:T(8,128)(2,1)S(1)}, bf16[160,2560]{1,0:T(8,128)(2,1)S(1)}, u32[]{:S(2)}, u32[]{:S(2)}) collective-permute-start(bf16[160,2560]{1,0:T(8,128)(2,1)S(1)} %stack.1.refs_0_), channel_id=1, source_target_pairs={{0,16},{8,24},{16,0},{24,8},{1,17},{9,25},{17,1},{25,9},{2,18},{10... | collective-permute-start | bytes 2457608 | tf_op jit(solution)/shard_map/ppermute | solution.py:242
  30.3 39.8 %all-gather.4 = f16[2624,640]{1,0:T(8,128)(2,1)S(1)} all-gather(f16[328,640]{1,0:T(8,128)(2,1)S(1)} %convert_element_type.12), channel_id=2, replica_groups=mesh['layer'=8,'y'=4,'z'=8] {'z'}, dimensions={0}, use_global_device_ids=true | all-gather | bytes 3778560 | tf_op jit(solution)/shard_map/all_gather | solution.py:264
  70.1 0.6 convert_element_type.16
  70.8 2.3 %collective-permute-start.7 = (bf16[160,2560]{1,0:T(8,128)(2,1)S(1)}, bf16[160,2560]{1,0:T(8,128)(2,1)S(1)}, u32[]{:S(2)}, u32[]{:S(2)}) collective-permute-start(bf16[160,2560]{1,0:T(8,128)(2,1)S(1)} %stack.1.refs_0_), channel_id=1, source_target_pairs={{0,24},{8,0},{16,8},{24,16},{1,25},{9,1},{17,9},{25,17},{2,26},{10... | collective-permute-start | bytes 2457608 | tf_op jit(solution)/shard_map/ppermute | solution.py:242
  73.1 1.8 %reduced.1 = bf16[328,640]{1,0:T(8,128)(2,1)S(1)} custom-call(bf16[8,328,640]{2,1,0:T(8,128)(2,1)S(1)} %bitcast.8, bf16[320,640]{1,0:T(8,128)(2,1)S(1)} %bitcast.12, bf16[80,2560]{1,0:T(8,128)(2,1)S(1)} %bitcast.17, bf16[80,2560]{1,0:T(8,128)(2,1)S(1)} %collective-permute-done.2.refs_1_, bf16[80,2560]{1,0:T(8,128)(2,1)S(1)} %collective-permute-done.3.refs_2_, ...), custom_call_target="tpu_custom_call" | custom-call | flops 1048576000 | bytes 5826560 | tf_op jit(solution)/shard_map/reduced/pallas_call | solution.py:20
  75.0 35.5 %all-gather.5 = f16[2624,640]{1,0:T(8,128)(2,1)S(1)} all-gather(f16[328,640]{1,0:T(8,128)(2,1)S(1)} %convert_element_type.14), channel_id=3, replica_groups=mesh['layer'=8,'y'=4,'z'=8] {'z'}, dimensions={0}, use_global_device_ids=true | all-gather | bytes 3778560 | tf_op jit(solution)/shard_map/all_gather | solution.py:264
  110.5 0.6 convert_element_type.17
  111.1 2.8 %middle.1 = (bf16[320,640]{1,0:T(8,128)(2,1)S(1)}, bf16[2560,640]{1,0:T(8,128)(2,1)S(1)}) custom-call(bf16[8,328,640]{2,1,0:T(8,128)(2,1)S(1)} %bitcast.7, bf16[5,128,128]{2,1,0:T(8,128)(2,1)S(1)} %get-tuple-element.18.table_ref, bf16[160,2560]{1,0:T(8,128)(2,1)S(1)} %stack.1.refs_0_, bf16[160,2560]{1,0:T(8,128)(2,1)S(1)} %collective-permute-done.5.refs_1_, ...), custom_call_target="tpu_custom_call" | custom-call | flops 1048576000 | bytes 10485760 | tf_op jit(solution)/shard_map/middle/pallas_call | solution.py:20
  113.9 1.9 %collective-permute-start.8 = (bf16[320,640]{1,0:T(8,128)(2,1)S(1)}, bf16[320,640]{1,0:T(8,128)(2,1)S(1)}, u32[]{:S(2)}, u32[]{:S(2)}) collective-permute-start(bf16[320,640]{1,0:T(8,128)(2,1)S(1)} %get-tuple-element.22), channel_id=1, source_target_pairs={{0,32},{32,64},{64,96},{96,128},{128,160},{160,192},{192,224},{1,3... | collective-permute-start | bytes 1228808 | tf_op jit(solution)/shard_map/ppermute | solution.py:38
  115.8 2.6 %local.1.local_ref = f32[320,640]{1,0:T(8,128)S(1)} custom-call(bf16[2560,640]{1,0:T(8,128)(2,1)S(1)} %get-tuple-element.21.panel_ref, bf16[5,128,128]{2,1,0:T(8,128)(2,1)S(1)} %get-tuple-element.18.table_ref, bf16[160,2560]{1,0:T(8,128)(2,1)S(1)} %stack.1.refs_0_, bf16[160,2560]{1,0:T(8,128)(2,1)S(1)} %collective-permute-done.5.refs_1_, ...), custom_call_target="tpu_custom_call" | custom-call | flops 1048576000 | bytes 7536640 | tf_op jit(solution)/shard_map/local/pallas_call | solution.py:20
  118.4 4.8 %collective-permute-done.8.middle_ref = bf16[320,640]{1,0:T(8,128)(2,1)S(1)} collective-permute-done((bf16[320,640]{1,0:T(8,128)(2,1)S(1)}, bf16[320,640]{1,0:T(8,128)(2,1)S(1)}, u32[]{:S(2)}, u32[]{:S(2)}) %collective-permute-start.8) | collective-permute-done | bytes 409632 | tf_op jit(solution)/shard_map/ppermute | solution.py:38
  123.4 10.2 %all_to_all.23 = bf16[4,80,640]{2,1,0:T(8,128)(2,1)S(1)} all-to-all(bf16[4,80,640]{2,1,0:T(8,128)(2,1)S(1)} %bitcast.9), channel_id=1, replica_groups=mesh['layer'=8,'y'=4,'z'=8] {'y'}, dimensions={0} | all-to-all | bytes 819200 | tf_op jit(solution)/shard_map/all_to_all | solution.py:246
  133.6 0.8 join.1
  (12 shorter events, 0.4 us)
Async XLA Ops:
  13.8 13.5 %collective-permute-start = (bf16[320,640]{1,0:T(8,128)(2,1)S(1)}, bf16[320,640]{1,0:T(8,128)(2,1)S(1)}, u32[]{:S(2)}, u32[]{:S(2)}) collective-permute-start(bf16[320,640]{1,0:T(8,128)(2,1)S(1)} %bitcast.11), channel_id=1, source_target_pairs={{32,0},{64,32},{96,64},{128,96},{160,128},{192,160},{224,192},{33,... | collective-permute-start | bytes 1228808 | tf_op jit(solution)/shard_map/ppermute | solution.py:38
  15.7 6.6 %collective-permute-start.1 = (bf16[5,128,128]{2,1,0:T(8,128)(2,1)S(1)}, bf16[5,128,128]{2,1,0:T(8,128)(2,1)S(1)}, u32[]{:S(2)}, u32[]{:S(2)}) collective-permute-start(bf16[5,128,128]{2,1,0:T(8,128)(2,1)S(1)} %get-tuple-element.16.table_ref), channel_id=1, source_target_pairs={{0,32},{32,64},{64,96},{96,128},{128,160},{160,192},{192,224},{1,3... | collective-permute-start | bytes 491528 | tf_op jit(solution)/shard_map/ppermute | solution.py:38
  22.3 48.4 %collective-permute-start.2 = (bf16[80,2560]{1,0:T(8,128)(2,1)}, bf16[80,2560]{1,0:T(8,128)(2,1)S(1)}, u32[]{:S(2)}, u32[]{:S(2)}) collective-permute-start(bf16[80,2560]{1,0:T(8,128)(2,1)} %bitcast.14), channel_id=1, source_target_pairs={{0,8},{8,16},{16,24},{24,0},{1,9},{9,17},{17,25},{25,1},{2,10},{10... | collective-permute-start | bytes 1228808 | tf_op jit(solution)/shard_map/ppermute | solution.py:242
  22.9 50.2 %collective-permute-start.3 = (bf16[80,2560]{1,0:T(8,128)(2,1)}, bf16[80,2560]{1,0:T(8,128)(2,1)S(1)}, u32[]{:S(2)}, u32[]{:S(2)}) collective-permute-start(bf16[80,2560]{1,0:T(8,128)(2,1)} %bitcast.15), channel_id=1, source_target_pairs={{0,16},{8,24},{16,0},{24,8},{1,17},{9,25},{17,1},{25,9},{2,18},{10... | collective-permute-start | bytes 1228808 | tf_op jit(solution)/shard_map/ppermute | solution.py:242
  25.0 48.1 %collective-permute-start.4 = (bf16[80,2560]{1,0:T(8,128)(2,1)}, bf16[80,2560]{1,0:T(8,128)(2,1)S(1)}, u32[]{:S(2)}, u32[]{:S(2)}) collective-permute-start(bf16[80,2560]{1,0:T(8,128)(2,1)} %bitcast.16), channel_id=1, source_target_pairs={{0,24},{8,0},{16,8},{24,16},{1,25},{9,1},{17,9},{25,17},{2,26},{10... | collective-permute-start | bytes 1228808 | tf_op jit(solution)/shard_map/ppermute | solution.py:242
  27.7 83.4 %collective-permute-start.5 = (bf16[160,2560]{1,0:T(8,128)(2,1)S(1)}, bf16[160,2560]{1,0:T(8,128)(2,1)S(1)}, u32[]{:S(2)}, u32[]{:S(2)}) collective-permute-start(bf16[160,2560]{1,0:T(8,128)(2,1)S(1)} %stack.1.refs_0_), channel_id=1, source_target_pairs={{0,8},{8,16},{16,24},{24,0},{1,9},{9,17},{17,25},{25,1},{2,10},{10... | collective-permute-start | bytes 2457608 | tf_op jit(solution)/shard_map/ppermute | solution.py:242
  28.7 82.4 %collective-permute-start.6 = (bf16[160,2560]{1,0:T(8,128)(2,1)S(1)}, bf16[160,2560]{1,0:T(8,128)(2,1)S(1)}, u32[]{:S(2)}, u32[]{:S(2)}) collective-permute-start(bf16[160,2560]{1,0:T(8,128)(2,1)S(1)} %stack.1.refs_0_), channel_id=1, source_target_pairs={{0,16},{8,24},{16,0},{24,8},{1,17},{9,25},{17,1},{25,9},{2,18},{10... | collective-permute-start | bytes 2457608 | tf_op jit(solution)/shard_map/ppermute | solution.py:242
  70.1 3.0 %copy-start = (bf16[1,80,2560]{2,1,0:T(8,128)(2,1)S(1)}, bf16[1,80,2560]{2,1,0:T(8,128)(2,1)}, u32[]{:S(2)}) copy-start(bf16[1,80,2560]{2,1,0:T(8,128)(2,1)} %param.8) | copy-start | bytes 1228804
  70.8 40.4 %collective-permute-start.7 = (bf16[160,2560]{1,0:T(8,128)(2,1)S(1)}, bf16[160,2560]{1,0:T(8,128)(2,1)S(1)}, u32[]{:S(2)}, u32[]{:S(2)}) collective-permute-start(bf16[160,2560]{1,0:T(8,128)(2,1)S(1)} %stack.1.refs_0_), channel_id=1, source_target_pairs={{0,24},{8,0},{16,8},{24,16},{1,25},{9,1},{17,9},{25,17},{2,26},{10... | collective-permute-start | bytes 2457608 | tf_op jit(solution)/shard_map/ppermute | solution.py:242
  113.9 9.3 %collective-permute-start.8 = (bf16[320,640]{1,0:T(8,128)(2,1)S(1)}, bf16[320,640]{1,0:T(8,128)(2,1)S(1)}, u32[]{:S(2)}, u32[]{:S(2)}) collective-permute-start(bf16[320,640]{1,0:T(8,128)(2,1)S(1)} %get-tuple-element.22), channel_id=1, source_target_pairs={{0,32},{32,64},{64,96},{96,128},{128,160},{160,192},{192,224},{1,3... | collective-permute-start | bytes 1228808 | tf_op jit(solution)/shard_map/ppermute | solution.py:38

commit v5 on v4

--- a/solution.py
+++ b/solution.py
@@ -42,13 +42,12 @@
     return [(at, min(256, width - at)) for at in range(0, width, 256)]
 
 
-def store_scaled(out_ref, values, at, shards, rows):
-    width = values.shape[1]
+def store_scaled(out_ref, parts, owners, at):
+    rows, width = parts[0].shape
     cols = pl.ds(at, width)
     line = lax.broadcasted_iota(jnp.int32, (CODE, width), 0)
     codes = jnp.full((CODE, width), 1.0, F32)
-    for k in range(shards):
-        part = values[k * rows : (k + 1) * rows]
+    for part, owner in zip(parts, owners, strict=True):
         top = jnp.max(jnp.abs(part), axis=0, keepdims=True)
         scale = jnp.ones_like(top)
         code = jnp.full_like(top, 128.0)
@@ -58,9 +57,27 @@
             top = top * grow
             scale = scale * grow
             code = code * jnp.where(small, 2.0 ** (-(bits // 8)), 1.0)
-        out_ref[pl.ds(k * rows, rows), cols] = (part * scale).astype(BF)
-        codes = jnp.where(line == k, code, codes)
-    out_ref[pl.ds(shards * rows, CODE), cols] = codes.astype(BF)
+        out_ref[rows_of(owner, rows), cols] = (part * scale).astype(BF)
+        codes = jnp.where(line == owner, code, codes)
+    out_ref[pl.ds(len(parts) * rows, CODE), cols] = codes.astype(BF)
+
+
+def rows_of(owner, rows):
+    return pl.ds(owner * rows if isinstance(owner, int) else pl.multiple_of(owner * rows, 16), rows)
+
+
+def blocks_of(values, count):
+    rows = values.shape[0] // count
+    return [values[k * rows : (k + 1) * rows] for k in range(count)]
+
+
+def owners_of(shards):
+    y = lax.axis_index("y")
+    return [lax.rem(y + (shards - k), shards) for k in range(shards)]
+
+
+def joined(pieces, rows, first=0):
+    return jnp.concatenate([piece[pl.ds(first, rows), :] for piece in pieces], axis=0)
 
 
 def load_scaled(in_ref, panel_ref, at, width, shards, rows):
@@ -86,7 +103,7 @@
             near = lax.dot_general(
                 above_ref[:, pl.ds(b * BLK, BLK)], block, (((1,), (1,)), ((), ())), preferred_element_type=F32
             )
-            store_scaled(out_ref, near.astype(BF).astype(F32), b * BLK, shards, tile // shards)
+            store_scaled(out_ref, blocks_of(near.astype(BF).astype(F32), shards), list(range(shards)), b * BLK)
 
     return call(kernel, like(tile + CODE, width, BF), "near", [above, table], flops=2 * tile * width * BLK)
 
@@ -96,93 +113,87 @@
     depth, rows = factor[0].shape[1], tile // shards
 
     def kernel(panel_in, grad_ref, *refs):
-        pieces, (out_ref, panel_ref, factor_ref) = refs[:shards], refs[shards:]
-        gather_rows(pieces, factor_ref, rows)
+        pieces, (out_ref, panel_ref) = refs[:shards], refs[shards:]
+        owners = owners_of(shards)
         for at, w in chunks_of(width):
             cols = pl.ds(at, w)
             load_scaled(panel_in, panel_ref, at, w, shards, rows)
-            coupled = jnp.dot(factor_ref[...], panel_ref[:, cols], preferred_element_type=F32)
-            reduced = (grad_ref[:, cols].astype(F32) - coupled).astype(BF).astype(F32)
-            store_scaled(out_ref, reduced, at, shards, rows)
+            coupled = jnp.dot(joined(pieces, rows), panel_ref[:, cols], preferred_element_type=F32)
+            parts = [
+                (grad_ref[rows_of(owner, rows), cols].astype(F32) - part).astype(BF).astype(F32)
+                for owner, part in zip(owners, blocks_of(coupled, shards), strict=True)
+            ]
+            store_scaled(out_ref, parts, owners, at)
 
     return call(
         kernel,
         like(tile + CODE, width, BF),
         "reduced",
         [panel, grad, *factor],
-        [pltpu.VMEM((depth, width), BF), pltpu.VMEM((tile, depth), BF)],
+        [pltpu.VMEM((depth, width), BF)],
         flops=2 * tile * depth * width,
     )
 
 
-def gather_rows(pieces, factor_ref, rows, first=0):
-    y, shards = lax.axis_index("y"), len(pieces)
-    for k in range(shards):
-        at = pl.multiple_of(lax.rem(y + (shards - k), shards) * rows, 16)
-        factor_ref[pl.ds(at, rows), :] = pieces[k][pl.ds(first, rows), :]
-
-
-def middle_tile(panel, factor, table, shards):
+def pushed_tile(panel, factor, inverse, coupling, shards):
     rows, depth = factor[0].shape[0] // 2, factor[0].shape[1]
     tile, width = shards * rows, panel.shape[2]
 
-    def kernel(panel_in, table_ref, *refs):
-        pieces, (middle_ref, panel_ref, factor_ref) = refs[:shards], refs[shards:]
-        gather_rows(pieces, factor_ref, rows, rows)
+    def kernel(panel_in, inverse_ref, coupling_ref, *refs):
+        pieces, (pushed_ref, panel_ref) = refs[:shards], refs[shards:]
+        owners = owners_of(shards)
+        carried = []
         for at, w in chunks_of(width):
             load_scaled(panel_in, panel_ref, at, w, shards, rows)
-            carried = jnp.dot(factor_ref[...], panel_ref[:, pl.ds(at, w)], preferred_element_type=F32).astype(BF)
-            for b in range(w // BLK):
-                product = jnp.dot(
-                    carried[:, b * BLK : (b + 1) * BLK], table_ref[at // BLK + b], preferred_element_type=F32
-                )
-                middle_ref[:, pl.ds(at + b * BLK, BLK)] = product.astype(BF)
+            both = jnp.dot(joined(pieces, rows, rows), panel_ref[:, pl.ds(at, w)], preferred_element_type=F32)
+            carried += [both[:, i : i + BLK].astype(BF) for i in range(0, w, BLK)]
+        middle = [
+            jnp.dot(x, inverse_ref[b], preferred_element_type=F32).astype(BF) for b, x in enumerate(carried)
+        ]
+        for b, x in enumerate(middle):
+            pushed = jnp.dot(x, coupling_ref[b], preferred_element_type=F32).astype(BF)
+            for owner, part in zip(owners, blocks_of(pushed, shards), strict=True):
+                pushed_ref[rows_of(owner, rows), pl.ds(b * BLK, BLK)] = part
 
     return call(
         kernel,
         (like(tile, width, BF), like(depth, width, BF)),
-        "middle",
-        [panel, table, *factor],
-        [pltpu.VMEM((tile, depth), BF)],
+        "pushed",
+        [panel, inverse, coupling, *factor],
         flops=2 * tile * depth * width,
     )
 
 
-def local_tile(panel, factor, table, shards):
+def local_tile(panel, factor, inverse, shards):
     rows, depth = factor[0].shape[0] // 2, factor[0].shape[1]
     tile, width = shards * rows, panel.shape[1]
 
-    def kernel(panel_ref, table_ref, *refs):
-        pieces, (local_ref, factor_ref) = refs[:shards], refs[shards:]
-        gather_rows(pieces, factor_ref, rows)
+    def kernel(panel_ref, inverse_ref, *refs):
+        pieces, (local_ref,) = refs[:shards], refs[shards:]
+        owners = owners_of(shards)
+        whitened = []
         for at, w in chunks_of(width):
-            whitened = jnp.dot(factor_ref[...], panel_ref[:, pl.ds(at, w)], preferred_element_type=F32).astype(BF)
-            for b in range(w // BLK):
-                local_ref[:, pl.ds(at + b * BLK, BLK)] = jnp.dot(
-                    whitened[:, b * BLK : (b + 1) * BLK], table_ref[at // BLK + b], preferred_element_type=F32
-                )
+            both = jnp.dot(joined(pieces, rows), panel_ref[:, pl.ds(at, w)], preferred_element_type=F32)
+            whitened += [both[:, i : i + BLK].astype(BF) for i in range(0, w, BLK)]
+        for b, x in enumerate(whitened):
+            product = jnp.dot(x, inverse_ref[b], preferred_element_type=F32)
+            for owner, part in zip(owners, blocks_of(product, shards), strict=True):
+                local_ref[rows_of(owner, rows), pl.ds(b * BLK, BLK)] = part
 
     return call(
         kernel,
         like(tile, width, F32),
         "local",
-        [panel, table, *factor],
-        [pltpu.VMEM((tile, depth), BF)],
+        [panel, inverse, *factor],
         flops=2 * tile * depth * width,
     )
 
 
-def update_tile(local_term, middle, table):
-    tile, width = middle.shape
-    blocks = width // BLK
-
-    def kernel(local_ref, middle_ref, table_ref, out_ref):
-        for b in range(blocks):
-            cols = pl.ds(b * BLK, BLK)
-            pushed = jnp.dot(middle_ref[:, cols], table_ref[b], preferred_element_type=F32)
-            out_ref[:, cols] = (local_ref[:, cols] - pushed).astype(BF)
-
-    return call(kernel, like(tile, width, BF), "update", [local_term, middle, table], flops=2 * tile * width * BLK)
+def update_tile(local_term, pushed):
+    def kernel(local_ref, pushed_ref, out_ref):
+        out_ref[...] = (local_ref[...] - pushed_ref[...].astype(F32)).astype(BF)
+
+    return call(kernel, like(*pushed.shape, BF), "update", [local_term, pushed])
 
 
 def copies(kernel, out, name, operands, count):
@@ -264,24 +275,21 @@
     return lax.all_gather(tile.astype(HALF), "z", axis=0).astype(BF)
 
 
-def from_peers(x, shards):
-    return [x] + [hop_y(x, k) for k in range(1, shards)]
-
-
 def local(gradient, in_inverse, in_coupling, in_carry, out_inverse, out_coupling):
     shards = lax.axis_size("y")
     split, inv, psi = prepare(gradient, out_inverse, out_coupling, shards)
-    psi_below = hop_layer(psi, 1)
     grad = exchange(split)
     above = hop_layer(grad, -1)
-    coupling = from_peers(after(in_coupling, grad)[0], shards)
-    both = stack([after(in_inverse, grad), in_carry])
-    near = near_tile(above, after(psi, psi_below), shards)
-    factors = from_peers(after(both, near), shards)
+    coupling = after(in_coupling, grad)[0]
+    coupling = [coupling] + [hop_y(coupling, k) for k in range(1, shards)]
+    pair = stack([after(in_inverse, split), in_carry])
+    near = near_tile(above, psi, shards)
+    early, late = after(pair, grad), after(pair, near)
+    factors = [pair] + [hop_y(early if k == 2 else late, k) for k in range(1, shards)]
     reduced = reduced_tile(gather_panel(near), coupling, grad, shards)
-    middle, panel = middle_tile(gather_panel(reduced), factors, inv, shards)
+    pushed, panel = pushed_tile(gather_panel(reduced), factors, inv, psi, shards)
     local_term = local_tile(panel, factors, inv, shards)
-    update = update_tile(local_term, hop_layer(middle, 1), psi_below)
+    update = update_tile(local_term, hop_layer(pushed, 1))
     return join_columns(exchange(update), shards)
 
 

time: 135 us -> 128 us (0.948)
  waiting for transfers between devices: 9 us -> 5.62 us
  Pallas kernels: 11 us -> 9.18 us
  starting transfers between devices: 14.9 us -> 13.4 us
    ppermute x3 -> x2, waiting for transfers between devices: 8.99 us -> 5.6 us  [hop_layer(): lax.ppermute(x, 'layer', [(i, i + by) for i in range(size) if 0 <= i + by...]
    ppermute x3 -> x2, starting transfers between devices: 6.24 us -> 3.83 us  [hop_layer(): lax.ppermute(x, 'layer', [(i, i + by) for i in range(size) if 0 <= i + by...]
    pallas_call x6, Pallas kernels: 8.58 us -> 6.74 us  [call(): pl.pallas_call(kernel, out_shape=out, in_specs=[HBM if i in far else VMEM...]
  transfers between devices with their start and end apart: 9 -> 8, of which waited for: 2 -> 1; matrix products, arithmetic and copies ran while one was open for 1% -> 1% of each run, Pallas kernels for 4% -> 4%
where the time goes in v5:
time: 128 us
  blocking collectives  98.5 us (77%)
  starting transfers between devices  13.4 us (10%)
  Pallas kernels  9.18 us (7%)
  waiting for transfers between devices  5.62 us (4%)
  other arithmetic  1.42 us (1%)
    all_gather x2, blocking collectives, gather_panel(): return lax.all_gather(tile.astype(HALF), 'z', axis=0).astype(BF)  75.9 us
    all_to_all x2, blocking collectives, exchange(): return lax.all_to_all(x, 'y', split_axis=0, concat_axis=0, tiled=True)  22.6 us
    ppermute x6, starting transfers between devices, hop_y(): return lax.ppermute(x, 'y', [(i, (i + by) % size) for i in range(size)])  9.54 us
    pallas_call x6, Pallas kernels, call(): pl.pallas_call(kernel, out_shape=out, in_specs=[HBM if i in far else VMEM...  6.74 us
    ppermute x2, waiting for transfers between devices, hop_layer(): lax.ppermute(x, 'layer', [(i, i + by) for i in range(size) if 0 <= i + by...  5.6 us
    ppermute x2, starting transfers between devices, hop_layer(): lax.ppermute(x, 'layer', [(i, i + by) for i in range(size) if 0 <= i + by...  3.83 us
  transfers between devices with their start and end apart: 8, of which 1 were waited for; matrix products, arithmetic and copies ran while one was open for 1% of the time, Pallas kernels for 4%

profile of v5, /device:TPU:2, one launch (start us, length us, event | category | flops | bytes accessed | tf_op | source)
XLA Modules:
  0.0 128.2 jit_solution(18418812602765370117)
XLA Ops:
  0.0 1.3 %prepare.1 = (bf16[320,640]{1,0:T(8,128)(2,1)S(1)}, bf16[5,128,128]{2,1,0:T(8,128)(2,1)S(1)}, bf16[5,128,128]{2,1,0:T(8,128)(2,1)S(1)}) custom-call(bf16[1,80,2560]{2,1,0:T(8,128)(2,1)} %refs_0_.1, bf16[1,20,128,128]{3,2,1,0:T(8,128)(2,1)} %refs_1_.2, bf16[1,20,128,128]{3,2,1,0:T(8,128)(2,1)} %refs_2_.1), custom_call_target="tpu_custom_call" | custom-call | bytes 1474560 | tf_op jit(solution)/shard_map/prepare/pallas_call | solution.py:211
  1.3 12.5 %all_to_all.22 = bf16[4,80,640]{2,1,0:T(8,128)(2,1)S(1)} all-to-all(bf16[4,80,640]{2,1,0:T(8,128)(2,1)S(1)} %bitcast.13), channel_id=1, replica_groups=mesh['layer'=8,'y'=4,'z'=8] {'y'}, dimensions={0} | all-to-all | bytes 819200 | tf_op jit(solution)/shard_map/all_to_all | solution.py:257
  13.8 1.9 %collective-permute-start = (bf16[320,640]{1,0:T(8,128)(2,1)S(1)}, bf16[320,640]{1,0:T(8,128)(2,1)S(1)}, u32[]{:S(2)}, u32[]{:S(2)}) collective-permute-start(bf16[320,640]{1,0:T(8,128)(2,1)S(1)} %bitcast.11), channel_id=1, source_target_pairs={{32,0},{64,32},{96,64},{128,96},{160,128},{192,160},{224,192},{33,... | collective-permute-start | bytes 1228808 | tf_op jit(solution)/shard_map/ppermute | solution.py:38
  15.7 1.1 stack.1.refs_0_
  16.9 0.6 collective-permute-start.1
  17.5 2.1 %collective-permute-start.2 = (bf16[80,2560]{1,0:T(8,128)(2,1)S(1)}, bf16[80,2560]{1,0:T(8,128)(2,1)S(1)}, u32[]{:S(2)}, u32[]{:S(2)}) collective-permute-start(bf16[80,2560]{1,0:T(8,128)(2,1)S(1)} %bitcast.15), channel_id=1, source_target_pairs={{0,16},{8,24},{16,0},{24,8},{1,17},{9,25},{17,1},{25,9},{2,18},{10... | collective-permute-start | bytes 1228808 | tf_op jit(solution)/shard_map/ppermute | solution.py:253
  19.6 1.1 collective-permute-start.3
  20.7 2.4 %collective-permute-start.5 = (bf16[160,2560]{1,0:T(8,128)(2,1)S(1)}, bf16[160,2560]{1,0:T(8,128)(2,1)S(1)}, u32[]{:S(2)}, u32[]{:S(2)}) collective-permute-start(bf16[160,2560]{1,0:T(8,128)(2,1)S(1)} %stack.1.refs_0_), channel_id=1, source_target_pairs={{0,16},{8,24},{16,0},{24,8},{1,17},{9,25},{17,1},{25,9},{2,18},{10... | collective-permute-start | bytes 2457608 | tf_op jit(solution)/shard_map/ppermute | solution.py:253
  23.1 0.4 near.1
  23.5 0.1 convert_element_type.12
  23.6 40.2 %all-gather.4 = f16[2624,640]{1,0:T(8,128)(2,1)S(1)} all-gather(f16[328,640]{1,0:T(8,128)(2,1)S(1)} %convert_element_type.12), channel_id=2, replica_groups=mesh['layer'=8,'y'=4,'z'=8] {'z'}, dimensions={0}, use_global_device_ids=true | all-gather | bytes 3778560 | tf_op jit(solution)/shard_map/all_gather | solution.py:275
  63.8 0.6 convert_element_type.16
  64.5 0.1 collective-permute-start.4
  64.6 3.2 %collective-permute-start.6 = (bf16[160,2560]{1,0:T(8,128)(2,1)S(1)}, bf16[160,2560]{1,0:T(8,128)(2,1)S(1)}, u32[]{:S(2)}, u32[]{:S(2)}) collective-permute-start(bf16[160,2560]{1,0:T(8,128)(2,1)S(1)} %stack.1.refs_0_), channel_id=1, source_target_pairs={{0,24},{8,0},{16,8},{24,16},{1,25},{9,1},{17,9},{25,17},{2,26},{10... | collective-permute-start | bytes 2457608 | tf_op jit(solution)/shard_map/ppermute | solution.py:253
  67.8 1.7 %reduced.1 = bf16[328,640]{1,0:T(8,128)(2,1)S(1)} custom-call(bf16[8,328,640]{2,1,0:T(8,128)(2,1)S(1)} %bitcast.7, bf16[320,640]{1,0:T(8,128)(2,1)S(1)} %bitcast.12, bf16[80,2560]{1,0:T(8,128)(2,1)S(1)} %bitcast.17, bf16[80,2560]{1,0:T(8,128)(2,1)S(1)} %collective-permute-done.1.refs_1_, bf16[80,2560]{1,0:T(8,128)(2,1)S(1)} %collective-permute-done.2.refs_2_, ...), custom_call_target="tpu_custom_call" | custom-call | flops 1048576000 | bytes 5826560 | tf_op jit(solution)/shard_map/reduced/pallas_call | solution.py:20
  69.5 0.1 convert_element_type.14
  69.6 35.7 %all-gather.5 = f16[2624,640]{1,0:T(8,128)(2,1)S(1)} all-gather(f16[328,640]{1,0:T(8,128)(2,1)S(1)} %convert_element_type.14), channel_id=3, replica_groups=mesh['layer'=8,'y'=4,'z'=8] {'z'}, dimensions={0}, use_global_device_ids=true | all-gather | bytes 3778560 | tf_op jit(solution)/shard_map/all_gather | solution.py:275
  105.3 0.6 convert_element_type.17
  105.9 2.1 %pushed.1 = (bf16[320,640]{1,0:T(8,128)(2,1)S(1)}, bf16[2560,640]{1,0:T(8,128)(2,1)S(1)}) custom-call(bf16[8,328,640]{2,1,0:T(8,128)(2,1)S(1)} %bitcast.8, bf16[5,128,128]{2,1,0:T(8,128)(2,1)S(1)} %get-tuple-element.17.inverse_ref, bf16[5,128,128]{2,1,0:T(8,128)(2,1)S(1)} %get-tuple-element.15.table_ref.coupling_ref, bf16[160,2560]{1,0:T(8,128)(2,1)S(1)} %stack.1.refs_0_, ...), custom_call_target="tpu_custom_call" | custom-call | flops 1048576000 | bytes 10649600 | tf_op jit(solution)/shard_map/pushed/pallas_call | solution.py:20
  108.0 1.9 %collective-permute-start.7 = (bf16[320,640]{1,0:T(8,128)(2,1)S(1)}, bf16[320,640]{1,0:T(8,128)(2,1)S(1)}, u32[]{:S(2)}, u32[]{:S(2)}) collective-permute-start(bf16[320,640]{1,0:T(8,128)(2,1)S(1)} %get-tuple-element.22), channel_id=1, source_target_pairs={{0,32},{32,64},{64,96},{96,128},{128,160},{160,192},{192,224},{1,3... | collective-permute-start | bytes 1228808 | tf_op jit(solution)/shard_map/ppermute | solution.py:38
  110.0 1.7 %local.1.local_ref = f32[320,640]{1,0:T(8,128)S(1)} custom-call(bf16[2560,640]{1,0:T(8,128)(2,1)S(1)} %get-tuple-element.21.panel_ref, bf16[5,128,128]{2,1,0:T(8,128)(2,1)S(1)} %get-tuple-element.17.inverse_ref, bf16[160,2560]{1,0:T(8,128)(2,1)S(1)} %stack.1.refs_0_, bf16[160,2560]{1,0:T(8,128)(2,1)S(1)} %collective-permute-done.4.refs_1_, ...), custom_call_target="tpu_custom_call" | custom-call | flops 1048576000 | bytes 7536640 | tf_op jit(solution)/shard_map/local/pallas_call | solution.py:20
  111.7 5.6 %collective-permute-done.7.pushed_ref = bf16[320,640]{1,0:T(8,128)(2,1)S(1)} collective-permute-done((bf16[320,640]{1,0:T(8,128)(2,1)S(1)}, bf16[320,640]{1,0:T(8,128)(2,1)S(1)}, u32[]{:S(2)}, u32[]{:S(2)}) %collective-permute-start.7) | collective-permute-done | bytes 409632 | tf_op jit(solution)/shard_map/ppermute | solution.py:38
  117.4 10.1 %all_to_all.23 = bf16[4,80,640]{2,1,0:T(8,128)(2,1)S(1)} all-to-all(bf16[4,80,640]{2,1,0:T(8,128)(2,1)S(1)} %bitcast.9), channel_id=1, replica_groups=mesh['layer'=8,'y'=4,'z'=8] {'y'}, dimensions={0} | all-to-all | bytes 819200 | tf_op jit(solution)/shard_map/all_to_all | solution.py:257
  127.4 0.8 join.1
  (10 shorter events, 0.1 us)
Async XLA Ops:
  0.0 16.9 %copy-start = (bf16[1,80,2560]{2,1,0:T(8,128)(2,1)S(1)}, bf16[1,80,2560]{2,1,0:T(8,128)(2,1)}, u32[]{:S(2)}) copy-start(bf16[1,80,2560]{2,1,0:T(8,128)(2,1)} %param.8) | copy-start | bytes 1228804
  13.8 9.3 %collective-permute-start = (bf16[320,640]{1,0:T(8,128)(2,1)S(1)}, bf16[320,640]{1,0:T(8,128)(2,1)S(1)}, u32[]{:S(2)}, u32[]{:S(2)}) collective-permute-start(bf16[320,640]{1,0:T(8,128)(2,1)S(1)} %bitcast.11), channel_id=1, source_target_pairs={{32,0},{64,32},{96,64},{128,96},{160,128},{192,160},{224,192},{33,... | collective-permute-start | bytes 1228808 | tf_op jit(solution)/shard_map/ppermute | solution.py:38
  16.9 47.7 %collective-permute-start.1 = (bf16[80,2560]{1,0:T(8,128)(2,1)S(1)}, bf16[80,2560]{1,0:T(8,128)(2,1)S(1)}, u32[]{:S(2)}, u32[]{:S(2)}) collective-permute-start(bf16[80,2560]{1,0:T(8,128)(2,1)S(1)} %bitcast.14), channel_id=1, source_target_pairs={{0,8},{8,16},{16,24},{24,0},{1,9},{9,17},{17,25},{25,1},{2,10},{10... | collective-permute-start | bytes 1228808 | tf_op jit(solution)/shard_map/ppermute | solution.py:253
  17.5 50.3 %collective-permute-start.2 = (bf16[80,2560]{1,0:T(8,128)(2,1)S(1)}, bf16[80,2560]{1,0:T(8,128)(2,1)S(1)}, u32[]{:S(2)}, u32[]{:S(2)}) collective-permute-start(bf16[80,2560]{1,0:T(8,128)(2,1)S(1)} %bitcast.15), channel_id=1, source_target_pairs={{0,16},{8,24},{16,0},{24,8},{1,17},{9,25},{17,1},{25,9},{2,18},{10... | collective-permute-start | bytes 1228808 | tf_op jit(solution)/shard_map/ppermute | solution.py:253
  19.6 48.2 %collective-permute-start.3 = (bf16[80,2560]{1,0:T(8,128)(2,1)S(1)}, bf16[80,2560]{1,0:T(8,128)(2,1)S(1)}, u32[]{:S(2)}, u32[]{:S(2)}) collective-permute-start(bf16[80,2560]{1,0:T(8,128)(2,1)S(1)} %bitcast.16), channel_id=1, source_target_pairs={{0,24},{8,0},{16,8},{24,16},{1,25},{9,1},{17,9},{25,17},{2,26},{10... | collective-permute-start | bytes 1228808 | tf_op jit(solution)/shard_map/ppermute | solution.py:253
  20.7 85.2 %collective-permute-start.5 = (bf16[160,2560]{1,0:T(8,128)(2,1)S(1)}, bf16[160,2560]{1,0:T(8,128)(2,1)S(1)}, u32[]{:S(2)}, u32[]{:S(2)}) collective-permute-start(bf16[160,2560]{1,0:T(8,128)(2,1)S(1)} %stack.1.refs_0_), channel_id=1, source_target_pairs={{0,16},{8,24},{16,0},{24,8},{1,17},{9,25},{17,1},{25,9},{2,18},{10... | collective-permute-start | bytes 2457608 | tf_op jit(solution)/shard_map/ppermute | solution.py:253
  64.5 41.4 %collective-permute-start.4 = (bf16[160,2560]{1,0:T(8,128)(2,1)S(1)}, bf16[160,2560]{1,0:T(8,128)(2,1)S(1)}, u32[]{:S(2)}, u32[]{:S(2)}) collective-permute-start(bf16[160,2560]{1,0:T(8,128)(2,1)S(1)} %stack.1.refs_0_), channel_id=1, source_target_pairs={{0,8},{8,16},{16,24},{24,0},{1,9},{9,17},{17,25},{25,1},{2,10},{10... | collective-permute-start | bytes 2457608 | tf_op jit(solution)/shard_map/ppermute | solution.py:253
  64.6 41.3 %collective-permute-start.6 = (bf16[160,2560]{1,0:T(8,128)(2,1)S(1)}, bf16[160,2560]{1,0:T(8,128)(2,1)S(1)}, u32[]{:S(2)}, u32[]{:S(2)}) collective-permute-start(bf16[160,2560]{1,0:T(8,128)(2,1)S(1)} %stack.1.refs_0_), channel_id=1, source_target_pairs={{0,24},{8,0},{16,8},{24,16},{1,25},{9,1},{17,9},{25,17},{2,26},{10... | collective-permute-start | bytes 2457608 | tf_op jit(solution)/shard_map/ppermute | solution.py:253
  108.0 9.3 %collective-permute-start.7 = (bf16[320,640]{1,0:T(8,128)(2,1)S(1)}, bf16[320,640]{1,0:T(8,128)(2,1)S(1)}, u32[]{:S(2)}, u32[]{:S(2)}) collective-permute-start(bf16[320,640]{1,0:T(8,128)(2,1)S(1)} %get-tuple-element.22), channel_id=1, source_target_pairs={{0,32},{32,64},{64,96},{96,128},{128,160},{160,192},{192,224},{1,3... | collective-permute-start | bytes 1228808 | tf_op jit(solution)/shard_map/ppermute | solution.py:38

commit v6 on v5

--- a/solution.py
+++ b/solution.py
@@ -189,11 +189,16 @@
     )
 
 
-def update_tile(local_term, pushed):
-    def kernel(local_ref, pushed_ref, out_ref):
-        out_ref[...] = (local_ref[...] - pushed_ref[...].astype(F32)).astype(BF)
-
-    return call(kernel, like(*pushed.shape, BF), "update", [local_term, pushed])
+def update_pieces(local_term, pushed, shards):
+    rows, width = pushed.shape[0] // shards, pushed.shape[1]
+
+    def kernel(local_ref, pushed_ref, *out_refs):
+        y = lax.axis_index("y")
+        for k in range(shards):
+            here = rows_of(lax.rem(y + k, shards), rows)
+            out_refs[k][...] = (local_ref[here, :] - pushed_ref[here, :].astype(F32)).astype(BF)
+
+    return call(kernel, tuple(like(rows, width, BF) for _ in range(shards)), "update", [local_term, pushed])
 
 
 def copies(kernel, out, name, operands, count):
@@ -226,15 +231,29 @@
     blocks = out_inverse.shape[1] // shards
     table = jax.ShapeDtypeStruct((blocks, BLK, BLK), BF)
 
-    def kernel(grad_ref, inverse_ref, coupling_ref, split_ref, inv_ref, psi_ref):
-        mine = pl.ds(lax.axis_index("y") * blocks, blocks)
+    def kernel(grad_ref, inverse_ref, coupling_ref, *out_refs):
+        y = lax.axis_index("y")
+        mine = pl.ds(y * blocks, blocks)
         for k in range(shards):
-            yield grad_ref.at[0, :, pl.ds(k * width, width)], split_ref.at[pl.ds(k * rows, rows), :]
-        yield coupling_ref.at[0, mine], psi_ref
-        yield inverse_ref.at[0, mine], inv_ref
-
-    out = (like(shards * rows, width, BF), table, table)
-    return copies(kernel, out, "prepare", [gradient, out_inverse, out_coupling], shards + 2)
+            at = pl.multiple_of(lax.rem(y + k, shards) * width, BLK)
+            yield grad_ref.at[0, :, pl.ds(at, width)], out_refs[k]
+        yield inverse_ref.at[0, mine], out_refs[shards]
+        yield coupling_ref.at[0, mine], out_refs[shards + 1]
+
+    out = (*[like(rows, width, BF)] * shards, table, table)
+    out = copies(kernel, out, "prepare", [gradient, out_inverse, out_coupling], shards + 2)
+    return out[:shards], *out[shards:]
+
+
+def assemble(pieces):
+    rows, width = pieces[0].shape
+    shards = len(pieces)
+
+    def kernel(*refs):
+        for k, owner in enumerate(owners_of(shards)):
+            refs[shards][rows_of(owner, rows), :] = refs[k][...]
+
+    return call(kernel, like(shards * rows, width, BF), "assemble", pieces)
 
 
 def stack(parts):
@@ -253,22 +272,23 @@
     return lax.ppermute(x, "y", [(i, (i + by) % size) for i in range(size)])
 
 
-def exchange(x):
-    return lax.all_to_all(x, "y", split_axis=0, concat_axis=0, tiled=True)
+def exchange(pieces):
+    return [pieces[0]] + [hop_y(pieces[k], k) for k in range(1, len(pieces))]
 
 
 def after(x, *others):
     return lax.optimization_barrier((x, *others))[0]
 
 
-def join_columns(x, shards):
-    rows, width = x.shape[0] // shards, x.shape[1]
-
-    def kernel(in_ref, out_ref):
-        for k in range(shards):
-            out_ref[0, :, pl.ds(k * width, width)] = in_ref[pl.ds(k * rows, rows), :]
-
-    return call(kernel, jax.ShapeDtypeStruct((1, rows, shards * width), x.dtype), "join", [x])
+def join_columns(pieces):
+    rows, width = pieces[0].shape
+    shards = len(pieces)
+
+    def kernel(*refs):
+        for k, owner in enumerate(owners_of(shards)):
+            refs[shards][0, :, pl.ds(pl.multiple_of(owner * width, BLK), width)] = refs[k][...]
+
+    return call(kernel, jax.ShapeDtypeStruct((1, rows, shards * width), BF), "join", pieces)
 
 
 def gather_panel(tile):
@@ -277,20 +297,21 @@
 
 def local(gradient, in_inverse, in_coupling, in_carry, out_inverse, out_coupling):
     shards = lax.axis_size("y")
-    split, inv, psi = prepare(gradient, out_inverse, out_coupling, shards)
-    grad = exchange(split)
+    slices, inv, psi = prepare(gradient, out_inverse, out_coupling, shards)
+    pieces = exchange(slices)
+    pair = stack([after(in_inverse, slices[0]), in_carry])
+    grad = assemble(lax.optimization_barrier((*pieces, pair))[:shards])
     above = hop_layer(grad, -1)
-    coupling = after(in_coupling, grad)[0]
-    coupling = [coupling] + [hop_y(coupling, k) for k in range(1, shards)]
-    pair = stack([after(in_inverse, split), in_carry])
+    coupling = after(in_coupling, slices[0])[0]
+    later = after(coupling, grad)
+    coupling = [coupling] + [hop_y(coupling if k < 3 else later, k) for k in range(1, shards)]
     near = near_tile(above, psi, shards)
     early, late = after(pair, grad), after(pair, near)
     factors = [pair] + [hop_y(early if k == 2 else late, k) for k in range(1, shards)]
     reduced = reduced_tile(gather_panel(near), coupling, grad, shards)
     pushed, panel = pushed_tile(gather_panel(reduced), factors, inv, psi, shards)
     local_term = local_tile(panel, factors, inv, shards)
-    update = update_tile(local_term, hop_layer(pushed, 1))
-    return join_columns(exchange(update), shards)
+    return join_columns(exchange(update_pieces(local_term, hop_layer(pushed, 1), shards)))
 
 
 def solution(mesh):

time: 128 us -> 123 us (0.961)
  blocking collectives: 98.5 us -> 76.8 us
  starting transfers between devices: 13.4 us -> 23.7 us
  waiting for transfers between devices: 5.62 us -> 11.8 us
    all_to_all x2 -> x0, blocking collectives: 22.6 us -> none  [exchange(): return lax.all_to_all(x, 'y', split_axis=0, concat_axis=0, tiled=True)]
    ppermute x6 -> x12, starting transfers between devices: 9.54 us -> 19.6 us  [hop_y(): return lax.ppermute(x, 'y', [(i, (i + by) % size) for i in range(size)])]
    ppermute x6 -> x12, waiting for transfers between devices: 0.02 us -> 6.35 us  [hop_y(): return lax.ppermute(x, 'y', [(i, (i + by) % size) for i in range(size)])]
    pallas_call x6 -> x7, Pallas kernels: 6.74 us -> 6.81 us  [call(): pl.pallas_call(kernel, out_shape=out, in_specs=[HBM if i in far else VMEM...]
  transfers between devices with their start and end apart: 8 -> 14, of which waited for: 1 -> 4; matrix products, arithmetic and copies ran while one was open for 1% -> 1% of each run, Pallas kernels for 4% -> 4%
where the time goes in v6:
time: 123 us
  blocking collectives  76.8 us (62%)
  starting transfers between devices  23.7 us (19%)
  waiting for transfers between devices  11.8 us (10%)
  Pallas kernels  9.25 us (8%)
  other arithmetic  1.42 us (1%)
    all_gather x2, blocking collectives, gather_panel(): return lax.all_gather(tile.astype(HALF), 'z', axis=0).astype(BF)  76.8 us
    ppermute x12, starting transfers between devices, hop_y(): return lax.ppermute(x, 'y', [(i, (i + by) % size) for i in range(size)])  19.6 us
    pallas_call x7, Pallas kernels, call(): pl.pallas_call(kernel, out_shape=out, in_specs=[HBM if i in far else VMEM...  6.81 us
    ppermute x12, waiting for transfers between devices, hop_y(): return lax.ppermute(x, 'y', [(i, (i + by) % size) for i in range(size)])  6.35 us
    ppermute x2, waiting for transfers between devices, hop_layer(): lax.ppermute(x, 'layer', [(i, i + by) for i in range(size) if 0 <= i + by...  5.42 us
    ppermute x2, starting transfers between devices, hop_layer(): lax.ppermute(x, 'layer', [(i, i + by) for i in range(size) if 0 <= i + by...  4.02 us
  transfers between devices with their start and end apart: 14, of which 4 were waited for; matrix products, arithmetic and copies ran while one was open for 1% of the time, Pallas kernels for 4%

profile of v6, /device:TPU:2, one launch (start us, length us, event | category | flops | bytes accessed | tf_op | source)
XLA Modules:
  0.0 123.0 jit_solution(10976048975666975740)
XLA Ops:
  0.0 1.3 %prepare.1 = (bf16[80,640]{1,0:T(8,128)(2,1)S(1)}, bf16[80,640]{1,0:T(8,128)(2,1)S(1)}, bf16[80,640]{1,0:T(8,128)(2,1)S(1)}, bf16[80,640]{1,0:T(8,128)(2,1)S(1)}...) custom-call(bf16[1,80,2560]{2,1,0:T(8,128)(2,1)} %refs_0_.1, bf16[1,20,128,128]{3,2,1,0:T(8,128)(2,1)} %refs_1_.2, ...), custom_call_target="tpu_custom_call" | custom-call | bytes 1474560 | tf_op jit(solution)/shard_map/prepare/pallas_call | solution.py:216
  1.3 1.7 %collective-permute-start = (bf16[80,640]{1,0:T(8,128)(2,1)S(1)}, bf16[80,640]{1,0:T(8,128)(2,1)S(1)}, u32[]{:S(2)}, u32[]{:S(2)}) collective-permute-start(bf16[80,640]{1,0:T(8,128)(2,1)S(1)} %get-tuple-element.27), channel_id=1, source_target_pairs={{0,8},{8,16},{16,24},{24,0},{1,9},{9,17},{17,25},{25,1},{2,10},{10... | collective-permute-start | bytes 307208 | tf_op jit(solution)/shard_map/ppermute | solution.py:272
  3.0 2.9 %collective-permute-start.1 = (bf16[80,640]{1,0:T(8,128)(2,1)S(1)}, bf16[80,640]{1,0:T(8,128)(2,1)S(1)}, u32[]{:S(2)}, u32[]{:S(2)}) collective-permute-start(bf16[80,640]{1,0:T(8,128)(2,1)S(1)} %get-tuple-element.28), channel_id=1, source_target_pairs={{0,16},{8,24},{16,0},{24,8},{1,17},{9,25},{17,1},{25,9},{2,18},{10... | collective-permute-start | bytes 307208 | tf_op jit(solution)/shard_map/ppermute | solution.py:272
  5.9 1.3 %collective-permute-start.2 = (bf16[80,640]{1,0:T(8,128)(2,1)S(1)}, bf16[80,640]{1,0:T(8,128)(2,1)S(1)}, u32[]{:S(2)}, u32[]{:S(2)}) collective-permute-start(bf16[80,640]{1,0:T(8,128)(2,1)S(1)} %get-tuple-element.29), channel_id=1, source_target_pairs={{0,24},{8,0},{16,8},{24,16},{1,25},{9,1},{17,9},{25,17},{2,26},{10... | collective-permute-start | bytes 307208 | tf_op jit(solution)/shard_map/ppermute | solution.py:272
  7.2 1.1 stack.1.refs_0_
  8.4 2.3 %collective-permute-done.1.refs_2_ = bf16[80,640]{1,0:T(8,128)(2,1)S(1)} collective-permute-done((bf16[80,640]{1,0:T(8,128)(2,1)S(1)}, bf16[80,640]{1,0:T(8,128)(2,1)S(1)}, u32[]{:S(2)}, u32[]{:S(2)}) %collective-permute-start.1) | collective-permute-done | bytes 102432 | tf_op jit(solution)/shard_map/ppermute | solution.py:272
  10.7 1.9 %collective-permute-start.3 = (bf16[320,640]{1,0:T(8,128)(2,1)S(1)}, bf16[320,640]{1,0:T(8,128)(2,1)S(1)}, u32[]{:S(2)}, u32[]{:S(2)}) collective-permute-start(bf16[320,640]{1,0:T(8,128)(2,1)S(1)} %assemble.1.grad_ref), channel_id=1, source_target_pairs={{32,0},{64,32},{96,64},{128,96},{160,128},{192,160},{224,192},{33,... | collective-permute-start | bytes 1228808 | tf_op jit(solution)/shard_map/ppermute | solution.py:38
  12.6 1.3 %collective-permute-start.4 = (bf16[80,2560]{1,0:T(8,128)(2,1)S(1)}, bf16[80,2560]{1,0:T(8,128)(2,1)S(1)}, u32[]{:S(2)}, u32[]{:S(2)}) collective-permute-start(bf16[80,2560]{1,0:T(8,128)(2,1)S(1)} %bitcast.5), channel_id=1, source_target_pairs={{0,8},{8,16},{16,24},{24,0},{1,9},{9,17},{17,25},{25,1},{2,10},{10... | collective-permute-start | bytes 1228808 | tf_op jit(solution)/shard_map/ppermute | solution.py:272
  14.0 2.7 %collective-permute-start.5 = (bf16[80,2560]{1,0:T(8,128)(2,1)S(1)}, bf16[80,2560]{1,0:T(8,128)(2,1)S(1)}, u32[]{:S(2)}, u32[]{:S(2)}) collective-permute-start(bf16[80,2560]{1,0:T(8,128)(2,1)S(1)} %bitcast.6), channel_id=1, source_target_pairs={{0,16},{8,24},{16,0},{24,8},{1,17},{9,25},{17,1},{25,9},{2,18},{10... | collective-permute-start | bytes 1228808 | tf_op jit(solution)/shard_map/ppermute | solution.py:272
  16.6 1.3 %collective-permute-start.6 = (bf16[80,2560]{1,0:T(8,128)(2,1)S(1)}, bf16[80,2560]{1,0:T(8,128)(2,1)S(1)}, u32[]{:S(2)}, u32[]{:S(2)}) collective-permute-start(bf16[80,2560]{1,0:T(8,128)(2,1)S(1)} %bitcast.7), channel_id=1, source_target_pairs={{0,24},{8,0},{16,8},{24,16},{1,25},{9,1},{17,9},{25,17},{2,26},{10... | collective-permute-start | bytes 1228808 | tf_op jit(solution)/shard_map/ppermute | solution.py:272
  17.9 1.0 collective-permute-start.8
  19.4 40.8 %all-gather.4 = f16[2624,640]{1,0:T(8,128)(2,1)S(1)} all-gather(f16[328,640]{1,0:T(8,128)(2,1)S(1)} %convert_element_type.12), channel_id=2, replica_groups=mesh['layer'=8,'y'=4,'z'=8] {'z'}, dimensions={0}, use_global_device_ids=true | all-gather | bytes 3778560 | tf_op jit(solution)/shard_map/all_gather | solution.py:295
  60.1 0.6 convert_element_type.16
  60.9 3.2 %collective-permute-start.9 = (bf16[160,2560]{1,0:T(8,128)(2,1)S(1)}, bf16[160,2560]{1,0:T(8,128)(2,1)S(1)}, u32[]{:S(2)}, u32[]{:S(2)}) collective-permute-start(bf16[160,2560]{1,0:T(8,128)(2,1)S(1)} %stack.1.refs_0_), channel_id=1, source_target_pairs={{0,24},{8,0},{16,8},{24,16},{1,25},{9,1},{17,9},{25,17},{2,26},{10... | collective-permute-start | bytes 2457608 | tf_op jit(solution)/shard_map/ppermute | solution.py:272
  64.1 1.7 %reduced.1 = bf16[328,640]{1,0:T(8,128)(2,1)S(1)} custom-call(bf16[8,328,640]{2,1,0:T(8,128)(2,1)S(1)} %bitcast.3, bf16[320,640]{1,0:T(8,128)(2,1)S(1)} %assemble.1.grad_ref, bf16[80,2560]{1,0:T(8,128)(2,1)S(1)} %bitcast.8, bf16[80,2560]{1,0:T(8,128)(2,1)S(1)} %collective-permute-done.4.refs_1_, bf16[80,2560]{1,0:T(8,128)(2,1)S(1)} %collective-permute-done.5.refs_2_, ...), custom_call_target="tpu_custom_call" | custom-call | flops 1048576000 | bytes 5826560 | tf_op jit(solution)/shard_map/reduced/pallas_call | solution.py:20
  65.8 36.0 %all-gather.5 = f16[2624,640]{1,0:T(8,128)(2,1)S(1)} all-gather(f16[328,640]{1,0:T(8,128)(2,1)S(1)} %convert_element_type.14), channel_id=3, replica_groups=mesh['layer'=8,'y'=4,'z'=8] {'z'}, dimensions={0}, use_global_device_ids=true | all-gather | bytes 3778560 | tf_op jit(solution)/shard_map/all_gather | solution.py:295
  102.5 2.1 %pushed.1 = (bf16[320,640]{1,0:T(8,128)(2,1)S(1)}, bf16[2560,640]{1,0:T(8,128)(2,1)S(1)}) custom-call(bf16[8,328,640]{2,1,0:T(8,128)(2,1)S(1)} %bitcast.4, bf16[5,128,128]{2,1,0:T(8,128)(2,1)S(1)} %get-tuple-element.38.inverse_ref, bf16[5,128,128]{2,1,0:T(8,128)(2,1)S(1)} %get-tuple-element.35.table_ref.coupling_ref, bf16[160,2560]{1,0:T(8,128)(2,1)S(1)} %stack.1.refs_0_, ...), custom_call_target="tpu_custom_call" | custom-call | flops 1048576000 | bytes 10649600 | tf_op jit(solution)/shard_map/pushed/pallas_call | solution.py:20
  104.6 2.1 %collective-permute-start.10 = (bf16[320,640]{1,0:T(8,128)(2,1)S(1)}, bf16[320,640]{1,0:T(8,128)(2,1)S(1)}, u32[]{:S(2)}, u32[]{:S(2)}) collective-permute-start(bf16[320,640]{1,0:T(8,128)(2,1)S(1)} %get-tuple-element.42), channel_id=1, source_target_pairs={{0,32},{32,64},{64,96},{96,128},{128,160},{160,192},{192,224},{1,3... | collective-permute-start | bytes 1228808 | tf_op jit(solution)/shard_map/ppermute | solution.py:38
  106.7 1.7 %local.1.local_ref = f32[320,640]{1,0:T(8,128)S(1)} custom-call(bf16[2560,640]{1,0:T(8,128)(2,1)S(1)} %get-tuple-element.41.panel_ref, bf16[5,128,128]{2,1,0:T(8,128)(2,1)S(1)} %get-tuple-element.38.inverse_ref, bf16[160,2560]{1,0:T(8,128)(2,1)S(1)} %stack.1.refs_0_, bf16[160,2560]{1,0:T(8,128)(2,1)S(1)} %collective-permute-done.7.refs_1_, ...), custom_call_target="tpu_custom_call" | custom-call | flops 1048576000 | bytes 7536640 | tf_op jit(solution)/shard_map/local/pallas_call | solution.py:20
  108.5 5.4 %collective-permute-done.10.pushed_ref = bf16[320,640]{1,0:T(8,128)(2,1)S(1)} collective-permute-done((bf16[320,640]{1,0:T(8,128)(2,1)S(1)}, bf16[320,640]{1,0:T(8,128)(2,1)S(1)}, u32[]{:S(2)}, u32[]{:S(2)}) %collective-permute-start.10) | collective-permute-done | bytes 409632 | tf_op jit(solution)/shard_map/ppermute | solution.py:38
  114.1 2.7 %collective-permute-start.12 = (bf16[80,640]{1,0:T(8,128)(2,1)S(1)}, bf16[80,640]{1,0:T(8,128)(2,1)S(1)}, u32[]{:S(2)}, u32[]{:S(2)}) collective-permute-start(bf16[80,640]{1,0:T(8,128)(2,1)S(1)} %get-tuple-element.45), channel_id=1, source_target_pairs={{0,16},{8,24},{16,0},{24,8},{1,17},{9,25},{17,1},{25,9},{2,18},{10... | collective-permute-start | bytes 307208 | tf_op jit(solution)/shard_map/ppermute | solution.py:272
  116.7 1.5 %collective-permute-start.13 = (bf16[80,640]{1,0:T(8,128)(2,1)S(1)}, bf16[80,640]{1,0:T(8,128)(2,1)S(1)}, u32[]{:S(2)}, u32[]{:S(2)}) collective-permute-start(bf16[80,640]{1,0:T(8,128)(2,1)S(1)} %get-tuple-element.46), channel_id=1, source_target_pairs={{0,24},{8,0},{16,8},{24,16},{1,25},{9,1},{17,9},{25,17},{2,26},{10... | collective-permute-start | bytes 307208 | tf_op jit(solution)/shard_map/ppermute | solution.py:272
  118.2 3.5 %collective-permute-done.11.refs_1_ = bf16[80,640]{1,0:T(8,128)(2,1)S(1)} collective-permute-done((bf16[80,640]{1,0:T(8,128)(2,1)S(1)}, bf16[80,640]{1,0:T(8,128)(2,1)S(1)}, u32[]{:S(2)}, u32[]{:S(2)}) %collective-permute-start.11) | collective-permute-done | bytes 102432 | tf_op jit(solution)/shard_map/ppermute | solution.py:272
  122.2 0.8 join.1
  (21 shorter events, 2.1 us)
Async XLA Ops:
  0.0 12.6 %copy-start = (bf16[1,80,2560]{2,1,0:T(8,128)(2,1)S(1)}, bf16[1,80,2560]{2,1,0:T(8,128)(2,1)}, u32[]{:S(2)}) copy-start(bf16[1,80,2560]{2,1,0:T(8,128)(2,1)} %param.8) | copy-start | bytes 1228804
  1.3 7.1 %collective-permute-start = (bf16[80,640]{1,0:T(8,128)(2,1)S(1)}, bf16[80,640]{1,0:T(8,128)(2,1)S(1)}, u32[]{:S(2)}, u32[]{:S(2)}) collective-permute-start(bf16[80,640]{1,0:T(8,128)(2,1)S(1)} %get-tuple-element.27), channel_id=1, source_target_pairs={{0,8},{8,16},{16,24},{24,0},{1,9},{9,17},{17,25},{25,1},{2,10},{10... | collective-permute-start | bytes 307208 | tf_op jit(solution)/shard_map/ppermute | solution.py:272
  3.0 7.7 %collective-permute-start.1 = (bf16[80,640]{1,0:T(8,128)(2,1)S(1)}, bf16[80,640]{1,0:T(8,128)(2,1)S(1)}, u32[]{:S(2)}, u32[]{:S(2)}) collective-permute-start(bf16[80,640]{1,0:T(8,128)(2,1)S(1)} %get-tuple-element.28), channel_id=1, source_target_pairs={{0,16},{8,24},{16,0},{24,8},{1,17},{9,25},{17,1},{25,9},{2,18},{10... | collective-permute-start | bytes 307208 | tf_op jit(solution)/shard_map/ppermute | solution.py:272
  5.9 4.8 %collective-permute-start.2 = (bf16[80,640]{1,0:T(8,128)(2,1)S(1)}, bf16[80,640]{1,0:T(8,128)(2,1)S(1)}, u32[]{:S(2)}, u32[]{:S(2)}) collective-permute-start(bf16[80,640]{1,0:T(8,128)(2,1)S(1)} %get-tuple-element.29), channel_id=1, source_target_pairs={{0,24},{8,0},{16,8},{24,16},{1,25},{9,1},{17,9},{25,17},{2,26},{10... | collective-permute-start | bytes 307208 | tf_op jit(solution)/shard_map/ppermute | solution.py:272
  10.7 8.2 %collective-permute-start.3 = (bf16[320,640]{1,0:T(8,128)(2,1)S(1)}, bf16[320,640]{1,0:T(8,128)(2,1)S(1)}, u32[]{:S(2)}, u32[]{:S(2)}) collective-permute-start(bf16[320,640]{1,0:T(8,128)(2,1)S(1)} %assemble.1.grad_ref), channel_id=1, source_target_pairs={{32,0},{64,32},{96,64},{128,96},{160,128},{192,160},{224,192},{33,... | collective-permute-start | bytes 1228808 | tf_op jit(solution)/shard_map/ppermute | solution.py:38
  12.6 48.2 %collective-permute-start.4 = (bf16[80,2560]{1,0:T(8,128)(2,1)S(1)}, bf16[80,2560]{1,0:T(8,128)(2,1)S(1)}, u32[]{:S(2)}, u32[]{:S(2)}) collective-permute-start(bf16[80,2560]{1,0:T(8,128)(2,1)S(1)} %bitcast.5), channel_id=1, source_target_pairs={{0,8},{8,16},{16,24},{24,0},{1,9},{9,17},{17,25},{25,1},{2,10},{10... | collective-permute-start | bytes 1228808 | tf_op jit(solution)/shard_map/ppermute | solution.py:272
  14.0 50.1 %collective-permute-start.5 = (bf16[80,2560]{1,0:T(8,128)(2,1)S(1)}, bf16[80,2560]{1,0:T(8,128)(2,1)S(1)}, u32[]{:S(2)}, u32[]{:S(2)}) collective-permute-start(bf16[80,2560]{1,0:T(8,128)(2,1)S(1)} %bitcast.6), channel_id=1, source_target_pairs={{0,16},{8,24},{16,0},{24,8},{1,17},{9,25},{17,1},{25,9},{2,18},{10... | collective-permute-start | bytes 1228808 | tf_op jit(solution)/shard_map/ppermute | solution.py:272
  16.6 47.5 %collective-permute-start.6 = (bf16[80,2560]{1,0:T(8,128)(2,1)S(1)}, bf16[80,2560]{1,0:T(8,128)(2,1)S(1)}, u32[]{:S(2)}, u32[]{:S(2)}) collective-permute-start(bf16[80,2560]{1,0:T(8,128)(2,1)S(1)} %bitcast.7), channel_id=1, source_target_pairs={{0,24},{8,0},{16,8},{24,16},{1,25},{9,1},{17,9},{25,17},{2,26},{10... | collective-permute-start | bytes 1228808 | tf_op jit(solution)/shard_map/ppermute | solution.py:272
  17.9 84.5 %collective-permute-start.8 = (bf16[160,2560]{1,0:T(8,128)(2,1)S(1)}, bf16[160,2560]{1,0:T(8,128)(2,1)S(1)}, u32[]{:S(2)}, u32[]{:S(2)}) collective-permute-start(bf16[160,2560]{1,0:T(8,128)(2,1)S(1)} %stack.1.refs_0_), channel_id=1, source_target_pairs={{0,16},{8,24},{16,0},{24,8},{1,17},{9,25},{17,1},{25,9},{2,18},{10... | collective-permute-start | bytes 2457608 | tf_op jit(solution)/shard_map/ppermute | solution.py:272
  60.8 41.7 %collective-permute-start.7 = (bf16[160,2560]{1,0:T(8,128)(2,1)S(1)}, bf16[160,2560]{1,0:T(8,128)(2,1)S(1)}, u32[]{:S(2)}, u32[]{:S(2)}) collective-permute-start(bf16[160,2560]{1,0:T(8,128)(2,1)S(1)} %stack.1.refs_0_), channel_id=1, source_target_pairs={{0,8},{8,16},{16,24},{24,0},{1,9},{9,17},{17,25},{25,1},{2,10},{10... | collective-permute-start | bytes 2457608 | tf_op jit(solution)/shard_map/ppermute | solution.py:272
  60.9 41.6 %collective-permute-start.9 = (bf16[160,2560]{1,0:T(8,128)(2,1)S(1)}, bf16[160,2560]{1,0:T(8,128)(2,1)S(1)}, u32[]{:S(2)}, u32[]{:S(2)}) collective-permute-start(bf16[160,2560]{1,0:T(8,128)(2,1)S(1)} %stack.1.refs_0_), channel_id=1, source_target_pairs={{0,24},{8,0},{16,8},{24,16},{1,25},{9,1},{17,9},{25,17},{2,26},{10... | collective-permute-start | bytes 2457608 | tf_op jit(solution)/shard_map/ppermute | solution.py:272
  104.6 9.3 %collective-permute-start.10 = (bf16[320,640]{1,0:T(8,128)(2,1)S(1)}, bf16[320,640]{1,0:T(8,128)(2,1)S(1)}, u32[]{:S(2)}, u32[]{:S(2)}) collective-permute-start(bf16[320,640]{1,0:T(8,128)(2,1)S(1)} %get-tuple-element.42), channel_id=1, source_target_pairs={{0,32},{32,64},{64,96},{96,128},{128,160},{160,192},{192,224},{1,3... | collective-permute-start | bytes 1228808 | tf_op jit(solution)/shard_map/ppermute | solution.py:38
  114.0 7.7 %collective-permute-start.11 = (bf16[80,640]{1,0:T(8,128)(2,1)S(1)}, bf16[80,640]{1,0:T(8,128)(2,1)S(1)}, u32[]{:S(2)}, u32[]{:S(2)}) collective-permute-start(bf16[80,640]{1,0:T(8,128)(2,1)S(1)} %get-tuple-element.44), channel_id=1, source_target_pairs={{0,8},{8,16},{16,24},{24,0},{1,9},{9,17},{17,25},{25,1},{2,10},{10... | collective-permute-start | bytes 307208 | tf_op jit(solution)/shard_map/ppermute | solution.py:272
  114.1 7.6 %collective-permute-start.12 = (bf16[80,640]{1,0:T(8,128)(2,1)S(1)}, bf16[80,640]{1,0:T(8,128)(2,1)S(1)}, u32[]{:S(2)}, u32[]{:S(2)}) collective-permute-start(bf16[80,640]{1,0:T(8,128)(2,1)S(1)} %get-tuple-element.45), channel_id=1, source_target_pairs={{0,16},{8,24},{16,0},{24,8},{1,17},{9,25},{17,1},{25,9},{2,18},{10... | collective-permute-start | bytes 307208 | tf_op jit(solution)/shard_map/ppermute | solution.py:272
  116.7 5.5 %collective-permute-start.13 = (bf16[80,640]{1,0:T(8,128)(2,1)S(1)}, bf16[80,640]{1,0:T(8,128)(2,1)S(1)}, u32[]{:S(2)}, u32[]{:S(2)}) collective-permute-start(bf16[80,640]{1,0:T(8,128)(2,1)S(1)} %get-tuple-element.46), channel_id=1, source_target_pairs={{0,24},{8,0},{16,8},{24,16},{1,25},{9,1},{17,9},{25,17},{2,26},{10... | collective-permute-start | bytes 307208 | tf_op jit(solution)/shard_map/ppermute | solution.py:272

commit v7 on v6

--- a/solution.py
+++ b/solution.py
@@ -93,6 +93,44 @@
             panel_ref[pl.ds((k * count + j) * rows, rows), cols] = part.astype(BF)
 
 
+def hop_z(x, by):
+    size = lax.axis_size("z")
+    return lax.ppermute(x, "z", [(i, (i + by) % size) for i in range(size)])
+
+
+def ring_step(pair):
+    up, down = pair
+    return lax.optimization_barrier((hop_z(up, 1), hop_z(down, -1)))
+
+
+def ring_steps(tile):
+    steps = [(tile, tile)]
+    for _ in range(lax.axis_size("z") // 2 - 1):
+        steps.append(ring_step(steps[-1]))
+    return steps
+
+
+def panel_pieces(steps):
+    tile = steps[0][0]
+    half, far = tile.shape[0] // 2, len(steps)
+    pieces = [(tile, 0, 0)]
+    for step in range(1, far):
+        up, down = steps[step]
+        pieces += [(up, 0, -step), (down, 0, step)]
+    up, down = steps[-1]
+    up, down = ring_step((up[:half], down[half:]))
+    return pieces + [(up, 0, -far), (down, half, far)]
+
+
+def spread(refs, places, panel_ref, rows):
+    z, zs = lax.axis_index("z"), lax.axis_size("z")
+    for ref, (first, distance) in zip(refs, places, strict=True):
+        source = lax.rem(z + (distance + zs), zs)
+        for k in range(ref.shape[0] // rows):
+            at = pl.multiple_of(((first // rows + k) * zs + source) * rows, 16)
+            panel_ref[pl.ds(at, rows), :] = ref[pl.ds(k * rows, rows), :]
+
+
 def near_tile(above, table, shards):
     tile, width = above.shape
     blocks = width // BLK
@@ -119,15 +157,13 @@
             cols = pl.ds(at, w)
             load_scaled(panel_in, panel_ref, at, w, shards, rows)
             coupled = jnp.dot(joined(pieces, rows), panel_ref[:, cols], preferred_element_type=F32)
-            parts = [
-                (grad_ref[rows_of(owner, rows), cols].astype(F32) - part).astype(BF).astype(F32)
-                for owner, part in zip(owners, blocks_of(coupled, shards), strict=True)
-            ]
-            store_scaled(out_ref, parts, owners, at)
+            for owner, part in zip(owners, blocks_of(coupled, shards), strict=True):
+                here = rows_of(owner, rows)
+                out_ref[here, cols] = (grad_ref[here, cols].astype(F32) - part).astype(BF)
 
     return call(
         kernel,
-        like(tile + CODE, width, BF),
+        like(tile, width, BF),
         "reduced",
         [panel, grad, *factor],
         [pltpu.VMEM((depth, width), BF)],
@@ -135,16 +171,18 @@
     )
 
 
-def pushed_tile(panel, factor, inverse, coupling, shards):
+def pushed_tile(line, factor, inverse, coupling, shards):
     rows, depth = factor[0].shape[0] // 2, factor[0].shape[1]
-    tile, width = shards * rows, panel.shape[2]
-
-    def kernel(panel_in, inverse_ref, coupling_ref, *refs):
-        pieces, (pushed_ref, panel_ref) = refs[:shards], refs[shards:]
+    tiles, places = [p[0] for p in line], [p[1:] for p in line]
+    tile, width = tiles[0].shape
+    count = len(tiles)
+
+    def kernel(*refs):
+        pieces, (inverse_ref, coupling_ref, pushed_ref, panel_ref) = refs[count : count + shards], refs[count + shards :]
         owners = owners_of(shards)
+        spread(refs[:count], places, panel_ref, rows)
         carried = []
         for at, w in chunks_of(width):
-            load_scaled(panel_in, panel_ref, at, w, shards, rows)
             both = jnp.dot(joined(pieces, rows, rows), panel_ref[:, pl.ds(at, w)], preferred_element_type=F32)
             carried += [both[:, i : i + BLK].astype(BF) for i in range(0, w, BLK)]
         middle = [
@@ -159,7 +197,7 @@
         kernel,
         (like(tile, width, BF), like(depth, width, BF)),
         "pushed",
-        [panel, inverse, coupling, *factor],
+        [*tiles, *factor, inverse, coupling],
         flops=2 * tile * depth * width,
     )
 
@@ -306,10 +344,13 @@
     later = after(coupling, grad)
     coupling = [coupling] + [hop_y(coupling if k < 3 else later, k) for k in range(1, shards)]
     near = near_tile(above, psi, shards)
-    early, late = after(pair, grad), after(pair, near)
-    factors = [pair] + [hop_y(early if k == 2 else late, k) for k in range(1, shards)]
-    reduced = reduced_tile(gather_panel(near), coupling, grad, shards)
-    pushed, panel = pushed_tile(gather_panel(reduced), factors, inv, psi, shards)
+    pair = after(pair, grad)
+    ahead, behind = hop_y(pair, 1), hop_y(pair, -1)
+    panel = gather_panel(near)
+    panel, ahead, behind = lax.optimization_barrier((panel, ahead, behind))
+    reduced = reduced_tile(panel, coupling, grad, shards)
+    factors = [pair, ahead, hop_y(behind, -1), behind]
+    pushed, panel = pushed_tile(panel_pieces(ring_steps(reduced)), factors, inv, psi, shards)
     local_term = local_tile(panel, factors, inv, shards)
     return join_columns(exchange(update_pieces(local_term, hop_layer(pushed, 1), shards)))
 

time: 123 us -> 129 us (1.049)
  blocking collectives: 76.8 us -> 40.2 us
  waiting for transfers between devices: 11.8 us -> 44.5 us
  starting transfers between devices: 23.7 us -> 33.8 us
    all_gather x2 -> x1, blocking collectives: 76.8 us -> 40.2 us  [gather_panel(): return lax.all_gather(tile.astype(HALF), 'z', axis=0).astype(BF)]
    ppermute x0 -> x8, waiting for transfers between devices: none -> 32.3 us  [hop_z(): return lax.ppermute(x, 'z', [(i, (i + by) % size) for i in range(size)])]
    ppermute x0 -> x8, starting transfers between devices: none -> 12 us  [hop_z(): return lax.ppermute(x, 'z', [(i, (i + by) % size) for i in range(size)])]
    ppermute x12, starting transfers between devices: 19.6 us -> 18 us  [hop_y(): return lax.ppermute(x, 'y', [(i, (i + by) % size) for i in range(size)])]
  transfers between devices with their start and end apart: 14 -> 22, of which waited for: 4 -> 9; matrix products, arithmetic and copies ran while one was open for 1% -> 1% of each run, Pallas kernels for 4% -> 3%
where the time goes in v7:
time: 129 us
  waiting for transfers between devices  44.5 us (34%)
  blocking collectives  40.2 us (31%)
  starting transfers between devices  33.8 us (26%)
  Pallas kernels  9.33 us (7%)
    all_gather x1, blocking collectives, gather_panel(): return lax.all_gather(tile.astype(HALF), 'z', axis=0).astype(BF)  40.2 us
    ppermute x8, waiting for transfers between devices, hop_z(): return lax.ppermute(x, 'z', [(i, (i + by) % size) for i in range(size)])  32.3 us
    ppermute x12, starting transfers between devices, hop_y(): return lax.ppermute(x, 'y', [(i, (i + by) % size) for i in range(size)])  18 us
    ppermute x8, starting transfers between devices, hop_z(): return lax.ppermute(x, 'z', [(i, (i + by) % size) for i in range(size)])  12 us
    pallas_call x7, Pallas kernels, call(): pl.pallas_call(kernel, out_shape=out, in_specs=[HBM if i in far else VMEM...  6.89 us
    ppermute x12, waiting for transfers between devices, hop_y(): return lax.ppermute(x, 'y', [(i, (i + by) % size) for i in range(size)])  6.68 us
    ppermute x2, waiting for transfers between devices, hop_layer(): lax.ppermute(x, 'layer', [(i, i + by) for i in range(size) if 0 <= i + by...  5.6 us
    ppermute x2, starting transfers between devices, hop_layer(): lax.ppermute(x, 'layer', [(i, i + by) for i in range(size) if 0 <= i + by...  3.84 us
  transfers between devices with their start and end apart: 22, of which 9 were waited for; matrix products, arithmetic and copies ran while one was open for 1% of the time, Pallas kernels for 3%

profile of v7, /device:TPU:2, one launch (start us, length us, event | category | flops | bytes accessed | tf_op | source)
XLA Modules:
  0.0 128.8 jit_solution(1825815385515670972)
XLA Ops:
  1.3 1.7 %collective-permute-start = (bf16[80,640]{1,0:T(8,128)(2,1)S(1)}, bf16[80,640]{1,0:T(8,128)(2,1)S(1)}, u32[]{:S(2)}, u32[]{:S(2)}) collective-permute-start(bf16[80,640]{1,0:T(8,128)(2,1)S(1)} %get-tuple-element.37), channel_id=1, source_target_pairs={{0,8},{8,16},{16,24},{24,0},{1,9},{9,17},{17,25},{25,1},{2,10},{10... | collective-permute-start | bytes 307208 | tf_op jit(solution)/shard_map/ppermute | solution.py:310
  3.0 2.9 %collective-permute-start.1 = (bf16[80,640]{1,0:T(8,128)(2,1)S(1)}, bf16[80,640]{1,0:T(8,128)(2,1)S(1)}, u32[]{:S(2)}, u32[]{:S(2)}) collective-permute-start(bf16[80,640]{1,0:T(8,128)(2,1)S(1)} %get-tuple-element.38), channel_id=1, source_target_pairs={{0,16},{8,24},{16,0},{24,8},{1,17},{9,25},{17,1},{25,9},{2,18},{10... | collective-permute-start | bytes 307208 | tf_op jit(solution)/shard_map/ppermute | solution.py:310
  5.9 1.3 %collective-permute-start.2 = (bf16[80,640]{1,0:T(8,128)(2,1)S(1)}, bf16[80,640]{1,0:T(8,128)(2,1)S(1)}, u32[]{:S(2)}, u32[]{:S(2)}) collective-permute-start(bf16[80,640]{1,0:T(8,128)(2,1)S(1)} %get-tuple-element.39), channel_id=1, source_target_pairs={{0,24},{8,0},{16,8},{24,16},{1,25},{9,1},{17,9},{25,17},{2,26},{10... | collective-permute-start | bytes 307208 | tf_op jit(solution)/shard_map/ppermute | solution.py:310
  8.4 2.3 %collective-permute-done.1.refs_2_ = bf16[80,640]{1,0:T(8,128)(2,1)S(1)} collective-permute-done((bf16[80,640]{1,0:T(8,128)(2,1)S(1)}, bf16[80,640]{1,0:T(8,128)(2,1)S(1)}, u32[]{:S(2)}, u32[]{:S(2)}) %collective-permute-start.1) | collective-permute-done | bytes 102432 | tf_op jit(solution)/shard_map/ppermute | solution.py:310
  10.7 1.9 %collective-permute-start.3 = (bf16[320,640]{1,0:T(8,128)(2,1)S(1)}, bf16[320,640]{1,0:T(8,128)(2,1)S(1)}, u32[]{:S(2)}, u32[]{:S(2)}) collective-permute-start(bf16[320,640]{1,0:T(8,128)(2,1)S(1)} %assemble.1.grad_ref), channel_id=1, source_target_pairs={{32,0},{64,32},{96,64},{128,96},{160,128},{192,160},{224,192},{33,... | collective-permute-start | bytes 1228808 | tf_op jit(solution)/shard_map/ppermute | solution.py:38
  14.0 2.7 %collective-permute-start.7 = (bf16[80,2560]{1,0:T(8,128)(2,1)S(1)}, bf16[80,2560]{1,0:T(8,128)(2,1)S(1)}, u32[]{:S(2)}, u32[]{:S(2)}) collective-permute-start(bf16[80,2560]{1,0:T(8,128)(2,1)S(1)} %bitcast.4), channel_id=1, source_target_pairs={{0,16},{8,24},{16,0},{24,8},{1,17},{9,25},{17,1},{25,9},{2,18},{10... | collective-permute-start | bytes 1228808 | tf_op jit(solution)/shard_map/ppermute | solution.py:310
  16.8 3.0 %collective-permute-start.5 = (bf16[160,2560]{1,0:T(8,128)(2,1)S(1)}, bf16[160,2560]{1,0:T(8,128)(2,1)S(1)}, u32[]{:S(2)}, u32[]{:S(2)}) collective-permute-start(bf16[160,2560]{1,0:T(8,128)(2,1)S(1)} %stack.1.refs_9_.refs_0_), channel_id=1, source_target_pairs={{0,24},{8,0},{16,8},{24,16},{1,25},{9,1},{17,9},{25,17},{2,26},{10... | collective-permute-start | bytes 2457608 | tf_op jit(solution)/shard_map/ppermute | solution.py:310
  21.0 40.2 %all-gather.2 = f16[2624,640]{1,0:T(8,128)(2,1)S(1)} all-gather(f16[328,640]{1,0:T(8,128)(2,1)S(1)} %convert_element_type.6), channel_id=2, replica_groups=mesh['layer'=8,'y'=4,'z'=8] {'z'}, dimensions={0}, use_global_device_ids=true | all-gather | bytes 3778560 | tf_op jit(solution)/shard_map/all_gather | solution.py:333
  61.9 1.5 %reduced.1.refs_0_ = bf16[320,640]{1,0:T(8,128)(2,1)S(1)} custom-call(bf16[8,328,640]{2,1,0:T(8,128)(2,1)S(1)} %bitcast.2, bf16[320,640]{1,0:T(8,128)(2,1)S(1)} %assemble.1.grad_ref, bf16[80,2560]{1,0:T(8,128)(2,1)S(1)} %bitcast.6, bf16[80,2560]{1,0:T(8,128)(2,1)S(1)} %collective-permute-done.6.refs_1_, bf16[80,2560]{1,0:T(8,128)(2,1)S(1)} %collective-permute-done.7.refs_2_, ...), custom_call_target="tpu_custom_call" | custom-call | flops 1048576000 | bytes 5816320 | tf_op jit(solution)/shard_map/reduced/pallas_call | solution.py:20
  63.4 1.7 %collective-permute-start.10 = (bf16[320,640]{1,0:T(8,128)(2,1)S(1)}, bf16[320,640]{1,0:T(8,128)(2,1)S(1)}, u32[]{:S(2)}, u32[]{:S(2)}) collective-permute-start(bf16[320,640]{1,0:T(8,128)(2,1)S(1)} %reduced.1.refs_0_), channel_id=1, source_target_pairs={{0,7},{1,0},{2,1},{3,2},{4,3},{5,4},{6,5},{7,6},{8,15},{9,8},{10,9... | collective-permute-start | bytes 1228808 | tf_op jit(solution)/shard_map/ppermute | solution.py:98
  65.5 9.7 %collective-permute-done.10.refs_2_ = bf16[320,640]{1,0:T(8,128)(2,1)S(1)} collective-permute-done((bf16[320,640]{1,0:T(8,128)(2,1)S(1)}, bf16[320,640]{1,0:T(8,128)(2,1)S(1)}, u32[]{:S(2)}, u32[]{:S(2)}) %collective-permute-start.10) | collective-permute-done | bytes 409632 | tf_op jit(solution)/shard_map/ppermute | solution.py:98
  75.2 2.8 %collective-permute-done.9.refs_1_ = bf16[320,640]{1,0:T(8,128)(2,1)S(1)} collective-permute-done((bf16[320,640]{1,0:T(8,128)(2,1)S(1)}, bf16[320,640]{1,0:T(8,128)(2,1)S(1)}, u32[]{:S(2)}, u32[]{:S(2)}) %collective-permute-start.9) | collective-permute-done | bytes 409632 | tf_op jit(solution)/shard_map/ppermute | solution.py:98
  78.0 3.2 %collective-permute-start.12 = (bf16[320,640]{1,0:T(8,128)(2,1)S(1)}, bf16[320,640]{1,0:T(8,128)(2,1)S(1)}, u32[]{:S(2)}, u32[]{:S(2)}) collective-permute-start(bf16[320,640]{1,0:T(8,128)(2,1)S(1)} %collective-permute-done.10.refs_2_), channel_id=1, source_target_pairs={{0,7},{1,0},{2,1},{3,2},{4,3},{5,4},{6,5},{7,6},{8,15},{9,8},{10,9... | collective-permute-start | bytes 1228808 | tf_op jit(solution)/shard_map/ppermute | solution.py:98
  82.0 8.2 %collective-permute-done.11.refs_3_ = bf16[320,640]{1,0:T(8,128)(2,1)S(1)} collective-permute-done((bf16[320,640]{1,0:T(8,128)(2,1)S(1)}, bf16[320,640]{1,0:T(8,128)(2,1)S(1)}, u32[]{:S(2)}, u32[]{:S(2)}) %collective-permute-start.11) | collective-permute-done | bytes 409632 | tf_op jit(solution)/shard_map/ppermute | solution.py:98
  90.1 3.2 %collective-permute-start.14 = (bf16[320,640]{1,0:T(8,128)(2,1)S(1)}, bf16[320,640]{1,0:T(8,128)(2,1)S(1)}, u32[]{:S(2)}, u32[]{:S(2)}) collective-permute-start(bf16[320,640]{1,0:T(8,128)(2,1)S(1)} %collective-permute-done.12.refs_4_), channel_id=1, source_target_pairs={{0,7},{1,0},{2,1},{3,2},{4,3},{5,4},{6,5},{7,6},{8,15},{9,8},{10,9... | collective-permute-start | bytes 1228808 | tf_op jit(solution)/shard_map/ppermute | solution.py:98
  93.4 7.9 %collective-permute-done.13.refs_5_ = bf16[320,640]{1,0:T(8,128)(2,1)S(1)} collective-permute-done((bf16[320,640]{1,0:T(8,128)(2,1)S(1)}, bf16[320,640]{1,0:T(8,128)(2,1)S(1)}, u32[]{:S(2)}, u32[]{:S(2)}) %collective-permute-start.13) | collective-permute-done | bytes 409632 | tf_op jit(solution)/shard_map/ppermute | solution.py:98
  101.5 3.3 %collective-permute-start.16 = (bf16[160,640]{1,0:T(8,128)(2,1)S(1)}, bf16[160,640]{1,0:T(8,128)(2,1)S(1)}, u32[]{:S(2)}, u32[]{:S(2)}) collective-permute-start(bf16[160,640]{1,0:T(8,128)(2,1)S(1)} %slice.7), channel_id=1, source_target_pairs={{0,7},{1,0},{2,1},{3,2},{4,3},{5,4},{6,5},{7,6},{8,15},{9,8},{10,9... | collective-permute-start | bytes 614408 | tf_op jit(solution)/shard_map/ppermute | solution.py:98
  104.8 3.6 %collective-permute-done.15.refs_7_ = bf16[160,640]{1,0:T(8,128)(2,1)S(1)} collective-permute-done((bf16[160,640]{1,0:T(8,128)(2,1)S(1)}, bf16[160,640]{1,0:T(8,128)(2,1)S(1)}, u32[]{:S(2)}, u32[]{:S(2)}) %collective-permute-start.15) | collective-permute-done | bytes 204832 | tf_op jit(solution)/shard_map/ppermute | solution.py:98
  108.4 2.3 %pushed.1 = (bf16[320,640]{1,0:T(8,128)(2,1)S(1)}, bf16[2560,640]{1,0:T(8,128)(2,1)S(1)}) custom-call(bf16[320,640]{1,0:T(8,128)(2,1)S(1)} %reduced.1.refs_0_, bf16[320,640]{1,0:T(8,128)(2,1)S(1)} %collective-permute-done.9.refs_1_, bf16[320,640]{1,0:T(8,128)(2,1)S(1)} %collective-permute-done.10.refs_2_, ...), custom_call_target="tpu_custom_call" | custom-call | flops 1048576000 | bytes 10567680 | tf_op jit(solution)/shard_map/pushed/pallas_call | solution.py:20
  110.7 1.9 %collective-permute-start.18 = (bf16[320,640]{1,0:T(8,128)(2,1)S(1)}, bf16[320,640]{1,0:T(8,128)(2,1)S(1)}, u32[]{:S(2)}, u32[]{:S(2)}) collective-permute-start(bf16[320,640]{1,0:T(8,128)(2,1)S(1)} %get-tuple-element.62), channel_id=1, source_target_pairs={{0,32},{32,64},{64,96},{96,128},{128,160},{160,192},{192,224},{1,3... | collective-permute-start | bytes 1228808 | tf_op jit(solution)/shard_map/ppermute | solution.py:38
  112.6 1.7 %local.1.local_ref = f32[320,640]{1,0:T(8,128)S(1)} custom-call(bf16[2560,640]{1,0:T(8,128)(2,1)S(1)} %get-tuple-element.61.panel_ref, bf16[5,128,128]{2,1,0:T(8,128)(2,1)S(1)} %get-tuple-element.60.refs_13_.inverse_ref, bf16[160,2560]{1,0:T(8,128)(2,1)S(1)} %stack.1.refs_9_.refs_0_, bf16[160,2560]{1,0:T(8,128)(2,1)S(1)} %collective-permute-done.4.refs_10_.refs_1_, ...), custom_call_target="tpu_custom_call" | custom-call | flops 1048576000 | bytes 7536640 | tf_op jit(solution)/shard_map/local/pallas_call | solution.py:20
  114.4 5.6 %collective-permute-done.18.pushed_ref = bf16[320,640]{1,0:T(8,128)(2,1)S(1)} collective-permute-done((bf16[320,640]{1,0:T(8,128)(2,1)S(1)}, bf16[320,640]{1,0:T(8,128)(2,1)S(1)}, u32[]{:S(2)}, u32[]{:S(2)}) %collective-permute-start.18) | collective-permute-done | bytes 409632 | tf_op jit(solution)/shard_map/ppermute | solution.py:38
  120.2 2.2 %collective-permute-start.20 = (bf16[80,640]{1,0:T(8,128)(2,1)S(1)}, bf16[80,640]{1,0:T(8,128)(2,1)S(1)}, u32[]{:S(2)}, u32[]{:S(2)}) collective-permute-start(bf16[80,640]{1,0:T(8,128)(2,1)S(1)} %get-tuple-element.65), channel_id=1, source_target_pairs={{0,16},{8,24},{16,0},{24,8},{1,17},{9,25},{17,1},{25,9},{2,18},{10... | collective-permute-start | bytes 307208 | tf_op jit(solution)/shard_map/ppermute | solution.py:310
  123.6 3.5 %collective-permute-done.19.refs_1_ = bf16[80,640]{1,0:T(8,128)(2,1)S(1)} collective-permute-done((bf16[80,640]{1,0:T(8,128)(2,1)S(1)}, bf16[80,640]{1,0:T(8,128)(2,1)S(1)}, u32[]{:S(2)}, u32[]{:S(2)}) %collective-permute-start.19) | collective-permute-done | bytes 102432 | tf_op jit(solution)/shard_map/ppermute | solution.py:310
  (36 shorter events, 10.2 us)
Async XLA Ops:
  0.0 12.6 %copy-start = (bf16[1,80,2560]{2,1,0:T(8,128)(2,1)S(1)}, bf16[1,80,2560]{2,1,0:T(8,128)(2,1)}, u32[]{:S(2)}) copy-start(bf16[1,80,2560]{2,1,0:T(8,128)(2,1)} %param.8) | copy-start | bytes 1228804
  1.3 7.1 %collective-permute-start = (bf16[80,640]{1,0:T(8,128)(2,1)S(1)}, bf16[80,640]{1,0:T(8,128)(2,1)S(1)}, u32[]{:S(2)}, u32[]{:S(2)}) collective-permute-start(bf16[80,640]{1,0:T(8,128)(2,1)S(1)} %get-tuple-element.37), channel_id=1, source_target_pairs={{0,8},{8,16},{16,24},{24,0},{1,9},{9,17},{17,25},{25,1},{2,10},{10... | collective-permute-start | bytes 307208 | tf_op jit(solution)/shard_map/ppermute | solution.py:310
  3.0 7.7 %collective-permute-start.1 = (bf16[80,640]{1,0:T(8,128)(2,1)S(1)}, bf16[80,640]{1,0:T(8,128)(2,1)S(1)}, u32[]{:S(2)}, u32[]{:S(2)}) collective-permute-start(bf16[80,640]{1,0:T(8,128)(2,1)S(1)} %get-tuple-element.38), channel_id=1, source_target_pairs={{0,16},{8,24},{16,0},{24,8},{1,17},{9,25},{17,1},{25,9},{2,18},{10... | collective-permute-start | bytes 307208 | tf_op jit(solution)/shard_map/ppermute | solution.py:310
  5.9 4.8 %collective-permute-start.2 = (bf16[80,640]{1,0:T(8,128)(2,1)S(1)}, bf16[80,640]{1,0:T(8,128)(2,1)S(1)}, u32[]{:S(2)}, u32[]{:S(2)}) collective-permute-start(bf16[80,640]{1,0:T(8,128)(2,1)S(1)} %get-tuple-element.39), channel_id=1, source_target_pairs={{0,24},{8,0},{16,8},{24,16},{1,25},{9,1},{17,9},{25,17},{2,26},{10... | collective-permute-start | bytes 307208 | tf_op jit(solution)/shard_map/ppermute | solution.py:310
  10.7 9.1 %collective-permute-start.3 = (bf16[320,640]{1,0:T(8,128)(2,1)S(1)}, bf16[320,640]{1,0:T(8,128)(2,1)S(1)}, u32[]{:S(2)}, u32[]{:S(2)}) collective-permute-start(bf16[320,640]{1,0:T(8,128)(2,1)S(1)} %assemble.1.grad_ref), channel_id=1, source_target_pairs={{32,0},{64,32},{96,64},{128,96},{160,128},{192,160},{224,192},{33,... | collective-permute-start | bytes 1228808 | tf_op jit(solution)/shard_map/ppermute | solution.py:38
  12.6 49.2 %collective-permute-start.6 = (bf16[80,2560]{1,0:T(8,128)(2,1)S(1)}, bf16[80,2560]{1,0:T(8,128)(2,1)S(1)}, u32[]{:S(2)}, u32[]{:S(2)}) collective-permute-start(bf16[80,2560]{1,0:T(8,128)(2,1)S(1)} %bitcast.3), channel_id=1, source_target_pairs={{0,8},{8,16},{16,24},{24,0},{1,9},{9,17},{17,25},{25,1},{2,10},{10... | collective-permute-start | bytes 1228808 | tf_op jit(solution)/shard_map/ppermute | solution.py:310
  14.0 47.9 %collective-permute-start.7 = (bf16[80,2560]{1,0:T(8,128)(2,1)S(1)}, bf16[80,2560]{1,0:T(8,128)(2,1)S(1)}, u32[]{:S(2)}, u32[]{:S(2)}) collective-permute-start(bf16[80,2560]{1,0:T(8,128)(2,1)S(1)} %bitcast.4), channel_id=1, source_target_pairs={{0,16},{8,24},{16,0},{24,8},{1,17},{9,25},{17,1},{25,9},{2,18},{10... | collective-permute-start | bytes 1228808 | tf_op jit(solution)/shard_map/ppermute | solution.py:310
  16.6 45.2 %collective-permute-start.4 = (bf16[160,2560]{1,0:T(8,128)(2,1)S(1)}, bf16[160,2560]{1,0:T(8,128)(2,1)S(1)}, u32[]{:S(2)}, u32[]{:S(2)}) collective-permute-start(bf16[160,2560]{1,0:T(8,128)(2,1)S(1)} %stack.1.refs_9_.refs_0_), channel_id=1, source_target_pairs={{0,8},{8,16},{16,24},{24,0},{1,9},{9,17},{17,25},{25,1},{2,10},{10... | collective-permute-start | bytes 2457608 | tf_op jit(solution)/shard_map/ppermute | solution.py:310
  16.8 45.0 %collective-permute-start.5 = (bf16[160,2560]{1,0:T(8,128)(2,1)S(1)}, bf16[160,2560]{1,0:T(8,128)(2,1)S(1)}, u32[]{:S(2)}, u32[]{:S(2)}) collective-permute-start(bf16[160,2560]{1,0:T(8,128)(2,1)S(1)} %stack.1.refs_9_.refs_0_), channel_id=1, source_target_pairs={{0,24},{8,0},{16,8},{24,16},{1,25},{9,1},{17,9},{25,17},{2,26},{10... | collective-permute-start | bytes 2457608 | tf_op jit(solution)/shard_map/ppermute | solution.py:310
  19.9 42.0 %collective-permute-start.8 = (bf16[80,2560]{1,0:T(8,128)(2,1)S(1)}, bf16[80,2560]{1,0:T(8,128)(2,1)S(1)}, u32[]{:S(2)}, u32[]{:S(2)}) collective-permute-start(bf16[80,2560]{1,0:T(8,128)(2,1)S(1)} %bitcast.5), channel_id=1, source_target_pairs={{0,24},{8,0},{16,8},{24,16},{1,25},{9,1},{17,9},{25,17},{2,26},{10... | collective-permute-start | bytes 1228808 | tf_op jit(solution)/shard_map/ppermute | solution.py:310
  63.4 11.8 %collective-permute-start.10 = (bf16[320,640]{1,0:T(8,128)(2,1)S(1)}, bf16[320,640]{1,0:T(8,128)(2,1)S(1)}, u32[]{:S(2)}, u32[]{:S(2)}) collective-permute-start(bf16[320,640]{1,0:T(8,128)(2,1)S(1)} %reduced.1.refs_0_), channel_id=1, source_target_pairs={{0,7},{1,0},{2,1},{3,2},{4,3},{5,4},{6,5},{7,6},{8,15},{9,8},{10,9... | collective-permute-start | bytes 1228808 | tf_op jit(solution)/shard_map/ppermute | solution.py:98
  65.1 12.9 %collective-permute-start.9 = (bf16[320,640]{1,0:T(8,128)(2,1)S(1)}, bf16[320,640]{1,0:T(8,128)(2,1)S(1)}, u32[]{:S(2)}, u32[]{:S(2)}) collective-permute-start(bf16[320,640]{1,0:T(8,128)(2,1)S(1)} %reduced.1.refs_0_), channel_id=1, source_target_pairs={{0,1},{1,2},{2,3},{3,4},{4,5},{5,6},{6,7},{7,0},{8,9},{9,10},{10,1... | collective-permute-start | bytes 1228808 | tf_op jit(solution)/shard_map/ppermute | solution.py:98
  78.0 12.1 %collective-permute-start.11 = (bf16[320,640]{1,0:T(8,128)(2,1)S(1)}, bf16[320,640]{1,0:T(8,128)(2,1)S(1)}, u32[]{:S(2)}, u32[]{:S(2)}) collective-permute-start(bf16[320,640]{1,0:T(8,128)(2,1)S(1)} %collective-permute-done.9.refs_1_), channel_id=1, source_target_pairs={{0,1},{1,2},{2,3},{3,4},{4,5},{5,6},{6,7},{7,0},{8,9},{9,10},{10,1... | collective-permute-start | bytes 1228808 | tf_op jit(solution)/shard_map/ppermute | solution.py:98
  78.0 12.1 %collective-permute-start.12 = (bf16[320,640]{1,0:T(8,128)(2,1)S(1)}, bf16[320,640]{1,0:T(8,128)(2,1)S(1)}, u32[]{:S(2)}, u32[]{:S(2)}) collective-permute-start(bf16[320,640]{1,0:T(8,128)(2,1)S(1)} %collective-permute-done.10.refs_2_), channel_id=1, source_target_pairs={{0,7},{1,0},{2,1},{3,2},{4,3},{5,4},{6,5},{7,6},{8,15},{9,8},{10,9... | collective-permute-start | bytes 1228808 | tf_op jit(solution)/shard_map/ppermute | solution.py:98
  81.3 27.1 %collective-permute-start.17 = (bf16[160,2560]{1,0:T(8,128)(2,1)S(1)}, bf16[160,2560]{1,0:T(8,128)(2,1)S(1)}, u32[]{:S(2)}, u32[]{:S(2)}) collective-permute-start(bf16[160,2560]{1,0:T(8,128)(2,1)S(1)} %collective-permute-done.5.refs_12_.refs_3_), channel_id=1, source_target_pairs={{0,24},{8,0},{16,8},{24,16},{1,25},{9,1},{17,9},{25,17},{2,26},{10... | collective-permute-start | bytes 2457608 | tf_op jit(solution)/shard_map/ppermute | solution.py:310
  90.1 11.2 %collective-permute-start.13 = (bf16[320,640]{1,0:T(8,128)(2,1)S(1)}, bf16[320,640]{1,0:T(8,128)(2,1)S(1)}, u32[]{:S(2)}, u32[]{:S(2)}) collective-permute-start(bf16[320,640]{1,0:T(8,128)(2,1)S(1)} %collective-permute-done.11.refs_3_), channel_id=1, source_target_pairs={{0,1},{1,2},{2,3},{3,4},{4,5},{5,6},{6,7},{7,0},{8,9},{9,10},{10,1... | collective-permute-start | bytes 1228808 | tf_op jit(solution)/shard_map/ppermute | solution.py:98
  90.1 11.2 %collective-permute-start.14 = (bf16[320,640]{1,0:T(8,128)(2,1)S(1)}, bf16[320,640]{1,0:T(8,128)(2,1)S(1)}, u32[]{:S(2)}, u32[]{:S(2)}) collective-permute-start(bf16[320,640]{1,0:T(8,128)(2,1)S(1)} %collective-permute-done.12.refs_4_), channel_id=1, source_target_pairs={{0,7},{1,0},{2,1},{3,2},{4,3},{5,4},{6,5},{7,6},{8,15},{9,8},{10,9... | collective-permute-start | bytes 1228808 | tf_op jit(solution)/shard_map/ppermute | solution.py:98
  101.3 7.0 %collective-permute-start.15 = (bf16[160,640]{1,0:T(8,128)(2,1)S(1)}, bf16[160,640]{1,0:T(8,128)(2,1)S(1)}, u32[]{:S(2)}, u32[]{:S(2)}) collective-permute-start(bf16[160,640]{1,0:T(8,128)(2,1)S(1)} %slice.6), channel_id=1, source_target_pairs={{0,1},{1,2},{2,3},{3,4},{4,5},{5,6},{6,7},{7,0},{8,9},{9,10},{10,1... | collective-permute-start | bytes 614408 | tf_op jit(solution)/shard_map/ppermute | solution.py:98
  101.5 6.9 %collective-permute-start.16 = (bf16[160,640]{1,0:T(8,128)(2,1)S(1)}, bf16[160,640]{1,0:T(8,128)(2,1)S(1)}, u32[]{:S(2)}, u32[]{:S(2)}) collective-permute-start(bf16[160,640]{1,0:T(8,128)(2,1)S(1)} %slice.7), channel_id=1, source_target_pairs={{0,7},{1,0},{2,1},{3,2},{4,3},{5,4},{6,5},{7,6},{8,15},{9,8},{10,9... | collective-permute-start | bytes 614408 | tf_op jit(solution)/shard_map/ppermute | solution.py:98
  110.7 9.3 %collective-permute-start.18 = (bf16[320,640]{1,0:T(8,128)(2,1)S(1)}, bf16[320,640]{1,0:T(8,128)(2,1)S(1)}, u32[]{:S(2)}, u32[]{:S(2)}) collective-permute-start(bf16[320,640]{1,0:T(8,128)(2,1)S(1)} %get-tuple-element.62), channel_id=1, source_target_pairs={{0,32},{32,64},{64,96},{96,128},{128,160},{160,192},{192,224},{1,3... | collective-permute-start | bytes 1228808 | tf_op jit(solution)/shard_map/ppermute | solution.py:38
  120.1 7.0 %collective-permute-start.19 = (bf16[80,640]{1,0:T(8,128)(2,1)S(1)}, bf16[80,640]{1,0:T(8,128)(2,1)S(1)}, u32[]{:S(2)}, u32[]{:S(2)}) collective-permute-start(bf16[80,640]{1,0:T(8,128)(2,1)S(1)} %get-tuple-element.64), channel_id=1, source_target_pairs={{0,8},{8,16},{16,24},{24,0},{1,9},{9,17},{17,25},{25,1},{2,10},{10... | collective-permute-start | bytes 307208 | tf_op jit(solution)/shard_map/ppermute | solution.py:310
  120.2 7.0 %collective-permute-start.20 = (bf16[80,640]{1,0:T(8,128)(2,1)S(1)}, bf16[80,640]{1,0:T(8,128)(2,1)S(1)}, u32[]{:S(2)}, u32[]{:S(2)}) collective-permute-start(bf16[80,640]{1,0:T(8,128)(2,1)S(1)} %get-tuple-element.65), channel_id=1, source_target_pairs={{0,16},{8,24},{16,0},{24,8},{1,17},{9,25},{17,1},{25,9},{2,18},{10... | collective-permute-start | bytes 307208 | tf_op jit(solution)/shard_map/ppermute | solution.py:310
  122.3 5.7 %collective-permute-start.21 = (bf16[80,640]{1,0:T(8,128)(2,1)S(1)}, bf16[80,640]{1,0:T(8,128)(2,1)S(1)}, u32[]{:S(2)}, u32[]{:S(2)}) collective-permute-start(bf16[80,640]{1,0:T(8,128)(2,1)S(1)} %get-tuple-element.66), channel_id=1, source_target_pairs={{0,24},{8,0},{16,8},{24,16},{1,25},{9,1},{17,9},{25,17},{2,26},{10... | collective-permute-start | bytes 307208 | tf_op jit(solution)/shard_map/ppermute | solution.py:310

commit v8 on v6

--- a/solution.py
+++ b/solution.py
@@ -201,7 +201,7 @@
     return call(kernel, tuple(like(rows, width, BF) for _ in range(shards)), "update", [local_term, pushed])
 
 
-def copies(kernel, out, name, operands, count):
+def copies(kernel, out, name, operands, count, near=HBM, far=VMEM):
     def body(*refs):
         sems = refs[-1]
         started = []
@@ -216,13 +216,13 @@
     return pl.pallas_call(
         body,
         out_shape=out,
-        in_specs=[HBM] * len(operands),
-        out_specs=jax.tree.map(lambda _: VMEM, out),
+        in_specs=[near] * len(operands),
+        out_specs=jax.tree.map(lambda _: far, out),
         scratch_shapes=[pltpu.SemaphoreType.DMA((count,))],
         compiler_params=pltpu.CompilerParams(vmem_limit_bytes=16 << 20),
         cost_estimate=pl.CostEstimate(flops=0, bytes_accessed=moved, transcendentals=0),
         name=name,
-    )(*[pltpu.with_memory_space_constraint(x, pltpu.HBM) for x in operands])
+    )(*[pltpu.with_memory_space_constraint(x, pltpu.HBM) if near is HBM else x for x in operands])
 
 
 def prepare(gradient, out_inverse, out_coupling, shards):
@@ -286,9 +286,10 @@
 
     def kernel(*refs):
         for k, owner in enumerate(owners_of(shards)):
-            refs[shards][0, :, pl.ds(pl.multiple_of(owner * width, BLK), width)] = refs[k][...]
-
-    return call(kernel, jax.ShapeDtypeStruct((1, rows, shards * width), BF), "join", pieces)
+            yield refs[k], refs[shards].at[0, :, pl.ds(pl.multiple_of(owner * width, BLK), width)]
+
+    out = jax.ShapeDtypeStruct((1, rows, shards * width), BF)
+    return copies(kernel, out, "join", pieces, shards, near=VMEM, far=HBM)
 
 
 def gather_panel(tile):
@@ -306,9 +307,11 @@
     later = after(coupling, grad)
     coupling = [coupling] + [hop_y(coupling if k < 3 else later, k) for k in range(1, shards)]
     near = near_tile(above, psi, shards)
-    early, late = after(pair, grad), after(pair, near)
-    factors = [pair] + [hop_y(early if k == 2 else late, k) for k in range(1, shards)]
-    reduced = reduced_tile(gather_panel(near), coupling, grad, shards)
+    pair = after(pair, grad)
+    ahead, behind = hop_y(pair, 1), hop_y(pair, -1)
+    panel = gather_panel(near)
+    reduced = reduced_tile(panel, coupling, grad, shards)
+    factors = [pair, ahead, hop_y(behind, -1), behind]
     pushed, panel = pushed_tile(gather_panel(reduced), factors, inv, psi, shards)
     local_term = local_tile(panel, factors, inv, shards)
     return join_columns(exchange(update_pieces(local_term, hop_layer(pushed, 1), shards)))

time: 123 us -> 123 us (level)
    pallas_call x7 -> x6, Pallas kernels: 6.81 us -> 6.01 us  [call(): pl.pallas_call(kernel, out_shape=out, in_specs=[HBM if i in far else VMEM...]
    pallas_call x2 -> x3, Pallas kernels: 2.44 us -> 3.22 us  [copies(): pl.pallas_call(body, out_shape=out, in_specs=[near] * len(operands), out_...]
where the time goes in v8:
time: 123 us; the launch traced here: 122 us
  blocking collectives  76.8 us (62%)
  starting transfers between devices  23.4 us (19%)
  waiting for transfers between devices  11.1 us (9%)
  Pallas kernels  9.23 us (8%)
  other arithmetic  1.42 us (1%)
    all_gather x2, blocking collectives, gather_panel(): return lax.all_gather(tile.astype(HALF), 'z', axis=0).astype(BF)  76.8 us
    ppermute x12, starting transfers between devices, hop_y(): return lax.ppermute(x, 'y', [(i, (i + by) % size) for i in range(size)])  19.4 us
    pallas_call x6, Pallas kernels, call(): pl.pallas_call(kernel, out_shape=out, in_specs=[HBM if i in far else VMEM...  6.01 us
    ppermute x12, waiting for transfers between devices, hop_y(): return lax.ppermute(x, 'y', [(i, (i + by) % size) for i in range(size)])  5.7 us
    ppermute x2, waiting for transfers between devices, hop_layer(): lax.ppermute(x, 'layer', [(i, i + by) for i in range(size) if 0 <= i + by...  5.42 us
    ppermute x2, starting transfers between devices, hop_layer(): lax.ppermute(x, 'layer', [(i, i + by) for i in range(size) if 0 <= i + by...  4.02 us
    pallas_call x3, Pallas kernels, copies(): pl.pallas_call(body, out_shape=out, in_specs=[near] * len(operands), out_...  3.22 us
  transfers between devices with their start and end apart: 14, of which 4 were waited for; matrix products, arithmetic and copies ran while one was open for 1% of the time, Pallas kernels for 4%

profile of v8, /device:TPU:2, one launch (start us, length us, event | category | flops | bytes accessed | tf_op | source)
XLA Modules:
  0.0 122.3 jit_solution(5864511109665822974)
XLA Ops:
  0.0 1.3 %prepare.1 = (bf16[80,640]{1,0:T(8,128)(2,1)S(1)}, bf16[80,640]{1,0:T(8,128)(2,1)S(1)}, bf16[80,640]{1,0:T(8,128)(2,1)S(1)}, bf16[80,640]{1,0:T(8,128)(2,1)S(1)}...) custom-call(bf16[1,80,2560]{2,1,0:T(8,128)(2,1)} %refs_0_.1, bf16[1,20,128,128]{3,2,1,0:T(8,128)(2,1)} %refs_1_.2, ...), custom_call_target="tpu_custom_call" | custom-call | bytes 1474560 | tf_op jit(solution)/shard_map/prepare/pallas_call | solution.py:216
  1.3 1.7 %collective-permute-start = (bf16[80,640]{1,0:T(8,128)(2,1)S(1)}, bf16[80,640]{1,0:T(8,128)(2,1)S(1)}, u32[]{:S(2)}, u32[]{:S(2)}) collective-permute-start(bf16[80,640]{1,0:T(8,128)(2,1)S(1)} %get-tuple-element.26), channel_id=1, source_target_pairs={{0,8},{8,16},{16,24},{24,0},{1,9},{9,17},{17,25},{25,1},{2,10},{10... | collective-permute-start | bytes 307208 | tf_op jit(solution)/shard_map/ppermute | solution.py:272
  3.0 2.9 %collective-permute-start.1 = (bf16[80,640]{1,0:T(8,128)(2,1)S(1)}, bf16[80,640]{1,0:T(8,128)(2,1)S(1)}, u32[]{:S(2)}, u32[]{:S(2)}) collective-permute-start(bf16[80,640]{1,0:T(8,128)(2,1)S(1)} %get-tuple-element.27), channel_id=1, source_target_pairs={{0,16},{8,24},{16,0},{24,8},{1,17},{9,25},{17,1},{25,9},{2,18},{10... | collective-permute-start | bytes 307208 | tf_op jit(solution)/shard_map/ppermute | solution.py:272
  5.9 1.3 %collective-permute-start.2 = (bf16[80,640]{1,0:T(8,128)(2,1)S(1)}, bf16[80,640]{1,0:T(8,128)(2,1)S(1)}, u32[]{:S(2)}, u32[]{:S(2)}) collective-permute-start(bf16[80,640]{1,0:T(8,128)(2,1)S(1)} %get-tuple-element.28), channel_id=1, source_target_pairs={{0,24},{8,0},{16,8},{24,16},{1,25},{9,1},{17,9},{25,17},{2,26},{10... | collective-permute-start | bytes 307208 | tf_op jit(solution)/shard_map/ppermute | solution.py:272
  7.2 1.1 stack.1.refs_0_
  8.4 2.3 %collective-permute-done.1.refs_2_ = bf16[80,640]{1,0:T(8,128)(2,1)S(1)} collective-permute-done((bf16[80,640]{1,0:T(8,128)(2,1)S(1)}, bf16[80,640]{1,0:T(8,128)(2,1)S(1)}, u32[]{:S(2)}, u32[]{:S(2)}) %collective-permute-start.1) | collective-permute-done | bytes 102432 | tf_op jit(solution)/shard_map/ppermute | solution.py:272
  10.7 1.9 %collective-permute-start.3 = (bf16[320,640]{1,0:T(8,128)(2,1)S(1)}, bf16[320,640]{1,0:T(8,128)(2,1)S(1)}, u32[]{:S(2)}, u32[]{:S(2)}) collective-permute-start(bf16[320,640]{1,0:T(8,128)(2,1)S(1)} %assemble.1.grad_ref), channel_id=1, source_target_pairs={{32,0},{64,32},{96,64},{128,96},{160,128},{192,160},{224,192},{33,... | collective-permute-start | bytes 1228808 | tf_op jit(solution)/shard_map/ppermute | solution.py:38
  12.6 1.3 %collective-permute-start.4 = (bf16[80,2560]{1,0:T(8,128)(2,1)S(1)}, bf16[80,2560]{1,0:T(8,128)(2,1)S(1)}, u32[]{:S(2)}, u32[]{:S(2)}) collective-permute-start(bf16[80,2560]{1,0:T(8,128)(2,1)S(1)} %bitcast.5), channel_id=1, source_target_pairs={{0,8},{8,16},{16,24},{24,0},{1,9},{9,17},{17,25},{25,1},{2,10},{10... | collective-permute-start | bytes 1228808 | tf_op jit(solution)/shard_map/ppermute | solution.py:272
  14.0 2.7 %collective-permute-start.5 = (bf16[80,2560]{1,0:T(8,128)(2,1)S(1)}, bf16[80,2560]{1,0:T(8,128)(2,1)S(1)}, u32[]{:S(2)}, u32[]{:S(2)}) collective-permute-start(bf16[80,2560]{1,0:T(8,128)(2,1)S(1)} %bitcast.6), channel_id=1, source_target_pairs={{0,16},{8,24},{16,0},{24,8},{1,17},{9,25},{17,1},{25,9},{2,18},{10... | collective-permute-start | bytes 1228808 | tf_op jit(solution)/shard_map/ppermute | solution.py:272
  16.6 1.3 %collective-permute-start.8 = (bf16[160,2560]{1,0:T(8,128)(2,1)S(1)}, bf16[160,2560]{1,0:T(8,128)(2,1)S(1)}, u32[]{:S(2)}, u32[]{:S(2)}) collective-permute-start(bf16[160,2560]{1,0:T(8,128)(2,1)S(1)} %stack.1.refs_0_), channel_id=1, source_target_pairs={{0,24},{8,0},{16,8},{24,16},{1,25},{9,1},{17,9},{25,17},{2,26},{10... | collective-permute-start | bytes 2457608 | tf_op jit(solution)/shard_map/ppermute | solution.py:272
  17.9 0.7 collective-permute-start.7
  18.6 2.5 %collective-permute-start.6 = (bf16[80,2560]{1,0:T(8,128)(2,1)S(1)}, bf16[80,2560]{1,0:T(8,128)(2,1)S(1)}, u32[]{:S(2)}, u32[]{:S(2)}) collective-permute-start(bf16[80,2560]{1,0:T(8,128)(2,1)S(1)} %bitcast.7), channel_id=1, source_target_pairs={{0,24},{8,0},{16,8},{24,16},{1,25},{9,1},{17,9},{25,17},{2,26},{10... | collective-permute-start | bytes 1228808 | tf_op jit(solution)/shard_map/ppermute | solution.py:272
  21.6 40.7 %all-gather.4 = f16[2624,640]{1,0:T(8,128)(2,1)S(1)} all-gather(f16[328,640]{1,0:T(8,128)(2,1)S(1)} %convert_element_type.12), channel_id=2, replica_groups=mesh['layer'=8,'y'=4,'z'=8] {'z'}, dimensions={0}, use_global_device_ids=true | all-gather | bytes 3778560 | tf_op jit(solution)/shard_map/all_gather | solution.py:296
  63.0 1.7 %reduced.1 = bf16[328,640]{1,0:T(8,128)(2,1)S(1)} custom-call(bf16[8,328,640]{2,1,0:T(8,128)(2,1)S(1)} %bitcast.3, bf16[320,640]{1,0:T(8,128)(2,1)S(1)} %assemble.1.grad_ref, bf16[80,2560]{1,0:T(8,128)(2,1)S(1)} %bitcast.8, bf16[80,2560]{1,0:T(8,128)(2,1)S(1)} %collective-permute-done.4.refs_1_, bf16[80,2560]{1,0:T(8,128)(2,1)S(1)} %collective-permute-done.5.refs_2_, ...), custom_call_target="tpu_custom_call" | custom-call | flops 1048576000 | bytes 5826560 | tf_op jit(solution)/shard_map/reduced/pallas_call | solution.py:20
  64.9 36.1 %all-gather.5 = f16[2624,640]{1,0:T(8,128)(2,1)S(1)} all-gather(f16[328,640]{1,0:T(8,128)(2,1)S(1)} %convert_element_type.14), channel_id=3, replica_groups=mesh['layer'=8,'y'=4,'z'=8] {'z'}, dimensions={0}, use_global_device_ids=true | all-gather | bytes 3778560 | tf_op jit(solution)/shard_map/all_gather | solution.py:296
  101.6 2.1 %pushed.1 = (bf16[320,640]{1,0:T(8,128)(2,1)S(1)}, bf16[2560,640]{1,0:T(8,128)(2,1)S(1)}) custom-call(bf16[8,328,640]{2,1,0:T(8,128)(2,1)S(1)} %bitcast.4, bf16[5,128,128]{2,1,0:T(8,128)(2,1)S(1)} %get-tuple-element.37.inverse_ref, bf16[5,128,128]{2,1,0:T(8,128)(2,1)S(1)} %get-tuple-element.34.table_ref.coupling_ref, bf16[160,2560]{1,0:T(8,128)(2,1)S(1)} %stack.1.refs_0_, ...), custom_call_target="tpu_custom_call" | custom-call | flops 1048576000 | bytes 10649600 | tf_op jit(solution)/shard_map/pushed/pallas_call | solution.py:20
  103.7 2.1 %collective-permute-start.10 = (bf16[320,640]{1,0:T(8,128)(2,1)S(1)}, bf16[320,640]{1,0:T(8,128)(2,1)S(1)}, u32[]{:S(2)}, u32[]{:S(2)}) collective-permute-start(bf16[320,640]{1,0:T(8,128)(2,1)S(1)} %get-tuple-element.40), channel_id=1, source_target_pairs={{0,32},{32,64},{64,96},{96,128},{128,160},{160,192},{192,224},{1,3... | collective-permute-start | bytes 1228808 | tf_op jit(solution)/shard_map/ppermute | solution.py:38
  105.8 1.7 %local.1.local_ref = f32[320,640]{1,0:T(8,128)S(1)} custom-call(bf16[2560,640]{1,0:T(8,128)(2,1)S(1)} %get-tuple-element.39.panel_ref, bf16[5,128,128]{2,1,0:T(8,128)(2,1)S(1)} %get-tuple-element.37.inverse_ref, bf16[160,2560]{1,0:T(8,128)(2,1)S(1)} %stack.1.refs_0_, bf16[160,2560]{1,0:T(8,128)(2,1)S(1)} %collective-permute-done.7.refs_1_, ...), custom_call_target="tpu_custom_call" | custom-call | flops 1048576000 | bytes 7536640 | tf_op jit(solution)/shard_map/local/pallas_call | solution.py:20
  107.6 5.4 %collective-permute-done.10.pushed_ref = bf16[320,640]{1,0:T(8,128)(2,1)S(1)} collective-permute-done((bf16[320,640]{1,0:T(8,128)(2,1)S(1)}, bf16[320,640]{1,0:T(8,128)(2,1)S(1)}, u32[]{:S(2)}, u32[]{:S(2)}) %collective-permute-start.10) | collective-permute-done | bytes 409632 | tf_op jit(solution)/shard_map/ppermute | solution.py:38
  113.1 2.1 %collective-permute-start.11 = (bf16[80,640]{1,0:T(8,128)(2,1)S(1)}, bf16[80,640]{1,0:T(8,128)(2,1)S(1)}, u32[]{:S(2)}, u32[]{:S(2)}) collective-permute-start(bf16[80,640]{1,0:T(8,128)(2,1)S(1)} %get-tuple-element.42), channel_id=1, source_target_pairs={{0,8},{8,16},{16,24},{24,0},{1,9},{9,17},{17,25},{25,1},{2,10},{10... | collective-permute-start | bytes 307208 | tf_op jit(solution)/shard_map/ppermute | solution.py:272
  115.2 2.8 %collective-permute-start.13 = (bf16[80,640]{1,0:T(8,128)(2,1)S(1)}, bf16[80,640]{1,0:T(8,128)(2,1)S(1)}, u32[]{:S(2)}, u32[]{:S(2)}) collective-permute-start(bf16[80,640]{1,0:T(8,128)(2,1)S(1)} %get-tuple-element.44), channel_id=1, source_target_pairs={{0,24},{8,0},{16,8},{24,16},{1,25},{9,1},{17,9},{25,17},{2,26},{10... | collective-permute-start | bytes 307208 | tf_op jit(solution)/shard_map/ppermute | solution.py:272
  118.0 2.2 %collective-permute-done.11.refs_1_ = bf16[80,640]{1,0:T(8,128)(2,1)S(1)} collective-permute-done((bf16[80,640]{1,0:T(8,128)(2,1)S(1)}, bf16[80,640]{1,0:T(8,128)(2,1)S(1)}, u32[]{:S(2)}, u32[]{:S(2)}) %collective-permute-start.11) | collective-permute-done | bytes 102432 | tf_op jit(solution)/shard_map/ppermute | solution.py:272
  120.1 1.2 %collective-permute-done.12.refs_2_ = bf16[80,640]{1,0:T(8,128)(2,1)S(1)} collective-permute-done((bf16[80,640]{1,0:T(8,128)(2,1)S(1)}, bf16[80,640]{1,0:T(8,128)(2,1)S(1)}, u32[]{:S(2)}, u32[]{:S(2)}) %collective-permute-start.12) | collective-permute-done | bytes 102432 | tf_op jit(solution)/shard_map/ppermute | solution.py:272
  121.4 0.8 join.1
  (21 shorter events, 2.0 us)
Async XLA Ops:
  0.0 12.6 %copy-start = (bf16[1,80,2560]{2,1,0:T(8,128)(2,1)S(1)}, bf16[1,80,2560]{2,1,0:T(8,128)(2,1)}, u32[]{:S(2)}) copy-start(bf16[1,80,2560]{2,1,0:T(8,128)(2,1)} %param.8) | copy-start | bytes 1228804
  1.3 7.1 %collective-permute-start = (bf16[80,640]{1,0:T(8,128)(2,1)S(1)}, bf16[80,640]{1,0:T(8,128)(2,1)S(1)}, u32[]{:S(2)}, u32[]{:S(2)}) collective-permute-start(bf16[80,640]{1,0:T(8,128)(2,1)S(1)} %get-tuple-element.26), channel_id=1, source_target_pairs={{0,8},{8,16},{16,24},{24,0},{1,9},{9,17},{17,25},{25,1},{2,10},{10... | collective-permute-start | bytes 307208 | tf_op jit(solution)/shard_map/ppermute | solution.py:272
  3.0 7.7 %collective-permute-start.1 = (bf16[80,640]{1,0:T(8,128)(2,1)S(1)}, bf16[80,640]{1,0:T(8,128)(2,1)S(1)}, u32[]{:S(2)}, u32[]{:S(2)}) collective-permute-start(bf16[80,640]{1,0:T(8,128)(2,1)S(1)} %get-tuple-element.27), channel_id=1, source_target_pairs={{0,16},{8,24},{16,0},{24,8},{1,17},{9,25},{17,1},{25,9},{2,18},{10... | collective-permute-start | bytes 307208 | tf_op jit(solution)/shard_map/ppermute | solution.py:272
  5.9 4.8 %collective-permute-start.2 = (bf16[80,640]{1,0:T(8,128)(2,1)S(1)}, bf16[80,640]{1,0:T(8,128)(2,1)S(1)}, u32[]{:S(2)}, u32[]{:S(2)}) collective-permute-start(bf16[80,640]{1,0:T(8,128)(2,1)S(1)} %get-tuple-element.28), channel_id=1, source_target_pairs={{0,24},{8,0},{16,8},{24,16},{1,25},{9,1},{17,9},{25,17},{2,26},{10... | collective-permute-start | bytes 307208 | tf_op jit(solution)/shard_map/ppermute | solution.py:272
  10.7 7.9 %collective-permute-start.3 = (bf16[320,640]{1,0:T(8,128)(2,1)S(1)}, bf16[320,640]{1,0:T(8,128)(2,1)S(1)}, u32[]{:S(2)}, u32[]{:S(2)}) collective-permute-start(bf16[320,640]{1,0:T(8,128)(2,1)S(1)} %assemble.1.grad_ref), channel_id=1, source_target_pairs={{32,0},{64,32},{96,64},{128,96},{160,128},{192,160},{224,192},{33,... | collective-permute-start | bytes 1228808 | tf_op jit(solution)/shard_map/ppermute | solution.py:38
  12.6 50.3 %collective-permute-start.4 = (bf16[80,2560]{1,0:T(8,128)(2,1)S(1)}, bf16[80,2560]{1,0:T(8,128)(2,1)S(1)}, u32[]{:S(2)}, u32[]{:S(2)}) collective-permute-start(bf16[80,2560]{1,0:T(8,128)(2,1)S(1)} %bitcast.5), channel_id=1, source_target_pairs={{0,8},{8,16},{16,24},{24,0},{1,9},{9,17},{17,25},{25,1},{2,10},{10... | collective-permute-start | bytes 1228808 | tf_op jit(solution)/shard_map/ppermute | solution.py:272
  14.0 49.0 %collective-permute-start.5 = (bf16[80,2560]{1,0:T(8,128)(2,1)S(1)}, bf16[80,2560]{1,0:T(8,128)(2,1)S(1)}, u32[]{:S(2)}, u32[]{:S(2)}) collective-permute-start(bf16[80,2560]{1,0:T(8,128)(2,1)S(1)} %bitcast.6), channel_id=1, source_target_pairs={{0,16},{8,24},{16,0},{24,8},{1,17},{9,25},{17,1},{25,9},{2,18},{10... | collective-permute-start | bytes 1228808 | tf_op jit(solution)/shard_map/ppermute | solution.py:272
  16.6 48.1 %collective-permute-start.8 = (bf16[160,2560]{1,0:T(8,128)(2,1)S(1)}, bf16[160,2560]{1,0:T(8,128)(2,1)S(1)}, u32[]{:S(2)}, u32[]{:S(2)}) collective-permute-start(bf16[160,2560]{1,0:T(8,128)(2,1)S(1)} %stack.1.refs_0_), channel_id=1, source_target_pairs={{0,24},{8,0},{16,8},{24,16},{1,25},{9,1},{17,9},{25,17},{2,26},{10... | collective-permute-start | bytes 2457608 | tf_op jit(solution)/shard_map/ppermute | solution.py:272
  17.9 83.7 %collective-permute-start.7 = (bf16[160,2560]{1,0:T(8,128)(2,1)S(1)}, bf16[160,2560]{1,0:T(8,128)(2,1)S(1)}, u32[]{:S(2)}, u32[]{:S(2)}) collective-permute-start(bf16[160,2560]{1,0:T(8,128)(2,1)S(1)} %stack.1.refs_0_), channel_id=1, source_target_pairs={{0,8},{8,16},{16,24},{24,0},{1,9},{9,17},{17,25},{25,1},{2,10},{10... | collective-permute-start | bytes 2457608 | tf_op jit(solution)/shard_map/ppermute | solution.py:272
  18.6 44.4 %collective-permute-start.6 = (bf16[80,2560]{1,0:T(8,128)(2,1)S(1)}, bf16[80,2560]{1,0:T(8,128)(2,1)S(1)}, u32[]{:S(2)}, u32[]{:S(2)}) collective-permute-start(bf16[80,2560]{1,0:T(8,128)(2,1)S(1)} %bitcast.7), channel_id=1, source_target_pairs={{0,24},{8,0},{16,8},{24,16},{1,25},{9,1},{17,9},{25,17},{2,26},{10... | collective-permute-start | bytes 1228808 | tf_op jit(solution)/shard_map/ppermute | solution.py:272
  64.8 36.9 %collective-permute-start.9 = (bf16[160,2560]{1,0:T(8,128)(2,1)S(1)}, bf16[160,2560]{1,0:T(8,128)(2,1)S(1)}, u32[]{:S(2)}, u32[]{:S(2)}) collective-permute-start(bf16[160,2560]{1,0:T(8,128)(2,1)S(1)} %collective-permute-done.8.refs_3_), channel_id=1, source_target_pairs={{0,24},{8,0},{16,8},{24,16},{1,25},{9,1},{17,9},{25,17},{2,26},{10... | collective-permute-start | bytes 2457608 | tf_op jit(solution)/shard_map/ppermute | solution.py:272
  103.7 9.3 %collective-permute-start.10 = (bf16[320,640]{1,0:T(8,128)(2,1)S(1)}, bf16[320,640]{1,0:T(8,128)(2,1)S(1)}, u32[]{:S(2)}, u32[]{:S(2)}) collective-permute-start(bf16[320,640]{1,0:T(8,128)(2,1)S(1)} %get-tuple-element.40), channel_id=1, source_target_pairs={{0,32},{32,64},{64,96},{96,128},{128,160},{160,192},{192,224},{1,3... | collective-permute-start | bytes 1228808 | tf_op jit(solution)/shard_map/ppermute | solution.py:38
  113.1 7.0 %collective-permute-start.11 = (bf16[80,640]{1,0:T(8,128)(2,1)S(1)}, bf16[80,640]{1,0:T(8,128)(2,1)S(1)}, u32[]{:S(2)}, u32[]{:S(2)}) collective-permute-start(bf16[80,640]{1,0:T(8,128)(2,1)S(1)} %get-tuple-element.42), channel_id=1, source_target_pairs={{0,8},{8,16},{16,24},{24,0},{1,9},{9,17},{17,25},{25,1},{2,10},{10... | collective-permute-start | bytes 307208 | tf_op jit(solution)/shard_map/ppermute | solution.py:272
  115.2 6.2 %collective-permute-start.12 = (bf16[80,640]{1,0:T(8,128)(2,1)S(1)}, bf16[80,640]{1,0:T(8,128)(2,1)S(1)}, u32[]{:S(2)}, u32[]{:S(2)}) collective-permute-start(bf16[80,640]{1,0:T(8,128)(2,1)S(1)} %get-tuple-element.43), channel_id=1, source_target_pairs={{0,16},{8,24},{16,0},{24,8},{1,17},{9,25},{17,1},{25,9},{2,18},{10... | collective-permute-start | bytes 307208 | tf_op jit(solution)/shard_map/ppermute | solution.py:272
  115.2 6.2 %collective-permute-start.13 = (bf16[80,640]{1,0:T(8,128)(2,1)S(1)}, bf16[80,640]{1,0:T(8,128)(2,1)S(1)}, u32[]{:S(2)}, u32[]{:S(2)}) collective-permute-start(bf16[80,640]{1,0:T(8,128)(2,1)S(1)} %get-tuple-element.44), channel_id=1, source_target_pairs={{0,24},{8,0},{16,8},{24,16},{1,25},{9,1},{17,9},{25,17},{2,26},{10... | collective-permute-start | bytes 307208 | tf_op jit(solution)/shard_map/ppermute | solution.py:272

commit v9 on v8

--- a/solution.py
+++ b/solution.py
@@ -73,7 +73,7 @@
 
 def owners_of(shards):
     y = lax.axis_index("y")
-    return [lax.rem(y + (shards - k), shards) for k in range(shards)]
+    return [lax.rem(y + (shards - k), shards) for k in distances(shards)]
 
 
 def joined(pieces, rows, first=0):
@@ -194,9 +194,9 @@
 
     def kernel(local_ref, pushed_ref, *out_refs):
         y = lax.axis_index("y")
-        for k in range(shards):
+        for k, out_ref in zip(distances(shards), out_refs, strict=True):
             here = rows_of(lax.rem(y + k, shards), rows)
-            out_refs[k][...] = (local_ref[here, :] - pushed_ref[here, :].astype(F32)).astype(BF)
+            out_ref[...] = (local_ref[here, :] - pushed_ref[here, :].astype(F32)).astype(BF)
 
     return call(kernel, tuple(like(rows, width, BF) for _ in range(shards)), "update", [local_term, pushed])
 
@@ -225,24 +225,33 @@
     )(*[pltpu.with_memory_space_constraint(x, pltpu.HBM) if near is HBM else x for x in operands])
 
 
-def prepare(gradient, out_inverse, out_coupling, shards):
+def column_blocks(gradient, shards):
     _, rows, width = gradient.shape
     width //= shards
+
+    def kernel(grad_ref, *out_refs):
+        y = lax.axis_index("y")
+        for k, out_ref in zip(distances(shards), out_refs, strict=True):
+            at = pl.multiple_of(lax.rem(y + k, shards) * width, BLK)
+            yield grad_ref.at[0, :, pl.ds(at, width)], out_ref
+
+    return copies(kernel, (like(rows, width, BF),) * shards, "blocks", [gradient], shards)
+
+
+def operands(in_inverse, in_carry, out_inverse, out_coupling, shards):
+    _, rows, width = in_inverse.shape
     blocks = out_inverse.shape[1] // shards
     table = jax.ShapeDtypeStruct((blocks, BLK, BLK), BF)
 
-    def kernel(grad_ref, inverse_ref, coupling_ref, *out_refs):
-        y = lax.axis_index("y")
-        mine = pl.ds(y * blocks, blocks)
-        for k in range(shards):
-            at = pl.multiple_of(lax.rem(y + k, shards) * width, BLK)
-            yield grad_ref.at[0, :, pl.ds(at, width)], out_refs[k]
-        yield inverse_ref.at[0, mine], out_refs[shards]
-        yield coupling_ref.at[0, mine], out_refs[shards + 1]
-
-    out = (*[like(rows, width, BF)] * shards, table, table)
-    out = copies(kernel, out, "prepare", [gradient, out_inverse, out_coupling], shards + 2)
-    return out[:shards], *out[shards:]
+    def kernel(first_ref, second_ref, inverse_ref, coupling_ref, pair_ref, inv_ref, psi_ref):
+        mine = pl.ds(lax.axis_index("y") * blocks, blocks)
+        yield first_ref.at[0], pair_ref.at[pl.ds(0, rows), :]
+        yield second_ref.at[0], pair_ref.at[pl.ds(rows, rows), :]
+        yield coupling_ref.at[0, mine], psi_ref
+        yield inverse_ref.at[0, mine], inv_ref
+
+    out = (like(2 * rows, width, BF), table, table)
+    return copies(kernel, out, "operands", [in_inverse, in_carry, out_inverse, out_coupling], 4)
 
 
 def assemble(pieces):
@@ -256,24 +265,17 @@
     return call(kernel, like(shards * rows, width, BF), "assemble", pieces)
 
 
-def stack(parts):
-    rows, width = parts[0].shape[1:]
-    count = len(parts)
-
-    def kernel(*refs):
-        for i in range(count):
-            yield refs[i].at[0], refs[count].at[pl.ds(i * rows, rows), :]
-
-    return copies(kernel, like(count * rows, width, BF), "stack", parts, count)
-
-
 def hop_y(x, by):
     size = lax.axis_size("y")
     return lax.ppermute(x, "y", [(i, (i + by) % size) for i in range(size)])
 
 
+def distances(shards):
+    return [0] + sorted(range(1, shards), key=lambda k: -min(k, shards - k))
+
+
 def exchange(pieces):
-    return [pieces[0]] + [hop_y(pieces[k], k) for k in range(1, len(pieces))]
+    return [hop_y(piece, k) if k else piece for piece, k in zip(pieces, distances(len(pieces)), strict=True)]
 
 
 def after(x, *others):
@@ -298,20 +300,18 @@
 
 def local(gradient, in_inverse, in_coupling, in_carry, out_inverse, out_coupling):
     shards = lax.axis_size("y")
-    slices, inv, psi = prepare(gradient, out_inverse, out_coupling, shards)
+    slices = column_blocks(gradient, shards)
     pieces = exchange(slices)
-    pair = stack([after(in_inverse, slices[0]), in_carry])
+    pair, inv, psi = operands(after(in_inverse, slices[0]), in_carry, out_inverse, out_coupling, shards)
     grad = assemble(lax.optimization_barrier((*pieces, pair))[:shards])
     above = hop_layer(grad, -1)
-    coupling = after(in_coupling, slices[0])[0]
-    later = after(coupling, grad)
-    coupling = [coupling] + [hop_y(coupling if k < 3 else later, k) for k in range(1, shards)]
+    coupling = after(in_coupling, grad)[0]
+    coupling = exchange([coupling] * shards)
     near = near_tile(above, psi, shards)
     pair = after(pair, grad)
     ahead, behind = hop_y(pair, 1), hop_y(pair, -1)
-    panel = gather_panel(near)
-    reduced = reduced_tile(panel, coupling, grad, shards)
-    factors = [pair, ahead, hop_y(behind, -1), behind]
+    reduced = reduced_tile(gather_panel(near), coupling, grad, shards)
+    factors = [pair, hop_y(behind, -1), ahead, behind]
     pushed, panel = pushed_tile(gather_panel(reduced), factors, inv, psi, shards)
     local_term = local_tile(panel, factors, inv, shards)
     return join_columns(exchange(update_pieces(local_term, hop_layer(pushed, 1), shards)))

time: 123 us -> 122 us (level)
  transfers between devices with their start and end apart: 14 -> 14, of which waited for: 4 -> 5; matrix products, arithmetic and copies ran while one was open for 1% -> 1% of each run, Pallas kernels for 4% -> 4%
where the time goes in v9:
time: 122 us
  blocking collectives  76.8 us (63%)
  starting transfers between devices  23.9 us (20%)
  waiting for transfers between devices  10.2 us (8%)
  Pallas kernels  9.17 us (8%)
  other arithmetic  1.42 us (1%)
    all_gather x2, blocking collectives, gather_panel(): return lax.all_gather(tile.astype(HALF), 'z', axis=0).astype(BF)  76.8 us
    ppermute x12, starting transfers between devices, hop_y(): return lax.ppermute(x, 'y', [(i, (i + by) % size) for i in range(size)])  19.3 us
    pallas_call x6, Pallas kernels, call(): pl.pallas_call(kernel, out_shape=out, in_specs=[HBM if i in far else VMEM...  6.01 us
    ppermute x2, waiting for transfers between devices, hop_layer(): lax.ppermute(x, 'layer', [(i, i + by) for i in range(size) if 0 <= i + by...  5.62 us
    ppermute x2, starting transfers between devices, hop_layer(): lax.ppermute(x, 'layer', [(i, i + by) for i in range(size) if 0 <= i + by...  4.56 us
    ppermute x12, waiting for transfers between devices, hop_y(): return lax.ppermute(x, 'y', [(i, (i + by) % size) for i in range(size)])  4.56 us
    pallas_call x3, Pallas kernels, copies(): pl.pallas_call(body, out_shape=out, in_specs=[near] * len(operands), out_...  3.15 us
  transfers between devices with their start and end apart: 14, of which 5 were waited for; matrix products, arithmetic and copies ran while one was open for 1% of the time, Pallas kernels for 4%

profile of v9, /device:TPU:2, one launch (start us, length us, event | category | flops | bytes accessed | tf_op | source)
XLA Modules:
  0.0 121.7 jit_solution(3328102941528711373)
XLA Ops:
  0.0 1.1 blocks.1
  1.1 3.3 %collective-permute-start = (bf16[80,640]{1,0:T(8,128)(2,1)S(1)}, bf16[80,640]{1,0:T(8,128)(2,1)S(1)}, u32[]{:S(2)}, u32[]{:S(2)}) collective-permute-start(bf16[80,640]{1,0:T(8,128)(2,1)S(1)} %get-tuple-element.26), channel_id=1, source_target_pairs={{0,16},{8,24},{16,0},{24,8},{1,17},{9,25},{17,1},{25,9},{2,18},{10... | collective-permute-start | bytes 307208 | tf_op jit(solution)/shard_map/ppermute | solution.py:270
  5.1 2.6 %collective-permute-start.2 = (bf16[80,640]{1,0:T(8,128)(2,1)S(1)}, bf16[80,640]{1,0:T(8,128)(2,1)S(1)}, u32[]{:S(2)}, u32[]{:S(2)}) collective-permute-start(bf16[80,640]{1,0:T(8,128)(2,1)S(1)} %get-tuple-element.28), channel_id=1, source_target_pairs={{0,24},{8,0},{16,8},{24,16},{1,25},{9,1},{17,9},{25,17},{2,26},{10... | collective-permute-start | bytes 307208 | tf_op jit(solution)/shard_map/ppermute | solution.py:270
  7.7 1.2 %operands.1 = (bf16[160,2560]{1,0:T(8,128)(2,1)S(1)}, bf16[5,128,128]{2,1,0:T(8,128)(2,1)S(1)}, bf16[5,128,128]{2,1,0:T(8,128)(2,1)S(1)}) custom-call(bf16[1,80,2560]{2,1,0:T(8,128)(2,1)} %refs_0_.2, bf16[1,80,2560]{2,1,0:T(8,128)(2,1)} %refs_1_.1, bf16[1,20,128,128]{3,2,1,0:T(8,128)(2,1)} %refs_2_.1, bf16[1,20,128,128]{3,2,1,0:T(8,128)(2,1)} %refs_3_.1), custom_call_target="tpu_custom_call" | custom-call | bytes 2293760 | tf_op jit(solution)/shard_map/operands/pallas_call | solution.py:216
  8.9 1.4 %collective-permute-done.1.refs_2_ = bf16[80,640]{1,0:T(8,128)(2,1)S(1)} collective-permute-done((bf16[80,640]{1,0:T(8,128)(2,1)S(1)}, bf16[80,640]{1,0:T(8,128)(2,1)S(1)}, u32[]{:S(2)}, u32[]{:S(2)}) %collective-permute-start.1) | collective-permute-done | bytes 102432 | tf_op jit(solution)/shard_map/ppermute | solution.py:270
  10.3 2.5 %collective-permute-start.3 = (bf16[320,640]{1,0:T(8,128)(2,1)S(1)}, bf16[320,640]{1,0:T(8,128)(2,1)S(1)}, u32[]{:S(2)}, u32[]{:S(2)}) collective-permute-start(bf16[320,640]{1,0:T(8,128)(2,1)S(1)} %assemble.1.grad_ref), channel_id=1, source_target_pairs={{32,0},{64,32},{96,64},{128,96},{160,128},{192,160},{224,192},{33,... | collective-permute-start | bytes 1228808 | tf_op jit(solution)/shard_map/ppermute | solution.py:38
  12.8 1.2 collective-permute-start.4
  14.0 2.4 %collective-permute-start.5 = (bf16[80,2560]{1,0:T(8,128)(2,1)S(1)}, bf16[80,2560]{1,0:T(8,128)(2,1)S(1)}, u32[]{:S(2)}, u32[]{:S(2)}) collective-permute-start(bf16[80,2560]{1,0:T(8,128)(2,1)S(1)} %bitcast.6), channel_id=1, source_target_pairs={{0,8},{8,16},{16,24},{24,0},{1,9},{9,17},{17,25},{25,1},{2,10},{10... | collective-permute-start | bytes 1228808 | tf_op jit(solution)/shard_map/ppermute | solution.py:270
  16.5 0.8 collective-permute-start.6
  17.3 0.8 collective-permute-start.7
  18.3 1.0 collective-permute-start.9
  19.8 40.7 %all-gather.4 = f16[2624,640]{1,0:T(8,128)(2,1)S(1)} all-gather(f16[328,640]{1,0:T(8,128)(2,1)S(1)} %convert_element_type.12), channel_id=2, replica_groups=mesh['layer'=8,'y'=4,'z'=8] {'z'}, dimensions={0}, use_global_device_ids=true | all-gather | bytes 3778560 | tf_op jit(solution)/shard_map/all_gather | solution.py:298
  61.1 1.7 %reduced.1 = bf16[328,640]{1,0:T(8,128)(2,1)S(1)} custom-call(bf16[8,328,640]{2,1,0:T(8,128)(2,1)S(1)} %bitcast.3, bf16[320,640]{1,0:T(8,128)(2,1)S(1)} %assemble.1.grad_ref, bf16[80,2560]{1,0:T(8,128)(2,1)S(1)} %bitcast.8, bf16[80,2560]{1,0:T(8,128)(2,1)S(1)} %collective-permute-done.4.refs_1_, bf16[80,2560]{1,0:T(8,128)(2,1)S(1)} %collective-permute-done.5.refs_2_, ...), custom_call_target="tpu_custom_call" | custom-call | flops 1048576000 | bytes 5826560 | tf_op jit(solution)/shard_map/reduced/pallas_call | solution.py:20
  62.9 1.6 %collective-permute-start.8 = (bf16[160,2560]{1,0:T(8,128)(2,1)S(1)}, bf16[160,2560]{1,0:T(8,128)(2,1)S(1)}, u32[]{:S(2)}, u32[]{:S(2)}) collective-permute-start(bf16[160,2560]{1,0:T(8,128)(2,1)S(1)} %collective-permute-done.7.refs_3_), channel_id=1, source_target_pairs={{0,24},{8,0},{16,8},{24,16},{1,25},{9,1},{17,9},{25,17},{2,26},{10... | collective-permute-start | bytes 2457608 | tf_op jit(solution)/shard_map/ppermute | solution.py:270
  64.5 36.1 %all-gather.5 = f16[2624,640]{1,0:T(8,128)(2,1)S(1)} all-gather(f16[328,640]{1,0:T(8,128)(2,1)S(1)} %convert_element_type.14), channel_id=3, replica_groups=mesh['layer'=8,'y'=4,'z'=8] {'z'}, dimensions={0}, use_global_device_ids=true | all-gather | bytes 3778560 | tf_op jit(solution)/shard_map/all_gather | solution.py:298
  101.3 2.1 %pushed.1 = (bf16[320,640]{1,0:T(8,128)(2,1)S(1)}, bf16[2560,640]{1,0:T(8,128)(2,1)S(1)}) custom-call(bf16[8,328,640]{2,1,0:T(8,128)(2,1)S(1)} %bitcast.4, bf16[5,128,128]{2,1,0:T(8,128)(2,1)S(1)} %get-tuple-element.37.inverse_ref, bf16[5,128,128]{2,1,0:T(8,128)(2,1)S(1)} %get-tuple-element.35.table_ref.coupling_ref, ...), custom_call_target="tpu_custom_call" | custom-call | flops 1048576000 | bytes 10649600 | tf_op jit(solution)/shard_map/pushed/pallas_call | solution.py:20
  103.4 2.1 %collective-permute-start.10 = (bf16[320,640]{1,0:T(8,128)(2,1)S(1)}, bf16[320,640]{1,0:T(8,128)(2,1)S(1)}, u32[]{:S(2)}, u32[]{:S(2)}) collective-permute-start(bf16[320,640]{1,0:T(8,128)(2,1)S(1)} %get-tuple-element.40), channel_id=1, source_target_pairs={{0,32},{32,64},{64,96},{96,128},{128,160},{160,192},{192,224},{1,3... | collective-permute-start | bytes 1228808 | tf_op jit(solution)/shard_map/ppermute | solution.py:38
  105.5 1.7 %local.1.local_ref = f32[320,640]{1,0:T(8,128)S(1)} custom-call(bf16[2560,640]{1,0:T(8,128)(2,1)S(1)} %get-tuple-element.39.panel_ref, bf16[5,128,128]{2,1,0:T(8,128)(2,1)S(1)} %get-tuple-element.37.inverse_ref, bf16[160,2560]{1,0:T(8,128)(2,1)S(1)} %get-tuple-element.38.refs_0_, bf16[160,2560]{1,0:T(8,128)(2,1)S(1)} %collective-permute-done.8.refs_1_, ...), custom_call_target="tpu_custom_call" | custom-call | flops 1048576000 | bytes 7536640 | tf_op jit(solution)/shard_map/local/pallas_call | solution.py:20
  107.2 5.4 %collective-permute-done.10.pushed_ref = bf16[320,640]{1,0:T(8,128)(2,1)S(1)} collective-permute-done((bf16[320,640]{1,0:T(8,128)(2,1)S(1)}, bf16[320,640]{1,0:T(8,128)(2,1)S(1)}, u32[]{:S(2)}, u32[]{:S(2)}) %collective-permute-start.10) | collective-permute-done | bytes 409632 | tf_op jit(solution)/shard_map/ppermute | solution.py:38
  112.7 1.7 %collective-permute-start.11 = (bf16[80,640]{1,0:T(8,128)(2,1)S(1)}, bf16[80,640]{1,0:T(8,128)(2,1)S(1)}, u32[]{:S(2)}, u32[]{:S(2)}) collective-permute-start(bf16[80,640]{1,0:T(8,128)(2,1)S(1)} %get-tuple-element.42), channel_id=1, source_target_pairs={{0,16},{8,24},{16,0},{24,8},{1,17},{9,25},{17,1},{25,9},{2,18},{10... | collective-permute-start | bytes 307208 | tf_op jit(solution)/shard_map/ppermute | solution.py:270
  114.4 1.0 collective-permute-start.12
  115.4 2.3 %collective-permute-start.13 = (bf16[80,640]{1,0:T(8,128)(2,1)S(1)}, bf16[80,640]{1,0:T(8,128)(2,1)S(1)}, u32[]{:S(2)}, u32[]{:S(2)}) collective-permute-start(bf16[80,640]{1,0:T(8,128)(2,1)S(1)} %get-tuple-element.44), channel_id=1, source_target_pairs={{0,24},{8,0},{16,8},{24,16},{1,25},{9,1},{17,9},{25,17},{2,26},{10... | collective-permute-start | bytes 307208 | tf_op jit(solution)/shard_map/ppermute | solution.py:270
  117.6 2.1 %collective-permute-done.11.refs_1_ = bf16[80,640]{1,0:T(8,128)(2,1)S(1)} collective-permute-done((bf16[80,640]{1,0:T(8,128)(2,1)S(1)}, bf16[80,640]{1,0:T(8,128)(2,1)S(1)}, u32[]{:S(2)}, u32[]{:S(2)}) %collective-permute-start.11) | collective-permute-done | bytes 102432 | tf_op jit(solution)/shard_map/ppermute | solution.py:270
  119.7 1.0 collective-permute-done.12.refs_2_
  (21 shorter events, 3.6 us)
Async XLA Ops:
  0.0 12.8 %copy-start = (bf16[1,80,2560]{2,1,0:T(8,128)(2,1)S(1)}, bf16[1,80,2560]{2,1,0:T(8,128)(2,1)}, u32[]{:S(2)}) copy-start(bf16[1,80,2560]{2,1,0:T(8,128)(2,1)} %param.8) | copy-start | bytes 1228804
  1.1 7.8 %collective-permute-start = (bf16[80,640]{1,0:T(8,128)(2,1)S(1)}, bf16[80,640]{1,0:T(8,128)(2,1)S(1)}, u32[]{:S(2)}, u32[]{:S(2)}) collective-permute-start(bf16[80,640]{1,0:T(8,128)(2,1)S(1)} %get-tuple-element.26), channel_id=1, source_target_pairs={{0,16},{8,24},{16,0},{24,8},{1,17},{9,25},{17,1},{25,9},{2,18},{10... | collective-permute-start | bytes 307208 | tf_op jit(solution)/shard_map/ppermute | solution.py:270
  4.4 5.9 %collective-permute-start.1 = (bf16[80,640]{1,0:T(8,128)(2,1)S(1)}, bf16[80,640]{1,0:T(8,128)(2,1)S(1)}, u32[]{:S(2)}, u32[]{:S(2)}) collective-permute-start(bf16[80,640]{1,0:T(8,128)(2,1)S(1)} %get-tuple-element.27), channel_id=1, source_target_pairs={{0,8},{8,16},{16,24},{24,0},{1,9},{9,17},{17,25},{25,1},{2,10},{10... | collective-permute-start | bytes 307208 | tf_op jit(solution)/shard_map/ppermute | solution.py:270
  5.1 5.2 %collective-permute-start.2 = (bf16[80,640]{1,0:T(8,128)(2,1)S(1)}, bf16[80,640]{1,0:T(8,128)(2,1)S(1)}, u32[]{:S(2)}, u32[]{:S(2)}) collective-permute-start(bf16[80,640]{1,0:T(8,128)(2,1)S(1)} %get-tuple-element.28), channel_id=1, source_target_pairs={{0,24},{8,0},{16,8},{24,16},{1,25},{9,1},{17,9},{25,17},{2,26},{10... | collective-permute-start | bytes 307208 | tf_op jit(solution)/shard_map/ppermute | solution.py:270
  10.3 7.9 %collective-permute-start.3 = (bf16[320,640]{1,0:T(8,128)(2,1)S(1)}, bf16[320,640]{1,0:T(8,128)(2,1)S(1)}, u32[]{:S(2)}, u32[]{:S(2)}) collective-permute-start(bf16[320,640]{1,0:T(8,128)(2,1)S(1)} %assemble.1.grad_ref), channel_id=1, source_target_pairs={{32,0},{64,32},{96,64},{128,96},{160,128},{192,160},{224,192},{33,... | collective-permute-start | bytes 1228808 | tf_op jit(solution)/shard_map/ppermute | solution.py:38
  12.8 48.3 %collective-permute-start.4 = (bf16[80,2560]{1,0:T(8,128)(2,1)S(1)}, bf16[80,2560]{1,0:T(8,128)(2,1)S(1)}, u32[]{:S(2)}, u32[]{:S(2)}) collective-permute-start(bf16[80,2560]{1,0:T(8,128)(2,1)S(1)} %bitcast.5), channel_id=1, source_target_pairs={{0,16},{8,24},{16,0},{24,8},{1,17},{9,25},{17,1},{25,9},{2,18},{10... | collective-permute-start | bytes 1228808 | tf_op jit(solution)/shard_map/ppermute | solution.py:270
  14.0 47.1 %collective-permute-start.5 = (bf16[80,2560]{1,0:T(8,128)(2,1)S(1)}, bf16[80,2560]{1,0:T(8,128)(2,1)S(1)}, u32[]{:S(2)}, u32[]{:S(2)}) collective-permute-start(bf16[80,2560]{1,0:T(8,128)(2,1)S(1)} %bitcast.6), channel_id=1, source_target_pairs={{0,8},{8,16},{16,24},{24,0},{1,9},{9,17},{17,25},{25,1},{2,10},{10... | collective-permute-start | bytes 1228808 | tf_op jit(solution)/shard_map/ppermute | solution.py:270
  16.5 44.7 %collective-permute-start.6 = (bf16[80,2560]{1,0:T(8,128)(2,1)S(1)}, bf16[80,2560]{1,0:T(8,128)(2,1)S(1)}, u32[]{:S(2)}, u32[]{:S(2)}) collective-permute-start(bf16[80,2560]{1,0:T(8,128)(2,1)S(1)} %bitcast.7), channel_id=1, source_target_pairs={{0,24},{8,0},{16,8},{24,16},{1,25},{9,1},{17,9},{25,17},{2,26},{10... | collective-permute-start | bytes 1228808 | tf_op jit(solution)/shard_map/ppermute | solution.py:270
  17.3 45.6 %collective-permute-start.7 = (bf16[160,2560]{1,0:T(8,128)(2,1)S(1)}, bf16[160,2560]{1,0:T(8,128)(2,1)S(1)}, u32[]{:S(2)}, u32[]{:S(2)}) collective-permute-start(bf16[160,2560]{1,0:T(8,128)(2,1)S(1)} %get-tuple-element.38.refs_0_), channel_id=1, source_target_pairs={{0,24},{8,0},{16,8},{24,16},{1,25},{9,1},{17,9},{25,17},{2,26},{10... | collective-permute-start | bytes 2457608 | tf_op jit(solution)/shard_map/ppermute | solution.py:270
  18.3 83.0 %collective-permute-start.9 = (bf16[160,2560]{1,0:T(8,128)(2,1)S(1)}, bf16[160,2560]{1,0:T(8,128)(2,1)S(1)}, u32[]{:S(2)}, u32[]{:S(2)}) collective-permute-start(bf16[160,2560]{1,0:T(8,128)(2,1)S(1)} %get-tuple-element.38.refs_0_), channel_id=1, source_target_pairs={{0,8},{8,16},{16,24},{24,0},{1,9},{9,17},{17,25},{25,1},{2,10},{10... | collective-permute-start | bytes 2457608 | tf_op jit(solution)/shard_map/ppermute | solution.py:270
  62.9 38.3 %collective-permute-start.8 = (bf16[160,2560]{1,0:T(8,128)(2,1)S(1)}, bf16[160,2560]{1,0:T(8,128)(2,1)S(1)}, u32[]{:S(2)}, u32[]{:S(2)}) collective-permute-start(bf16[160,2560]{1,0:T(8,128)(2,1)S(1)} %collective-permute-done.7.refs_3_), channel_id=1, source_target_pairs={{0,24},{8,0},{16,8},{24,16},{1,25},{9,1},{17,9},{25,17},{2,26},{10... | collective-permute-start | bytes 2457608 | tf_op jit(solution)/shard_map/ppermute | solution.py:270
  103.4 9.3 %collective-permute-start.10 = (bf16[320,640]{1,0:T(8,128)(2,1)S(1)}, bf16[320,640]{1,0:T(8,128)(2,1)S(1)}, u32[]{:S(2)}, u32[]{:S(2)}) collective-permute-start(bf16[320,640]{1,0:T(8,128)(2,1)S(1)} %get-tuple-element.40), channel_id=1, source_target_pairs={{0,32},{32,64},{64,96},{96,128},{128,160},{160,192},{192,224},{1,3... | collective-permute-start | bytes 1228808 | tf_op jit(solution)/shard_map/ppermute | solution.py:38
  112.7 7.0 %collective-permute-start.11 = (bf16[80,640]{1,0:T(8,128)(2,1)S(1)}, bf16[80,640]{1,0:T(8,128)(2,1)S(1)}, u32[]{:S(2)}, u32[]{:S(2)}) collective-permute-start(bf16[80,640]{1,0:T(8,128)(2,1)S(1)} %get-tuple-element.42), channel_id=1, source_target_pairs={{0,16},{8,24},{16,0},{24,8},{1,17},{9,25},{17,1},{25,9},{2,18},{10... | collective-permute-start | bytes 307208 | tf_op jit(solution)/shard_map/ppermute | solution.py:270
  114.4 6.4 %collective-permute-start.12 = (bf16[80,640]{1,0:T(8,128)(2,1)S(1)}, bf16[80,640]{1,0:T(8,128)(2,1)S(1)}, u32[]{:S(2)}, u32[]{:S(2)}) collective-permute-start(bf16[80,640]{1,0:T(8,128)(2,1)S(1)} %get-tuple-element.43), channel_id=1, source_target_pairs={{0,8},{8,16},{16,24},{24,0},{1,9},{9,17},{17,25},{25,1},{2,10},{10... | collective-permute-start | bytes 307208 | tf_op jit(solution)/shard_map/ppermute | solution.py:270
  115.4 5.4 %collective-permute-start.13 = (bf16[80,640]{1,0:T(8,128)(2,1)S(1)}, bf16[80,640]{1,0:T(8,128)(2,1)S(1)}, u32[]{:S(2)}, u32[]{:S(2)}) collective-permute-start(bf16[80,640]{1,0:T(8,128)(2,1)S(1)} %get-tuple-element.44), channel_id=1, source_target_pairs={{0,24},{8,0},{16,8},{24,16},{1,25},{9,1},{17,9},{25,17},{2,26},{10... | collective-permute-start | bytes 307208 | tf_op jit(solution)/shard_map/ppermute | solution.py:270

commit v10 on v9

--- a/solution.py
+++ b/solution.py
@@ -76,8 +76,9 @@
     return [lax.rem(y + (shards - k), shards) for k in distances(shards)]
 
 
-def joined(pieces, rows, first=0):
-    return jnp.concatenate([piece[pl.ds(first, rows), :] for piece in pieces], axis=0)
+def joined(pieces, rows, last=None):
+    firsts = [piece.shape[0] - last if last else 0 for piece in pieces]
+    return jnp.concatenate([piece[pl.ds(first, rows), :] for first, piece in zip(firsts, pieces, strict=True)], axis=0)
 
 
 def load_scaled(in_ref, panel_ref, at, width, shards, rows):
@@ -89,8 +90,8 @@
         codes = codes * codes
         codes = codes * codes
         for k in range(shards):
-            part = in_ref[j, pl.ds(k * rows, rows), cols].astype(F32) * codes[k : k + 1]
-            panel_ref[pl.ds((k * count + j) * rows, rows), cols] = part.astype(BF)
+            undo = jnp.broadcast_to(codes[k : k + 1], (rows, width)).astype(BF)
+            panel_ref[pl.ds((k * count + j) * rows, rows), cols] = in_ref[j, pl.ds(k * rows, rows), cols] * undo
 
 
 def near_tile(above, table, shards):
@@ -173,7 +174,7 @@
         owners = owners_of(shards)
         whitened = []
         for at, w in chunks_of(width):
-            both = jnp.dot(joined(pieces, rows), panel_ref[:, pl.ds(at, w)], preferred_element_type=F32)
+            both = jnp.dot(joined(pieces, rows, 2 * rows), panel_ref[:, pl.ds(at, w)], preferred_element_type=F32)
             whitened += [both[:, i : i + BLK].astype(BF) for i in range(0, w, BLK)]
         for b, x in enumerate(whitened):
             product = jnp.dot(x, inverse_ref[b], preferred_element_type=F32)
@@ -238,20 +239,22 @@
     return copies(kernel, (like(rows, width, BF),) * shards, "blocks", [gradient], shards)
 
 
-def operands(in_inverse, in_carry, out_inverse, out_coupling, shards):
+def operands(in_coupling, in_inverse, in_carry, out_inverse, out_coupling, shards):
     _, rows, width = in_inverse.shape
     blocks = out_inverse.shape[1] // shards
     table = jax.ShapeDtypeStruct((blocks, BLK, BLK), BF)
 
-    def kernel(first_ref, second_ref, inverse_ref, coupling_ref, pair_ref, inv_ref, psi_ref):
+    def kernel(rows_ref, first_ref, second_ref, inverse_ref, coupling_ref, pair_ref, trio_ref, inv_ref, psi_ref):
         mine = pl.ds(lax.axis_index("y") * blocks, blocks)
-        yield first_ref.at[0], pair_ref.at[pl.ds(0, rows), :]
-        yield second_ref.at[0], pair_ref.at[pl.ds(rows, rows), :]
+        for i, ref in enumerate((rows_ref, first_ref, second_ref)):
+            yield ref.at[0], trio_ref.at[pl.ds(i * rows, rows), :]
+            if i:
+                yield ref.at[0], pair_ref.at[pl.ds((i - 1) * rows, rows), :]
         yield coupling_ref.at[0, mine], psi_ref
         yield inverse_ref.at[0, mine], inv_ref
 
-    out = (like(2 * rows, width, BF), table, table)
-    return copies(kernel, out, "operands", [in_inverse, in_carry, out_inverse, out_coupling], 4)
+    out = (like(2 * rows, width, BF), like(3 * rows, width, BF), table, table)
+    return copies(kernel, out, "operands", [in_coupling, in_inverse, in_carry, out_inverse, out_coupling], 7)
 
 
 def assemble(pieces):
@@ -302,14 +305,14 @@
     shards = lax.axis_size("y")
     slices = column_blocks(gradient, shards)
     pieces = exchange(slices)
-    pair, inv, psi = operands(after(in_inverse, slices[0]), in_carry, out_inverse, out_coupling, shards)
+    first = after(in_coupling, slices[0])
+    pair, trio, inv, psi = operands(first, in_inverse, in_carry, out_inverse, out_coupling, shards)
     grad = assemble(lax.optimization_barrier((*pieces, pair))[:shards])
     above = hop_layer(grad, -1)
-    coupling = after(in_coupling, grad)[0]
-    coupling = exchange([coupling] * shards)
+    pair, trio, own = lax.optimization_barrier((pair, trio, in_coupling[0], grad))[:3]
+    ahead, behind = hop_y(pair, 1), hop_y(trio, -1)
+    coupling = [own, hop_y(own, 2), hop_y(own, 1), behind]
     near = near_tile(above, psi, shards)
-    pair = after(pair, grad)
-    ahead, behind = hop_y(pair, 1), hop_y(pair, -1)
     reduced = reduced_tile(gather_panel(near), coupling, grad, shards)
     factors = [pair, hop_y(behind, -1), ahead, behind]
     pushed, panel = pushed_tile(gather_panel(reduced), factors, inv, psi, shards)

time: 122 us -> 121 us (level)
  starting transfers between devices: 23.9 us -> 21.9 us
    ppermute x12 -> x11, starting transfers between devices: 19.3 us -> 17.3 us  [hop_y(): return lax.ppermute(x, 'y', [(i, (i + by) % size) for i in range(size)])]
    ppermute x12 -> x11, waiting for transfers between devices: 4.56 us -> 4.91 us  [hop_y(): return lax.ppermute(x, 'y', [(i, (i + by) % size) for i in range(size)])]
  transfers between devices with their start and end apart: 14 -> 13, of which waited for: 5 -> 4; matrix products, arithmetic and copies ran while one was open for 1% -> 1% of each run, Pallas kernels for 4% -> 5%
where the time goes in v10:
time: 121 us
  blocking collectives  77.2 us (64%)
  starting transfers between devices  21.9 us (18%)
  waiting for transfers between devices  10.3 us (9%)
  Pallas kernels  9.56 us (8%)
  other arithmetic  1.42 us (1%)
    all_gather x2, blocking collectives, gather_panel(): return lax.all_gather(tile.astype(HALF), 'z', axis=0).astype(BF)  77.2 us
    ppermute x11, starting transfers between devices, hop_y(): return lax.ppermute(x, 'y', [(i, (i + by) % size) for i in range(size)])  17.3 us
    pallas_call x6, Pallas kernels, call(): pl.pallas_call(kernel, out_shape=out, in_specs=[HBM if i in far else VMEM...  5.92 us
    ppermute x2, waiting for transfers between devices, hop_layer(): lax.ppermute(x, 'layer', [(i, i + by) for i in range(size) if 0 <= i + by...  5.42 us
    ppermute x11, waiting for transfers between devices, hop_y(): return lax.ppermute(x, 'y', [(i, (i + by) % size) for i in range(size)])  4.91 us
    ppermute x2, starting transfers between devices, hop_layer(): lax.ppermute(x, 'layer', [(i, i + by) for i in range(size) if 0 <= i + by...  4.56 us
    pallas_call x3, Pallas kernels, copies(): pl.pallas_call(body, out_shape=out, in_specs=[near] * len(operands), out_...  3.64 us
  transfers between devices with their start and end apart: 13, of which 4 were waited for; matrix products, arithmetic and copies ran while one was open for 1% of the time, Pallas kernels for 5%

profile of v10, /device:TPU:2, one launch (start us, length us, event | category | flops | bytes accessed | tf_op | source)
XLA Modules:
  0.0 120.7 jit_solution(13940974496349641092)
XLA Ops:
  0.0 1.1 blocks.1
  1.1 3.3 %collective-permute-start = (bf16[80,640]{1,0:T(8,128)(2,1)S(1)}, bf16[80,640]{1,0:T(8,128)(2,1)S(1)}, u32[]{:S(2)}, u32[]{:S(2)}) collective-permute-start(bf16[80,640]{1,0:T(8,128)(2,1)S(1)} %get-tuple-element.28), channel_id=1, source_target_pairs={{0,16},{8,24},{16,0},{24,8},{1,17},{9,25},{17,1},{25,9},{2,18},{10... | collective-permute-start | bytes 307208 | tf_op jit(solution)/shard_map/ppermute | solution.py:273
  4.4 0.7 collective-permute-start.1
  5.1 2.6 %collective-permute-start.2 = (bf16[80,640]{1,0:T(8,128)(2,1)S(1)}, bf16[80,640]{1,0:T(8,128)(2,1)S(1)}, u32[]{:S(2)}, u32[]{:S(2)}) collective-permute-start(bf16[80,640]{1,0:T(8,128)(2,1)S(1)} %get-tuple-element.30), channel_id=1, source_target_pairs={{0,24},{8,0},{16,8},{24,16},{1,25},{9,1},{17,9},{25,17},{2,26},{10... | collective-permute-start | bytes 307208 | tf_op jit(solution)/shard_map/ppermute | solution.py:273
  7.7 1.7 %operands.1 = (bf16[160,2560]{1,0:T(8,128)(2,1)S(1)}, bf16[240,2560]{1,0:T(8,128)(2,1)S(1)}, bf16[5,128,128]{2,1,0:T(8,128)(2,1)S(1)}, bf16[5,128,128]{2,1,0:T(8,128)(2,1)S(1)}) custom-call(bf16[1,80,2560]{2,1,0:T(8,128)(2,1)} %refs_0_.2, bf16[1,80,2560]{2,1,0:T(8,128)(2,1)} %refs_1_.1, bf16[1,80,2560]{2,1,0:T(8,128)(2,1)} %refs_2_.1, ...), custom_call_target="tpu_custom_call" | custom-call | bytes 4751360 | tf_op jit(solution)/shard_map/operands/pallas_call | solution.py:217
  9.4 0.9 collective-permute-done.1.refs_2_
  10.3 2.5 %collective-permute-start.3 = (bf16[320,640]{1,0:T(8,128)(2,1)S(1)}, bf16[320,640]{1,0:T(8,128)(2,1)S(1)}, u32[]{:S(2)}, u32[]{:S(2)}) collective-permute-start(bf16[320,640]{1,0:T(8,128)(2,1)S(1)} %assemble.1.grad_ref), channel_id=1, source_target_pairs={{32,0},{64,32},{96,64},{128,96},{160,128},{192,160},{224,192},{33,... | collective-permute-start | bytes 1228808 | tf_op jit(solution)/shard_map/ppermute | solution.py:38
  12.8 1.2 %collective-permute-start.4 = (bf16[80,2560]{1,0:T(8,128)(2,1)S(1)}, bf16[80,2560]{1,0:T(8,128)(2,1)S(1)}, u32[]{:S(2)}, u32[]{:S(2)}) collective-permute-start(bf16[80,2560]{1,0:T(8,128)(2,1)S(1)} %bitcast.5), channel_id=1, source_target_pairs={{0,16},{8,24},{16,0},{24,8},{1,17},{9,25},{17,1},{25,9},{2,18},{10... | collective-permute-start | bytes 1228808 | tf_op jit(solution)/shard_map/ppermute | solution.py:273
  14.0 2.4 %collective-permute-start.5 = (bf16[80,2560]{1,0:T(8,128)(2,1)S(1)}, bf16[80,2560]{1,0:T(8,128)(2,1)S(1)}, u32[]{:S(2)}, u32[]{:S(2)}) collective-permute-start(bf16[80,2560]{1,0:T(8,128)(2,1)S(1)} %bitcast.6), channel_id=1, source_target_pairs={{0,8},{8,16},{16,24},{24,0},{1,9},{9,17},{17,25},{25,1},{2,10},{10... | collective-permute-start | bytes 1228808 | tf_op jit(solution)/shard_map/ppermute | solution.py:273
  16.5 0.8 collective-permute-start.6
  17.3 1.2 %collective-permute-start.8 = (bf16[160,2560]{1,0:T(8,128)(2,1)S(1)}, bf16[160,2560]{1,0:T(8,128)(2,1)S(1)}, u32[]{:S(2)}, u32[]{:S(2)}) collective-permute-start(bf16[160,2560]{1,0:T(8,128)(2,1)S(1)} %get-tuple-element.42.refs_0_), channel_id=1, source_target_pairs={{0,8},{8,16},{16,24},{24,0},{1,9},{9,17},{17,25},{25,1},{2,10},{10... | collective-permute-start | bytes 2457608 | tf_op jit(solution)/shard_map/ppermute | solution.py:273
  19.0 40.7 %all-gather.4 = f16[2624,640]{1,0:T(8,128)(2,1)S(1)} all-gather(f16[328,640]{1,0:T(8,128)(2,1)S(1)} %convert_element_type.12), channel_id=2, replica_groups=mesh['layer'=8,'y'=4,'z'=8] {'z'}, dimensions={0}, use_global_device_ids=true | all-gather | bytes 3778560 | tf_op jit(solution)/shard_map/all_gather | solution.py:301
  60.3 1.6 %reduced.1 = bf16[328,640]{1,0:T(8,128)(2,1)S(1)} custom-call(bf16[8,328,640]{2,1,0:T(8,128)(2,1)S(1)} %bitcast.3, bf16[320,640]{1,0:T(8,128)(2,1)S(1)} %assemble.1.grad_ref, bf16[80,2560]{1,0:T(8,128)(2,1)S(1)} %bitcast.7, bf16[80,2560]{1,0:T(8,128)(2,1)S(1)} %collective-permute-done.4.refs_1_, bf16[80,2560]{1,0:T(8,128)(2,1)S(1)} %collective-permute-done.5.refs_2_, ...), custom_call_target="tpu_custom_call" | custom-call | flops 1048576000 | bytes 6645760 | tf_op jit(solution)/shard_map/reduced/pallas_call | solution.py:20
  62.0 1.7 %collective-permute-start.7 = (bf16[240,2560]{1,0:T(8,128)(2,1)S(1)}, bf16[240,2560]{1,0:T(8,128)(2,1)S(1)}, u32[]{:S(2)}, u32[]{:S(2)}) collective-permute-start(bf16[240,2560]{1,0:T(8,128)(2,1)S(1)} %collective-permute-done.6.refs_3_), channel_id=1, source_target_pairs={{0,24},{8,0},{16,8},{24,16},{1,25},{9,1},{17,9},{25,17},{2,26},{10... | collective-permute-start | bytes 3686408 | tf_op jit(solution)/shard_map/ppermute | solution.py:273
  63.8 36.5 %all-gather.5 = f16[2624,640]{1,0:T(8,128)(2,1)S(1)} all-gather(f16[328,640]{1,0:T(8,128)(2,1)S(1)} %convert_element_type.14), channel_id=3, replica_groups=mesh['layer'=8,'y'=4,'z'=8] {'z'}, dimensions={0}, use_global_device_ids=true | all-gather | bytes 3778560 | tf_op jit(solution)/shard_map/all_gather | solution.py:301
  100.9 2.0 %pushed.1 = (bf16[320,640]{1,0:T(8,128)(2,1)S(1)}, bf16[2560,640]{1,0:T(8,128)(2,1)S(1)}) custom-call(bf16[8,328,640]{2,1,0:T(8,128)(2,1)S(1)} %bitcast.4, bf16[5,128,128]{2,1,0:T(8,128)(2,1)S(1)} %get-tuple-element.41.inverse_ref, bf16[5,128,128]{2,1,0:T(8,128)(2,1)S(1)} %get-tuple-element.37.table_ref.coupling_ref, ...), custom_call_target="tpu_custom_call" | custom-call | flops 1048576000 | bytes 11468800 | tf_op jit(solution)/shard_map/pushed/pallas_call | solution.py:20
  103.0 2.1 %collective-permute-start.9 = (bf16[320,640]{1,0:T(8,128)(2,1)S(1)}, bf16[320,640]{1,0:T(8,128)(2,1)S(1)}, u32[]{:S(2)}, u32[]{:S(2)}) collective-permute-start(bf16[320,640]{1,0:T(8,128)(2,1)S(1)} %get-tuple-element.44), channel_id=1, source_target_pairs={{0,32},{32,64},{64,96},{96,128},{128,160},{160,192},{192,224},{1,3... | collective-permute-start | bytes 1228808 | tf_op jit(solution)/shard_map/ppermute | solution.py:38
  105.1 1.7 %local.1.local_ref = f32[320,640]{1,0:T(8,128)S(1)} custom-call(bf16[2560,640]{1,0:T(8,128)(2,1)S(1)} %get-tuple-element.43.panel_ref, bf16[5,128,128]{2,1,0:T(8,128)(2,1)S(1)} %get-tuple-element.41.inverse_ref, bf16[160,2560]{1,0:T(8,128)(2,1)S(1)} %get-tuple-element.42.refs_0_, bf16[240,2560]{1,0:T(8,128)(2,1)S(1)} %collective-permute-done.7.refs_1_, ...), custom_call_target="tpu_custom_call" | custom-call | flops 1048576000 | bytes 8355840 | tf_op jit(solution)/shard_map/local/pallas_call | solution.py:20
  106.9 5.4 %collective-permute-done.9.pushed_ref = bf16[320,640]{1,0:T(8,128)(2,1)S(1)} collective-permute-done((bf16[320,640]{1,0:T(8,128)(2,1)S(1)}, bf16[320,640]{1,0:T(8,128)(2,1)S(1)}, u32[]{:S(2)}, u32[]{:S(2)}) %collective-permute-start.9) | collective-permute-done | bytes 409632 | tf_op jit(solution)/shard_map/ppermute | solution.py:38
  112.5 1.1 collective-permute-start.11
  113.6 2.2 %collective-permute-start.12 = (bf16[80,640]{1,0:T(8,128)(2,1)S(1)}, bf16[80,640]{1,0:T(8,128)(2,1)S(1)}, u32[]{:S(2)}, u32[]{:S(2)}) collective-permute-start(bf16[80,640]{1,0:T(8,128)(2,1)S(1)} %get-tuple-element.48), channel_id=1, source_target_pairs={{0,24},{8,0},{16,8},{24,16},{1,25},{9,1},{17,9},{25,17},{2,26},{10... | collective-permute-start | bytes 307208 | tf_op jit(solution)/shard_map/ppermute | solution.py:273
  115.8 3.2 %collective-permute-done.10.refs_1_ = bf16[80,640]{1,0:T(8,128)(2,1)S(1)} collective-permute-done((bf16[80,640]{1,0:T(8,128)(2,1)S(1)}, bf16[80,640]{1,0:T(8,128)(2,1)S(1)}, u32[]{:S(2)}, u32[]{:S(2)}) %collective-permute-start.10) | collective-permute-done | bytes 102432 | tf_op jit(solution)/shard_map/ppermute | solution.py:273
  119.0 0.8 collective-permute-done.11.refs_2_
  119.8 0.8 join.1
  (19 shorter events, 2.1 us)
Async XLA Ops:
  0.0 12.8 %copy-start = (bf16[1,80,2560]{2,1,0:T(8,128)(2,1)S(1)}, bf16[1,80,2560]{2,1,0:T(8,128)(2,1)}, u32[]{:S(2)}) copy-start(bf16[1,80,2560]{2,1,0:T(8,128)(2,1)} %refs_0_.2) | copy-start | bytes 1228804
  1.1 8.3 %collective-permute-start = (bf16[80,640]{1,0:T(8,128)(2,1)S(1)}, bf16[80,640]{1,0:T(8,128)(2,1)S(1)}, u32[]{:S(2)}, u32[]{:S(2)}) collective-permute-start(bf16[80,640]{1,0:T(8,128)(2,1)S(1)} %get-tuple-element.28), channel_id=1, source_target_pairs={{0,16},{8,24},{16,0},{24,8},{1,17},{9,25},{17,1},{25,9},{2,18},{10... | collective-permute-start | bytes 307208 | tf_op jit(solution)/shard_map/ppermute | solution.py:273
  4.4 5.9 %collective-permute-start.1 = (bf16[80,640]{1,0:T(8,128)(2,1)S(1)}, bf16[80,640]{1,0:T(8,128)(2,1)S(1)}, u32[]{:S(2)}, u32[]{:S(2)}) collective-permute-start(bf16[80,640]{1,0:T(8,128)(2,1)S(1)} %get-tuple-element.29), channel_id=1, source_target_pairs={{0,8},{8,16},{16,24},{24,0},{1,9},{9,17},{17,25},{25,1},{2,10},{10... | collective-permute-start | bytes 307208 | tf_op jit(solution)/shard_map/ppermute | solution.py:273
  5.1 5.2 %collective-permute-start.2 = (bf16[80,640]{1,0:T(8,128)(2,1)S(1)}, bf16[80,640]{1,0:T(8,128)(2,1)S(1)}, u32[]{:S(2)}, u32[]{:S(2)}) collective-permute-start(bf16[80,640]{1,0:T(8,128)(2,1)S(1)} %get-tuple-element.30), channel_id=1, source_target_pairs={{0,24},{8,0},{16,8},{24,16},{1,25},{9,1},{17,9},{25,17},{2,26},{10... | collective-permute-start | bytes 307208 | tf_op jit(solution)/shard_map/ppermute | solution.py:273
  10.3 8.1 %collective-permute-start.3 = (bf16[320,640]{1,0:T(8,128)(2,1)S(1)}, bf16[320,640]{1,0:T(8,128)(2,1)S(1)}, u32[]{:S(2)}, u32[]{:S(2)}) collective-permute-start(bf16[320,640]{1,0:T(8,128)(2,1)S(1)} %assemble.1.grad_ref), channel_id=1, source_target_pairs={{32,0},{64,32},{96,64},{128,96},{160,128},{192,160},{224,192},{33,... | collective-permute-start | bytes 1228808 | tf_op jit(solution)/shard_map/ppermute | solution.py:38
  12.8 47.5 %collective-permute-start.4 = (bf16[80,2560]{1,0:T(8,128)(2,1)S(1)}, bf16[80,2560]{1,0:T(8,128)(2,1)S(1)}, u32[]{:S(2)}, u32[]{:S(2)}) collective-permute-start(bf16[80,2560]{1,0:T(8,128)(2,1)S(1)} %bitcast.5), channel_id=1, source_target_pairs={{0,16},{8,24},{16,0},{24,8},{1,17},{9,25},{17,1},{25,9},{2,18},{10... | collective-permute-start | bytes 1228808 | tf_op jit(solution)/shard_map/ppermute | solution.py:273
  14.0 46.3 %collective-permute-start.5 = (bf16[80,2560]{1,0:T(8,128)(2,1)S(1)}, bf16[80,2560]{1,0:T(8,128)(2,1)S(1)}, u32[]{:S(2)}, u32[]{:S(2)}) collective-permute-start(bf16[80,2560]{1,0:T(8,128)(2,1)S(1)} %bitcast.6), channel_id=1, source_target_pairs={{0,8},{8,16},{16,24},{24,0},{1,9},{9,17},{17,25},{25,1},{2,10},{10... | collective-permute-start | bytes 1228808 | tf_op jit(solution)/shard_map/ppermute | solution.py:273
  16.5 43.9 %collective-permute-start.6 = (bf16[240,2560]{1,0:T(8,128)(2,1)S(1)}, bf16[240,2560]{1,0:T(8,128)(2,1)S(1)}, u32[]{:S(2)}, u32[]{:S(2)}) collective-permute-start(bf16[240,2560]{1,0:T(8,128)(2,1)S(1)} %get-tuple-element.40), channel_id=1, source_target_pairs={{0,24},{8,0},{16,8},{24,16},{1,25},{9,1},{17,9},{25,17},{2,26},{10... | collective-permute-start | bytes 3686408 | tf_op jit(solution)/shard_map/ppermute | solution.py:273
  17.3 83.7 %collective-permute-start.8 = (bf16[160,2560]{1,0:T(8,128)(2,1)S(1)}, bf16[160,2560]{1,0:T(8,128)(2,1)S(1)}, u32[]{:S(2)}, u32[]{:S(2)}) collective-permute-start(bf16[160,2560]{1,0:T(8,128)(2,1)S(1)} %get-tuple-element.42.refs_0_), channel_id=1, source_target_pairs={{0,8},{8,16},{16,24},{24,0},{1,9},{9,17},{17,25},{25,1},{2,10},{10... | collective-permute-start | bytes 2457608 | tf_op jit(solution)/shard_map/ppermute | solution.py:273
  62.0 38.9 %collective-permute-start.7 = (bf16[240,2560]{1,0:T(8,128)(2,1)S(1)}, bf16[240,2560]{1,0:T(8,128)(2,1)S(1)}, u32[]{:S(2)}, u32[]{:S(2)}) collective-permute-start(bf16[240,2560]{1,0:T(8,128)(2,1)S(1)} %collective-permute-done.6.refs_3_), channel_id=1, source_target_pairs={{0,24},{8,0},{16,8},{24,16},{1,25},{9,1},{17,9},{25,17},{2,26},{10... | collective-permute-start | bytes 3686408 | tf_op jit(solution)/shard_map/ppermute | solution.py:273
  103.0 9.3 %collective-permute-start.9 = (bf16[320,640]{1,0:T(8,128)(2,1)S(1)}, bf16[320,640]{1,0:T(8,128)(2,1)S(1)}, u32[]{:S(2)}, u32[]{:S(2)}) collective-permute-start(bf16[320,640]{1,0:T(8,128)(2,1)S(1)} %get-tuple-element.44), channel_id=1, source_target_pairs={{0,32},{32,64},{64,96},{96,128},{128,160},{160,192},{192,224},{1,3... | collective-permute-start | bytes 1228808 | tf_op jit(solution)/shard_map/ppermute | solution.py:38
  112.4 6.6 %collective-permute-start.10 = (bf16[80,640]{1,0:T(8,128)(2,1)S(1)}, bf16[80,640]{1,0:T(8,128)(2,1)S(1)}, u32[]{:S(2)}, u32[]{:S(2)}) collective-permute-start(bf16[80,640]{1,0:T(8,128)(2,1)S(1)} %get-tuple-element.46), channel_id=1, source_target_pairs={{0,16},{8,24},{16,0},{24,8},{1,17},{9,25},{17,1},{25,9},{2,18},{10... | collective-permute-start | bytes 307208 | tf_op jit(solution)/shard_map/ppermute | solution.py:273
  112.5 7.3 %collective-permute-start.11 = (bf16[80,640]{1,0:T(8,128)(2,1)S(1)}, bf16[80,640]{1,0:T(8,128)(2,1)S(1)}, u32[]{:S(2)}, u32[]{:S(2)}) collective-permute-start(bf16[80,640]{1,0:T(8,128)(2,1)S(1)} %get-tuple-element.47), channel_id=1, source_target_pairs={{0,8},{8,16},{16,24},{24,0},{1,9},{9,17},{17,25},{25,1},{2,10},{10... | collective-permute-start | bytes 307208 | tf_op jit(solution)/shard_map/ppermute | solution.py:273
  113.6 6.2 %collective-permute-start.12 = (bf16[80,640]{1,0:T(8,128)(2,1)S(1)}, bf16[80,640]{1,0:T(8,128)(2,1)S(1)}, u32[]{:S(2)}, u32[]{:S(2)}) collective-permute-start(bf16[80,640]{1,0:T(8,128)(2,1)S(1)} %get-tuple-element.48), channel_id=1, source_target_pairs={{0,24},{8,0},{16,8},{24,16},{1,25},{9,1},{17,9},{25,17},{2,26},{10... | collective-permute-start | bytes 307208 | tf_op jit(solution)/shard_map/ppermute | solution.py:273

commit v11 on v10

--- a/solution.py
+++ b/solution.py
@@ -94,35 +94,42 @@
             panel_ref[pl.ds((k * count + j) * rows, rows), cols] = in_ref[j, pl.ds(k * rows, rows), cols] * undo
 
 
-def near_tile(above, table, shards):
-    tile, width = above.shape
-    blocks = width // BLK
-
-    def kernel(above_ref, table_ref, out_ref):
-        for b in range(blocks):
-            block = table_ref[b]
-            near = lax.dot_general(
-                above_ref[:, pl.ds(b * BLK, BLK)], block, (((1,), (1,)), ((), ())), preferred_element_type=F32
-            )
-            store_scaled(out_ref, blocks_of(near.astype(BF).astype(F32), shards), list(range(shards)), b * BLK)
-
-    return call(kernel, like(tile + CODE, width, BF), "near", [above, table], flops=2 * tile * width * BLK)
-
-
-def reduced_tile(panel, factor, grad, shards):
-    tile, width = grad.shape
+def near_tile(halves, table, shards):
+    part, width = halves[0].shape
+    tile = part * len(halves)
+    rows = tile // shards
+
+    def kernel(*refs):
+        above_refs, (table_ref, out_ref) = refs[: len(halves)], refs[len(halves) :]
+        owners = owners_of(shards)
+        for b in range(width // BLK):
+            parts = []
+            for ref in above_refs:
+                near = lax.dot_general(
+                    ref[:, pl.ds(b * BLK, BLK)], table_ref[b], (((1,), (1,)), ((), ())), preferred_element_type=F32
+                )
+                parts += blocks_of(near.astype(BF).astype(F32), part // rows)
+            store_scaled(out_ref, parts, owners, b * BLK)
+
+    return call(kernel, like(tile + CODE, width, BF), "near", [*halves, table], flops=2 * tile * width * BLK)
+
+
+def reduced_tile(panel, factor, halves, shards):
+    part, width = halves[0].shape
+    tile = part * len(halves)
     depth, rows = factor[0].shape[1], tile // shards
 
-    def kernel(panel_in, grad_ref, *refs):
-        pieces, (out_ref, panel_ref) = refs[:shards], refs[shards:]
+    def kernel(panel_in, *refs):
+        pieces, grad_refs, (out_ref, panel_ref) = refs[:shards], refs[shards:-2], refs[-2:]
         owners = owners_of(shards)
         for at, w in chunks_of(width):
             cols = pl.ds(at, w)
             load_scaled(panel_in, panel_ref, at, w, shards, rows)
             coupled = jnp.dot(joined(pieces, rows), panel_ref[:, cols], preferred_element_type=F32)
+            grads = [ref[pl.ds(at_row, rows), cols] for ref in grad_refs for at_row in range(0, part, rows)]
             parts = [
-                (grad_ref[rows_of(owner, rows), cols].astype(F32) - part).astype(BF).astype(F32)
-                for owner, part in zip(owners, blocks_of(coupled, shards), strict=True)
+                (grad.astype(F32) - block).astype(BF).astype(F32)
+                for grad, block in zip(grads, blocks_of(coupled, shards), strict=True)
             ]
             store_scaled(out_ref, parts, owners, at)
 
@@ -130,19 +137,30 @@
         kernel,
         like(tile + CODE, width, BF),
         "reduced",
-        [panel, grad, *factor],
+        [panel, *factor, *halves],
         [pltpu.VMEM((depth, width), BF)],
         flops=2 * tile * depth * width,
     )
 
 
+def halves_out(shards):
+    order = distances(shards)
+    order = order[1:] + order[:1]
+    return order[: shards // 2], order[shards // 2 :]
+
+
+def places_out(shards):
+    halves = halves_out(shards)
+    where = {k: (half, place) for half, ks in enumerate(halves) for place, k in enumerate(ks)}
+    return [where[(shards - k) % shards] for k in distances(shards)]
+
+
 def pushed_tile(panel, factor, inverse, coupling, shards):
     rows, depth = factor[0].shape[0] // 2, factor[0].shape[1]
     tile, width = shards * rows, panel.shape[2]
 
     def kernel(panel_in, inverse_ref, coupling_ref, *refs):
-        pieces, (pushed_ref, panel_ref) = refs[:shards], refs[shards:]
-        owners = owners_of(shards)
+        pieces, (*pushed_refs, panel_ref) = refs[:shards], refs[shards:]
         carried = []
         for at, w in chunks_of(width):
             load_scaled(panel_in, panel_ref, at, w, shards, rows)
@@ -153,12 +171,12 @@
         ]
         for b, x in enumerate(middle):
             pushed = jnp.dot(x, coupling_ref[b], preferred_element_type=F32).astype(BF)
-            for owner, part in zip(owners, blocks_of(pushed, shards), strict=True):
-                pushed_ref[rows_of(owner, rows), pl.ds(b * BLK, BLK)] = part
+            for (half, place), part in zip(places_out(shards), blocks_of(pushed, shards), strict=True):
+                pushed_refs[half][pl.ds(place * rows, rows), pl.ds(b * BLK, BLK)] = part
 
     return call(
         kernel,
-        (like(tile, width, BF), like(depth, width, BF)),
+        (*[like(tile // 2, width, BF)] * 2, like(depth, width, BF)),
         "pushed",
         [panel, inverse, coupling, *factor],
         flops=2 * tile * depth * width,
@@ -170,36 +188,34 @@
     tile, width = shards * rows, panel.shape[1]
 
     def kernel(panel_ref, inverse_ref, *refs):
-        pieces, (local_ref,) = refs[:shards], refs[shards:]
-        owners = owners_of(shards)
+        pieces, local_refs = refs[:shards], refs[shards:]
         whitened = []
         for at, w in chunks_of(width):
             both = jnp.dot(joined(pieces, rows, 2 * rows), panel_ref[:, pl.ds(at, w)], preferred_element_type=F32)
             whitened += [both[:, i : i + BLK].astype(BF) for i in range(0, w, BLK)]
         for b, x in enumerate(whitened):
             product = jnp.dot(x, inverse_ref[b], preferred_element_type=F32)
-            for owner, part in zip(owners, blocks_of(product, shards), strict=True):
-                local_ref[rows_of(owner, rows), pl.ds(b * BLK, BLK)] = part
+            for (half, place), part in zip(places_out(shards), blocks_of(product, shards), strict=True):
+                local_refs[half][pl.ds(place * rows, rows), pl.ds(b * BLK, BLK)] = part
 
     return call(
         kernel,
-        like(tile, width, F32),
+        (like(tile // 2, width, F32),) * 2,
         "local",
         [panel, inverse, *factor],
         flops=2 * tile * depth * width,
     )
 
 
-def update_pieces(local_term, pushed, shards):
-    rows, width = pushed.shape[0] // shards, pushed.shape[1]
+def update_pieces(local_term, pushed, count, name):
+    rows, width = pushed.shape[0] // count, pushed.shape[1]
 
     def kernel(local_ref, pushed_ref, *out_refs):
-        y = lax.axis_index("y")
-        for k, out_ref in zip(distances(shards), out_refs, strict=True):
-            here = rows_of(lax.rem(y + k, shards), rows)
+        for i, out_ref in enumerate(out_refs):
+            here = pl.ds(i * rows, rows)
             out_ref[...] = (local_ref[here, :] - pushed_ref[here, :].astype(F32)).astype(BF)
 
-    return call(kernel, tuple(like(rows, width, BF) for _ in range(shards)), "update", [local_term, pushed])
+    return call(kernel, tuple(like(rows, width, BF) for _ in range(count)), name, [local_term, pushed])
 
 
 def copies(kernel, out, name, operands, count, near=HBM, far=VMEM):
@@ -257,15 +273,15 @@
     return copies(kernel, out, "operands", [in_coupling, in_inverse, in_carry, out_inverse, out_coupling], 7)
 
 
-def assemble(pieces):
+def stacked(pieces, name):
     rows, width = pieces[0].shape
-    shards = len(pieces)
+    count = len(pieces)
 
     def kernel(*refs):
-        for k, owner in enumerate(owners_of(shards)):
-            refs[shards][rows_of(owner, rows), :] = refs[k][...]
-
-    return call(kernel, like(shards * rows, width, BF), "assemble", pieces)
+        for i in range(count):
+            refs[count][pl.ds(i * rows, rows), :] = refs[i][...]
+
+    return call(kernel, like(count * rows, width, BF), name, pieces)
 
 
 def hop_y(x, by):
@@ -307,17 +323,23 @@
     pieces = exchange(slices)
     first = after(in_coupling, slices[0])
     pair, trio, inv, psi = operands(first, in_inverse, in_carry, out_inverse, out_coupling, shards)
-    grad = assemble(lax.optimization_barrier((*pieces, pair))[:shards])
-    above = hop_layer(grad, -1)
-    pair, trio, own = lax.optimization_barrier((pair, trio, in_coupling[0], grad))[:3]
+    half = shards // 2
+    grads = [stacked(lax.optimization_barrier((*pieces[:half], pair))[:half], "early"), stacked(pieces[half:], "late")]
+    above = [hop_layer(grad, -1) for grad in grads]
+    pair, trio, own = lax.optimization_barrier((pair, trio, in_coupling[0], *grads))[:3]
     ahead, behind = hop_y(pair, 1), hop_y(trio, -1)
     coupling = [own, hop_y(own, 2), hop_y(own, 1), behind]
     near = near_tile(above, psi, shards)
-    reduced = reduced_tile(gather_panel(near), coupling, grad, shards)
+    reduced = reduced_tile(gather_panel(near), coupling, grads, shards)
     factors = [pair, hop_y(behind, -1), ahead, behind]
-    pushed, panel = pushed_tile(gather_panel(reduced), factors, inv, psi, shards)
-    local_term = local_tile(panel, factors, inv, shards)
-    return join_columns(exchange(update_pieces(local_term, hop_layer(pushed, 1), shards)))
+    *pushed, panel = pushed_tile(gather_panel(reduced), factors, inv, psi, shards)
+    pushed = [hop_layer(x, 1) for x in pushed]
+    local_terms = local_tile(panel, factors, inv, shards)
+    came = {}
+    for ks, mine, below, name in zip(halves_out(shards), local_terms, pushed, ("update_a", "update_b"), strict=True):
+        for k, piece in zip(ks, update_pieces(mine, below, len(ks), name), strict=True):
+            came[k] = hop_y(piece, k) if k else piece
+    return join_columns([came[k] for k in distances(shards)])
 
 
 def solution(mesh):

time: 121 us -> 122 us (level)
  starting transfers between devices: 21.9 us -> 28.3 us
  waiting for transfers between devices: 10.3 us -> 5.25 us
  blocking collectives: 77.2 us -> 75.8 us
    ppermute x2 -> x4, starting transfers between devices: 4.56 us -> 10.1 us  [hop_layer(): lax.ppermute(x, 'layer', [(i, i + by) for i in range(size) if 0 <= i + by...]
    ppermute x2 -> x4, waiting for transfers between devices: 5.42 us -> 0.39 us  [hop_layer(): lax.ppermute(x, 'layer', [(i, i + by) for i in range(size) if 0 <= i + by...]
    all_gather x2, blocking collectives: 77.2 us -> 75.8 us  [gather_panel(): return lax.all_gather(tile.astype(HALF), 'z', axis=0).astype(BF)]
    pallas_call x6 -> x8, Pallas kernels: 5.92 us -> 5.95 us  [call(): pl.pallas_call(kernel, out_shape=out, in_specs=[HBM if i in far else VMEM...]
  transfers between devices with their start and end apart: 13 -> 15, of which waited for: 4 -> 3; matrix products, arithmetic and copies ran while one was open for 1% -> 1% of each run, Pallas kernels for 5% -> 5%
where the time goes in v11:
time: 122 us; the launch traced here: 121 us
  blocking collectives  75.8 us (62%)
  starting transfers between devices  28.3 us (23%)
  Pallas kernels  9.59 us (8%)
  waiting for transfers between devices  5.25 us (4%)
  other arithmetic  1.38 us (1%)
    all_gather x2, blocking collectives, gather_panel(): return lax.all_gather(tile.astype(HALF), 'z', axis=0).astype(BF)  75.8 us
    ppermute x11, starting transfers between devices, hop_y(): return lax.ppermute(x, 'y', [(i, (i + by) % size) for i in range(size)])  18.2 us
    ppermute x4, starting transfers between devices, hop_layer(): lax.ppermute(x, 'layer', [(i, i + by) for i in range(size) if 0 <= i + by...  10.1 us
    pallas_call x8, Pallas kernels, call(): pl.pallas_call(kernel, out_shape=out, in_specs=[HBM if i in far else VMEM...  5.95 us
    ppermute x11, waiting for transfers between devices, hop_y(): return lax.ppermute(x, 'y', [(i, (i + by) % size) for i in range(size)])  4.85 us
    pallas_call x3, Pallas kernels, copies(): pl.pallas_call(body, out_shape=out, in_specs=[near] * len(operands), out_...  3.64 us
  transfers between devices with their start and end apart: 15, of which 3 were waited for; matrix products, arithmetic and copies ran while one was open for 1% of the time, Pallas kernels for 5%

profile of v11, /device:TPU:2, one launch (start us, length us, event | category | flops | bytes accessed | tf_op | source)
XLA Modules:
  0.0 120.7 jit_solution(9679357304579617135)
XLA Ops:
  0.0 1.1 blocks.1
  1.1 3.3 %collective-permute-start = (bf16[80,640]{1,0:T(8,128)(2,1)S(1)}, bf16[80,640]{1,0:T(8,128)(2,1)S(1)}, u32[]{:S(2)}, u32[]{:S(2)}) collective-permute-start(bf16[80,640]{1,0:T(8,128)(2,1)S(1)} %get-tuple-element.29), channel_id=1, source_target_pairs={{0,16},{8,24},{16,0},{24,8},{1,17},{9,25},{17,1},{25,9},{2,18},{10... | collective-permute-start | bytes 307208 | tf_op jit(solution)/shard_map/ppermute | solution.py:289
  4.4 0.7 collective-permute-start.2
  5.1 2.6 %collective-permute-start.3 = (bf16[80,640]{1,0:T(8,128)(2,1)S(1)}, bf16[80,640]{1,0:T(8,128)(2,1)S(1)}, u32[]{:S(2)}, u32[]{:S(2)}) collective-permute-start(bf16[80,640]{1,0:T(8,128)(2,1)S(1)} %get-tuple-element.35), channel_id=1, source_target_pairs={{0,24},{8,0},{16,8},{24,16},{1,25},{9,1},{17,9},{25,17},{2,26},{10... | collective-permute-start | bytes 307208 | tf_op jit(solution)/shard_map/ppermute | solution.py:289
  7.7 1.7 %operands.1 = (bf16[160,2560]{1,0:T(8,128)(2,1)S(1)}, bf16[240,2560]{1,0:T(8,128)(2,1)S(1)}, bf16[5,128,128]{2,1,0:T(8,128)(2,1)S(1)}, bf16[5,128,128]{2,1,0:T(8,128)(2,1)S(1)}) custom-call(bf16[1,80,2560]{2,1,0:T(8,128)(2,1)} %refs_0_.2, bf16[1,80,2560]{2,1,0:T(8,128)(2,1)} %refs_1_.1, bf16[1,80,2560]{2,1,0:T(8,128)(2,1)} %refs_2_.1, ...), custom_call_target="tpu_custom_call" | custom-call | bytes 4751360 | tf_op jit(solution)/shard_map/operands/pallas_call | solution.py:233
  9.4 1.9 %collective-permute-start.1 = (bf16[160,640]{1,0:T(8,128)(2,1)S(1)}, bf16[160,640]{1,0:T(8,128)(2,1)S(1)}, u32[]{:S(2)}, u32[]{:S(2)}) collective-permute-start(bf16[160,640]{1,0:T(8,128)(2,1)S(1)} %early.1.refs_4_), channel_id=1, source_target_pairs={{32,0},{64,32},{96,64},{128,96},{160,128},{192,160},{224,192},{33,... | collective-permute-start | bytes 614408 | tf_op jit(solution)/shard_map/ppermute | solution.py:38
  11.4 2.5 %collective-permute-start.4 = (bf16[160,640]{1,0:T(8,128)(2,1)S(1)}, bf16[160,640]{1,0:T(8,128)(2,1)S(1)}, u32[]{:S(2)}, u32[]{:S(2)}) collective-permute-start(bf16[160,640]{1,0:T(8,128)(2,1)S(1)} %late.1.refs_5_), channel_id=1, source_target_pairs={{32,0},{64,32},{96,64},{128,96},{160,128},{192,160},{224,192},{33,... | collective-permute-start | bytes 614408 | tf_op jit(solution)/shard_map/ppermute | solution.py:38
  14.0 2.4 %collective-permute-start.5 = (bf16[80,2560]{1,0:T(8,128)(2,1)S(1)}, bf16[80,2560]{1,0:T(8,128)(2,1)S(1)}, u32[]{:S(2)}, u32[]{:S(2)}) collective-permute-start(bf16[80,2560]{1,0:T(8,128)(2,1)S(1)} %bitcast.5), channel_id=1, source_target_pairs={{0,16},{8,24},{16,0},{24,8},{1,17},{9,25},{17,1},{25,9},{2,18},{10... | collective-permute-start | bytes 1228808 | tf_op jit(solution)/shard_map/ppermute | solution.py:289
  16.7 2.9 %collective-permute-start.7 = (bf16[240,2560]{1,0:T(8,128)(2,1)S(1)}, bf16[240,2560]{1,0:T(8,128)(2,1)S(1)}, u32[]{:S(2)}, u32[]{:S(2)}) collective-permute-start(bf16[240,2560]{1,0:T(8,128)(2,1)S(1)} %get-tuple-element.39), channel_id=1, source_target_pairs={{0,24},{8,0},{16,8},{24,16},{1,25},{9,1},{17,9},{25,17},{2,26},{10... | collective-permute-start | bytes 3686408 | tf_op jit(solution)/shard_map/ppermute | solution.py:289
  20.1 40.3 %all-gather.4 = f16[2624,640]{1,0:T(8,128)(2,1)S(1)} all-gather(f16[328,640]{1,0:T(8,128)(2,1)S(1)} %convert_element_type.12), channel_id=2, replica_groups=mesh['layer'=8,'y'=4,'z'=8] {'z'}, dimensions={0}, use_global_device_ids=true | all-gather | bytes 3778560 | tf_op jit(solution)/shard_map/all_gather | solution.py:317
  60.4 0.6 convert_element_type.16
  61.0 1.6 %reduced.1 = bf16[328,640]{1,0:T(8,128)(2,1)S(1)} custom-call(bf16[8,328,640]{2,1,0:T(8,128)(2,1)S(1)} %bitcast.3, bf16[80,2560]{1,0:T(8,128)(2,1)S(1)} %bitcast.7, bf16[80,2560]{1,0:T(8,128)(2,1)S(1)} %collective-permute-done.5.refs_1_, bf16[80,2560]{1,0:T(8,128)(2,1)S(1)} %collective-permute-done.6.refs_2_, ...), custom_call_target="tpu_custom_call" | custom-call | flops 1048576000 | bytes 6645760 | tf_op jit(solution)/shard_map/reduced/pallas_call | solution.py:20
  62.7 3.0 %collective-permute-start.8 = (bf16[240,2560]{1,0:T(8,128)(2,1)S(1)}, bf16[240,2560]{1,0:T(8,128)(2,1)S(1)}, u32[]{:S(2)}, u32[]{:S(2)}) collective-permute-start(bf16[240,2560]{1,0:T(8,128)(2,1)S(1)} %collective-permute-done.7.refs_3_), channel_id=1, source_target_pairs={{0,24},{8,0},{16,8},{24,16},{1,25},{9,1},{17,9},{25,17},{2,26},{10... | collective-permute-start | bytes 3686408 | tf_op jit(solution)/shard_map/ppermute | solution.py:289
  65.7 35.5 %all-gather.5 = f16[2624,640]{1,0:T(8,128)(2,1)S(1)} all-gather(f16[328,640]{1,0:T(8,128)(2,1)S(1)} %convert_element_type.14), channel_id=3, replica_groups=mesh['layer'=8,'y'=4,'z'=8] {'z'}, dimensions={0}, use_global_device_ids=true | all-gather | bytes 3778560 | tf_op jit(solution)/shard_map/all_gather | solution.py:317
  101.2 0.6 convert_element_type.17
  101.9 2.0 %pushed.1 = (bf16[160,640]{1,0:T(8,128)(2,1)S(1)}, bf16[160,640]{1,0:T(8,128)(2,1)S(1)}, bf16[2560,640]{1,0:T(8,128)(2,1)S(1)}) custom-call(bf16[8,328,640]{2,1,0:T(8,128)(2,1)S(1)} %bitcast.4, bf16[5,128,128]{2,1,0:T(8,128)(2,1)S(1)} %get-tuple-element.40.inverse_ref, bf16[5,128,128]{2,1,0:T(8,128)(2,1)S(1)} %get-tuple-element.36.refs_2_.coupling_ref, ...), custom_call_target="tpu_custom_call" | custom-call | flops 1048576000 | bytes 11468800 | tf_op jit(solution)/shard_map/pushed/pallas_call | solution.py:20
  103.9 1.9 %collective-permute-start.11 = (bf16[160,640]{1,0:T(8,128)(2,1)S(1)}, bf16[160,640]{1,0:T(8,128)(2,1)S(1)}, u32[]{:S(2)}, u32[]{:S(2)}) collective-permute-start(bf16[160,640]{1,0:T(8,128)(2,1)S(1)} %get-tuple-element.47), channel_id=1, source_target_pairs={{0,32},{32,64},{64,96},{96,128},{128,160},{160,192},{192,224},{1,3... | collective-permute-start | bytes 614408 | tf_op jit(solution)/shard_map/ppermute | solution.py:38
  105.8 3.7 %collective-permute-start.10 = (bf16[160,640]{1,0:T(8,128)(2,1)S(1)}, bf16[160,640]{1,0:T(8,128)(2,1)S(1)}, u32[]{:S(2)}, u32[]{:S(2)}) collective-permute-start(bf16[160,640]{1,0:T(8,128)(2,1)S(1)} %get-tuple-element.44), channel_id=1, source_target_pairs={{0,32},{32,64},{64,96},{96,128},{128,160},{160,192},{192,224},{1,3... | collective-permute-start | bytes 614408 | tf_op jit(solution)/shard_map/ppermute | solution.py:38
  109.5 1.7 %local.1 = (f32[160,640]{1,0:T(8,128)S(1)}, f32[160,640]{1,0:T(8,128)S(1)}) custom-call(bf16[2560,640]{1,0:T(8,128)(2,1)S(1)} %get-tuple-element.42.panel_ref, bf16[5,128,128]{2,1,0:T(8,128)(2,1)S(1)} %get-tuple-element.40.inverse_ref, bf16[160,2560]{1,0:T(8,128)(2,1)S(1)} %get-tuple-element.41.refs_0_, ...), custom_call_target="tpu_custom_call" | custom-call | flops 1048576000 | bytes 8355840 | tf_op jit(solution)/shard_map/local/pallas_call | solution.py:20
  111.4 1.4 %collective-permute-start.13 = (bf16[80,640]{1,0:T(8,128)(2,1)S(1)}, bf16[80,640]{1,0:T(8,128)(2,1)S(1)}, u32[]{:S(2)}, u32[]{:S(2)}) collective-permute-start(bf16[80,640]{1,0:T(8,128)(2,1)S(1)} %get-tuple-element.49), channel_id=1, source_target_pairs={{0,8},{8,16},{16,24},{24,0},{1,9},{9,17},{17,25},{25,1},{2,10},{10... | collective-permute-start | bytes 307208 | tf_op jit(solution)/shard_map/ppermute | solution.py:289
  113.2 1.6 %collective-permute-start.14 = (bf16[80,640]{1,0:T(8,128)(2,1)S(1)}, bf16[80,640]{1,0:T(8,128)(2,1)S(1)}, u32[]{:S(2)}, u32[]{:S(2)}) collective-permute-start(bf16[80,640]{1,0:T(8,128)(2,1)S(1)} %get-tuple-element.50), channel_id=1, source_target_pairs={{0,24},{8,0},{16,8},{24,16},{1,25},{9,1},{17,9},{25,17},{2,26},{10... | collective-permute-start | bytes 307208 | tf_op jit(solution)/shard_map/ppermute | solution.py:289
  114.9 3.8 %collective-permute-done.12.refs_1_ = bf16[80,640]{1,0:T(8,128)(2,1)S(1)} collective-permute-done((bf16[80,640]{1,0:T(8,128)(2,1)S(1)}, bf16[80,640]{1,0:T(8,128)(2,1)S(1)}, u32[]{:S(2)}, u32[]{:S(2)}) %collective-permute-start.12) | collective-permute-done | bytes 102432 | tf_op jit(solution)/shard_map/ppermute | solution.py:289
  118.7 1.0 collective-permute-done.13.refs_2_
  119.7 0.8 join.1
  (25 shorter events, 1.6 us)
Async XLA Ops:
  0.0 14.0 %copy-start = (bf16[1,80,2560]{2,1,0:T(8,128)(2,1)S(1)}, bf16[1,80,2560]{2,1,0:T(8,128)(2,1)}, u32[]{:S(2)}) copy-start(bf16[1,80,2560]{2,1,0:T(8,128)(2,1)} %refs_0_.2) | copy-start | bytes 1228804
  1.1 8.3 %collective-permute-start = (bf16[80,640]{1,0:T(8,128)(2,1)S(1)}, bf16[80,640]{1,0:T(8,128)(2,1)S(1)}, u32[]{:S(2)}, u32[]{:S(2)}) collective-permute-start(bf16[80,640]{1,0:T(8,128)(2,1)S(1)} %get-tuple-element.29), channel_id=1, source_target_pairs={{0,16},{8,24},{16,0},{24,8},{1,17},{9,25},{17,1},{25,9},{2,18},{10... | collective-permute-start | bytes 307208 | tf_op jit(solution)/shard_map/ppermute | solution.py:289
  4.4 6.9 %collective-permute-start.2 = (bf16[80,640]{1,0:T(8,128)(2,1)S(1)}, bf16[80,640]{1,0:T(8,128)(2,1)S(1)}, u32[]{:S(2)}, u32[]{:S(2)}) collective-permute-start(bf16[80,640]{1,0:T(8,128)(2,1)S(1)} %get-tuple-element.34), channel_id=1, source_target_pairs={{0,8},{8,16},{16,24},{24,0},{1,9},{9,17},{17,25},{25,1},{2,10},{10... | collective-permute-start | bytes 307208 | tf_op jit(solution)/shard_map/ppermute | solution.py:289
  5.1 6.3 %collective-permute-start.3 = (bf16[80,640]{1,0:T(8,128)(2,1)S(1)}, bf16[80,640]{1,0:T(8,128)(2,1)S(1)}, u32[]{:S(2)}, u32[]{:S(2)}) collective-permute-start(bf16[80,640]{1,0:T(8,128)(2,1)S(1)} %get-tuple-element.35), channel_id=1, source_target_pairs={{0,24},{8,0},{16,8},{24,16},{1,25},{9,1},{17,9},{25,17},{2,26},{10... | collective-permute-start | bytes 307208 | tf_op jit(solution)/shard_map/ppermute | solution.py:289
  9.4 10.1 %collective-permute-start.1 = (bf16[160,640]{1,0:T(8,128)(2,1)S(1)}, bf16[160,640]{1,0:T(8,128)(2,1)S(1)}, u32[]{:S(2)}, u32[]{:S(2)}) collective-permute-start(bf16[160,640]{1,0:T(8,128)(2,1)S(1)} %early.1.refs_4_), channel_id=1, source_target_pairs={{32,0},{64,32},{96,64},{128,96},{160,128},{192,160},{224,192},{33,... | collective-permute-start | bytes 614408 | tf_op jit(solution)/shard_map/ppermute | solution.py:38
  11.4 8.2 %collective-permute-start.4 = (bf16[160,640]{1,0:T(8,128)(2,1)S(1)}, bf16[160,640]{1,0:T(8,128)(2,1)S(1)}, u32[]{:S(2)}, u32[]{:S(2)}) collective-permute-start(bf16[160,640]{1,0:T(8,128)(2,1)S(1)} %late.1.refs_5_), channel_id=1, source_target_pairs={{32,0},{64,32},{96,64},{128,96},{160,128},{192,160},{224,192},{33,... | collective-permute-start | bytes 614408 | tf_op jit(solution)/shard_map/ppermute | solution.py:38
  14.0 47.0 %collective-permute-start.5 = (bf16[80,2560]{1,0:T(8,128)(2,1)S(1)}, bf16[80,2560]{1,0:T(8,128)(2,1)S(1)}, u32[]{:S(2)}, u32[]{:S(2)}) collective-permute-start(bf16[80,2560]{1,0:T(8,128)(2,1)S(1)} %bitcast.5), channel_id=1, source_target_pairs={{0,16},{8,24},{16,0},{24,8},{1,17},{9,25},{17,1},{25,9},{2,18},{10... | collective-permute-start | bytes 1228808 | tf_op jit(solution)/shard_map/ppermute | solution.py:289
  16.3 44.7 %collective-permute-start.6 = (bf16[80,2560]{1,0:T(8,128)(2,1)S(1)}, bf16[80,2560]{1,0:T(8,128)(2,1)S(1)}, u32[]{:S(2)}, u32[]{:S(2)}) collective-permute-start(bf16[80,2560]{1,0:T(8,128)(2,1)S(1)} %bitcast.6), channel_id=1, source_target_pairs={{0,8},{8,16},{16,24},{24,0},{1,9},{9,17},{17,25},{25,1},{2,10},{10... | collective-permute-start | bytes 1228808 | tf_op jit(solution)/shard_map/ppermute | solution.py:289
  16.7 44.4 %collective-permute-start.7 = (bf16[240,2560]{1,0:T(8,128)(2,1)S(1)}, bf16[240,2560]{1,0:T(8,128)(2,1)S(1)}, u32[]{:S(2)}, u32[]{:S(2)}) collective-permute-start(bf16[240,2560]{1,0:T(8,128)(2,1)S(1)} %get-tuple-element.39), channel_id=1, source_target_pairs={{0,24},{8,0},{16,8},{24,16},{1,25},{9,1},{17,9},{25,17},{2,26},{10... | collective-permute-start | bytes 3686408 | tf_op jit(solution)/shard_map/ppermute | solution.py:289
  19.6 82.3 %collective-permute-start.9 = (bf16[160,2560]{1,0:T(8,128)(2,1)S(1)}, bf16[160,2560]{1,0:T(8,128)(2,1)S(1)}, u32[]{:S(2)}, u32[]{:S(2)}) collective-permute-start(bf16[160,2560]{1,0:T(8,128)(2,1)S(1)} %get-tuple-element.41.refs_0_), channel_id=1, source_target_pairs={{0,8},{8,16},{16,24},{24,0},{1,9},{9,17},{17,25},{25,1},{2,10},{10... | collective-permute-start | bytes 2457608 | tf_op jit(solution)/shard_map/ppermute | solution.py:289
  62.7 39.1 %collective-permute-start.8 = (bf16[240,2560]{1,0:T(8,128)(2,1)S(1)}, bf16[240,2560]{1,0:T(8,128)(2,1)S(1)}, u32[]{:S(2)}, u32[]{:S(2)}) collective-permute-start(bf16[240,2560]{1,0:T(8,128)(2,1)S(1)} %collective-permute-done.7.refs_3_), channel_id=1, source_target_pairs={{0,24},{8,0},{16,8},{24,16},{1,25},{9,1},{17,9},{25,17},{2,26},{10... | collective-permute-start | bytes 3686408 | tf_op jit(solution)/shard_map/ppermute | solution.py:289
  103.9 7.4 %collective-permute-start.11 = (bf16[160,640]{1,0:T(8,128)(2,1)S(1)}, bf16[160,640]{1,0:T(8,128)(2,1)S(1)}, u32[]{:S(2)}, u32[]{:S(2)}) collective-permute-start(bf16[160,640]{1,0:T(8,128)(2,1)S(1)} %get-tuple-element.47), channel_id=1, source_target_pairs={{0,32},{32,64},{64,96},{96,128},{128,160},{160,192},{192,224},{1,3... | collective-permute-start | bytes 614408 | tf_op jit(solution)/shard_map/ppermute | solution.py:38
  105.8 7.3 %collective-permute-start.10 = (bf16[160,640]{1,0:T(8,128)(2,1)S(1)}, bf16[160,640]{1,0:T(8,128)(2,1)S(1)}, u32[]{:S(2)}, u32[]{:S(2)}) collective-permute-start(bf16[160,640]{1,0:T(8,128)(2,1)S(1)} %get-tuple-element.44), channel_id=1, source_target_pairs={{0,32},{32,64},{64,96},{96,128},{128,160},{160,192},{192,224},{1,3... | collective-permute-start | bytes 614408 | tf_op jit(solution)/shard_map/ppermute | solution.py:38
  111.3 7.4 %collective-permute-start.12 = (bf16[80,640]{1,0:T(8,128)(2,1)S(1)}, bf16[80,640]{1,0:T(8,128)(2,1)S(1)}, u32[]{:S(2)}, u32[]{:S(2)}) collective-permute-start(bf16[80,640]{1,0:T(8,128)(2,1)S(1)} %get-tuple-element.48), channel_id=1, source_target_pairs={{0,16},{8,24},{16,0},{24,8},{1,17},{9,25},{17,1},{25,9},{2,18},{10... | collective-permute-start | bytes 307208 | tf_op jit(solution)/shard_map/ppermute | solution.py:289
  111.4 8.3 %collective-permute-start.13 = (bf16[80,640]{1,0:T(8,128)(2,1)S(1)}, bf16[80,640]{1,0:T(8,128)(2,1)S(1)}, u32[]{:S(2)}, u32[]{:S(2)}) collective-permute-start(bf16[80,640]{1,0:T(8,128)(2,1)S(1)} %get-tuple-element.49), channel_id=1, source_target_pairs={{0,8},{8,16},{16,24},{24,0},{1,9},{9,17},{17,25},{25,1},{2,10},{10... | collective-permute-start | bytes 307208 | tf_op jit(solution)/shard_map/ppermute | solution.py:289
  113.2 6.5 %collective-permute-start.14 = (bf16[80,640]{1,0:T(8,128)(2,1)S(1)}, bf16[80,640]{1,0:T(8,128)(2,1)S(1)}, u32[]{:S(2)}, u32[]{:S(2)}) collective-permute-start(bf16[80,640]{1,0:T(8,128)(2,1)S(1)} %get-tuple-element.50), channel_id=1, source_target_pairs={{0,24},{8,0},{16,8},{24,16},{1,25},{9,1},{17,9},{25,17},{2,26},{10... | collective-permute-start | bytes 307208 | tf_op jit(solution)/shard_map/ppermute | solution.py:289

commit v12 on v11

--- a/solution.py
+++ b/solution.py
@@ -323,8 +323,7 @@
     pieces = exchange(slices)
     first = after(in_coupling, slices[0])
     pair, trio, inv, psi = operands(first, in_inverse, in_carry, out_inverse, out_coupling, shards)
-    half = shards // 2
-    grads = [stacked(lax.optimization_barrier((*pieces[:half], pair))[:half], "early"), stacked(pieces[half:], "late")]
+    grads = [stacked(lax.optimization_barrier((*pieces, pair))[:shards], "stacked")]
     above = [hop_layer(grad, -1) for grad in grads]
     pair, trio, own = lax.optimization_barrier((pair, trio, in_coupling[0], *grads))[:3]
     ahead, behind = hop_y(pair, 1), hop_y(trio, -1)

time: 122 us -> 121 us (level)
  starting transfers between devices: 28.3 us -> 24.7 us
  blocking collectives: 75.8 us -> 77.2 us
    ppermute x4 -> x3, starting transfers between devices: 10.1 us -> 7.99 us  [hop_layer(): lax.ppermute(x, 'layer', [(i, i + by) for i in range(size) if 0 <= i + by...]
    ppermute x11, starting transfers between devices: 18.2 us -> 16.7 us  [hop_y(): return lax.ppermute(x, 'y', [(i, (i + by) % size) for i in range(size)])]
    all_gather x2, blocking collectives: 75.8 us -> 77.2 us  [gather_panel(): return lax.all_gather(tile.astype(HALF), 'z', axis=0).astype(BF)]
    pallas_call x8 -> x7, Pallas kernels: 5.95 us -> 5.92 us  [call(): pl.pallas_call(kernel, out_shape=out, in_specs=[HBM if i in far else VMEM...]
  transfers between devices with their start and end apart: 15 -> 14, of which waited for: 3 -> 4; matrix products, arithmetic and copies ran while one was open for 1% -> 1% of each run, Pallas kernels for 5% -> 5%
where the time goes in v12:
time: 121 us; the launch traced here: 120 us
  blocking collectives  77.2 us (64%)
  starting transfers between devices  24.7 us (20%)
  Pallas kernels  9.56 us (8%)
  waiting for transfers between devices  6.41 us (5%)
  other arithmetic  1.42 us (1%)
    all_gather x2, blocking collectives, gather_panel(): return lax.all_gather(tile.astype(HALF), 'z', axis=0).astype(BF)  77.2 us
    ppermute x11, starting transfers between devices, hop_y(): return lax.ppermute(x, 'y', [(i, (i + by) % size) for i in range(size)])  16.7 us
    ppermute x3, starting transfers between devices, hop_layer(): lax.ppermute(x, 'layer', [(i, i + by) for i in range(size) if 0 <= i + by...  7.99 us
    pallas_call x7, Pallas kernels, call(): pl.pallas_call(kernel, out_shape=out, in_specs=[HBM if i in far else VMEM...  5.92 us
    ppermute x11, waiting for transfers between devices, hop_y(): return lax.ppermute(x, 'y', [(i, (i + by) % size) for i in range(size)])  5.73 us
    pallas_call x3, Pallas kernels, copies(): pl.pallas_call(body, out_shape=out, in_specs=[near] * len(operands), out_...  3.64 us
  transfers between devices with their start and end apart: 14, of which 4 were waited for; matrix products, arithmetic and copies ran while one was open for 1% of the time, Pallas kernels for 5%

profile of v12, /device:TPU:2, one launch (start us, length us, event | category | flops | bytes accessed | tf_op | source)
XLA Modules:
  0.0 119.6 jit_solution(17234815040796529860)
XLA Ops:
  0.0 1.1 blocks.1
  1.1 3.3 %collective-permute-start = (bf16[80,640]{1,0:T(8,128)(2,1)S(1)}, bf16[80,640]{1,0:T(8,128)(2,1)S(1)}, u32[]{:S(2)}, u32[]{:S(2)}) collective-permute-start(bf16[80,640]{1,0:T(8,128)(2,1)S(1)} %get-tuple-element.31), channel_id=1, source_target_pairs={{0,16},{8,24},{16,0},{24,8},{1,17},{9,25},{17,1},{25,9},{2,18},{10... | collective-permute-start | bytes 307208 | tf_op jit(solution)/shard_map/ppermute | solution.py:289
  4.4 0.7 collective-permute-start.1
  5.1 2.6 %collective-permute-start.2 = (bf16[80,640]{1,0:T(8,128)(2,1)S(1)}, bf16[80,640]{1,0:T(8,128)(2,1)S(1)}, u32[]{:S(2)}, u32[]{:S(2)}) collective-permute-start(bf16[80,640]{1,0:T(8,128)(2,1)S(1)} %get-tuple-element.33), channel_id=1, source_target_pairs={{0,24},{8,0},{16,8},{24,16},{1,25},{9,1},{17,9},{25,17},{2,26},{10... | collective-permute-start | bytes 307208 | tf_op jit(solution)/shard_map/ppermute | solution.py:289
  7.7 1.7 %operands.1 = (bf16[160,2560]{1,0:T(8,128)(2,1)S(1)}, bf16[240,2560]{1,0:T(8,128)(2,1)S(1)}, bf16[5,128,128]{2,1,0:T(8,128)(2,1)S(1)}, bf16[5,128,128]{2,1,0:T(8,128)(2,1)S(1)}) custom-call(bf16[1,80,2560]{2,1,0:T(8,128)(2,1)} %refs_0_.2, bf16[1,80,2560]{2,1,0:T(8,128)(2,1)} %refs_1_.1, bf16[1,80,2560]{2,1,0:T(8,128)(2,1)} %refs_2_.1, ...), custom_call_target="tpu_custom_call" | custom-call | bytes 4751360 | tf_op jit(solution)/shard_map/operands/pallas_call | solution.py:233
  9.4 0.9 collective-permute-done.1.refs_2_
  10.3 2.5 %collective-permute-start.3 = (bf16[320,640]{1,0:T(8,128)(2,1)S(1)}, bf16[320,640]{1,0:T(8,128)(2,1)S(1)}, u32[]{:S(2)}, u32[]{:S(2)}) collective-permute-start(bf16[320,640]{1,0:T(8,128)(2,1)S(1)} %stacked.1.refs_4_), channel_id=1, source_target_pairs={{32,0},{64,32},{96,64},{128,96},{160,128},{192,160},{224,192},{33,... | collective-permute-start | bytes 1228808 | tf_op jit(solution)/shard_map/ppermute | solution.py:38
  12.8 1.2 %collective-permute-start.4 = (bf16[80,2560]{1,0:T(8,128)(2,1)S(1)}, bf16[80,2560]{1,0:T(8,128)(2,1)S(1)}, u32[]{:S(2)}, u32[]{:S(2)}) collective-permute-start(bf16[80,2560]{1,0:T(8,128)(2,1)S(1)} %bitcast.5), channel_id=1, source_target_pairs={{0,16},{8,24},{16,0},{24,8},{1,17},{9,25},{17,1},{25,9},{2,18},{10... | collective-permute-start | bytes 1228808 | tf_op jit(solution)/shard_map/ppermute | solution.py:289
  14.0 2.4 %collective-permute-start.5 = (bf16[80,2560]{1,0:T(8,128)(2,1)S(1)}, bf16[80,2560]{1,0:T(8,128)(2,1)S(1)}, u32[]{:S(2)}, u32[]{:S(2)}) collective-permute-start(bf16[80,2560]{1,0:T(8,128)(2,1)S(1)} %bitcast.6), channel_id=1, source_target_pairs={{0,8},{8,16},{16,24},{24,0},{1,9},{9,17},{17,25},{25,1},{2,10},{10... | collective-permute-start | bytes 1228808 | tf_op jit(solution)/shard_map/ppermute | solution.py:289
  16.5 0.8 collective-permute-start.6
  17.3 1.2 %collective-permute-start.8 = (bf16[160,2560]{1,0:T(8,128)(2,1)S(1)}, bf16[160,2560]{1,0:T(8,128)(2,1)S(1)}, u32[]{:S(2)}, u32[]{:S(2)}) collective-permute-start(bf16[160,2560]{1,0:T(8,128)(2,1)S(1)} %get-tuple-element.45.refs_0_), channel_id=1, source_target_pairs={{0,8},{8,16},{16,24},{24,0},{1,9},{9,17},{17,25},{25,1},{2,10},{10... | collective-permute-start | bytes 2457608 | tf_op jit(solution)/shard_map/ppermute | solution.py:289
  19.0 40.7 %all-gather.4 = f16[2624,640]{1,0:T(8,128)(2,1)S(1)} all-gather(f16[328,640]{1,0:T(8,128)(2,1)S(1)} %convert_element_type.12), channel_id=2, replica_groups=mesh['layer'=8,'y'=4,'z'=8] {'z'}, dimensions={0}, use_global_device_ids=true | all-gather | bytes 3778560 | tf_op jit(solution)/shard_map/all_gather | solution.py:317
  60.3 1.6 %reduced.1 = bf16[328,640]{1,0:T(8,128)(2,1)S(1)} custom-call(bf16[8,328,640]{2,1,0:T(8,128)(2,1)S(1)} %bitcast.3, bf16[80,2560]{1,0:T(8,128)(2,1)S(1)} %bitcast.7, bf16[80,2560]{1,0:T(8,128)(2,1)S(1)} %collective-permute-done.4.refs_1_, bf16[80,2560]{1,0:T(8,128)(2,1)S(1)} %collective-permute-done.5.refs_2_, ...), custom_call_target="tpu_custom_call" | custom-call | flops 1048576000 | bytes 6645760 | tf_op jit(solution)/shard_map/reduced/pallas_call | solution.py:20
  62.0 1.7 %collective-permute-start.7 = (bf16[240,2560]{1,0:T(8,128)(2,1)S(1)}, bf16[240,2560]{1,0:T(8,128)(2,1)S(1)}, u32[]{:S(2)}, u32[]{:S(2)}) collective-permute-start(bf16[240,2560]{1,0:T(8,128)(2,1)S(1)} %collective-permute-done.6.refs_3_), channel_id=1, source_target_pairs={{0,24},{8,0},{16,8},{24,16},{1,25},{9,1},{17,9},{25,17},{2,26},{10... | collective-permute-start | bytes 3686408 | tf_op jit(solution)/shard_map/ppermute | solution.py:289
  63.7 36.5 %all-gather.5 = f16[2624,640]{1,0:T(8,128)(2,1)S(1)} all-gather(f16[328,640]{1,0:T(8,128)(2,1)S(1)} %convert_element_type.14), channel_id=3, replica_groups=mesh['layer'=8,'y'=4,'z'=8] {'z'}, dimensions={0}, use_global_device_ids=true | all-gather | bytes 3778560 | tf_op jit(solution)/shard_map/all_gather | solution.py:317
  100.9 2.0 %pushed.1 = (bf16[160,640]{1,0:T(8,128)(2,1)S(1)}, bf16[160,640]{1,0:T(8,128)(2,1)S(1)}, bf16[2560,640]{1,0:T(8,128)(2,1)S(1)}) custom-call(bf16[8,328,640]{2,1,0:T(8,128)(2,1)S(1)} %bitcast.4, bf16[5,128,128]{2,1,0:T(8,128)(2,1)S(1)} %get-tuple-element.44.inverse_ref, bf16[5,128,128]{2,1,0:T(8,128)(2,1)S(1)} %get-tuple-element.40.refs_1_.coupling_ref, ...), custom_call_target="tpu_custom_call" | custom-call | flops 1048576000 | bytes 11468800 | tf_op jit(solution)/shard_map/pushed/pallas_call | solution.py:20
  103.0 1.9 %collective-permute-start.10 = (bf16[160,640]{1,0:T(8,128)(2,1)S(1)}, bf16[160,640]{1,0:T(8,128)(2,1)S(1)}, u32[]{:S(2)}, u32[]{:S(2)}) collective-permute-start(bf16[160,640]{1,0:T(8,128)(2,1)S(1)} %get-tuple-element.51), channel_id=1, source_target_pairs={{0,32},{32,64},{64,96},{96,128},{128,160},{160,192},{192,224},{1,3... | collective-permute-start | bytes 614408 | tf_op jit(solution)/shard_map/ppermute | solution.py:38
  104.9 3.6 %collective-permute-start.9 = (bf16[160,640]{1,0:T(8,128)(2,1)S(1)}, bf16[160,640]{1,0:T(8,128)(2,1)S(1)}, u32[]{:S(2)}, u32[]{:S(2)}) collective-permute-start(bf16[160,640]{1,0:T(8,128)(2,1)S(1)} %get-tuple-element.48), channel_id=1, source_target_pairs={{0,32},{32,64},{64,96},{96,128},{128,160},{160,192},{192,224},{1,3... | collective-permute-start | bytes 614408 | tf_op jit(solution)/shard_map/ppermute | solution.py:38
  108.5 1.7 %local.1 = (f32[160,640]{1,0:T(8,128)S(1)}, f32[160,640]{1,0:T(8,128)S(1)}) custom-call(bf16[2560,640]{1,0:T(8,128)(2,1)S(1)} %get-tuple-element.46.panel_ref, bf16[5,128,128]{2,1,0:T(8,128)(2,1)S(1)} %get-tuple-element.44.inverse_ref, bf16[160,2560]{1,0:T(8,128)(2,1)S(1)} %get-tuple-element.45.refs_0_, ...), custom_call_target="tpu_custom_call" | custom-call | flops 1048576000 | bytes 8355840 | tf_op jit(solution)/shard_map/local/pallas_call | solution.py:20
  110.4 1.1 collective-permute-start.12
  112.3 1.6 %collective-permute-start.13 = (bf16[80,640]{1,0:T(8,128)(2,1)S(1)}, bf16[80,640]{1,0:T(8,128)(2,1)S(1)}, u32[]{:S(2)}, u32[]{:S(2)}) collective-permute-start(bf16[80,640]{1,0:T(8,128)(2,1)S(1)} %get-tuple-element.54), channel_id=1, source_target_pairs={{0,24},{8,0},{16,8},{24,16},{1,25},{9,1},{17,9},{25,17},{2,26},{10... | collective-permute-start | bytes 307208 | tf_op jit(solution)/shard_map/ppermute | solution.py:289
  113.9 3.8 %collective-permute-done.11.refs_1_ = bf16[80,640]{1,0:T(8,128)(2,1)S(1)} collective-permute-done((bf16[80,640]{1,0:T(8,128)(2,1)S(1)}, bf16[80,640]{1,0:T(8,128)(2,1)S(1)}, u32[]{:S(2)}, u32[]{:S(2)}) %collective-permute-start.11) | collective-permute-done | bytes 102432 | tf_op jit(solution)/shard_map/ppermute | solution.py:289
  117.7 1.0 collective-permute-done.12.refs_2_
  118.7 0.8 join.1
  (22 shorter events, 2.7 us)
Async XLA Ops:
  0.0 12.8 %copy-start = (bf16[1,80,2560]{2,1,0:T(8,128)(2,1)S(1)}, bf16[1,80,2560]{2,1,0:T(8,128)(2,1)}, u32[]{:S(2)}) copy-start(bf16[1,80,2560]{2,1,0:T(8,128)(2,1)} %refs_0_.2) | copy-start | bytes 1228804
  1.1 8.3 %collective-permute-start = (bf16[80,640]{1,0:T(8,128)(2,1)S(1)}, bf16[80,640]{1,0:T(8,128)(2,1)S(1)}, u32[]{:S(2)}, u32[]{:S(2)}) collective-permute-start(bf16[80,640]{1,0:T(8,128)(2,1)S(1)} %get-tuple-element.31), channel_id=1, source_target_pairs={{0,16},{8,24},{16,0},{24,8},{1,17},{9,25},{17,1},{25,9},{2,18},{10... | collective-permute-start | bytes 307208 | tf_op jit(solution)/shard_map/ppermute | solution.py:289
  4.4 5.9 %collective-permute-start.1 = (bf16[80,640]{1,0:T(8,128)(2,1)S(1)}, bf16[80,640]{1,0:T(8,128)(2,1)S(1)}, u32[]{:S(2)}, u32[]{:S(2)}) collective-permute-start(bf16[80,640]{1,0:T(8,128)(2,1)S(1)} %get-tuple-element.32), channel_id=1, source_target_pairs={{0,8},{8,16},{16,24},{24,0},{1,9},{9,17},{17,25},{25,1},{2,10},{10... | collective-permute-start | bytes 307208 | tf_op jit(solution)/shard_map/ppermute | solution.py:289
  5.1 5.2 %collective-permute-start.2 = (bf16[80,640]{1,0:T(8,128)(2,1)S(1)}, bf16[80,640]{1,0:T(8,128)(2,1)S(1)}, u32[]{:S(2)}, u32[]{:S(2)}) collective-permute-start(bf16[80,640]{1,0:T(8,128)(2,1)S(1)} %get-tuple-element.33), channel_id=1, source_target_pairs={{0,24},{8,0},{16,8},{24,16},{1,25},{9,1},{17,9},{25,17},{2,26},{10... | collective-permute-start | bytes 307208 | tf_op jit(solution)/shard_map/ppermute | solution.py:289
  10.3 8.1 %collective-permute-start.3 = (bf16[320,640]{1,0:T(8,128)(2,1)S(1)}, bf16[320,640]{1,0:T(8,128)(2,1)S(1)}, u32[]{:S(2)}, u32[]{:S(2)}) collective-permute-start(bf16[320,640]{1,0:T(8,128)(2,1)S(1)} %stacked.1.refs_4_), channel_id=1, source_target_pairs={{32,0},{64,32},{96,64},{128,96},{160,128},{192,160},{224,192},{33,... | collective-permute-start | bytes 1228808 | tf_op jit(solution)/shard_map/ppermute | solution.py:38
  12.8 47.5 %collective-permute-start.4 = (bf16[80,2560]{1,0:T(8,128)(2,1)S(1)}, bf16[80,2560]{1,0:T(8,128)(2,1)S(1)}, u32[]{:S(2)}, u32[]{:S(2)}) collective-permute-start(bf16[80,2560]{1,0:T(8,128)(2,1)S(1)} %bitcast.5), channel_id=1, source_target_pairs={{0,16},{8,24},{16,0},{24,8},{1,17},{9,25},{17,1},{25,9},{2,18},{10... | collective-permute-start | bytes 1228808 | tf_op jit(solution)/shard_map/ppermute | solution.py:289
  14.0 46.3 %collective-permute-start.5 = (bf16[80,2560]{1,0:T(8,128)(2,1)S(1)}, bf16[80,2560]{1,0:T(8,128)(2,1)S(1)}, u32[]{:S(2)}, u32[]{:S(2)}) collective-permute-start(bf16[80,2560]{1,0:T(8,128)(2,1)S(1)} %bitcast.6), channel_id=1, source_target_pairs={{0,8},{8,16},{16,24},{24,0},{1,9},{9,17},{17,25},{25,1},{2,10},{10... | collective-permute-start | bytes 1228808 | tf_op jit(solution)/shard_map/ppermute | solution.py:289
  16.5 43.9 %collective-permute-start.6 = (bf16[240,2560]{1,0:T(8,128)(2,1)S(1)}, bf16[240,2560]{1,0:T(8,128)(2,1)S(1)}, u32[]{:S(2)}, u32[]{:S(2)}) collective-permute-start(bf16[240,2560]{1,0:T(8,128)(2,1)S(1)} %get-tuple-element.43), channel_id=1, source_target_pairs={{0,24},{8,0},{16,8},{24,16},{1,25},{9,1},{17,9},{25,17},{2,26},{10... | collective-permute-start | bytes 3686408 | tf_op jit(solution)/shard_map/ppermute | solution.py:289
  17.3 83.6 %collective-permute-start.8 = (bf16[160,2560]{1,0:T(8,128)(2,1)S(1)}, bf16[160,2560]{1,0:T(8,128)(2,1)S(1)}, u32[]{:S(2)}, u32[]{:S(2)}) collective-permute-start(bf16[160,2560]{1,0:T(8,128)(2,1)S(1)} %get-tuple-element.45.refs_0_), channel_id=1, source_target_pairs={{0,8},{8,16},{16,24},{24,0},{1,9},{9,17},{17,25},{25,1},{2,10},{10... | collective-permute-start | bytes 2457608 | tf_op jit(solution)/shard_map/ppermute | solution.py:289
  62.0 38.9 %collective-permute-start.7 = (bf16[240,2560]{1,0:T(8,128)(2,1)S(1)}, bf16[240,2560]{1,0:T(8,128)(2,1)S(1)}, u32[]{:S(2)}, u32[]{:S(2)}) collective-permute-start(bf16[240,2560]{1,0:T(8,128)(2,1)S(1)} %collective-permute-done.6.refs_3_), channel_id=1, source_target_pairs={{0,24},{8,0},{16,8},{24,16},{1,25},{9,1},{17,9},{25,17},{2,26},{10... | collective-permute-start | bytes 3686408 | tf_op jit(solution)/shard_map/ppermute | solution.py:289
  103.0 7.3 %collective-permute-start.10 = (bf16[160,640]{1,0:T(8,128)(2,1)S(1)}, bf16[160,640]{1,0:T(8,128)(2,1)S(1)}, u32[]{:S(2)}, u32[]{:S(2)}) collective-permute-start(bf16[160,640]{1,0:T(8,128)(2,1)S(1)} %get-tuple-element.51), channel_id=1, source_target_pairs={{0,32},{32,64},{64,96},{96,128},{128,160},{160,192},{192,224},{1,3... | collective-permute-start | bytes 614408 | tf_op jit(solution)/shard_map/ppermute | solution.py:38
  104.9 7.3 %collective-permute-start.9 = (bf16[160,640]{1,0:T(8,128)(2,1)S(1)}, bf16[160,640]{1,0:T(8,128)(2,1)S(1)}, u32[]{:S(2)}, u32[]{:S(2)}) collective-permute-start(bf16[160,640]{1,0:T(8,128)(2,1)S(1)} %get-tuple-element.48), channel_id=1, source_target_pairs={{0,32},{32,64},{64,96},{96,128},{128,160},{160,192},{192,224},{1,3... | collective-permute-start | bytes 614408 | tf_op jit(solution)/shard_map/ppermute | solution.py:38
  110.3 7.4 %collective-permute-start.11 = (bf16[80,640]{1,0:T(8,128)(2,1)S(1)}, bf16[80,640]{1,0:T(8,128)(2,1)S(1)}, u32[]{:S(2)}, u32[]{:S(2)}) collective-permute-start(bf16[80,640]{1,0:T(8,128)(2,1)S(1)} %get-tuple-element.52), channel_id=1, source_target_pairs={{0,16},{8,24},{16,0},{24,8},{1,17},{9,25},{17,1},{25,9},{2,18},{10... | collective-permute-start | bytes 307208 | tf_op jit(solution)/shard_map/ppermute | solution.py:289
  110.4 8.3 %collective-permute-start.12 = (bf16[80,640]{1,0:T(8,128)(2,1)S(1)}, bf16[80,640]{1,0:T(8,128)(2,1)S(1)}, u32[]{:S(2)}, u32[]{:S(2)}) collective-permute-start(bf16[80,640]{1,0:T(8,128)(2,1)S(1)} %get-tuple-element.53), channel_id=1, source_target_pairs={{0,8},{8,16},{16,24},{24,0},{1,9},{9,17},{17,25},{25,1},{2,10},{10... | collective-permute-start | bytes 307208 | tf_op jit(solution)/shard_map/ppermute | solution.py:289
  112.3 6.4 %collective-permute-start.13 = (bf16[80,640]{1,0:T(8,128)(2,1)S(1)}, bf16[80,640]{1,0:T(8,128)(2,1)S(1)}, u32[]{:S(2)}, u32[]{:S(2)}) collective-permute-start(bf16[80,640]{1,0:T(8,128)(2,1)S(1)} %get-tuple-element.54), channel_id=1, source_target_pairs={{0,24},{8,0},{16,8},{24,16},{1,25},{9,1},{17,9},{25,17},{2,26},{10... | collective-permute-start | bytes 307208 | tf_op jit(solution)/shard_map/ppermute | solution.py:289

commit v13 on v12

--- a/solution.py
+++ b/solution.py
@@ -149,62 +149,48 @@
     return order[: shards // 2], order[shards // 2 :]
 
 
-def places_out(shards):
-    halves = halves_out(shards)
-    where = {k: (half, place) for half, ks in enumerate(halves) for place, k in enumerate(ks)}
-    return [where[(shards - k) % shards] for k in distances(shards)]
-
-
-def pushed_tile(panel, factor, inverse, coupling, shards):
-    rows, depth = factor[0].shape[0] // 2, factor[0].shape[1]
-    tile, width = shards * rows, panel.shape[2]
-
-    def kernel(panel_in, inverse_ref, coupling_ref, *refs):
-        pieces, (*pushed_refs, panel_ref) = refs[:shards], refs[shards:]
-        carried = []
+def halves_of(factors):
+    shards = len(factors)
+    order = distances(shards)
+    return [[factors[order.index((shards - k) % shards)] for k in ks] for ks in halves_out(shards)]
+
+
+def product_rows(panel, pieces, tables, rows, last, kind, name, shards=0, below=None):
+    depth, width = pieces[0].shape[1], panel.shape[-1]
+    tile, count = len(pieces) * rows, len(pieces)
+    operands_in = [panel, *pieces, *tables] + ([] if below is None else [below])
+
+    def kernel(*refs):
+        panel_in, piece_refs, table_refs = refs[0], refs[1 : 1 + count], refs[1 + count : 1 + count + len(tables)]
+        out_refs = refs[len(operands_in) :]
+        panel_ref = out_refs[-1] if shards else panel_in
+        values = []
         for at, w in chunks_of(width):
-            load_scaled(panel_in, panel_ref, at, w, shards, rows)
-            both = jnp.dot(joined(pieces, rows, rows), panel_ref[:, pl.ds(at, w)], preferred_element_type=F32)
-            carried += [both[:, i : i + BLK].astype(BF) for i in range(0, w, BLK)]
-        middle = [
-            jnp.dot(x, inverse_ref[b], preferred_element_type=F32).astype(BF) for b, x in enumerate(carried)
-        ]
-        for b, x in enumerate(middle):
-            pushed = jnp.dot(x, coupling_ref[b], preferred_element_type=F32).astype(BF)
-            for (half, place), part in zip(places_out(shards), blocks_of(pushed, shards), strict=True):
-                pushed_refs[half][pl.ds(place * rows, rows), pl.ds(b * BLK, BLK)] = part
-
-    return call(
-        kernel,
-        (*[like(tile // 2, width, BF)] * 2, like(depth, width, BF)),
-        "pushed",
-        [panel, inverse, coupling, *factor],
-        flops=2 * tile * depth * width,
-    )
-
-
-def local_tile(panel, factor, inverse, shards):
-    rows, depth = factor[0].shape[0] // 2, factor[0].shape[1]
-    tile, width = shards * rows, panel.shape[1]
-
-    def kernel(panel_ref, inverse_ref, *refs):
-        pieces, local_refs = refs[:shards], refs[shards:]
-        whitened = []
-        for at, w in chunks_of(width):
-            both = jnp.dot(joined(pieces, rows, 2 * rows), panel_ref[:, pl.ds(at, w)], preferred_element_type=F32)
-            whitened += [both[:, i : i + BLK].astype(BF) for i in range(0, w, BLK)]
-        for b, x in enumerate(whitened):
-            product = jnp.dot(x, inverse_ref[b], preferred_element_type=F32)
-            for (half, place), part in zip(places_out(shards), blocks_of(product, shards), strict=True):
-                local_refs[half][pl.ds(place * rows, rows), pl.ds(b * BLK, BLK)] = part
-
-    return call(
-        kernel,
-        (like(tile // 2, width, F32),) * 2,
-        "local",
-        [panel, inverse, *factor],
-        flops=2 * tile * depth * width,
-    )
+            if shards:
+                load_scaled(panel_in, panel_ref, at, w, shards, rows)
+            both = jnp.dot(
+                joined(piece_refs, rows, last * rows), panel_ref[:, pl.ds(at, w)], preferred_element_type=F32
+            )
+            values += [both[:, i : i + BLK] for i in range(0, w, BLK)]
+        for table_ref in table_refs:
+            values = [
+                jnp.dot(x.astype(BF), table_ref[b], preferred_element_type=F32) for b, x in enumerate(values)
+            ]
+        for b, x in enumerate(values):
+            cols = pl.ds(b * BLK, BLK)
+            if below is None:
+                out_refs[0][:, cols] = x.astype(kind)
+            else:
+                x = (x - refs[len(operands_in) - 1][:, cols].astype(F32)).astype(kind)
+                for out_ref, part in zip(out_refs, blocks_of(x, count), strict=True):
+                    out_ref[:, cols] = part
+
+    out = like(tile, width, kind)
+    if shards:
+        out = (out, like(depth, width, BF))
+    if below is not None:
+        out = (like(rows, width, kind),) * count
+    return call(kernel, out, name, operands_in, flops=2 * tile * depth * width)
 
 
 def update_pieces(local_term, pushed, count, name):
@@ -331,12 +317,17 @@
     near = near_tile(above, psi, shards)
     reduced = reduced_tile(gather_panel(near), coupling, grads, shards)
     factors = [pair, hop_y(behind, -1), ahead, behind]
-    *pushed, panel = pushed_tile(gather_panel(reduced), factors, inv, psi, shards)
-    pushed = [hop_layer(x, 1) for x in pushed]
-    local_terms = local_tile(panel, factors, inv, shards)
+    early, late = halves_of(factors)
+    rows = own.shape[0]
+    pushed_a, panel = product_rows(gather_panel(reduced), early, [inv, psi], rows, 1, BF, "pushed_a", shards)
+    pushed_b = product_rows(panel, late, [inv, psi], rows, 1, BF, "pushed_b")
+    below_a, below_b = hop_layer(pushed_a, 1), hop_layer(pushed_b, 1)
+    local_a = product_rows(panel, early, [inv], rows, 2, F32, "local_a")
+    pieces_a = update_pieces(local_a, below_a, len(early), "update_a")
+    pieces_b = product_rows(panel, late, [inv], rows, 2, BF, "update_b", below=below_b)
     came = {}
-    for ks, mine, below, name in zip(halves_out(shards), local_terms, pushed, ("update_a", "update_b"), strict=True):
-        for k, piece in zip(ks, update_pieces(mine, below, len(ks), name), strict=True):
+    for ks, pieces in zip(halves_out(shards), (pieces_a, pieces_b), strict=True):
+        for k, piece in zip(ks, pieces, strict=True):
             came[k] = hop_y(piece, k) if k else piece
     return join_columns([came[k] for k in distances(shards)])
 

time: 121 us -> 120 us (level)
    pallas_call x7 -> x8, Pallas kernels: 5.92 us -> 6.2 us  [call(): pl.pallas_call(kernel, out_shape=out, in_specs=[HBM if i in far else VMEM...]
  transfers between devices with their start and end apart: 14 -> 14, of which waited for: 4 -> 4; matrix products, arithmetic and copies ran while one was open for 1% -> 1% of each run, Pallas kernels for 5% -> 7%
where the time goes in v13:
time: 120 us; the launch traced here: 119 us
  blocking collectives  77.2 us (64%)
  starting transfers between devices  24.2 us (20%)
  Pallas kernels  9.84 us (8%)
  waiting for transfers between devices  6.06 us (5%)
  other arithmetic  1.42 us (1%)
    all_gather x2, blocking collectives, gather_panel(): return lax.all_gather(tile.astype(HALF), 'z', axis=0).astype(BF)  77.2 us
    ppermute x11, starting transfers between devices, hop_y(): return lax.ppermute(x, 'y', [(i, (i + by) % size) for i in range(size)])  16.4 us
    ppermute x3, starting transfers between devices, hop_layer(): lax.ppermute(x, 'layer', [(i, i + by) for i in range(size) if 0 <= i + by...  7.8 us
    pallas_call x8, Pallas kernels, call(): pl.pallas_call(kernel, out_shape=out, in_specs=[HBM if i in far else VMEM...  6.2 us
    ppermute x11, waiting for transfers between devices, hop_y(): return lax.ppermute(x, 'y', [(i, (i + by) % size) for i in range(size)])  4.85 us
    pallas_call x3, Pallas kernels, copies(): pl.pallas_call(body, out_shape=out, in_specs=[near] * len(operands), out_...  3.64 us
  transfers between devices with their start and end apart: 14, of which 4 were waited for; matrix products, arithmetic and copies ran while one was open for 1% of the time, Pallas kernels for 7%

profile of v13, /device:TPU:2, one launch (start us, length us, event | category | flops | bytes accessed | tf_op | source)
XLA Modules:
  0.0 119.0 jit_solution(9664952989159818374)
XLA Ops:
  0.0 1.1 blocks.1
  1.1 3.3 %collective-permute-start = (bf16[80,640]{1,0:T(8,128)(2,1)S(1)}, bf16[80,640]{1,0:T(8,128)(2,1)S(1)}, u32[]{:S(2)}, u32[]{:S(2)}) collective-permute-start(bf16[80,640]{1,0:T(8,128)(2,1)S(1)} %get-tuple-element.28), channel_id=1, source_target_pairs={{0,16},{8,24},{16,0},{24,8},{1,17},{9,25},{17,1},{25,9},{2,18},{10... | collective-permute-start | bytes 307208 | tf_op jit(solution)/shard_map/ppermute | solution.py:275
  5.1 2.6 %collective-permute-start.2 = (bf16[80,640]{1,0:T(8,128)(2,1)S(1)}, bf16[80,640]{1,0:T(8,128)(2,1)S(1)}, u32[]{:S(2)}, u32[]{:S(2)}) collective-permute-start(bf16[80,640]{1,0:T(8,128)(2,1)S(1)} %get-tuple-element.30), channel_id=1, source_target_pairs={{0,24},{8,0},{16,8},{24,16},{1,25},{9,1},{17,9},{25,17},{2,26},{10... | collective-permute-start | bytes 307208 | tf_op jit(solution)/shard_map/ppermute | solution.py:275
  7.7 1.7 %operands.1 = (bf16[160,2560]{1,0:T(8,128)(2,1)S(1)}, bf16[240,2560]{1,0:T(8,128)(2,1)S(1)}, bf16[5,128,128]{2,1,0:T(8,128)(2,1)S(1)}, bf16[5,128,128]{2,1,0:T(8,128)(2,1)S(1)}) custom-call(bf16[1,80,2560]{2,1,0:T(8,128)(2,1)} %refs_0_.2, bf16[1,80,2560]{2,1,0:T(8,128)(2,1)} %refs_1_.1, bf16[1,80,2560]{2,1,0:T(8,128)(2,1)} %refs_2_.1, ...), custom_call_target="tpu_custom_call" | custom-call | bytes 4751360 | tf_op jit(solution)/shard_map/operands/pallas_call | solution.py:219
  9.4 0.9 collective-permute-done.1.refs_2_
  10.3 2.5 %collective-permute-start.3 = (bf16[320,640]{1,0:T(8,128)(2,1)S(1)}, bf16[320,640]{1,0:T(8,128)(2,1)S(1)}, u32[]{:S(2)}, u32[]{:S(2)}) collective-permute-start(bf16[320,640]{1,0:T(8,128)(2,1)S(1)} %stacked.1.refs_4_), channel_id=1, source_target_pairs={{32,0},{64,32},{96,64},{128,96},{160,128},{192,160},{224,192},{33,... | collective-permute-start | bytes 1228808 | tf_op jit(solution)/shard_map/ppermute | solution.py:38
  12.8 1.2 %collective-permute-start.4 = (bf16[80,2560]{1,0:T(8,128)(2,1)S(1)}, bf16[80,2560]{1,0:T(8,128)(2,1)S(1)}, u32[]{:S(2)}, u32[]{:S(2)}) collective-permute-start(bf16[80,2560]{1,0:T(8,128)(2,1)S(1)} %bitcast.5), channel_id=1, source_target_pairs={{0,16},{8,24},{16,0},{24,8},{1,17},{9,25},{17,1},{25,9},{2,18},{10... | collective-permute-start | bytes 1228808 | tf_op jit(solution)/shard_map/ppermute | solution.py:275
  14.0 2.4 %collective-permute-start.5 = (bf16[80,2560]{1,0:T(8,128)(2,1)S(1)}, bf16[80,2560]{1,0:T(8,128)(2,1)S(1)}, u32[]{:S(2)}, u32[]{:S(2)}) collective-permute-start(bf16[80,2560]{1,0:T(8,128)(2,1)S(1)} %bitcast.6), channel_id=1, source_target_pairs={{0,8},{8,16},{16,24},{24,0},{1,9},{9,17},{17,25},{25,1},{2,10},{10... | collective-permute-start | bytes 1228808 | tf_op jit(solution)/shard_map/ppermute | solution.py:275
  17.3 1.2 %collective-permute-start.8 = (bf16[160,2560]{1,0:T(8,128)(2,1)S(1)}, bf16[160,2560]{1,0:T(8,128)(2,1)S(1)}, u32[]{:S(2)}, u32[]{:S(2)}) collective-permute-start(bf16[160,2560]{1,0:T(8,128)(2,1)S(1)} %get-tuple-element.43.refs_2_), channel_id=1, source_target_pairs={{0,8},{8,16},{16,24},{24,0},{1,9},{9,17},{17,25},{25,1},{2,10},{10... | collective-permute-start | bytes 2457608 | tf_op jit(solution)/shard_map/ppermute | solution.py:275
  19.0 40.7 %all-gather.4 = f16[2624,640]{1,0:T(8,128)(2,1)S(1)} all-gather(f16[328,640]{1,0:T(8,128)(2,1)S(1)} %convert_element_type.12), channel_id=2, replica_groups=mesh['layer'=8,'y'=4,'z'=8] {'z'}, dimensions={0}, use_global_device_ids=true | all-gather | bytes 3778560 | tf_op jit(solution)/shard_map/all_gather | solution.py:303
  60.3 1.6 %reduced.1 = bf16[328,640]{1,0:T(8,128)(2,1)S(1)} custom-call(bf16[8,328,640]{2,1,0:T(8,128)(2,1)S(1)} %bitcast.3, bf16[80,2560]{1,0:T(8,128)(2,1)S(1)} %bitcast.7, bf16[80,2560]{1,0:T(8,128)(2,1)S(1)} %collective-permute-done.4.refs_1_, bf16[80,2560]{1,0:T(8,128)(2,1)S(1)} %collective-permute-done.5.refs_2_, ...), custom_call_target="tpu_custom_call" | custom-call | flops 1048576000 | bytes 6645760 | tf_op jit(solution)/shard_map/reduced/pallas_call | solution.py:20
  62.0 1.7 %collective-permute-start.7 = (bf16[240,2560]{1,0:T(8,128)(2,1)S(1)}, bf16[240,2560]{1,0:T(8,128)(2,1)S(1)}, u32[]{:S(2)}, u32[]{:S(2)}) collective-permute-start(bf16[240,2560]{1,0:T(8,128)(2,1)S(1)} %collective-permute-done.6.refs_3_.refs_2_), channel_id=1, source_target_pairs={{0,24},{8,0},{16,8},{24,16},{1,25},{9,1},{17,9},{25,17},{2,26},{10... | collective-permute-start | bytes 3686408 | tf_op jit(solution)/shard_map/ppermute | solution.py:275
  63.7 36.5 %all-gather.5 = f16[2624,640]{1,0:T(8,128)(2,1)S(1)} all-gather(f16[328,640]{1,0:T(8,128)(2,1)S(1)} %convert_element_type.14), channel_id=3, replica_groups=mesh['layer'=8,'y'=4,'z'=8] {'z'}, dimensions={0}, use_global_device_ids=true | all-gather | bytes 3778560 | tf_op jit(solution)/shard_map/all_gather | solution.py:303
  100.9 1.2 pushed_a.1
  102.1 1.9 %collective-permute-start.10 = (bf16[160,640]{1,0:T(8,128)(2,1)S(1)}, bf16[160,640]{1,0:T(8,128)(2,1)S(1)}, u32[]{:S(2)}, u32[]{:S(2)}) collective-permute-start(bf16[160,640]{1,0:T(8,128)(2,1)S(1)} %get-tuple-element.45), channel_id=1, source_target_pairs={{0,32},{32,64},{64,96},{96,128},{128,160},{160,192},{192,224},{1,3... | collective-permute-start | bytes 614408 | tf_op jit(solution)/shard_map/ppermute | solution.py:38
  104.0 1.1 pushed_b.1
  105.1 3.4 %collective-permute-start.9 = (bf16[160,640]{1,0:T(8,128)(2,1)S(1)}, bf16[160,640]{1,0:T(8,128)(2,1)S(1)}, u32[]{:S(2)}, u32[]{:S(2)}) collective-permute-start(bf16[160,640]{1,0:T(8,128)(2,1)S(1)} %pushed_b.1), channel_id=1, source_target_pairs={{0,32},{32,64},{64,96},{96,128},{128,160},{160,192},{192,224},{1,3... | collective-permute-start | bytes 614408 | tf_op jit(solution)/shard_map/ppermute | solution.py:38
  108.5 0.9 local_a.1.local_ref
  109.8 1.2 collective-permute-start.12
  110.9 1.2 %collective-permute-done.9.refs_4_ = bf16[160,640]{1,0:T(8,128)(2,1)S(1)} collective-permute-done((bf16[160,640]{1,0:T(8,128)(2,1)S(1)}, bf16[160,640]{1,0:T(8,128)(2,1)S(1)}, u32[]{:S(2)}, u32[]{:S(2)}) %collective-permute-start.9) | collective-permute-done | bytes 204832 | tf_op jit(solution)/shard_map/ppermute | solution.py:38
  112.1 0.9 update_b.1
  113.1 1.0 collective-permute-start.13
  114.1 2.9 %collective-permute-done.11.refs_1_ = bf16[80,640]{1,0:T(8,128)(2,1)S(1)} collective-permute-done((bf16[80,640]{1,0:T(8,128)(2,1)S(1)}, bf16[80,640]{1,0:T(8,128)(2,1)S(1)}, u32[]{:S(2)}, u32[]{:S(2)}) %collective-permute-start.11) | collective-permute-done | bytes 102432 | tf_op jit(solution)/shard_map/ppermute | solution.py:275
  117.1 1.0 collective-permute-done.12.refs_2_
  (23 shorter events, 4.5 us)
Async XLA Ops:
  0.0 12.8 %copy-start = (bf16[1,80,2560]{2,1,0:T(8,128)(2,1)S(1)}, bf16[1,80,2560]{2,1,0:T(8,128)(2,1)}, u32[]{:S(2)}) copy-start(bf16[1,80,2560]{2,1,0:T(8,128)(2,1)} %refs_0_.2) | copy-start | bytes 1228804
  1.1 8.3 %collective-permute-start = (bf16[80,640]{1,0:T(8,128)(2,1)S(1)}, bf16[80,640]{1,0:T(8,128)(2,1)S(1)}, u32[]{:S(2)}, u32[]{:S(2)}) collective-permute-start(bf16[80,640]{1,0:T(8,128)(2,1)S(1)} %get-tuple-element.28), channel_id=1, source_target_pairs={{0,16},{8,24},{16,0},{24,8},{1,17},{9,25},{17,1},{25,9},{2,18},{10... | collective-permute-start | bytes 307208 | tf_op jit(solution)/shard_map/ppermute | solution.py:275
  4.4 5.9 %collective-permute-start.1 = (bf16[80,640]{1,0:T(8,128)(2,1)S(1)}, bf16[80,640]{1,0:T(8,128)(2,1)S(1)}, u32[]{:S(2)}, u32[]{:S(2)}) collective-permute-start(bf16[80,640]{1,0:T(8,128)(2,1)S(1)} %get-tuple-element.29), channel_id=1, source_target_pairs={{0,8},{8,16},{16,24},{24,0},{1,9},{9,17},{17,25},{25,1},{2,10},{10... | collective-permute-start | bytes 307208 | tf_op jit(solution)/shard_map/ppermute | solution.py:275
  5.1 5.2 %collective-permute-start.2 = (bf16[80,640]{1,0:T(8,128)(2,1)S(1)}, bf16[80,640]{1,0:T(8,128)(2,1)S(1)}, u32[]{:S(2)}, u32[]{:S(2)}) collective-permute-start(bf16[80,640]{1,0:T(8,128)(2,1)S(1)} %get-tuple-element.30), channel_id=1, source_target_pairs={{0,24},{8,0},{16,8},{24,16},{1,25},{9,1},{17,9},{25,17},{2,26},{10... | collective-permute-start | bytes 307208 | tf_op jit(solution)/shard_map/ppermute | solution.py:275
  10.3 8.1 %collective-permute-start.3 = (bf16[320,640]{1,0:T(8,128)(2,1)S(1)}, bf16[320,640]{1,0:T(8,128)(2,1)S(1)}, u32[]{:S(2)}, u32[]{:S(2)}) collective-permute-start(bf16[320,640]{1,0:T(8,128)(2,1)S(1)} %stacked.1.refs_4_), channel_id=1, source_target_pairs={{32,0},{64,32},{96,64},{128,96},{160,128},{192,160},{224,192},{33,... | collective-permute-start | bytes 1228808 | tf_op jit(solution)/shard_map/ppermute | solution.py:38
  12.8 47.5 %collective-permute-start.4 = (bf16[80,2560]{1,0:T(8,128)(2,1)S(1)}, bf16[80,2560]{1,0:T(8,128)(2,1)S(1)}, u32[]{:S(2)}, u32[]{:S(2)}) collective-permute-start(bf16[80,2560]{1,0:T(8,128)(2,1)S(1)} %bitcast.5), channel_id=1, source_target_pairs={{0,16},{8,24},{16,0},{24,8},{1,17},{9,25},{17,1},{25,9},{2,18},{10... | collective-permute-start | bytes 1228808 | tf_op jit(solution)/shard_map/ppermute | solution.py:275
  14.0 46.3 %collective-permute-start.5 = (bf16[80,2560]{1,0:T(8,128)(2,1)S(1)}, bf16[80,2560]{1,0:T(8,128)(2,1)S(1)}, u32[]{:S(2)}, u32[]{:S(2)}) collective-permute-start(bf16[80,2560]{1,0:T(8,128)(2,1)S(1)} %bitcast.6), channel_id=1, source_target_pairs={{0,8},{8,16},{16,24},{24,0},{1,9},{9,17},{17,25},{25,1},{2,10},{10... | collective-permute-start | bytes 1228808 | tf_op jit(solution)/shard_map/ppermute | solution.py:275
  16.5 43.9 %collective-permute-start.6 = (bf16[240,2560]{1,0:T(8,128)(2,1)S(1)}, bf16[240,2560]{1,0:T(8,128)(2,1)S(1)}, u32[]{:S(2)}, u32[]{:S(2)}) collective-permute-start(bf16[240,2560]{1,0:T(8,128)(2,1)S(1)} %get-tuple-element.40), channel_id=1, source_target_pairs={{0,24},{8,0},{16,8},{24,16},{1,25},{9,1},{17,9},{25,17},{2,26},{10... | collective-permute-start | bytes 3686408 | tf_op jit(solution)/shard_map/ppermute | solution.py:275
  17.3 86.7 %collective-permute-start.8 = (bf16[160,2560]{1,0:T(8,128)(2,1)S(1)}, bf16[160,2560]{1,0:T(8,128)(2,1)S(1)}, u32[]{:S(2)}, u32[]{:S(2)}) collective-permute-start(bf16[160,2560]{1,0:T(8,128)(2,1)S(1)} %get-tuple-element.43.refs_2_), channel_id=1, source_target_pairs={{0,8},{8,16},{16,24},{24,0},{1,9},{9,17},{17,25},{25,1},{2,10},{10... | collective-permute-start | bytes 2457608 | tf_op jit(solution)/shard_map/ppermute | solution.py:275
  62.0 38.9 %collective-permute-start.7 = (bf16[240,2560]{1,0:T(8,128)(2,1)S(1)}, bf16[240,2560]{1,0:T(8,128)(2,1)S(1)}, u32[]{:S(2)}, u32[]{:S(2)}) collective-permute-start(bf16[240,2560]{1,0:T(8,128)(2,1)S(1)} %collective-permute-done.6.refs_3_.refs_2_), channel_id=1, source_target_pairs={{0,24},{8,0},{16,8},{24,16},{1,25},{9,1},{17,9},{25,17},{2,26},{10... | collective-permute-start | bytes 3686408 | tf_op jit(solution)/shard_map/ppermute | solution.py:275
  102.1 7.4 %collective-permute-start.10 = (bf16[160,640]{1,0:T(8,128)(2,1)S(1)}, bf16[160,640]{1,0:T(8,128)(2,1)S(1)}, u32[]{:S(2)}, u32[]{:S(2)}) collective-permute-start(bf16[160,640]{1,0:T(8,128)(2,1)S(1)} %get-tuple-element.45), channel_id=1, source_target_pairs={{0,32},{32,64},{64,96},{96,128},{128,160},{160,192},{192,224},{1,3... | collective-permute-start | bytes 614408 | tf_op jit(solution)/shard_map/ppermute | solution.py:38
  105.1 7.1 %collective-permute-start.9 = (bf16[160,640]{1,0:T(8,128)(2,1)S(1)}, bf16[160,640]{1,0:T(8,128)(2,1)S(1)}, u32[]{:S(2)}, u32[]{:S(2)}) collective-permute-start(bf16[160,640]{1,0:T(8,128)(2,1)S(1)} %pushed_b.1), channel_id=1, source_target_pairs={{0,32},{32,64},{64,96},{96,128},{128,160},{160,192},{192,224},{1,3... | collective-permute-start | bytes 614408 | tf_op jit(solution)/shard_map/ppermute | solution.py:38
  109.5 7.6 %collective-permute-start.11 = (bf16[80,640]{1,0:T(8,128)(2,1)S(1)}, bf16[80,640]{1,0:T(8,128)(2,1)S(1)}, u32[]{:S(2)}, u32[]{:S(2)}) collective-permute-start(bf16[80,640]{1,0:T(8,128)(2,1)S(1)} %get-tuple-element.46), channel_id=1, source_target_pairs={{0,16},{8,24},{16,0},{24,8},{1,17},{9,25},{17,1},{25,9},{2,18},{10... | collective-permute-start | bytes 307208 | tf_op jit(solution)/shard_map/ppermute | solution.py:275
  109.8 8.3 %collective-permute-start.12 = (bf16[80,640]{1,0:T(8,128)(2,1)S(1)}, bf16[80,640]{1,0:T(8,128)(2,1)S(1)}, u32[]{:S(2)}, u32[]{:S(2)}) collective-permute-start(bf16[80,640]{1,0:T(8,128)(2,1)S(1)} %get-tuple-element.47), channel_id=1, source_target_pairs={{0,8},{8,16},{16,24},{24,0},{1,9},{9,17},{17,25},{25,1},{2,10},{10... | collective-permute-start | bytes 307208 | tf_op jit(solution)/shard_map/ppermute | solution.py:275
  113.1 5.0 %collective-permute-start.13 = (bf16[80,640]{1,0:T(8,128)(2,1)S(1)}, bf16[80,640]{1,0:T(8,128)(2,1)S(1)}, u32[]{:S(2)}, u32[]{:S(2)}) collective-permute-start(bf16[80,640]{1,0:T(8,128)(2,1)S(1)} %get-tuple-element.48), channel_id=1, source_target_pairs={{0,24},{8,0},{16,8},{24,16},{1,25},{9,1},{17,9},{25,17},{2,26},{10... | collective-permute-start | bytes 307208 | tf_op jit(solution)/shard_map/ppermute | solution.py:275

commit v14 on v13

--- a/solution.py
+++ b/solution.py
@@ -312,8 +312,8 @@
     grads = [stacked(lax.optimization_barrier((*pieces, pair))[:shards], "stacked")]
     above = [hop_layer(grad, -1) for grad in grads]
     pair, trio, own = lax.optimization_barrier((pair, trio, in_coupling[0], *grads))[:3]
-    ahead, behind = hop_y(pair, 1), hop_y(trio, -1)
-    coupling = [own, hop_y(own, 2), hop_y(own, 1), behind]
+    ahead, behind = hop_y(trio, 1), hop_y(trio, -1)
+    coupling = [own, hop_y(own, 2), ahead, behind]
     near = near_tile(above, psi, shards)
     reduced = reduced_tile(gather_panel(near), coupling, grads, shards)
     factors = [pair, hop_y(behind, -1), ahead, behind]

time: 120 us -> 120 us (level)
  blocking collectives: 77.2 us -> 75.8 us
  waiting for transfers between devices: 6.06 us -> 7.43 us
    ppermute x3, waiting for transfers between devices: 1.21 us -> 2.59 us  [hop_layer(): lax.ppermute(x, 'layer', [(i, i + by) for i in range(size) if 0 <= i + by...]
    all_gather x2, blocking collectives: 77.2 us -> 75.8 us  [gather_panel(): return lax.all_gather(tile.astype(HALF), 'z', axis=0).astype(BF)]
    ppermute x11 -> x10, starting transfers between devices: 16.4 us -> 16.2 us  [hop_y(): return lax.ppermute(x, 'y', [(i, (i + by) % size) for i in range(size)])]
    ppermute x11 -> x10, waiting for transfers between devices: 4.85 us -> 4.84 us  [hop_y(): return lax.ppermute(x, 'y', [(i, (i + by) % size) for i in range(size)])]
  transfers between devices with their start and end apart: 14 -> 13, of which waited for: 4 -> 5; matrix products, arithmetic and copies ran while one was open for 1% -> 1% of each run, Pallas kernels for 7% -> 4%
where the time goes in v14:
time: 120 us; the launch traced here: 119 us
  blocking collectives  75.8 us (63%)
  starting transfers between devices  24 us (20%)
  Pallas kernels  9.84 us (8%)
  waiting for transfers between devices  7.43 us (6%)
  other arithmetic  1.42 us (1%)
    all_gather x2, blocking collectives, gather_panel(): return lax.all_gather(tile.astype(HALF), 'z', axis=0).astype(BF)  75.8 us
    ppermute x10, starting transfers between devices, hop_y(): return lax.ppermute(x, 'y', [(i, (i + by) % size) for i in range(size)])  16.2 us
    ppermute x3, starting transfers between devices, hop_layer(): lax.ppermute(x, 'layer', [(i, i + by) for i in range(size) if 0 <= i + by...  7.81 us
    pallas_call x8, Pallas kernels, call(): pl.pallas_call(kernel, out_shape=out, in_specs=[HBM if i in far else VMEM...  6.2 us
    ppermute x10, waiting for transfers between devices, hop_y(): return lax.ppermute(x, 'y', [(i, (i + by) % size) for i in range(size)])  4.84 us
    pallas_call x3, Pallas kernels, copies(): pl.pallas_call(body, out_shape=out, in_specs=[near] * len(operands), out_...  3.64 us
    ppermute x3, waiting for transfers between devices, hop_layer(): lax.ppermute(x, 'layer', [(i, i + by) for i in range(size) if 0 <= i + by...  2.59 us
  transfers between devices with their start and end apart: 13, of which 5 were waited for; matrix products, arithmetic and copies ran while one was open for 1% of the time, Pallas kernels for 4%

profile of v14, /device:TPU:2, one launch (start us, length us, event | category | flops | bytes accessed | tf_op | source)
XLA Modules:
  0.0 118.7 jit_solution(10668985162194874934)
XLA Ops:
  0.0 1.1 blocks.1
  1.1 3.3 %collective-permute-start = (bf16[80,640]{1,0:T(8,128)(2,1)S(1)}, bf16[80,640]{1,0:T(8,128)(2,1)S(1)}, u32[]{:S(2)}, u32[]{:S(2)}) collective-permute-start(bf16[80,640]{1,0:T(8,128)(2,1)S(1)} %get-tuple-element.28), channel_id=1, source_target_pairs={{0,16},{8,24},{16,0},{24,8},{1,17},{9,25},{17,1},{25,9},{2,18},{10... | collective-permute-start | bytes 307208 | tf_op jit(solution)/shard_map/ppermute | solution.py:275
  5.1 2.6 %collective-permute-start.2 = (bf16[80,640]{1,0:T(8,128)(2,1)S(1)}, bf16[80,640]{1,0:T(8,128)(2,1)S(1)}, u32[]{:S(2)}, u32[]{:S(2)}) collective-permute-start(bf16[80,640]{1,0:T(8,128)(2,1)S(1)} %get-tuple-element.30), channel_id=1, source_target_pairs={{0,24},{8,0},{16,8},{24,16},{1,25},{9,1},{17,9},{25,17},{2,26},{10... | collective-permute-start | bytes 307208 | tf_op jit(solution)/shard_map/ppermute | solution.py:275
  7.7 1.7 %operands.1 = (bf16[160,2560]{1,0:T(8,128)(2,1)S(1)}, bf16[240,2560]{1,0:T(8,128)(2,1)S(1)}, bf16[5,128,128]{2,1,0:T(8,128)(2,1)S(1)}, bf16[5,128,128]{2,1,0:T(8,128)(2,1)S(1)}) custom-call(bf16[1,80,2560]{2,1,0:T(8,128)(2,1)} %refs_0_.2, bf16[1,80,2560]{2,1,0:T(8,128)(2,1)} %refs_1_.1, bf16[1,80,2560]{2,1,0:T(8,128)(2,1)} %refs_2_.1, ...), custom_call_target="tpu_custom_call" | custom-call | bytes 4751360 | tf_op jit(solution)/shard_map/operands/pallas_call | solution.py:219
  9.4 0.9 collective-permute-done.1.refs_2_
  10.3 2.5 %collective-permute-start.3 = (bf16[320,640]{1,0:T(8,128)(2,1)S(1)}, bf16[320,640]{1,0:T(8,128)(2,1)S(1)}, u32[]{:S(2)}, u32[]{:S(2)}) collective-permute-start(bf16[320,640]{1,0:T(8,128)(2,1)S(1)} %stacked.1.refs_4_), channel_id=1, source_target_pairs={{32,0},{64,32},{96,64},{128,96},{160,128},{192,160},{224,192},{33,... | collective-permute-start | bytes 1228808 | tf_op jit(solution)/shard_map/ppermute | solution.py:38
  13.3 2.8 %collective-permute-start.6 = (bf16[240,2560]{1,0:T(8,128)(2,1)S(1)}, bf16[240,2560]{1,0:T(8,128)(2,1)S(1)}, u32[]{:S(2)}, u32[]{:S(2)}) collective-permute-start(bf16[240,2560]{1,0:T(8,128)(2,1)S(1)} %get-tuple-element.40), channel_id=1, source_target_pairs={{0,24},{8,0},{16,8},{24,16},{1,25},{9,1},{17,9},{25,17},{2,26},{10... | collective-permute-start | bytes 3686408 | tf_op jit(solution)/shard_map/ppermute | solution.py:275
  16.1 0.9 collective-permute-start.4
  17.0 1.2 %collective-permute-done.3.refs_0_ = bf16[320,640]{1,0:T(8,128)(2,1)S(1)} collective-permute-done((bf16[320,640]{1,0:T(8,128)(2,1)S(1)}, bf16[320,640]{1,0:T(8,128)(2,1)S(1)}, u32[]{:S(2)}, u32[]{:S(2)}) %collective-permute-start.3) | collective-permute-done | bytes 409632 | tf_op jit(solution)/shard_map/ppermute | solution.py:38
  18.7 39.3 %all-gather.4 = f16[2624,640]{1,0:T(8,128)(2,1)S(1)} all-gather(f16[328,640]{1,0:T(8,128)(2,1)S(1)} %convert_element_type.12), channel_id=2, replica_groups=mesh['layer'=8,'y'=4,'z'=8] {'z'}, dimensions={0}, use_global_device_ids=true | all-gather | bytes 3778560 | tf_op jit(solution)/shard_map/all_gather | solution.py:303
  58.7 1.6 %reduced.1 = bf16[328,640]{1,0:T(8,128)(2,1)S(1)} custom-call(bf16[8,328,640]{2,1,0:T(8,128)(2,1)S(1)} %bitcast.3, bf16[80,2560]{1,0:T(8,128)(2,1)S(1)} %bitcast.6, bf16[80,2560]{1,0:T(8,128)(2,1)S(1)} %collective-permute-done.4.refs_1_, bf16[240,2560]{1,0:T(8,128)(2,1)S(1)} %collective-permute-done.5.refs_2_.refs_1_, ...), custom_call_target="tpu_custom_call" | custom-call | flops 1048576000 | bytes 7464960 | tf_op jit(solution)/shard_map/reduced/pallas_call | solution.py:20
  60.4 3.3 %collective-permute-start.7 = (bf16[240,2560]{1,0:T(8,128)(2,1)S(1)}, bf16[240,2560]{1,0:T(8,128)(2,1)S(1)}, u32[]{:S(2)}, u32[]{:S(2)}) collective-permute-start(bf16[240,2560]{1,0:T(8,128)(2,1)S(1)} %collective-permute-done.6.refs_3_.refs_2_), channel_id=1, source_target_pairs={{0,24},{8,0},{16,8},{24,16},{1,25},{9,1},{17,9},{25,17},{2,26},{10... | collective-permute-start | bytes 3686408 | tf_op jit(solution)/shard_map/ppermute | solution.py:275
  63.7 36.5 %all-gather.5 = f16[2624,640]{1,0:T(8,128)(2,1)S(1)} all-gather(f16[328,640]{1,0:T(8,128)(2,1)S(1)} %convert_element_type.14), channel_id=3, replica_groups=mesh['layer'=8,'y'=4,'z'=8] {'z'}, dimensions={0}, use_global_device_ids=true | all-gather | bytes 3778560 | tf_op jit(solution)/shard_map/all_gather | solution.py:303
  100.9 1.2 pushed_a.1
  102.1 1.9 %collective-permute-start.9 = (bf16[160,640]{1,0:T(8,128)(2,1)S(1)}, bf16[160,640]{1,0:T(8,128)(2,1)S(1)}, u32[]{:S(2)}, u32[]{:S(2)}) collective-permute-start(bf16[160,640]{1,0:T(8,128)(2,1)S(1)} %get-tuple-element.45), channel_id=1, source_target_pairs={{0,32},{32,64},{64,96},{96,128},{128,160},{160,192},{192,224},{1,3... | collective-permute-start | bytes 614408 | tf_op jit(solution)/shard_map/ppermute | solution.py:38
  104.0 1.1 pushed_b.1
  105.1 3.4 %collective-permute-start.8 = (bf16[160,640]{1,0:T(8,128)(2,1)S(1)}, bf16[160,640]{1,0:T(8,128)(2,1)S(1)}, u32[]{:S(2)}, u32[]{:S(2)}) collective-permute-start(bf16[160,640]{1,0:T(8,128)(2,1)S(1)} %pushed_b.1), channel_id=1, source_target_pairs={{0,32},{32,64},{64,96},{96,128},{128,160},{160,192},{192,224},{1,3... | collective-permute-start | bytes 614408 | tf_op jit(solution)/shard_map/ppermute | solution.py:38
  108.5 0.9 local_a.1.local_ref
  109.6 1.2 collective-permute-start.11
  110.8 1.4 %collective-permute-done.8.refs_4_ = bf16[160,640]{1,0:T(8,128)(2,1)S(1)} collective-permute-done((bf16[160,640]{1,0:T(8,128)(2,1)S(1)}, bf16[160,640]{1,0:T(8,128)(2,1)S(1)}, u32[]{:S(2)}, u32[]{:S(2)}) %collective-permute-start.8) | collective-permute-done | bytes 204832 | tf_op jit(solution)/shard_map/ppermute | solution.py:38
  112.1 0.9 update_b.1
  113.1 0.9 collective-permute-start.12
  113.9 2.9 %collective-permute-done.10.refs_1_ = bf16[80,640]{1,0:T(8,128)(2,1)S(1)} collective-permute-done((bf16[80,640]{1,0:T(8,128)(2,1)S(1)}, bf16[80,640]{1,0:T(8,128)(2,1)S(1)}, u32[]{:S(2)}, u32[]{:S(2)}) %collective-permute-start.10) | collective-permute-done | bytes 102432 | tf_op jit(solution)/shard_map/ppermute | solution.py:275
  116.9 1.0 collective-permute-done.11.refs_2_
  (21 shorter events, 4.0 us)
Async XLA Ops:
  0.0 16.1 %copy-start = (bf16[1,80,2560]{2,1,0:T(8,128)(2,1)S(1)}, bf16[1,80,2560]{2,1,0:T(8,128)(2,1)}, u32[]{:S(2)}) copy-start(bf16[1,80,2560]{2,1,0:T(8,128)(2,1)} %refs_0_.2) | copy-start | bytes 1228804
  1.1 8.3 %collective-permute-start = (bf16[80,640]{1,0:T(8,128)(2,1)S(1)}, bf16[80,640]{1,0:T(8,128)(2,1)S(1)}, u32[]{:S(2)}, u32[]{:S(2)}) collective-permute-start(bf16[80,640]{1,0:T(8,128)(2,1)S(1)} %get-tuple-element.28), channel_id=1, source_target_pairs={{0,16},{8,24},{16,0},{24,8},{1,17},{9,25},{17,1},{25,9},{2,18},{10... | collective-permute-start | bytes 307208 | tf_op jit(solution)/shard_map/ppermute | solution.py:275
  4.4 5.9 %collective-permute-start.1 = (bf16[80,640]{1,0:T(8,128)(2,1)S(1)}, bf16[80,640]{1,0:T(8,128)(2,1)S(1)}, u32[]{:S(2)}, u32[]{:S(2)}) collective-permute-start(bf16[80,640]{1,0:T(8,128)(2,1)S(1)} %get-tuple-element.29), channel_id=1, source_target_pairs={{0,8},{8,16},{16,24},{24,0},{1,9},{9,17},{17,25},{25,1},{2,10},{10... | collective-permute-start | bytes 307208 | tf_op jit(solution)/shard_map/ppermute | solution.py:275
  5.1 5.2 %collective-permute-start.2 = (bf16[80,640]{1,0:T(8,128)(2,1)S(1)}, bf16[80,640]{1,0:T(8,128)(2,1)S(1)}, u32[]{:S(2)}, u32[]{:S(2)}) collective-permute-start(bf16[80,640]{1,0:T(8,128)(2,1)S(1)} %get-tuple-element.30), channel_id=1, source_target_pairs={{0,24},{8,0},{16,8},{24,16},{1,25},{9,1},{17,9},{25,17},{2,26},{10... | collective-permute-start | bytes 307208 | tf_op jit(solution)/shard_map/ppermute | solution.py:275
  10.3 7.9 %collective-permute-start.3 = (bf16[320,640]{1,0:T(8,128)(2,1)S(1)}, bf16[320,640]{1,0:T(8,128)(2,1)S(1)}, u32[]{:S(2)}, u32[]{:S(2)}) collective-permute-start(bf16[320,640]{1,0:T(8,128)(2,1)S(1)} %stacked.1.refs_4_), channel_id=1, source_target_pairs={{32,0},{64,32},{96,64},{128,96},{160,128},{192,160},{224,192},{33,... | collective-permute-start | bytes 1228808 | tf_op jit(solution)/shard_map/ppermute | solution.py:38
  12.8 45.9 %collective-permute-start.5 = (bf16[240,2560]{1,0:T(8,128)(2,1)S(1)}, bf16[240,2560]{1,0:T(8,128)(2,1)S(1)}, u32[]{:S(2)}, u32[]{:S(2)}) collective-permute-start(bf16[240,2560]{1,0:T(8,128)(2,1)S(1)} %get-tuple-element.40), channel_id=1, source_target_pairs={{0,8},{8,16},{16,24},{24,0},{1,9},{9,17},{17,25},{25,1},{2,10},{10... | collective-permute-start | bytes 3686408 | tf_op jit(solution)/shard_map/ppermute | solution.py:275
  13.3 45.4 %collective-permute-start.6 = (bf16[240,2560]{1,0:T(8,128)(2,1)S(1)}, bf16[240,2560]{1,0:T(8,128)(2,1)S(1)}, u32[]{:S(2)}, u32[]{:S(2)}) collective-permute-start(bf16[240,2560]{1,0:T(8,128)(2,1)S(1)} %get-tuple-element.40), channel_id=1, source_target_pairs={{0,24},{8,0},{16,8},{24,16},{1,25},{9,1},{17,9},{25,17},{2,26},{10... | collective-permute-start | bytes 3686408 | tf_op jit(solution)/shard_map/ppermute | solution.py:275
  16.1 42.6 %collective-permute-start.4 = (bf16[80,2560]{1,0:T(8,128)(2,1)S(1)}, bf16[80,2560]{1,0:T(8,128)(2,1)S(1)}, u32[]{:S(2)}, u32[]{:S(2)}) collective-permute-start(bf16[80,2560]{1,0:T(8,128)(2,1)S(1)} %bitcast.5), channel_id=1, source_target_pairs={{0,16},{8,24},{16,0},{24,8},{1,17},{9,25},{17,1},{25,9},{2,18},{10... | collective-permute-start | bytes 1228808 | tf_op jit(solution)/shard_map/ppermute | solution.py:275
  60.4 40.5 %collective-permute-start.7 = (bf16[240,2560]{1,0:T(8,128)(2,1)S(1)}, bf16[240,2560]{1,0:T(8,128)(2,1)S(1)}, u32[]{:S(2)}, u32[]{:S(2)}) collective-permute-start(bf16[240,2560]{1,0:T(8,128)(2,1)S(1)} %collective-permute-done.6.refs_3_.refs_2_), channel_id=1, source_target_pairs={{0,24},{8,0},{16,8},{24,16},{1,25},{9,1},{17,9},{25,17},{2,26},{10... | collective-permute-start | bytes 3686408 | tf_op jit(solution)/shard_map/ppermute | solution.py:275
  102.1 7.4 %collective-permute-start.9 = (bf16[160,640]{1,0:T(8,128)(2,1)S(1)}, bf16[160,640]{1,0:T(8,128)(2,1)S(1)}, u32[]{:S(2)}, u32[]{:S(2)}) collective-permute-start(bf16[160,640]{1,0:T(8,128)(2,1)S(1)} %get-tuple-element.45), channel_id=1, source_target_pairs={{0,32},{32,64},{64,96},{96,128},{128,160},{160,192},{192,224},{1,3... | collective-permute-start | bytes 614408 | tf_op jit(solution)/shard_map/ppermute | solution.py:38
  105.1 7.1 %collective-permute-start.8 = (bf16[160,640]{1,0:T(8,128)(2,1)S(1)}, bf16[160,640]{1,0:T(8,128)(2,1)S(1)}, u32[]{:S(2)}, u32[]{:S(2)}) collective-permute-start(bf16[160,640]{1,0:T(8,128)(2,1)S(1)} %pushed_b.1), channel_id=1, source_target_pairs={{0,32},{32,64},{64,96},{96,128},{128,160},{160,192},{192,224},{1,3... | collective-permute-start | bytes 614408 | tf_op jit(solution)/shard_map/ppermute | solution.py:38
  109.5 7.4 %collective-permute-start.10 = (bf16[80,640]{1,0:T(8,128)(2,1)S(1)}, bf16[80,640]{1,0:T(8,128)(2,1)S(1)}, u32[]{:S(2)}, u32[]{:S(2)}) collective-permute-start(bf16[80,640]{1,0:T(8,128)(2,1)S(1)} %get-tuple-element.46), channel_id=1, source_target_pairs={{0,16},{8,24},{16,0},{24,8},{1,17},{9,25},{17,1},{25,9},{2,18},{10... | collective-permute-start | bytes 307208 | tf_op jit(solution)/shard_map/ppermute | solution.py:275
  109.6 8.3 %collective-permute-start.11 = (bf16[80,640]{1,0:T(8,128)(2,1)S(1)}, bf16[80,640]{1,0:T(8,128)(2,1)S(1)}, u32[]{:S(2)}, u32[]{:S(2)}) collective-permute-start(bf16[80,640]{1,0:T(8,128)(2,1)S(1)} %get-tuple-element.47), channel_id=1, source_target_pairs={{0,8},{8,16},{16,24},{24,0},{1,9},{9,17},{17,25},{25,1},{2,10},{10... | collective-permute-start | bytes 307208 | tf_op jit(solution)/shard_map/ppermute | solution.py:275
  113.1 4.8 %collective-permute-start.12 = (bf16[80,640]{1,0:T(8,128)(2,1)S(1)}, bf16[80,640]{1,0:T(8,128)(2,1)S(1)}, u32[]{:S(2)}, u32[]{:S(2)}) collective-permute-start(bf16[80,640]{1,0:T(8,128)(2,1)S(1)} %get-tuple-element.48), channel_id=1, source_target_pairs={{0,24},{8,0},{16,8},{24,16},{1,25},{9,1},{17,9},{25,17},{2,26},{10... | collective-permute-start | bytes 307208 | tf_op jit(solution)/shard_map/ppermute | solution.py:275

commit v15 on v14

--- a/solution.py
+++ b/solution.py
@@ -316,7 +316,7 @@
     coupling = [own, hop_y(own, 2), ahead, behind]
     near = near_tile(above, psi, shards)
     reduced = reduced_tile(gather_panel(near), coupling, grads, shards)
-    factors = [pair, hop_y(behind, -1), ahead, behind]
+    factors = [pair, hop_y(pair, 2), ahead, behind]
     early, late = halves_of(factors)
     rows = own.shape[0]
     pushed_a, panel = product_rows(gather_panel(reduced), early, [inv, psi], rows, 1, BF, "pushed_a", shards)

time: 120 us -> 132 us (1.10)
  waiting for transfers between devices: 7.43 us -> 12.3 us
  blocking collectives: 75.8 us -> 80.2 us
  starting transfers between devices: 24 us -> 27.5 us
    ppermute x10, waiting for transfers between devices: 4.84 us -> 12.3 us  [hop_y(): return lax.ppermute(x, 'y', [(i, (i + by) % size) for i in range(size)])]
    all_gather x2, blocking collectives: 75.8 us -> 80.2 us  [gather_panel(): return lax.all_gather(tile.astype(HALF), 'z', axis=0).astype(BF)]
    ppermute x10, starting transfers between devices: 16.2 us -> 19.6 us  [hop_y(): return lax.ppermute(x, 'y', [(i, (i + by) % size) for i in range(size)])]
    ppermute x3, waiting for transfers between devices: 2.59 us -> 0.01 us  [hop_layer(): lax.ppermute(x, 'layer', [(i, i + by) for i in range(size) if 0 <= i + by...]
  transfers between devices with their start and end apart: 13 -> 13, of which waited for: 5 -> 4; matrix products, arithmetic and copies ran while one was open for 1% -> 1% of each run, Pallas kernels for 4% -> 5%
where the time goes in v15:
time: 132 us; the launch traced here: 131 us
  blocking collectives  80.2 us (61%)
  starting transfers between devices  27.5 us (21%)
  waiting for transfers between devices  12.3 us (9%)
  Pallas kernels  9.82 us (7%)
  other arithmetic  1.42 us (1%)
    all_gather x2, blocking collectives, gather_panel(): return lax.all_gather(tile.astype(HALF), 'z', axis=0).astype(BF)  80.2 us
    ppermute x10, starting transfers between devices, hop_y(): return lax.ppermute(x, 'y', [(i, (i + by) % size) for i in range(size)])  19.6 us
    ppermute x10, waiting for transfers between devices, hop_y(): return lax.ppermute(x, 'y', [(i, (i + by) % size) for i in range(size)])  12.3 us
    ppermute x3, starting transfers between devices, hop_layer(): lax.ppermute(x, 'layer', [(i, i + by) for i in range(size) if 0 <= i + by...  7.88 us
    pallas_call x8, Pallas kernels, call(): pl.pallas_call(kernel, out_shape=out, in_specs=[HBM if i in far else VMEM...  6.18 us
    pallas_call x3, Pallas kernels, copies(): pl.pallas_call(body, out_shape=out, in_specs=[near] * len(operands), out_...  3.64 us
  transfers between devices with their start and end apart: 13, of which 4 were waited for; matrix products, arithmetic and copies ran while one was open for 1% of the time, Pallas kernels for 5%

profile of v15, /device:TPU:2, one launch (start us, length us, event | category | flops | bytes accessed | tf_op | source)
XLA Modules:
  0.0 131.3 jit_solution(5024895844683474151)
XLA Ops:
  0.0 1.1 blocks.1
  1.1 3.3 %collective-permute-start = (bf16[80,640]{1,0:T(8,128)(2,1)S(1)}, bf16[80,640]{1,0:T(8,128)(2,1)S(1)}, u32[]{:S(2)}, u32[]{:S(2)}) collective-permute-start(bf16[80,640]{1,0:T(8,128)(2,1)S(1)} %get-tuple-element.28), channel_id=1, source_target_pairs={{0,16},{8,24},{16,0},{24,8},{1,17},{9,25},{17,1},{25,9},{2,18},{10... | collective-permute-start | bytes 307208 | tf_op jit(solution)/shard_map/ppermute | solution.py:275
  5.1 2.6 %collective-permute-start.2 = (bf16[80,640]{1,0:T(8,128)(2,1)S(1)}, bf16[80,640]{1,0:T(8,128)(2,1)S(1)}, u32[]{:S(2)}, u32[]{:S(2)}) collective-permute-start(bf16[80,640]{1,0:T(8,128)(2,1)S(1)} %get-tuple-element.30), channel_id=1, source_target_pairs={{0,24},{8,0},{16,8},{24,16},{1,25},{9,1},{17,9},{25,17},{2,26},{10... | collective-permute-start | bytes 307208 | tf_op jit(solution)/shard_map/ppermute | solution.py:275
  7.7 1.7 %operands.1 = (bf16[160,2560]{1,0:T(8,128)(2,1)S(1)}, bf16[240,2560]{1,0:T(8,128)(2,1)S(1)}, bf16[5,128,128]{2,1,0:T(8,128)(2,1)S(1)}, bf16[5,128,128]{2,1,0:T(8,128)(2,1)S(1)}) custom-call(bf16[1,80,2560]{2,1,0:T(8,128)(2,1)} %refs_0_.2, bf16[1,80,2560]{2,1,0:T(8,128)(2,1)} %refs_1_.1, bf16[1,80,2560]{2,1,0:T(8,128)(2,1)} %refs_2_.1, ...), custom_call_target="tpu_custom_call" | custom-call | bytes 4751360 | tf_op jit(solution)/shard_map/operands/pallas_call | solution.py:219
  9.4 0.9 collective-permute-done.1.refs_2_
  10.3 2.5 %collective-permute-start.3 = (bf16[320,640]{1,0:T(8,128)(2,1)S(1)}, bf16[320,640]{1,0:T(8,128)(2,1)S(1)}, u32[]{:S(2)}, u32[]{:S(2)}) collective-permute-start(bf16[320,640]{1,0:T(8,128)(2,1)S(1)} %stacked.1.refs_4_), channel_id=1, source_target_pairs={{32,0},{64,32},{96,64},{128,96},{160,128},{192,160},{224,192},{33,... | collective-permute-start | bytes 1228808 | tf_op jit(solution)/shard_map/ppermute | solution.py:38
  13.3 2.8 %collective-permute-start.6 = (bf16[240,2560]{1,0:T(8,128)(2,1)S(1)}, bf16[240,2560]{1,0:T(8,128)(2,1)S(1)}, u32[]{:S(2)}, u32[]{:S(2)}) collective-permute-start(bf16[240,2560]{1,0:T(8,128)(2,1)S(1)} %get-tuple-element.40), channel_id=1, source_target_pairs={{0,24},{8,0},{16,8},{24,16},{1,25},{9,1},{17,9},{25,17},{2,26},{10... | collective-permute-start | bytes 3686408 | tf_op jit(solution)/shard_map/ppermute | solution.py:275
  16.1 0.9 collective-permute-start.4
  17.0 2.6 %collective-permute-start.7 = (bf16[160,2560]{1,0:T(8,128)(2,1)S(1)}, bf16[160,2560]{1,0:T(8,128)(2,1)S(1)}, u32[]{:S(2)}, u32[]{:S(2)}) collective-permute-start(bf16[160,2560]{1,0:T(8,128)(2,1)S(1)} %get-tuple-element.41.refs_2_), channel_id=1, source_target_pairs={{0,16},{8,24},{16,0},{24,8},{1,17},{9,25},{17,1},{25,9},{2,18},{10... | collective-permute-start | bytes 2457608 | tf_op jit(solution)/shard_map/ppermute | solution.py:275
  20.1 39.9 %all-gather.4 = f16[2624,640]{1,0:T(8,128)(2,1)S(1)} all-gather(f16[328,640]{1,0:T(8,128)(2,1)S(1)} %convert_element_type.12), channel_id=2, replica_groups=mesh['layer'=8,'y'=4,'z'=8] {'z'}, dimensions={0}, use_global_device_ids=true | all-gather | bytes 3778560 | tf_op jit(solution)/shard_map/all_gather | solution.py:303
  60.7 8.3 %collective-permute-done.6.refs_3_.refs_2_ = bf16[240,2560]{1,0:T(8,128)(2,1)S(1)} collective-permute-done((bf16[240,2560]{1,0:T(8,128)(2,1)S(1)}, bf16[240,2560]{1,0:T(8,128)(2,1)S(1)}, u32[]{:S(2)}, u32[]{:S(2)}) %collective-permute-start.6) | collective-permute-done | bytes 1228832 | tf_op jit(solution)/shard_map/ppermute | solution.py:275
  69.0 1.6 %reduced.1 = bf16[328,640]{1,0:T(8,128)(2,1)S(1)} custom-call(bf16[8,328,640]{2,1,0:T(8,128)(2,1)S(1)} %bitcast.3, bf16[80,2560]{1,0:T(8,128)(2,1)S(1)} %bitcast.6, bf16[80,2560]{1,0:T(8,128)(2,1)S(1)} %collective-permute-done.4.refs_1_, bf16[240,2560]{1,0:T(8,128)(2,1)S(1)} %collective-permute-done.5.refs_2_.refs_1_, ...), custom_call_target="tpu_custom_call" | custom-call | flops 1048576000 | bytes 7464960 | tf_op jit(solution)/shard_map/reduced/pallas_call | solution.py:20
  70.7 40.3 %all-gather.5 = f16[2624,640]{1,0:T(8,128)(2,1)S(1)} all-gather(f16[328,640]{1,0:T(8,128)(2,1)S(1)} %convert_element_type.14), channel_id=3, replica_groups=mesh['layer'=8,'y'=4,'z'=8] {'z'}, dimensions={0}, use_global_device_ids=true | all-gather | bytes 3778560 | tf_op jit(solution)/shard_map/all_gather | solution.py:303
  111.6 1.2 pushed_a.1
  112.8 1.9 %collective-permute-start.9 = (bf16[160,640]{1,0:T(8,128)(2,1)S(1)}, bf16[160,640]{1,0:T(8,128)(2,1)S(1)}, u32[]{:S(2)}, u32[]{:S(2)}) collective-permute-start(bf16[160,640]{1,0:T(8,128)(2,1)S(1)} %get-tuple-element.45), channel_id=1, source_target_pairs={{0,32},{32,64},{64,96},{96,128},{128,160},{160,192},{192,224},{1,3... | collective-permute-start | bytes 614408 | tf_op jit(solution)/shard_map/ppermute | solution.py:38
  114.7 1.1 pushed_b.1
  115.8 3.5 %collective-permute-start.8 = (bf16[160,640]{1,0:T(8,128)(2,1)S(1)}, bf16[160,640]{1,0:T(8,128)(2,1)S(1)}, u32[]{:S(2)}, u32[]{:S(2)}) collective-permute-start(bf16[160,640]{1,0:T(8,128)(2,1)S(1)} %pushed_b.1), channel_id=1, source_target_pairs={{0,32},{32,64},{64,96},{96,128},{128,160},{160,192},{192,224},{1,3... | collective-permute-start | bytes 614408 | tf_op jit(solution)/shard_map/ppermute | solution.py:38
  119.3 0.9 local_a.1.local_ref
  120.4 4.5 %collective-permute-start.11 = (bf16[80,640]{1,0:T(8,128)(2,1)S(1)}, bf16[80,640]{1,0:T(8,128)(2,1)S(1)}, u32[]{:S(2)}, u32[]{:S(2)}) collective-permute-start(bf16[80,640]{1,0:T(8,128)(2,1)S(1)} %get-tuple-element.47), channel_id=1, source_target_pairs={{0,8},{8,16},{16,24},{24,0},{1,9},{9,17},{17,25},{25,1},{2,10},{10... | collective-permute-start | bytes 307208 | tf_op jit(solution)/shard_map/ppermute | solution.py:275
  124.8 0.9 update_b.1
  125.8 1.7 %collective-permute-start.12 = (bf16[80,640]{1,0:T(8,128)(2,1)S(1)}, bf16[80,640]{1,0:T(8,128)(2,1)S(1)}, u32[]{:S(2)}, u32[]{:S(2)}) collective-permute-start(bf16[80,640]{1,0:T(8,128)(2,1)S(1)} %get-tuple-element.48), channel_id=1, source_target_pairs={{0,24},{8,0},{16,8},{24,16},{1,25},{9,1},{17,9},{25,17},{2,26},{10... | collective-permute-start | bytes 307208 | tf_op jit(solution)/shard_map/ppermute | solution.py:275
  127.5 1.4 %collective-permute-done.11.refs_2_ = bf16[80,640]{1,0:T(8,128)(2,1)S(1)} collective-permute-done((bf16[80,640]{1,0:T(8,128)(2,1)S(1)}, bf16[80,640]{1,0:T(8,128)(2,1)S(1)}, u32[]{:S(2)}, u32[]{:S(2)}) %collective-permute-start.11) | collective-permute-done | bytes 102432 | tf_op jit(solution)/shard_map/ppermute | solution.py:275
  128.9 1.7 %collective-permute-done.12.refs_3_ = bf16[80,640]{1,0:T(8,128)(2,1)S(1)} collective-permute-done((bf16[80,640]{1,0:T(8,128)(2,1)S(1)}, bf16[80,640]{1,0:T(8,128)(2,1)S(1)}, u32[]{:S(2)}, u32[]{:S(2)}) %collective-permute-start.12) | collective-permute-done | bytes 102432 | tf_op jit(solution)/shard_map/ppermute | solution.py:275
  130.5 0.8 join.1
  (21 shorter events, 3.2 us)
Async XLA Ops:
  0.0 16.1 %copy-start = (bf16[1,80,2560]{2,1,0:T(8,128)(2,1)S(1)}, bf16[1,80,2560]{2,1,0:T(8,128)(2,1)}, u32[]{:S(2)}) copy-start(bf16[1,80,2560]{2,1,0:T(8,128)(2,1)} %refs_0_.2) | copy-start | bytes 1228804
  1.1 8.3 %collective-permute-start = (bf16[80,640]{1,0:T(8,128)(2,1)S(1)}, bf16[80,640]{1,0:T(8,128)(2,1)S(1)}, u32[]{:S(2)}, u32[]{:S(2)}) collective-permute-start(bf16[80,640]{1,0:T(8,128)(2,1)S(1)} %get-tuple-element.28), channel_id=1, source_target_pairs={{0,16},{8,24},{16,0},{24,8},{1,17},{9,25},{17,1},{25,9},{2,18},{10... | collective-permute-start | bytes 307208 | tf_op jit(solution)/shard_map/ppermute | solution.py:275
  4.4 5.9 %collective-permute-start.1 = (bf16[80,640]{1,0:T(8,128)(2,1)S(1)}, bf16[80,640]{1,0:T(8,128)(2,1)S(1)}, u32[]{:S(2)}, u32[]{:S(2)}) collective-permute-start(bf16[80,640]{1,0:T(8,128)(2,1)S(1)} %get-tuple-element.29), channel_id=1, source_target_pairs={{0,8},{8,16},{16,24},{24,0},{1,9},{9,17},{17,25},{25,1},{2,10},{10... | collective-permute-start | bytes 307208 | tf_op jit(solution)/shard_map/ppermute | solution.py:275
  5.1 5.2 %collective-permute-start.2 = (bf16[80,640]{1,0:T(8,128)(2,1)S(1)}, bf16[80,640]{1,0:T(8,128)(2,1)S(1)}, u32[]{:S(2)}, u32[]{:S(2)}) collective-permute-start(bf16[80,640]{1,0:T(8,128)(2,1)S(1)} %get-tuple-element.30), channel_id=1, source_target_pairs={{0,24},{8,0},{16,8},{24,16},{1,25},{9,1},{17,9},{25,17},{2,26},{10... | collective-permute-start | bytes 307208 | tf_op jit(solution)/shard_map/ppermute | solution.py:275
  10.3 9.3 %collective-permute-start.3 = (bf16[320,640]{1,0:T(8,128)(2,1)S(1)}, bf16[320,640]{1,0:T(8,128)(2,1)S(1)}, u32[]{:S(2)}, u32[]{:S(2)}) collective-permute-start(bf16[320,640]{1,0:T(8,128)(2,1)S(1)} %stacked.1.refs_4_), channel_id=1, source_target_pairs={{32,0},{64,32},{96,64},{128,96},{160,128},{192,160},{224,192},{33,... | collective-permute-start | bytes 1228808 | tf_op jit(solution)/shard_map/ppermute | solution.py:38
  12.8 47.9 %collective-permute-start.5 = (bf16[240,2560]{1,0:T(8,128)(2,1)S(1)}, bf16[240,2560]{1,0:T(8,128)(2,1)S(1)}, u32[]{:S(2)}, u32[]{:S(2)}) collective-permute-start(bf16[240,2560]{1,0:T(8,128)(2,1)S(1)} %get-tuple-element.40), channel_id=1, source_target_pairs={{0,8},{8,16},{16,24},{24,0},{1,9},{9,17},{17,25},{25,1},{2,10},{10... | collective-permute-start | bytes 3686408 | tf_op jit(solution)/shard_map/ppermute | solution.py:275
  13.3 55.6 %collective-permute-start.6 = (bf16[240,2560]{1,0:T(8,128)(2,1)S(1)}, bf16[240,2560]{1,0:T(8,128)(2,1)S(1)}, u32[]{:S(2)}, u32[]{:S(2)}) collective-permute-start(bf16[240,2560]{1,0:T(8,128)(2,1)S(1)} %get-tuple-element.40), channel_id=1, source_target_pairs={{0,24},{8,0},{16,8},{24,16},{1,25},{9,1},{17,9},{25,17},{2,26},{10... | collective-permute-start | bytes 3686408 | tf_op jit(solution)/shard_map/ppermute | solution.py:275
  16.1 44.5 %collective-permute-start.4 = (bf16[80,2560]{1,0:T(8,128)(2,1)S(1)}, bf16[80,2560]{1,0:T(8,128)(2,1)S(1)}, u32[]{:S(2)}, u32[]{:S(2)}) collective-permute-start(bf16[80,2560]{1,0:T(8,128)(2,1)S(1)} %bitcast.5), channel_id=1, source_target_pairs={{0,16},{8,24},{16,0},{24,8},{1,17},{9,25},{17,1},{25,9},{2,18},{10... | collective-permute-start | bytes 1228808 | tf_op jit(solution)/shard_map/ppermute | solution.py:275
  17.0 94.6 %collective-permute-start.7 = (bf16[160,2560]{1,0:T(8,128)(2,1)S(1)}, bf16[160,2560]{1,0:T(8,128)(2,1)S(1)}, u32[]{:S(2)}, u32[]{:S(2)}) collective-permute-start(bf16[160,2560]{1,0:T(8,128)(2,1)S(1)} %get-tuple-element.41.refs_2_), channel_id=1, source_target_pairs={{0,16},{8,24},{16,0},{24,8},{1,17},{9,25},{17,1},{25,9},{2,18},{10... | collective-permute-start | bytes 2457608 | tf_op jit(solution)/shard_map/ppermute | solution.py:275
  112.8 7.5 %collective-permute-start.9 = (bf16[160,640]{1,0:T(8,128)(2,1)S(1)}, bf16[160,640]{1,0:T(8,128)(2,1)S(1)}, u32[]{:S(2)}, u32[]{:S(2)}) collective-permute-start(bf16[160,640]{1,0:T(8,128)(2,1)S(1)} %get-tuple-element.45), channel_id=1, source_target_pairs={{0,32},{32,64},{64,96},{96,128},{128,160},{160,192},{192,224},{1,3... | collective-permute-start | bytes 614408 | tf_op jit(solution)/shard_map/ppermute | solution.py:38
  115.8 9.1 %collective-permute-start.8 = (bf16[160,640]{1,0:T(8,128)(2,1)S(1)}, bf16[160,640]{1,0:T(8,128)(2,1)S(1)}, u32[]{:S(2)}, u32[]{:S(2)}) collective-permute-start(bf16[160,640]{1,0:T(8,128)(2,1)S(1)} %pushed_b.1), channel_id=1, source_target_pairs={{0,32},{32,64},{64,96},{96,128},{128,160},{160,192},{192,224},{1,3... | collective-permute-start | bytes 614408 | tf_op jit(solution)/shard_map/ppermute | solution.py:38
  120.3 7.2 %collective-permute-start.10 = (bf16[80,640]{1,0:T(8,128)(2,1)S(1)}, bf16[80,640]{1,0:T(8,128)(2,1)S(1)}, u32[]{:S(2)}, u32[]{:S(2)}) collective-permute-start(bf16[80,640]{1,0:T(8,128)(2,1)S(1)} %get-tuple-element.46), channel_id=1, source_target_pairs={{0,16},{8,24},{16,0},{24,8},{1,17},{9,25},{17,1},{25,9},{2,18},{10... | collective-permute-start | bytes 307208 | tf_op jit(solution)/shard_map/ppermute | solution.py:275
  120.4 8.5 %collective-permute-start.11 = (bf16[80,640]{1,0:T(8,128)(2,1)S(1)}, bf16[80,640]{1,0:T(8,128)(2,1)S(1)}, u32[]{:S(2)}, u32[]{:S(2)}) collective-permute-start(bf16[80,640]{1,0:T(8,128)(2,1)S(1)} %get-tuple-element.47), channel_id=1, source_target_pairs={{0,8},{8,16},{16,24},{24,0},{1,9},{9,17},{17,25},{25,1},{2,10},{10... | collective-permute-start | bytes 307208 | tf_op jit(solution)/shard_map/ppermute | solution.py:275
  125.8 4.7 %collective-permute-start.12 = (bf16[80,640]{1,0:T(8,128)(2,1)S(1)}, bf16[80,640]{1,0:T(8,128)(2,1)S(1)}, u32[]{:S(2)}, u32[]{:S(2)}) collective-permute-start(bf16[80,640]{1,0:T(8,128)(2,1)S(1)} %get-tuple-element.48), channel_id=1, source_target_pairs={{0,24},{8,0},{16,8},{24,16},{1,25},{9,1},{17,9},{25,17},{2,26},{10... | collective-permute-start | bytes 307208 | tf_op jit(solution)/shard_map/ppermute | solution.py:275

commit v16 on v14

--- a/solution.py
+++ b/solution.py
@@ -309,7 +309,8 @@
     pieces = exchange(slices)
     first = after(in_coupling, slices[0])
     pair, trio, inv, psi = operands(first, in_inverse, in_carry, out_inverse, out_coupling, shards)
-    grads = [stacked(lax.optimization_barrier((*pieces, pair))[:shards], "stacked")]
+    half = shards // 2
+    grads = [stacked(lax.optimization_barrier((*pieces[:half], pair))[:half], "early"), stacked(pieces[half:], "late")]
     above = [hop_layer(grad, -1) for grad in grads]
     pair, trio, own = lax.optimization_barrier((pair, trio, in_coupling[0], *grads))[:3]
     ahead, behind = hop_y(trio, 1), hop_y(trio, -1)

time: 120 us -> 119 us (level)
  waiting for transfers between devices: 7.43 us -> 2.28 us
  starting transfers between devices: 24 us -> 26.9 us
  blocking collectives: 75.8 us -> 77 us
    ppermute x3 -> x4, waiting for transfers between devices: 2.59 us -> 0.01 us  [hop_layer(): lax.ppermute(x, 'layer', [(i, i + by) for i in range(size) if 0 <= i + by...]
    ppermute x10, waiting for transfers between devices: 4.84 us -> 2.27 us  [hop_y(): return lax.ppermute(x, 'y', [(i, (i + by) % size) for i in range(size)])]
    ppermute x3 -> x4, starting transfers between devices: 7.81 us -> 9.88 us  [hop_layer(): lax.ppermute(x, 'layer', [(i, i + by) for i in range(size) if 0 <= i + by...]
    pallas_call x8 -> x9, Pallas kernels: 6.2 us -> 6.25 us  [call(): pl.pallas_call(kernel, out_shape=out, in_specs=[HBM if i in far else VMEM...]
  transfers between devices with their start and end apart: 13 -> 14, of which waited for: 5 -> 2; matrix products, arithmetic and copies ran while one was open for 1% -> 1% of each run, Pallas kernels for 4% -> 4%
where the time goes in v16:
time: 119 us; the launch traced here: 118 us
  blocking collectives  77 us (65%)
  starting transfers between devices  26.9 us (23%)
  Pallas kernels  9.89 us (8%)
  waiting for transfers between devices  2.28 us (2%)
  other arithmetic  1.4 us (1%)
    all_gather x2, blocking collectives, gather_panel(): return lax.all_gather(tile.astype(HALF), 'z', axis=0).astype(BF)  77 us
    ppermute x10, starting transfers between devices, hop_y(): return lax.ppermute(x, 'y', [(i, (i + by) % size) for i in range(size)])  17.1 us
    ppermute x4, starting transfers between devices, hop_layer(): lax.ppermute(x, 'layer', [(i, i + by) for i in range(size) if 0 <= i + by...  9.88 us
    pallas_call x9, Pallas kernels, call(): pl.pallas_call(kernel, out_shape=out, in_specs=[HBM if i in far else VMEM...  6.25 us
    pallas_call x3, Pallas kernels, copies(): pl.pallas_call(body, out_shape=out, in_specs=[near] * len(operands), out_...  3.64 us
  transfers between devices with their start and end apart: 14, of which 2 were waited for; matrix products, arithmetic and copies ran while one was open for 1% of the time, Pallas kernels for 4%

profile of v16, /device:TPU:2, one launch (start us, length us, event | category | flops | bytes accessed | tf_op | source)
XLA Modules:
  0.0 117.7 jit_solution(10253899780950917637)
XLA Ops:
  0.0 1.1 blocks.1
  1.1 3.3 %collective-permute-start = (bf16[80,640]{1,0:T(8,128)(2,1)S(1)}, bf16[80,640]{1,0:T(8,128)(2,1)S(1)}, u32[]{:S(2)}, u32[]{:S(2)}) collective-permute-start(bf16[80,640]{1,0:T(8,128)(2,1)S(1)} %get-tuple-element.26), channel_id=1, source_target_pairs={{0,16},{8,24},{16,0},{24,8},{1,17},{9,25},{17,1},{25,9},{2,18},{10... | collective-permute-start | bytes 307208 | tf_op jit(solution)/shard_map/ppermute | solution.py:275
  4.4 0.7 collective-permute-start.2
  5.1 2.6 %collective-permute-start.3 = (bf16[80,640]{1,0:T(8,128)(2,1)S(1)}, bf16[80,640]{1,0:T(8,128)(2,1)S(1)}, u32[]{:S(2)}, u32[]{:S(2)}) collective-permute-start(bf16[80,640]{1,0:T(8,128)(2,1)S(1)} %get-tuple-element.32), channel_id=1, source_target_pairs={{0,24},{8,0},{16,8},{24,16},{1,25},{9,1},{17,9},{25,17},{2,26},{10... | collective-permute-start | bytes 307208 | tf_op jit(solution)/shard_map/ppermute | solution.py:275
  7.7 1.7 %operands.1 = (bf16[160,2560]{1,0:T(8,128)(2,1)S(1)}, bf16[240,2560]{1,0:T(8,128)(2,1)S(1)}, bf16[5,128,128]{2,1,0:T(8,128)(2,1)S(1)}, bf16[5,128,128]{2,1,0:T(8,128)(2,1)S(1)}) custom-call(bf16[1,80,2560]{2,1,0:T(8,128)(2,1)} %refs_0_.2, bf16[1,80,2560]{2,1,0:T(8,128)(2,1)} %refs_1_.1, bf16[1,80,2560]{2,1,0:T(8,128)(2,1)} %refs_2_.1, ...), custom_call_target="tpu_custom_call" | custom-call | bytes 4751360 | tf_op jit(solution)/shard_map/operands/pallas_call | solution.py:219
  9.4 1.9 %collective-permute-start.1 = (bf16[160,640]{1,0:T(8,128)(2,1)S(1)}, bf16[160,640]{1,0:T(8,128)(2,1)S(1)}, u32[]{:S(2)}, u32[]{:S(2)}) collective-permute-start(bf16[160,640]{1,0:T(8,128)(2,1)S(1)} %early.1.refs_4_), channel_id=1, source_target_pairs={{32,0},{64,32},{96,64},{128,96},{160,128},{192,160},{224,192},{33,... | collective-permute-start | bytes 614408 | tf_op jit(solution)/shard_map/ppermute | solution.py:38
  11.4 2.5 %collective-permute-start.4 = (bf16[160,640]{1,0:T(8,128)(2,1)S(1)}, bf16[160,640]{1,0:T(8,128)(2,1)S(1)}, u32[]{:S(2)}, u32[]{:S(2)}) collective-permute-start(bf16[160,640]{1,0:T(8,128)(2,1)S(1)} %late.1.refs_5_), channel_id=1, source_target_pairs={{32,0},{64,32},{96,64},{128,96},{160,128},{192,160},{224,192},{33,... | collective-permute-start | bytes 614408 | tf_op jit(solution)/shard_map/ppermute | solution.py:38
  14.0 1.8 %collective-permute-start.7 = (bf16[240,2560]{1,0:T(8,128)(2,1)S(1)}, bf16[240,2560]{1,0:T(8,128)(2,1)S(1)}, u32[]{:S(2)}, u32[]{:S(2)}) collective-permute-start(bf16[240,2560]{1,0:T(8,128)(2,1)S(1)} %get-tuple-element.36), channel_id=1, source_target_pairs={{0,24},{8,0},{16,8},{24,16},{1,25},{9,1},{17,9},{25,17},{2,26},{10... | collective-permute-start | bytes 3686408 | tf_op jit(solution)/shard_map/ppermute | solution.py:275
  16.1 2.3 %collective-permute-start.5 = (bf16[80,2560]{1,0:T(8,128)(2,1)S(1)}, bf16[80,2560]{1,0:T(8,128)(2,1)S(1)}, u32[]{:S(2)}, u32[]{:S(2)}) collective-permute-start(bf16[80,2560]{1,0:T(8,128)(2,1)S(1)} %bitcast.5), channel_id=1, source_target_pairs={{0,16},{8,24},{16,0},{24,8},{1,17},{9,25},{17,1},{25,9},{2,18},{10... | collective-permute-start | bytes 1228808 | tf_op jit(solution)/shard_map/ppermute | solution.py:275
  18.9 40.6 %all-gather.4 = f16[2624,640]{1,0:T(8,128)(2,1)S(1)} all-gather(f16[328,640]{1,0:T(8,128)(2,1)S(1)} %convert_element_type.12), channel_id=2, replica_groups=mesh['layer'=8,'y'=4,'z'=8] {'z'}, dimensions={0}, use_global_device_ids=true | all-gather | bytes 3778560 | tf_op jit(solution)/shard_map/all_gather | solution.py:303
  60.2 1.6 %reduced.1 = bf16[328,640]{1,0:T(8,128)(2,1)S(1)} custom-call(bf16[8,328,640]{2,1,0:T(8,128)(2,1)S(1)} %bitcast.3, bf16[80,2560]{1,0:T(8,128)(2,1)S(1)} %bitcast.6, bf16[80,2560]{1,0:T(8,128)(2,1)S(1)} %collective-permute-done.5.refs_1_, bf16[240,2560]{1,0:T(8,128)(2,1)S(1)} %collective-permute-done.6.refs_2_.refs_1_, ...), custom_call_target="tpu_custom_call" | custom-call | flops 1048576000 | bytes 7464960 | tf_op jit(solution)/shard_map/reduced/pallas_call | solution.py:20
  62.0 36.3 %all-gather.5 = f16[2624,640]{1,0:T(8,128)(2,1)S(1)} all-gather(f16[328,640]{1,0:T(8,128)(2,1)S(1)} %convert_element_type.14), channel_id=3, replica_groups=mesh['layer'=8,'y'=4,'z'=8] {'z'}, dimensions={0}, use_global_device_ids=true | all-gather | bytes 3778560 | tf_op jit(solution)/shard_map/all_gather | solution.py:303
  98.3 0.6 convert_element_type.17
  99.0 1.2 pushed_a.1
  100.1 1.9 %collective-permute-start.10 = (bf16[160,640]{1,0:T(8,128)(2,1)S(1)}, bf16[160,640]{1,0:T(8,128)(2,1)S(1)}, u32[]{:S(2)}, u32[]{:S(2)}) collective-permute-start(bf16[160,640]{1,0:T(8,128)(2,1)S(1)} %get-tuple-element.41), channel_id=1, source_target_pairs={{0,32},{32,64},{64,96},{96,128},{128,160},{160,192},{192,224},{1,3... | collective-permute-start | bytes 614408 | tf_op jit(solution)/shard_map/ppermute | solution.py:38
  102.1 1.1 pushed_b.1
  103.1 3.5 %collective-permute-start.9 = (bf16[160,640]{1,0:T(8,128)(2,1)S(1)}, bf16[160,640]{1,0:T(8,128)(2,1)S(1)}, u32[]{:S(2)}, u32[]{:S(2)}) collective-permute-start(bf16[160,640]{1,0:T(8,128)(2,1)S(1)} %pushed_b.1), channel_id=1, source_target_pairs={{0,32},{32,64},{64,96},{96,128},{128,160},{160,192},{192,224},{1,3... | collective-permute-start | bytes 614408 | tf_op jit(solution)/shard_map/ppermute | solution.py:38
  106.6 0.9 local_a.1.local_ref
  107.6 2.7 %collective-permute-start.11 = (bf16[80,640]{1,0:T(8,128)(2,1)S(1)}, bf16[80,640]{1,0:T(8,128)(2,1)S(1)}, u32[]{:S(2)}, u32[]{:S(2)}) collective-permute-start(bf16[80,640]{1,0:T(8,128)(2,1)S(1)} %get-tuple-element.42), channel_id=1, source_target_pairs={{0,16},{8,24},{16,0},{24,8},{1,17},{9,25},{17,1},{25,9},{2,18},{10... | collective-permute-start | bytes 307208 | tf_op jit(solution)/shard_map/ppermute | solution.py:275
  110.4 0.9 update_b.1
  111.3 3.3 %collective-permute-start.13 = (bf16[80,640]{1,0:T(8,128)(2,1)S(1)}, bf16[80,640]{1,0:T(8,128)(2,1)S(1)}, u32[]{:S(2)}, u32[]{:S(2)}) collective-permute-start(bf16[80,640]{1,0:T(8,128)(2,1)S(1)} %get-tuple-element.44), channel_id=1, source_target_pairs={{0,24},{8,0},{16,8},{24,16},{1,25},{9,1},{17,9},{25,17},{2,26},{10... | collective-permute-start | bytes 307208 | tf_op jit(solution)/shard_map/ppermute | solution.py:275
  114.6 1.6 %collective-permute-done.12.refs_2_ = bf16[80,640]{1,0:T(8,128)(2,1)S(1)} collective-permute-done((bf16[80,640]{1,0:T(8,128)(2,1)S(1)}, bf16[80,640]{1,0:T(8,128)(2,1)S(1)}, u32[]{:S(2)}, u32[]{:S(2)}) %collective-permute-start.12) | collective-permute-done | bytes 102432 | tf_op jit(solution)/shard_map/ppermute | solution.py:275
  116.2 0.6 collective-permute-done.13.refs_3_
  116.9 0.8 join.1
  (24 shorter events, 1.7 us)
Async XLA Ops:
  0.0 16.1 %copy-start = (bf16[1,80,2560]{2,1,0:T(8,128)(2,1)S(1)}, bf16[1,80,2560]{2,1,0:T(8,128)(2,1)}, u32[]{:S(2)}) copy-start(bf16[1,80,2560]{2,1,0:T(8,128)(2,1)} %refs_0_.2) | copy-start | bytes 1228804
  1.1 8.3 %collective-permute-start = (bf16[80,640]{1,0:T(8,128)(2,1)S(1)}, bf16[80,640]{1,0:T(8,128)(2,1)S(1)}, u32[]{:S(2)}, u32[]{:S(2)}) collective-permute-start(bf16[80,640]{1,0:T(8,128)(2,1)S(1)} %get-tuple-element.26), channel_id=1, source_target_pairs={{0,16},{8,24},{16,0},{24,8},{1,17},{9,25},{17,1},{25,9},{2,18},{10... | collective-permute-start | bytes 307208 | tf_op jit(solution)/shard_map/ppermute | solution.py:275
  4.4 6.9 %collective-permute-start.2 = (bf16[80,640]{1,0:T(8,128)(2,1)S(1)}, bf16[80,640]{1,0:T(8,128)(2,1)S(1)}, u32[]{:S(2)}, u32[]{:S(2)}) collective-permute-start(bf16[80,640]{1,0:T(8,128)(2,1)S(1)} %get-tuple-element.31), channel_id=1, source_target_pairs={{0,8},{8,16},{16,24},{24,0},{1,9},{9,17},{17,25},{25,1},{2,10},{10... | collective-permute-start | bytes 307208 | tf_op jit(solution)/shard_map/ppermute | solution.py:275
  5.1 6.3 %collective-permute-start.3 = (bf16[80,640]{1,0:T(8,128)(2,1)S(1)}, bf16[80,640]{1,0:T(8,128)(2,1)S(1)}, u32[]{:S(2)}, u32[]{:S(2)}) collective-permute-start(bf16[80,640]{1,0:T(8,128)(2,1)S(1)} %get-tuple-element.32), channel_id=1, source_target_pairs={{0,24},{8,0},{16,8},{24,16},{1,25},{9,1},{17,9},{25,17},{2,26},{10... | collective-permute-start | bytes 307208 | tf_op jit(solution)/shard_map/ppermute | solution.py:275
  9.4 8.9 %collective-permute-start.1 = (bf16[160,640]{1,0:T(8,128)(2,1)S(1)}, bf16[160,640]{1,0:T(8,128)(2,1)S(1)}, u32[]{:S(2)}, u32[]{:S(2)}) collective-permute-start(bf16[160,640]{1,0:T(8,128)(2,1)S(1)} %early.1.refs_4_), channel_id=1, source_target_pairs={{32,0},{64,32},{96,64},{128,96},{160,128},{192,160},{224,192},{33,... | collective-permute-start | bytes 614408 | tf_op jit(solution)/shard_map/ppermute | solution.py:38
  11.4 6.9 %collective-permute-start.4 = (bf16[160,640]{1,0:T(8,128)(2,1)S(1)}, bf16[160,640]{1,0:T(8,128)(2,1)S(1)}, u32[]{:S(2)}, u32[]{:S(2)}) collective-permute-start(bf16[160,640]{1,0:T(8,128)(2,1)S(1)} %late.1.refs_5_), channel_id=1, source_target_pairs={{32,0},{64,32},{96,64},{128,96},{160,128},{192,160},{224,192},{33,... | collective-permute-start | bytes 614408 | tf_op jit(solution)/shard_map/ppermute | solution.py:38
  14.0 46.2 %collective-permute-start.7 = (bf16[240,2560]{1,0:T(8,128)(2,1)S(1)}, bf16[240,2560]{1,0:T(8,128)(2,1)S(1)}, u32[]{:S(2)}, u32[]{:S(2)}) collective-permute-start(bf16[240,2560]{1,0:T(8,128)(2,1)S(1)} %get-tuple-element.36), channel_id=1, source_target_pairs={{0,24},{8,0},{16,8},{24,16},{1,25},{9,1},{17,9},{25,17},{2,26},{10... | collective-permute-start | bytes 3686408 | tf_op jit(solution)/shard_map/ppermute | solution.py:275
  15.8 44.4 %collective-permute-start.6 = (bf16[240,2560]{1,0:T(8,128)(2,1)S(1)}, bf16[240,2560]{1,0:T(8,128)(2,1)S(1)}, u32[]{:S(2)}, u32[]{:S(2)}) collective-permute-start(bf16[240,2560]{1,0:T(8,128)(2,1)S(1)} %get-tuple-element.36), channel_id=1, source_target_pairs={{0,8},{8,16},{16,24},{24,0},{1,9},{9,17},{17,25},{25,1},{2,10},{10... | collective-permute-start | bytes 3686408 | tf_op jit(solution)/shard_map/ppermute | solution.py:275
  16.1 44.1 %collective-permute-start.5 = (bf16[80,2560]{1,0:T(8,128)(2,1)S(1)}, bf16[80,2560]{1,0:T(8,128)(2,1)S(1)}, u32[]{:S(2)}, u32[]{:S(2)}) collective-permute-start(bf16[80,2560]{1,0:T(8,128)(2,1)S(1)} %bitcast.5), channel_id=1, source_target_pairs={{0,16},{8,24},{16,0},{24,8},{1,17},{9,25},{17,1},{25,9},{2,18},{10... | collective-permute-start | bytes 1228808 | tf_op jit(solution)/shard_map/ppermute | solution.py:275
  61.9 37.1 %collective-permute-start.8 = (bf16[240,2560]{1,0:T(8,128)(2,1)S(1)}, bf16[240,2560]{1,0:T(8,128)(2,1)S(1)}, u32[]{:S(2)}, u32[]{:S(2)}) collective-permute-start(bf16[240,2560]{1,0:T(8,128)(2,1)S(1)} %collective-permute-done.7.refs_3_.refs_2_), channel_id=1, source_target_pairs={{0,24},{8,0},{16,8},{24,16},{1,25},{9,1},{17,9},{25,17},{2,26},{10... | collective-permute-start | bytes 3686408 | tf_op jit(solution)/shard_map/ppermute | solution.py:275
  100.1 7.4 %collective-permute-start.10 = (bf16[160,640]{1,0:T(8,128)(2,1)S(1)}, bf16[160,640]{1,0:T(8,128)(2,1)S(1)}, u32[]{:S(2)}, u32[]{:S(2)}) collective-permute-start(bf16[160,640]{1,0:T(8,128)(2,1)S(1)} %get-tuple-element.41), channel_id=1, source_target_pairs={{0,32},{32,64},{64,96},{96,128},{128,160},{160,192},{192,224},{1,3... | collective-permute-start | bytes 614408 | tf_op jit(solution)/shard_map/ppermute | solution.py:38
  103.1 7.2 %collective-permute-start.9 = (bf16[160,640]{1,0:T(8,128)(2,1)S(1)}, bf16[160,640]{1,0:T(8,128)(2,1)S(1)}, u32[]{:S(2)}, u32[]{:S(2)}) collective-permute-start(bf16[160,640]{1,0:T(8,128)(2,1)S(1)} %pushed_b.1), channel_id=1, source_target_pairs={{0,32},{32,64},{64,96},{96,128},{128,160},{160,192},{192,224},{1,3... | collective-permute-start | bytes 614408 | tf_op jit(solution)/shard_map/ppermute | solution.py:38
  107.6 7.0 %collective-permute-start.11 = (bf16[80,640]{1,0:T(8,128)(2,1)S(1)}, bf16[80,640]{1,0:T(8,128)(2,1)S(1)}, u32[]{:S(2)}, u32[]{:S(2)}) collective-permute-start(bf16[80,640]{1,0:T(8,128)(2,1)S(1)} %get-tuple-element.42), channel_id=1, source_target_pairs={{0,16},{8,24},{16,0},{24,8},{1,17},{9,25},{17,1},{25,9},{2,18},{10... | collective-permute-start | bytes 307208 | tf_op jit(solution)/shard_map/ppermute | solution.py:275
  110.4 5.9 %collective-permute-start.12 = (bf16[80,640]{1,0:T(8,128)(2,1)S(1)}, bf16[80,640]{1,0:T(8,128)(2,1)S(1)}, u32[]{:S(2)}, u32[]{:S(2)}) collective-permute-start(bf16[80,640]{1,0:T(8,128)(2,1)S(1)} %get-tuple-element.43), channel_id=1, source_target_pairs={{0,8},{8,16},{16,24},{24,0},{1,9},{9,17},{17,25},{25,1},{2,10},{10... | collective-permute-start | bytes 307208 | tf_op jit(solution)/shard_map/ppermute | solution.py:275
  111.3 5.6 %collective-permute-start.13 = (bf16[80,640]{1,0:T(8,128)(2,1)S(1)}, bf16[80,640]{1,0:T(8,128)(2,1)S(1)}, u32[]{:S(2)}, u32[]{:S(2)}) collective-permute-start(bf16[80,640]{1,0:T(8,128)(2,1)S(1)} %get-tuple-element.44), channel_id=1, source_target_pairs={{0,24},{8,0},{16,8},{24,16},{1,25},{9,1},{17,9},{25,17},{2,26},{10... | collective-permute-start | bytes 307208 | tf_op jit(solution)/shard_map/ppermute | solution.py:275

commit v17 on v16

--- a/solution.py
+++ b/solution.py
@@ -246,17 +246,16 @@
     blocks = out_inverse.shape[1] // shards
     table = jax.ShapeDtypeStruct((blocks, BLK, BLK), BF)
 
-    def kernel(rows_ref, first_ref, second_ref, inverse_ref, coupling_ref, pair_ref, trio_ref, inv_ref, psi_ref):
+    def kernel(*refs):
+        row_refs, (inverse_ref, coupling_ref, trio_ref, inv_ref, psi_ref) = refs[:3], refs[3:]
         mine = pl.ds(lax.axis_index("y") * blocks, blocks)
-        for i, ref in enumerate((rows_ref, first_ref, second_ref)):
+        for i, ref in enumerate(row_refs):
             yield ref.at[0], trio_ref.at[pl.ds(i * rows, rows), :]
-            if i:
-                yield ref.at[0], pair_ref.at[pl.ds((i - 1) * rows, rows), :]
         yield coupling_ref.at[0, mine], psi_ref
         yield inverse_ref.at[0, mine], inv_ref
 
-    out = (like(2 * rows, width, BF), like(3 * rows, width, BF), table, table)
-    return copies(kernel, out, "operands", [in_coupling, in_inverse, in_carry, out_inverse, out_coupling], 7)
+    out = (like(3 * rows, width, BF), table, table)
+    return copies(kernel, out, "operands", [in_coupling, in_inverse, in_carry, out_inverse, out_coupling], 5)
 
 
 def stacked(pieces, name):
@@ -308,16 +307,16 @@
     slices = column_blocks(gradient, shards)
     pieces = exchange(slices)
     first = after(in_coupling, slices[0])
-    pair, trio, inv, psi = operands(first, in_inverse, in_carry, out_inverse, out_coupling, shards)
+    trio, inv, psi = operands(first, in_inverse, in_carry, out_inverse, out_coupling, shards)
     half = shards // 2
-    grads = [stacked(lax.optimization_barrier((*pieces[:half], pair))[:half], "early"), stacked(pieces[half:], "late")]
+    grads = [stacked(lax.optimization_barrier((*pieces[:half], trio))[:half], "early"), stacked(pieces[half:], "late")]
     above = [hop_layer(grad, -1) for grad in grads]
-    pair, trio, own = lax.optimization_barrier((pair, trio, in_coupling[0], *grads))[:3]
+    trio, own = lax.optimization_barrier((trio, in_coupling[0], *grads))[:2]
     ahead, behind = hop_y(trio, 1), hop_y(trio, -1)
-    coupling = [own, hop_y(own, 2), ahead, behind]
+    coupling = [trio, hop_y(own, 2), ahead, behind]
     near = near_tile(above, psi, shards)
     reduced = reduced_tile(gather_panel(near), coupling, grads, shards)
-    factors = [pair, hop_y(behind, -1), ahead, behind]
+    factors = [trio, hop_y(behind, -1), ahead, behind]
     early, late = halves_of(factors)
     rows = own.shape[0]
     pushed_a, panel = product_rows(gather_panel(reduced), early, [inv, psi], rows, 1, BF, "pushed_a", shards)

time: 119 us -> 118 us (level)
  no operation moved by 1% of the time
where the time goes in v17:
time: 118 us
  blocking collectives  76.7 us (65%)
  starting transfers between devices  27.6 us (23%)
  Pallas kernels  9.52 us (8%)
  waiting for transfers between devices  2.28 us (2%)
  other arithmetic  1.42 us (1%)
    all_gather x2, blocking collectives, gather_panel(): return lax.all_gather(tile.astype(HALF), 'z', axis=0).astype(BF)  76.7 us
    ppermute x10, starting transfers between devices, hop_y(): return lax.ppermute(x, 'y', [(i, (i + by) % size) for i in range(size)])  17.4 us
    ppermute x4, starting transfers between devices, hop_layer(): lax.ppermute(x, 'layer', [(i, i + by) for i in range(size) if 0 <= i + by...  10.1 us
    pallas_call x9, Pallas kernels, call(): pl.pallas_call(kernel, out_shape=out, in_specs=[HBM if i in far else VMEM...  6.23 us
    pallas_call x3, Pallas kernels, copies(): pl.pallas_call(body, out_shape=out, in_specs=[near] * len(operands), out_...  3.28 us
  transfers between devices with their start and end apart: 14, of which 2 were waited for; matrix products, arithmetic and copies ran while one was open for 1% of the time, Pallas kernels for 4%

profile of v17, /device:TPU:2, one launch (start us, length us, event | category | flops | bytes accessed | tf_op | source)
XLA Modules:
  0.0 117.6 jit_solution(5177307327819779962)
XLA Ops:
  0.0 1.1 blocks.1
  1.1 3.3 %collective-permute-start = (bf16[80,640]{1,0:T(8,128)(2,1)S(1)}, bf16[80,640]{1,0:T(8,128)(2,1)S(1)}, u32[]{:S(2)}, u32[]{:S(2)}) collective-permute-start(bf16[80,640]{1,0:T(8,128)(2,1)S(1)} %get-tuple-element.24), channel_id=1, source_target_pairs={{0,16},{8,24},{16,0},{24,8},{1,17},{9,25},{17,1},{25,9},{2,18},{10... | collective-permute-start | bytes 307208 | tf_op jit(solution)/shard_map/ppermute | solution.py:274
  4.4 0.7 collective-permute-start.2
  5.1 2.6 %collective-permute-start.3 = (bf16[80,640]{1,0:T(8,128)(2,1)S(1)}, bf16[80,640]{1,0:T(8,128)(2,1)S(1)}, u32[]{:S(2)}, u32[]{:S(2)}) collective-permute-start(bf16[80,640]{1,0:T(8,128)(2,1)S(1)} %get-tuple-element.30), channel_id=1, source_target_pairs={{0,24},{8,0},{16,8},{24,16},{1,25},{9,1},{17,9},{25,17},{2,26},{10... | collective-permute-start | bytes 307208 | tf_op jit(solution)/shard_map/ppermute | solution.py:274
  7.7 1.4 %operands.1 = (bf16[240,2560]{1,0:T(8,128)(2,1)S(1)}, bf16[5,128,128]{2,1,0:T(8,128)(2,1)S(1)}, bf16[5,128,128]{2,1,0:T(8,128)(2,1)S(1)}) custom-call(bf16[1,80,2560]{2,1,0:T(8,128)(2,1)} %refs_0_.2, bf16[1,80,2560]{2,1,0:T(8,128)(2,1)} %refs_1_.1, bf16[1,80,2560]{2,1,0:T(8,128)(2,1)} %refs_2_.1, bf16[1,20,128,128]{3,2,1,0:T(8,128)(2,1)} %refs_3_.1, ...), custom_call_target="tpu_custom_call" | custom-call | bytes 3112960 | tf_op jit(solution)/shard_map/operands/pallas_call | solution.py:219
  9.1 1.9 %collective-permute-start.1 = (bf16[160,640]{1,0:T(8,128)(2,1)S(1)}, bf16[160,640]{1,0:T(8,128)(2,1)S(1)}, u32[]{:S(2)}, u32[]{:S(2)}) collective-permute-start(bf16[160,640]{1,0:T(8,128)(2,1)S(1)} %early.1.refs_4_), channel_id=1, source_target_pairs={{32,0},{64,32},{96,64},{128,96},{160,128},{192,160},{224,192},{33,... | collective-permute-start | bytes 614408 | tf_op jit(solution)/shard_map/ppermute | solution.py:38
  11.1 2.8 %collective-permute-start.4 = (bf16[160,640]{1,0:T(8,128)(2,1)S(1)}, bf16[160,640]{1,0:T(8,128)(2,1)S(1)}, u32[]{:S(2)}, u32[]{:S(2)}) collective-permute-start(bf16[160,640]{1,0:T(8,128)(2,1)S(1)} %late.1.refs_5_), channel_id=1, source_target_pairs={{32,0},{64,32},{96,64},{128,96},{160,128},{192,160},{224,192},{33,... | collective-permute-start | bytes 614408 | tf_op jit(solution)/shard_map/ppermute | solution.py:38
  13.9 1.9 %collective-permute-start.7 = (bf16[240,2560]{1,0:T(8,128)(2,1)S(1)}, bf16[240,2560]{1,0:T(8,128)(2,1)S(1)}, u32[]{:S(2)}, u32[]{:S(2)}) collective-permute-start(bf16[240,2560]{1,0:T(8,128)(2,1)S(1)} %get-tuple-element.32.refs_0_.refs_2_), channel_id=1, source_target_pairs={{0,24},{8,0},{16,8},{24,16},{1,25},{9,1},{17,9},{25,17},{2,26},{10... | collective-permute-start | bytes 3686408 | tf_op jit(solution)/shard_map/ppermute | solution.py:274
  16.0 2.4 %collective-permute-start.5 = (bf16[80,2560]{1,0:T(8,128)(2,1)S(1)}, bf16[80,2560]{1,0:T(8,128)(2,1)S(1)}, u32[]{:S(2)}, u32[]{:S(2)}) collective-permute-start(bf16[80,2560]{1,0:T(8,128)(2,1)S(1)} %bitcast.5), channel_id=1, source_target_pairs={{0,16},{8,24},{16,0},{24,8},{1,17},{9,25},{17,1},{25,9},{2,18},{10... | collective-permute-start | bytes 1228808 | tf_op jit(solution)/shard_map/ppermute | solution.py:274
  18.9 40.3 %all-gather.4 = f16[2624,640]{1,0:T(8,128)(2,1)S(1)} all-gather(f16[328,640]{1,0:T(8,128)(2,1)S(1)} %convert_element_type.12), channel_id=2, replica_groups=mesh['layer'=8,'y'=4,'z'=8] {'z'}, dimensions={0}, use_global_device_ids=true | all-gather | bytes 3778560 | tf_op jit(solution)/shard_map/all_gather | solution.py:302
  59.2 0.6 convert_element_type.16
  59.9 1.6 %reduced.1 = bf16[328,640]{1,0:T(8,128)(2,1)S(1)} custom-call(bf16[8,328,640]{2,1,0:T(8,128)(2,1)S(1)} %bitcast.4, bf16[240,2560]{1,0:T(8,128)(2,1)S(1)} %get-tuple-element.32.refs_0_.refs_2_, bf16[80,2560]{1,0:T(8,128)(2,1)S(1)} %collective-permute-done.5.refs_1_, bf16[240,2560]{1,0:T(8,128)(2,1)S(1)} %collective-permute-done.6.refs_2_.refs_1_, ...), custom_call_target="tpu_custom_call" | custom-call | flops 1048576000 | bytes 8284160 | tf_op jit(solution)/shard_map/reduced/pallas_call | solution.py:20
  62.0 36.4 %all-gather.5 = f16[2624,640]{1,0:T(8,128)(2,1)S(1)} all-gather(f16[328,640]{1,0:T(8,128)(2,1)S(1)} %convert_element_type.14), channel_id=3, replica_groups=mesh['layer'=8,'y'=4,'z'=8] {'z'}, dimensions={0}, use_global_device_ids=true | all-gather | bytes 3778560 | tf_op jit(solution)/shard_map/all_gather | solution.py:302
  98.3 0.6 convert_element_type.17
  99.0 1.2 pushed_a.1
  100.2 1.9 %collective-permute-start.10 = (bf16[160,640]{1,0:T(8,128)(2,1)S(1)}, bf16[160,640]{1,0:T(8,128)(2,1)S(1)}, u32[]{:S(2)}, u32[]{:S(2)}) collective-permute-start(bf16[160,640]{1,0:T(8,128)(2,1)S(1)} %get-tuple-element.37), channel_id=1, source_target_pairs={{0,32},{32,64},{64,96},{96,128},{128,160},{160,192},{192,224},{1,3... | collective-permute-start | bytes 614408 | tf_op jit(solution)/shard_map/ppermute | solution.py:38
  102.1 1.1 pushed_b.1
  103.1 3.5 %collective-permute-start.9 = (bf16[160,640]{1,0:T(8,128)(2,1)S(1)}, bf16[160,640]{1,0:T(8,128)(2,1)S(1)}, u32[]{:S(2)}, u32[]{:S(2)}) collective-permute-start(bf16[160,640]{1,0:T(8,128)(2,1)S(1)} %pushed_b.1), channel_id=1, source_target_pairs={{0,32},{32,64},{64,96},{96,128},{128,160},{160,192},{192,224},{1,3... | collective-permute-start | bytes 614408 | tf_op jit(solution)/shard_map/ppermute | solution.py:38
  106.6 0.9 local_a.1.local_ref
  107.6 2.7 %collective-permute-start.11 = (bf16[80,640]{1,0:T(8,128)(2,1)S(1)}, bf16[80,640]{1,0:T(8,128)(2,1)S(1)}, u32[]{:S(2)}, u32[]{:S(2)}) collective-permute-start(bf16[80,640]{1,0:T(8,128)(2,1)S(1)} %get-tuple-element.38), channel_id=1, source_target_pairs={{0,16},{8,24},{16,0},{24,8},{1,17},{9,25},{17,1},{25,9},{2,18},{10... | collective-permute-start | bytes 307208 | tf_op jit(solution)/shard_map/ppermute | solution.py:274
  110.3 0.9 update_b.1
  111.3 3.3 %collective-permute-start.13 = (bf16[80,640]{1,0:T(8,128)(2,1)S(1)}, bf16[80,640]{1,0:T(8,128)(2,1)S(1)}, u32[]{:S(2)}, u32[]{:S(2)}) collective-permute-start(bf16[80,640]{1,0:T(8,128)(2,1)S(1)} %get-tuple-element.40), channel_id=1, source_target_pairs={{0,24},{8,0},{16,8},{24,16},{1,25},{9,1},{17,9},{25,17},{2,26},{10... | collective-permute-start | bytes 307208 | tf_op jit(solution)/shard_map/ppermute | solution.py:274
  114.6 1.6 %collective-permute-done.12.refs_2_ = bf16[80,640]{1,0:T(8,128)(2,1)S(1)} collective-permute-done((bf16[80,640]{1,0:T(8,128)(2,1)S(1)}, bf16[80,640]{1,0:T(8,128)(2,1)S(1)}, u32[]{:S(2)}, u32[]{:S(2)}) %collective-permute-start.12) | collective-permute-done | bytes 102432 | tf_op jit(solution)/shard_map/ppermute | solution.py:274
  116.9 0.8 join.1
  (24 shorter events, 1.9 us)
Async XLA Ops:
  0.0 16.0 %copy-start = (bf16[1,80,2560]{2,1,0:T(8,128)(2,1)S(1)}, bf16[1,80,2560]{2,1,0:T(8,128)(2,1)}, u32[]{:S(2)}) copy-start(bf16[1,80,2560]{2,1,0:T(8,128)(2,1)} %refs_0_.2) | copy-start | bytes 1228804
  1.1 7.9 %collective-permute-start = (bf16[80,640]{1,0:T(8,128)(2,1)S(1)}, bf16[80,640]{1,0:T(8,128)(2,1)S(1)}, u32[]{:S(2)}, u32[]{:S(2)}) collective-permute-start(bf16[80,640]{1,0:T(8,128)(2,1)S(1)} %get-tuple-element.24), channel_id=1, source_target_pairs={{0,16},{8,24},{16,0},{24,8},{1,17},{9,25},{17,1},{25,9},{2,18},{10... | collective-permute-start | bytes 307208 | tf_op jit(solution)/shard_map/ppermute | solution.py:274
  4.4 6.6 %collective-permute-start.2 = (bf16[80,640]{1,0:T(8,128)(2,1)S(1)}, bf16[80,640]{1,0:T(8,128)(2,1)S(1)}, u32[]{:S(2)}, u32[]{:S(2)}) collective-permute-start(bf16[80,640]{1,0:T(8,128)(2,1)S(1)} %get-tuple-element.29), channel_id=1, source_target_pairs={{0,8},{8,16},{16,24},{24,0},{1,9},{9,17},{17,25},{25,1},{2,10},{10... | collective-permute-start | bytes 307208 | tf_op jit(solution)/shard_map/ppermute | solution.py:274
  5.1 5.9 %collective-permute-start.3 = (bf16[80,640]{1,0:T(8,128)(2,1)S(1)}, bf16[80,640]{1,0:T(8,128)(2,1)S(1)}, u32[]{:S(2)}, u32[]{:S(2)}) collective-permute-start(bf16[80,640]{1,0:T(8,128)(2,1)S(1)} %get-tuple-element.30), channel_id=1, source_target_pairs={{0,24},{8,0},{16,8},{24,16},{1,25},{9,1},{17,9},{25,17},{2,26},{10... | collective-permute-start | bytes 307208 | tf_op jit(solution)/shard_map/ppermute | solution.py:274
  9.1 9.3 %collective-permute-start.1 = (bf16[160,640]{1,0:T(8,128)(2,1)S(1)}, bf16[160,640]{1,0:T(8,128)(2,1)S(1)}, u32[]{:S(2)}, u32[]{:S(2)}) collective-permute-start(bf16[160,640]{1,0:T(8,128)(2,1)S(1)} %early.1.refs_4_), channel_id=1, source_target_pairs={{32,0},{64,32},{96,64},{128,96},{160,128},{192,160},{224,192},{33,... | collective-permute-start | bytes 614408 | tf_op jit(solution)/shard_map/ppermute | solution.py:38
  11.1 7.3 %collective-permute-start.4 = (bf16[160,640]{1,0:T(8,128)(2,1)S(1)}, bf16[160,640]{1,0:T(8,128)(2,1)S(1)}, u32[]{:S(2)}, u32[]{:S(2)}) collective-permute-start(bf16[160,640]{1,0:T(8,128)(2,1)S(1)} %late.1.refs_5_), channel_id=1, source_target_pairs={{32,0},{64,32},{96,64},{128,96},{160,128},{192,160},{224,192},{33,... | collective-permute-start | bytes 614408 | tf_op jit(solution)/shard_map/ppermute | solution.py:38
  13.9 46.0 %collective-permute-start.7 = (bf16[240,2560]{1,0:T(8,128)(2,1)S(1)}, bf16[240,2560]{1,0:T(8,128)(2,1)S(1)}, u32[]{:S(2)}, u32[]{:S(2)}) collective-permute-start(bf16[240,2560]{1,0:T(8,128)(2,1)S(1)} %get-tuple-element.32.refs_0_.refs_2_), channel_id=1, source_target_pairs={{0,24},{8,0},{16,8},{24,16},{1,25},{9,1},{17,9},{25,17},{2,26},{10... | collective-permute-start | bytes 3686408 | tf_op jit(solution)/shard_map/ppermute | solution.py:274
  15.8 44.1 %collective-permute-start.6 = (bf16[240,2560]{1,0:T(8,128)(2,1)S(1)}, bf16[240,2560]{1,0:T(8,128)(2,1)S(1)}, u32[]{:S(2)}, u32[]{:S(2)}) collective-permute-start(bf16[240,2560]{1,0:T(8,128)(2,1)S(1)} %get-tuple-element.32.refs_0_.refs_2_), channel_id=1, source_target_pairs={{0,8},{8,16},{16,24},{24,0},{1,9},{9,17},{17,25},{25,1},{2,10},{10... | collective-permute-start | bytes 3686408 | tf_op jit(solution)/shard_map/ppermute | solution.py:274
  16.0 43.9 %collective-permute-start.5 = (bf16[80,2560]{1,0:T(8,128)(2,1)S(1)}, bf16[80,2560]{1,0:T(8,128)(2,1)S(1)}, u32[]{:S(2)}, u32[]{:S(2)}) collective-permute-start(bf16[80,2560]{1,0:T(8,128)(2,1)S(1)} %bitcast.5), channel_id=1, source_target_pairs={{0,16},{8,24},{16,0},{24,8},{1,17},{9,25},{17,1},{25,9},{2,18},{10... | collective-permute-start | bytes 1228808 | tf_op jit(solution)/shard_map/ppermute | solution.py:274
  61.6 37.4 %collective-permute-start.8 = (bf16[240,2560]{1,0:T(8,128)(2,1)S(1)}, bf16[240,2560]{1,0:T(8,128)(2,1)S(1)}, u32[]{:S(2)}, u32[]{:S(2)}) collective-permute-start(bf16[240,2560]{1,0:T(8,128)(2,1)S(1)} %collective-permute-done.7.refs_3_.refs_2_), channel_id=1, source_target_pairs={{0,24},{8,0},{16,8},{24,16},{1,25},{9,1},{17,9},{25,17},{2,26},{10... | collective-permute-start | bytes 3686408 | tf_op jit(solution)/shard_map/ppermute | solution.py:274
  100.2 7.4 %collective-permute-start.10 = (bf16[160,640]{1,0:T(8,128)(2,1)S(1)}, bf16[160,640]{1,0:T(8,128)(2,1)S(1)}, u32[]{:S(2)}, u32[]{:S(2)}) collective-permute-start(bf16[160,640]{1,0:T(8,128)(2,1)S(1)} %get-tuple-element.37), channel_id=1, source_target_pairs={{0,32},{32,64},{64,96},{96,128},{128,160},{160,192},{192,224},{1,3... | collective-permute-start | bytes 614408 | tf_op jit(solution)/shard_map/ppermute | solution.py:38
  103.1 7.2 %collective-permute-start.9 = (bf16[160,640]{1,0:T(8,128)(2,1)S(1)}, bf16[160,640]{1,0:T(8,128)(2,1)S(1)}, u32[]{:S(2)}, u32[]{:S(2)}) collective-permute-start(bf16[160,640]{1,0:T(8,128)(2,1)S(1)} %pushed_b.1), channel_id=1, source_target_pairs={{0,32},{32,64},{64,96},{96,128},{128,160},{160,192},{192,224},{1,3... | collective-permute-start | bytes 614408 | tf_op jit(solution)/shard_map/ppermute | solution.py:38
  107.6 7.0 %collective-permute-start.11 = (bf16[80,640]{1,0:T(8,128)(2,1)S(1)}, bf16[80,640]{1,0:T(8,128)(2,1)S(1)}, u32[]{:S(2)}, u32[]{:S(2)}) collective-permute-start(bf16[80,640]{1,0:T(8,128)(2,1)S(1)} %get-tuple-element.38), channel_id=1, source_target_pairs={{0,16},{8,24},{16,0},{24,8},{1,17},{9,25},{17,1},{25,9},{2,18},{10... | collective-permute-start | bytes 307208 | tf_op jit(solution)/shard_map/ppermute | solution.py:274
  110.3 5.9 %collective-permute-start.12 = (bf16[80,640]{1,0:T(8,128)(2,1)S(1)}, bf16[80,640]{1,0:T(8,128)(2,1)S(1)}, u32[]{:S(2)}, u32[]{:S(2)}) collective-permute-start(bf16[80,640]{1,0:T(8,128)(2,1)S(1)} %get-tuple-element.39), channel_id=1, source_target_pairs={{0,8},{8,16},{16,24},{24,0},{1,9},{9,17},{17,25},{25,1},{2,10},{10... | collective-permute-start | bytes 307208 | tf_op jit(solution)/shard_map/ppermute | solution.py:274
  111.3 5.6 %collective-permute-start.13 = (bf16[80,640]{1,0:T(8,128)(2,1)S(1)}, bf16[80,640]{1,0:T(8,128)(2,1)S(1)}, u32[]{:S(2)}, u32[]{:S(2)}) collective-permute-start(bf16[80,640]{1,0:T(8,128)(2,1)S(1)} %get-tuple-element.40), channel_id=1, source_target_pairs={{0,24},{8,0},{16,8},{24,16},{1,25},{9,1},{17,9},{25,17},{2,26},{10... | collective-permute-start | bytes 307208 | tf_op jit(solution)/shard_map/ppermute | solution.py:274

commit v18 on v17

--- a/solution.py
+++ b/solution.py
@@ -311,7 +311,8 @@
     half = shards // 2
     grads = [stacked(lax.optimization_barrier((*pieces[:half], trio))[:half], "early"), stacked(pieces[half:], "late")]
     above = [hop_layer(grad, -1) for grad in grads]
-    trio, own = lax.optimization_barrier((trio, in_coupling[0], *grads))[:2]
+    trio = after(trio, *grads)
+    own = trio[: in_coupling.shape[1]]
     ahead, behind = hop_y(trio, 1), hop_y(trio, -1)
     coupling = [trio, hop_y(own, 2), ahead, behind]
     near = near_tile(above, psi, shards)

time: 118 us -> 118 us (level)
  transfers between devices with their start and end apart: 14 -> 14, of which waited for: 2 -> 4; matrix products, arithmetic and copies ran while one was open for 1% -> 1% of each run, Pallas kernels for 4% -> 4%
where the time goes in v18:
time: 118 us
  blocking collectives  76.4 us (65%)
  starting transfers between devices  27.7 us (23%)
  Pallas kernels  9.48 us (8%)
  waiting for transfers between devices  2.35 us (2%)
  other arithmetic  1.42 us (1%)
    all_gather x2, blocking collectives, gather_panel(): return lax.all_gather(tile.astype(HALF), 'z', axis=0).astype(BF)  76.4 us
    ppermute x10, starting transfers between devices, hop_y(): return lax.ppermute(x, 'y', [(i, (i + by) % size) for i in range(size)])  17.6 us
    ppermute x4, starting transfers between devices, hop_layer(): lax.ppermute(x, 'layer', [(i, i + by) for i in range(size) if 0 <= i + by...  10.1 us
    pallas_call x9, Pallas kernels, call(): pl.pallas_call(kernel, out_shape=out, in_specs=[HBM if i in far else VMEM...  6.25 us
    pallas_call x3, Pallas kernels, copies(): pl.pallas_call(body, out_shape=out, in_specs=[near] * len(operands), out_...  3.23 us
  transfers between devices with their start and end apart: 14, of which 4 were waited for; matrix products, arithmetic and copies ran while one was open for 1% of the time, Pallas kernels for 4%

profile of v18, /device:TPU:2, one launch (start us, length us, event | category | flops | bytes accessed | tf_op | source)
XLA Modules:
  0.0 117.6 jit_solution(7475096261212207329)
XLA Ops:
  0.0 1.1 blocks.1
  1.1 3.3 %collective-permute-start = (bf16[80,640]{1,0:T(8,128)(2,1)S(1)}, bf16[80,640]{1,0:T(8,128)(2,1)S(1)}, u32[]{:S(2)}, u32[]{:S(2)}) collective-permute-start(bf16[80,640]{1,0:T(8,128)(2,1)S(1)} %get-tuple-element.23), channel_id=1, source_target_pairs={{0,16},{8,24},{16,0},{24,8},{1,17},{9,25},{17,1},{25,9},{2,18},{10... | collective-permute-start | bytes 307208 | tf_op jit(solution)/shard_map/ppermute | solution.py:274
  4.4 0.7 collective-permute-start.2
  5.0 2.6 %collective-permute-start.3 = (bf16[80,640]{1,0:T(8,128)(2,1)S(1)}, bf16[80,640]{1,0:T(8,128)(2,1)S(1)}, u32[]{:S(2)}, u32[]{:S(2)}) collective-permute-start(bf16[80,640]{1,0:T(8,128)(2,1)S(1)} %get-tuple-element.29), channel_id=1, source_target_pairs={{0,24},{8,0},{16,8},{24,16},{1,25},{9,1},{17,9},{25,17},{2,26},{10... | collective-permute-start | bytes 307208 | tf_op jit(solution)/shard_map/ppermute | solution.py:274
  7.6 1.4 %operands.1 = (bf16[240,2560]{1,0:T(8,128)(2,1)S(1)}, bf16[5,128,128]{2,1,0:T(8,128)(2,1)S(1)}, bf16[5,128,128]{2,1,0:T(8,128)(2,1)S(1)}) custom-call(bf16[1,80,2560]{2,1,0:T(8,128)(2,1)} %refs_0_.2, bf16[1,80,2560]{2,1,0:T(8,128)(2,1)} %refs_1_.1, bf16[1,80,2560]{2,1,0:T(8,128)(2,1)} %refs_2_.1, bf16[1,20,128,128]{3,2,1,0:T(8,128)(2,1)} %refs_3_.1, ...), custom_call_target="tpu_custom_call" | custom-call | bytes 3112960 | tf_op jit(solution)/shard_map/operands/pallas_call | solution.py:219
  9.0 1.9 %collective-permute-start.1 = (bf16[160,640]{1,0:T(8,128)(2,1)S(1)}, bf16[160,640]{1,0:T(8,128)(2,1)S(1)}, u32[]{:S(2)}, u32[]{:S(2)}) collective-permute-start(bf16[160,640]{1,0:T(8,128)(2,1)S(1)} %early.1.refs_4_), channel_id=1, source_target_pairs={{32,0},{64,32},{96,64},{128,96},{160,128},{192,160},{224,192},{33,... | collective-permute-start | bytes 614408 | tf_op jit(solution)/shard_map/ppermute | solution.py:38
  11.0 2.8 %collective-permute-start.4 = (bf16[160,640]{1,0:T(8,128)(2,1)S(1)}, bf16[160,640]{1,0:T(8,128)(2,1)S(1)}, u32[]{:S(2)}, u32[]{:S(2)}) collective-permute-start(bf16[160,640]{1,0:T(8,128)(2,1)S(1)} %late.1.refs_5_), channel_id=1, source_target_pairs={{32,0},{64,32},{96,64},{128,96},{160,128},{192,160},{224,192},{33,... | collective-permute-start | bytes 614408 | tf_op jit(solution)/shard_map/ppermute | solution.py:38
  13.8 1.9 %collective-permute-start.7 = (bf16[240,2560]{1,0:T(8,128)(2,1)S(1)}, bf16[240,2560]{1,0:T(8,128)(2,1)S(1)}, u32[]{:S(2)}, u32[]{:S(2)}) collective-permute-start(bf16[240,2560]{1,0:T(8,128)(2,1)S(1)} %get-tuple-element.31.refs_0_.refs_2_), channel_id=1, source_target_pairs={{0,24},{8,0},{16,8},{24,16},{1,25},{9,1},{17,9},{25,17},{2,26},{10... | collective-permute-start | bytes 3686408 | tf_op jit(solution)/shard_map/ppermute | solution.py:274
  15.9 2.5 %collective-permute-start.5 = (bf16[80,2560]{1,0:T(8,128)(2,1)S(1)}, bf16[80,2560]{1,0:T(8,128)(2,1)S(1)}, u32[]{:S(2)}, u32[]{:S(2)}) collective-permute-start(bf16[80,2560]{1,0:T(8,128)(2,1)S(1)} %slice.3), channel_id=1, source_target_pairs={{0,16},{8,24},{16,0},{24,8},{1,17},{9,25},{17,1},{25,9},{2,18},{10... | collective-permute-start | bytes 1228808 | tf_op jit(solution)/shard_map/ppermute | solution.py:274
  18.9 40.2 %all-gather.4 = f16[2624,640]{1,0:T(8,128)(2,1)S(1)} all-gather(f16[328,640]{1,0:T(8,128)(2,1)S(1)} %convert_element_type.12), channel_id=2, replica_groups=mesh['layer'=8,'y'=4,'z'=8] {'z'}, dimensions={0}, use_global_device_ids=true | all-gather | bytes 3778560 | tf_op jit(solution)/shard_map/all_gather | solution.py:302
  59.1 0.6 convert_element_type.16
  59.8 1.6 %reduced.1 = bf16[328,640]{1,0:T(8,128)(2,1)S(1)} custom-call(bf16[8,328,640]{2,1,0:T(8,128)(2,1)S(1)} %bitcast.3, bf16[240,2560]{1,0:T(8,128)(2,1)S(1)} %get-tuple-element.31.refs_0_.refs_2_, bf16[80,2560]{1,0:T(8,128)(2,1)S(1)} %collective-permute-done.5.refs_1_, bf16[240,2560]{1,0:T(8,128)(2,1)S(1)} %collective-permute-done.6.refs_2_.refs_1_, ...), custom_call_target="tpu_custom_call" | custom-call | flops 1048576000 | bytes 8284160 | tf_op jit(solution)/shard_map/reduced/pallas_call | solution.py:20
  61.5 0.8 collective-permute-start.8
  62.3 36.2 %all-gather.5 = f16[2624,640]{1,0:T(8,128)(2,1)S(1)} all-gather(f16[328,640]{1,0:T(8,128)(2,1)S(1)} %convert_element_type.14), channel_id=3, replica_groups=mesh['layer'=8,'y'=4,'z'=8] {'z'}, dimensions={0}, use_global_device_ids=true | all-gather | bytes 3778560 | tf_op jit(solution)/shard_map/all_gather | solution.py:302
  99.1 1.2 pushed_a.1
  100.3 1.9 %collective-permute-start.10 = (bf16[160,640]{1,0:T(8,128)(2,1)S(1)}, bf16[160,640]{1,0:T(8,128)(2,1)S(1)}, u32[]{:S(2)}, u32[]{:S(2)}) collective-permute-start(bf16[160,640]{1,0:T(8,128)(2,1)S(1)} %get-tuple-element.35), channel_id=1, source_target_pairs={{0,32},{32,64},{64,96},{96,128},{128,160},{160,192},{192,224},{1,3... | collective-permute-start | bytes 614408 | tf_op jit(solution)/shard_map/ppermute | solution.py:38
  102.2 1.1 pushed_b.1
  103.3 3.5 %collective-permute-start.9 = (bf16[160,640]{1,0:T(8,128)(2,1)S(1)}, bf16[160,640]{1,0:T(8,128)(2,1)S(1)}, u32[]{:S(2)}, u32[]{:S(2)}) collective-permute-start(bf16[160,640]{1,0:T(8,128)(2,1)S(1)} %pushed_b.1), channel_id=1, source_target_pairs={{0,32},{32,64},{64,96},{96,128},{128,160},{160,192},{192,224},{1,3... | collective-permute-start | bytes 614408 | tf_op jit(solution)/shard_map/ppermute | solution.py:38
  106.8 0.9 local_a.1.local_ref
  107.8 2.5 %collective-permute-start.11 = (bf16[80,640]{1,0:T(8,128)(2,1)S(1)}, bf16[80,640]{1,0:T(8,128)(2,1)S(1)}, u32[]{:S(2)}, u32[]{:S(2)}) collective-permute-start(bf16[80,640]{1,0:T(8,128)(2,1)S(1)} %get-tuple-element.36), channel_id=1, source_target_pairs={{0,16},{8,24},{16,0},{24,8},{1,17},{9,25},{17,1},{25,9},{2,18},{10... | collective-permute-start | bytes 307208 | tf_op jit(solution)/shard_map/ppermute | solution.py:274
  110.4 0.9 update_b.1
  111.3 3.2 %collective-permute-start.13 = (bf16[80,640]{1,0:T(8,128)(2,1)S(1)}, bf16[80,640]{1,0:T(8,128)(2,1)S(1)}, u32[]{:S(2)}, u32[]{:S(2)}) collective-permute-start(bf16[80,640]{1,0:T(8,128)(2,1)S(1)} %get-tuple-element.38), channel_id=1, source_target_pairs={{0,24},{8,0},{16,8},{24,16},{1,25},{9,1},{17,9},{25,17},{2,26},{10... | collective-permute-start | bytes 307208 | tf_op jit(solution)/shard_map/ppermute | solution.py:274
  114.6 1.8 %collective-permute-done.12.refs_2_ = bf16[80,640]{1,0:T(8,128)(2,1)S(1)} collective-permute-done((bf16[80,640]{1,0:T(8,128)(2,1)S(1)}, bf16[80,640]{1,0:T(8,128)(2,1)S(1)}, u32[]{:S(2)}, u32[]{:S(2)}) %collective-permute-start.12) | collective-permute-done | bytes 102432 | tf_op jit(solution)/shard_map/ppermute | solution.py:274
  116.8 0.8 join.1
  (23 shorter events, 2.1 us)
Async XLA Ops:
  1.1 7.9 %collective-permute-start = (bf16[80,640]{1,0:T(8,128)(2,1)S(1)}, bf16[80,640]{1,0:T(8,128)(2,1)S(1)}, u32[]{:S(2)}, u32[]{:S(2)}) collective-permute-start(bf16[80,640]{1,0:T(8,128)(2,1)S(1)} %get-tuple-element.23), channel_id=1, source_target_pairs={{0,16},{8,24},{16,0},{24,8},{1,17},{9,25},{17,1},{25,9},{2,18},{10... | collective-permute-start | bytes 307208 | tf_op jit(solution)/shard_map/ppermute | solution.py:274
  4.4 6.6 %collective-permute-start.2 = (bf16[80,640]{1,0:T(8,128)(2,1)S(1)}, bf16[80,640]{1,0:T(8,128)(2,1)S(1)}, u32[]{:S(2)}, u32[]{:S(2)}) collective-permute-start(bf16[80,640]{1,0:T(8,128)(2,1)S(1)} %get-tuple-element.28), channel_id=1, source_target_pairs={{0,8},{8,16},{16,24},{24,0},{1,9},{9,17},{17,25},{25,1},{2,10},{10... | collective-permute-start | bytes 307208 | tf_op jit(solution)/shard_map/ppermute | solution.py:274
  5.0 5.9 %collective-permute-start.3 = (bf16[80,640]{1,0:T(8,128)(2,1)S(1)}, bf16[80,640]{1,0:T(8,128)(2,1)S(1)}, u32[]{:S(2)}, u32[]{:S(2)}) collective-permute-start(bf16[80,640]{1,0:T(8,128)(2,1)S(1)} %get-tuple-element.29), channel_id=1, source_target_pairs={{0,24},{8,0},{16,8},{24,16},{1,25},{9,1},{17,9},{25,17},{2,26},{10... | collective-permute-start | bytes 307208 | tf_op jit(solution)/shard_map/ppermute | solution.py:274
  9.0 9.4 %collective-permute-start.1 = (bf16[160,640]{1,0:T(8,128)(2,1)S(1)}, bf16[160,640]{1,0:T(8,128)(2,1)S(1)}, u32[]{:S(2)}, u32[]{:S(2)}) collective-permute-start(bf16[160,640]{1,0:T(8,128)(2,1)S(1)} %early.1.refs_4_), channel_id=1, source_target_pairs={{32,0},{64,32},{96,64},{128,96},{160,128},{192,160},{224,192},{33,... | collective-permute-start | bytes 614408 | tf_op jit(solution)/shard_map/ppermute | solution.py:38
  11.0 7.4 %collective-permute-start.4 = (bf16[160,640]{1,0:T(8,128)(2,1)S(1)}, bf16[160,640]{1,0:T(8,128)(2,1)S(1)}, u32[]{:S(2)}, u32[]{:S(2)}) collective-permute-start(bf16[160,640]{1,0:T(8,128)(2,1)S(1)} %late.1.refs_5_), channel_id=1, source_target_pairs={{32,0},{64,32},{96,64},{128,96},{160,128},{192,160},{224,192},{33,... | collective-permute-start | bytes 614408 | tf_op jit(solution)/shard_map/ppermute | solution.py:38
  13.8 46.0 %collective-permute-start.7 = (bf16[240,2560]{1,0:T(8,128)(2,1)S(1)}, bf16[240,2560]{1,0:T(8,128)(2,1)S(1)}, u32[]{:S(2)}, u32[]{:S(2)}) collective-permute-start(bf16[240,2560]{1,0:T(8,128)(2,1)S(1)} %get-tuple-element.31.refs_0_.refs_2_), channel_id=1, source_target_pairs={{0,24},{8,0},{16,8},{24,16},{1,25},{9,1},{17,9},{25,17},{2,26},{10... | collective-permute-start | bytes 3686408 | tf_op jit(solution)/shard_map/ppermute | solution.py:274
  15.7 44.0 %collective-permute-start.6 = (bf16[240,2560]{1,0:T(8,128)(2,1)S(1)}, bf16[240,2560]{1,0:T(8,128)(2,1)S(1)}, u32[]{:S(2)}, u32[]{:S(2)}) collective-permute-start(bf16[240,2560]{1,0:T(8,128)(2,1)S(1)} %get-tuple-element.31.refs_0_.refs_2_), channel_id=1, source_target_pairs={{0,8},{8,16},{16,24},{24,0},{1,9},{9,17},{17,25},{25,1},{2,10},{10... | collective-permute-start | bytes 3686408 | tf_op jit(solution)/shard_map/ppermute | solution.py:274
  15.9 43.8 %collective-permute-start.5 = (bf16[80,2560]{1,0:T(8,128)(2,1)S(1)}, bf16[80,2560]{1,0:T(8,128)(2,1)S(1)}, u32[]{:S(2)}, u32[]{:S(2)}) collective-permute-start(bf16[80,2560]{1,0:T(8,128)(2,1)S(1)} %slice.3), channel_id=1, source_target_pairs={{0,16},{8,24},{16,0},{24,8},{1,17},{9,25},{17,1},{25,9},{2,18},{10... | collective-permute-start | bytes 1228808 | tf_op jit(solution)/shard_map/ppermute | solution.py:274
  61.5 37.7 %collective-permute-start.8 = (bf16[240,2560]{1,0:T(8,128)(2,1)S(1)}, bf16[240,2560]{1,0:T(8,128)(2,1)S(1)}, u32[]{:S(2)}, u32[]{:S(2)}) collective-permute-start(bf16[240,2560]{1,0:T(8,128)(2,1)S(1)} %collective-permute-done.7.refs_3_.refs_2_), channel_id=1, source_target_pairs={{0,24},{8,0},{16,8},{24,16},{1,25},{9,1},{17,9},{25,17},{2,26},{10... | collective-permute-start | bytes 3686408 | tf_op jit(solution)/shard_map/ppermute | solution.py:274
  100.3 7.4 %collective-permute-start.10 = (bf16[160,640]{1,0:T(8,128)(2,1)S(1)}, bf16[160,640]{1,0:T(8,128)(2,1)S(1)}, u32[]{:S(2)}, u32[]{:S(2)}) collective-permute-start(bf16[160,640]{1,0:T(8,128)(2,1)S(1)} %get-tuple-element.35), channel_id=1, source_target_pairs={{0,32},{32,64},{64,96},{96,128},{128,160},{160,192},{192,224},{1,3... | collective-permute-start | bytes 614408 | tf_op jit(solution)/shard_map/ppermute | solution.py:38
  103.3 7.1 %collective-permute-start.9 = (bf16[160,640]{1,0:T(8,128)(2,1)S(1)}, bf16[160,640]{1,0:T(8,128)(2,1)S(1)}, u32[]{:S(2)}, u32[]{:S(2)}) collective-permute-start(bf16[160,640]{1,0:T(8,128)(2,1)S(1)} %pushed_b.1), channel_id=1, source_target_pairs={{0,32},{32,64},{64,96},{96,128},{128,160},{160,192},{192,224},{1,3... | collective-permute-start | bytes 614408 | tf_op jit(solution)/shard_map/ppermute | solution.py:38
  107.8 6.8 %collective-permute-start.11 = (bf16[80,640]{1,0:T(8,128)(2,1)S(1)}, bf16[80,640]{1,0:T(8,128)(2,1)S(1)}, u32[]{:S(2)}, u32[]{:S(2)}) collective-permute-start(bf16[80,640]{1,0:T(8,128)(2,1)S(1)} %get-tuple-element.36), channel_id=1, source_target_pairs={{0,16},{8,24},{16,0},{24,8},{1,17},{9,25},{17,1},{25,9},{2,18},{10... | collective-permute-start | bytes 307208 | tf_op jit(solution)/shard_map/ppermute | solution.py:274
  110.3 6.1 %collective-permute-start.12 = (bf16[80,640]{1,0:T(8,128)(2,1)S(1)}, bf16[80,640]{1,0:T(8,128)(2,1)S(1)}, u32[]{:S(2)}, u32[]{:S(2)}) collective-permute-start(bf16[80,640]{1,0:T(8,128)(2,1)S(1)} %get-tuple-element.37), channel_id=1, source_target_pairs={{0,8},{8,16},{16,24},{24,0},{1,9},{9,17},{17,25},{25,1},{2,10},{10... | collective-permute-start | bytes 307208 | tf_op jit(solution)/shard_map/ppermute | solution.py:274
  111.3 5.5 %collective-permute-start.13 = (bf16[80,640]{1,0:T(8,128)(2,1)S(1)}, bf16[80,640]{1,0:T(8,128)(2,1)S(1)}, u32[]{:S(2)}, u32[]{:S(2)}) collective-permute-start(bf16[80,640]{1,0:T(8,128)(2,1)S(1)} %get-tuple-element.38), channel_id=1, source_target_pairs={{0,24},{8,0},{16,8},{24,16},{1,25},{9,1},{17,9},{25,17},{2,26},{10... | collective-permute-start | bytes 307208 | tf_op jit(solution)/shard_map/ppermute | solution.py:274
